TPU v7x, 512 devices: a whole 4x8x8 slice. The times are simulated.
512 devices in a mesh: lat: 64 (over z, x, core), lev: 8 (over y).
Axes of the slice: x: 4, y: 8, z: 8, core: 2. Of those that a mesh axis runs over, the one named last changes fastest.
Arguments:
- wind_east: float32 [64, 192, 1152], P('lev', 'lat'), may hold values from -6 to 6
- wind_north: float32 [64, 192, 1152], P('lev', 'lat'), may hold values from -6 to 6
- layer_mass: float32 [64, 192, 1152], P('lev', 'lat'), may hold values from 0.5 to 1.5
- theta_field: float32 [64, 192, 1152], P('lev', 'lat'), may hold values from 0.4 to 2
- surface_height: float32 [192, 1152], P('lat'), may hold values from -6 to 6
- filter_cutoff: int32 [192], replicated, may hold values from 1 to 576, as said below
Outputs:
- new_east: float32 [64, 192, 1152], P('lev', 'lat')
- new_north: float32 [64, 192, 1152], P('lev', 'lat')
- new_mass: float32 [64, 192, 1152], P('lev', 'lat')
- new_heat: float32 [64, 192, 1152], P('lev', 'lat')
- height: float32 [64, 192, 1152], P('lev', 'lat')
Inputs may be any that keep to these rules, and one draw needn't show every extreme that they name: filter_cutoff[j] equals 1152/2 (no filtering) for every latitude j with 24 <= j < 168; only the first and last 24 latitudes are filtered.
All inputs are finite; a program needn't handle non-finite values.
Results may differ from a plain program's by a relative error of at most 0.0003.
Values sent between devices are 32-bit elements; how exact they have to be, the bound alone decides.
No kernel may reach another device: no remote copies, remote signals or barrier semaphores. Data moves between devices by JAX's collectives and lax.ppermute only.
A program may use at most 64 MiB of HBM per device.

v0:
```python
import numpy as np
import jax
import jax.numpy as jnp
from jax import lax
from jax.sharding import PartitionSpec as P

TIME_STEP = 0.25
GAS_CONST = 1.0
TOP_PRESSURE = 1.0


def extended(cells, sides, width):
    for axis, dim in sides:
        count = lax.axis_size(axis)
        ends = count - 1
        head = lax.slice_in_dim(cells, 0, width, axis=dim)
        tail = lax.slice_in_dim(cells, cells.shape[dim] - width, cells.shape[dim], axis=dim)
        cells = jnp.concatenate(
            [
                lax.ppermute(tail, axis, [(i, (i + 1) % count) for i in range(ends)]),
                cells,
                lax.ppermute(head, axis, [((i + 1) % count, i) for i in range(ends)]),
            ],
            axis=dim,
        )
    return cells


def from_behind(block, axis, distance):
    devices = range(lax.axis_size(axis))
    route = [(i - distance, i) for i in devices if i - distance in devices]
    return lax.ppermute(block, axis, route)


def face_lon(values):
    return (
        37.0 * (jnp.roll(values, 1, -1) + values)
        - 8.0 * (jnp.roll(values, 2, -1) + jnp.roll(values, -1, -1))
        + (jnp.roll(values, 3, -1) + jnp.roll(values, -2, -1))
    ) / 60.0


def face_lat(padded, count):
    return (
        37.0 * (padded[..., 2 : 2 + count, :] + padded[..., 3 : 3 + count, :])
        - 8.0 * (padded[..., 1 : 1 + count, :] + padded[..., 4 : 4 + count, :])
        + (padded[..., 0:count, :] + padded[..., 5 : 5 + count, :])
    ) / 60.0


FACTOR_ROWS = 9
FACTOR_LANES = 128


def fft_tables(length):
    rows, lanes = FACTOR_ROWS, FACTOR_LANES
    small = np.arange(rows)
    small_phase = 2.0 * np.pi * np.outer(small, small) / rows
    low = np.arange(rows)[:, None]
    high = np.arange(lanes)[None, :]
    twist = 2.0 * np.pi * ((low * high) % length) / length
    waves = np.arange(lanes)
    wave_phase = 2.0 * np.pi * (np.outer(waves, waves) % lanes) / lanes
    wc, ws = np.cos(wave_phase), np.sin(wave_phase)
    forward = np.block([[wc, -ws], [ws, wc]]).astype(np.float32)
    inverse = np.block([[wc, ws], [-ws, wc]]).astype(np.float32)
    number = np.arange(rows)[:, None] + rows * np.arange(lanes)[None, :]
    folded = np.minimum(number, length - number)
    folded = np.concatenate([folded, folded], axis=1)[:, None, :].astype(np.int32)
    return (
        np.cos(small_phase),
        np.sin(small_phase),
        np.cos(twist).reshape(1, length).astype(np.float32),
        np.sin(twist).reshape(1, length).astype(np.float32),
        forward,
        inverse,
        folded,
    )


def filter_rows(values, cuts):
    rows, lanes = FACTOR_ROWS, FACTOR_LANES
    count, length = values.shape
    c9, s9, twc, tws, forward, inverse, folded = fft_tables(length)
    highest = lax.Precision.HIGHEST
    parts = [values[:, n * lanes : (n + 1) * lanes] for n in range(rows)]
    real_a = jnp.concatenate(
        [sum(float(c9[k, n]) * parts[n] for n in range(rows)) for k in range(rows)], axis=1
    )
    imag_a = jnp.concatenate(
        [sum(float(-s9[k, n]) * parts[n] for n in range(rows)) for k in range(rows)], axis=1
    )
    real_b = real_a * twc + imag_a * tws
    imag_b = imag_a * twc - real_a * tws
    stacked = jnp.concatenate(
        [
            jnp.concatenate(
                [real_b[:, k * lanes : (k + 1) * lanes], imag_b[:, k * lanes : (k + 1) * lanes]],
                axis=1,
            )
            for k in range(rows)
        ],
        axis=0,
    )
    spectrum = jnp.dot(stacked, forward, precision=highest)
    keep = (folded <= cuts[None, :, None]).astype(jnp.float32).reshape(rows * count, 2 * lanes)
    back = jnp.dot(spectrum * keep, inverse, precision=highest)
    real_c = jnp.concatenate([back[k * count : (k + 1) * count, :lanes] for k in range(rows)], axis=1)
    imag_c = jnp.concatenate([back[k * count : (k + 1) * count, lanes:] for k in range(rows)], axis=1)
    real_d = real_c * twc - imag_c * tws
    imag_d = imag_c * twc + real_c * tws
    real_parts = [real_d[:, k * lanes : (k + 1) * lanes] for k in range(rows)]
    imag_parts = [imag_d[:, k * lanes : (k + 1) * lanes] for k in range(rows)]
    return jnp.concatenate(
        [
            sum(
                float(c9[k, n] / length) * real_parts[k] - float(s9[k, n] / length) * imag_parts[k]
                for k in range(rows)
            )
            for n in range(rows)
        ],
        axis=1,
    )


def prefix_over(value, axis, before):
    count = lax.axis_size(axis)
    total = jnp.zeros_like(value)
    for step in range(1, count):
        if before:
            route = [(i, i + step) for i in range(count - step)]
        else:
            route = [(i + step, i) for i in range(count - step)]
        total = total + lax.ppermute(value, axis, route)
    return total


def local(wind_east, wind_north, layer_mass, theta_field, surface_height, filter_cutoff):
    levels, lat_rows, length = wind_east.shape
    lat_count = lax.axis_size("lat")
    lat_rank = lax.axis_index("lat")
    nlat_all = lat_rows * lat_count
    first_row = lat_rank * lat_rows
    row_ids = first_row + jnp.arange(lat_rows, dtype=jnp.int32)
    coslat = jnp.sin(jnp.pi * row_ids.astype(jnp.float32) / nlat_all)[None, :, None]
    stacked = jnp.stack([layer_mass, theta_field])
    padded = extended(stacked, (("lat", 2),), 3)
    mass_faces = face_lat(padded[0], lat_rows)
    theta_faces = face_lat(padded[1], lat_rows + 1)
    flux_east = wind_east * face_lon(layer_mass)
    flux_north = wind_north * mass_faces * coslat
    fields = jnp.stack([wind_east, wind_north, flux_east, flux_north])
    own_cuts = lax.dynamic_slice_in_dim(filter_cutoff, first_row, lat_rows)
    row_cuts = jnp.broadcast_to(own_cuts, (4, levels, lat_rows)).reshape(-1)
    smooth = filter_rows(fields.reshape(-1, length), row_cuts).reshape(fields.shape)
    east_smooth = smooth[0]
    north_smooth = smooth[1]
    east_flux = smooth[2]
    north_flux = smooth[3]
    next_face = from_behind(north_flux[:, :1], "lat", -1)
    north_full = jnp.concatenate([north_flux, next_face], axis=1)
    new_mass = layer_mass - TIME_STEP * (
        jnp.roll(east_flux, -1, -1) - east_flux + (north_full[:, 1:] - north_full[:, :-1])
    )
    heat_east = east_flux * face_lon(theta_field)
    heat_north = north_full * theta_faces
    new_heat = theta_field * layer_mass - TIME_STEP * (
        jnp.roll(heat_east, -1, -1) - heat_east + (heat_north[:, 1:] - heat_north[:, :-1])
    )
    column = jnp.sum(layer_mass, axis=0)
    above_mass = prefix_over(column, "lev", True)
    bottom = TOP_PRESSURE + above_mass[None] + jnp.cumsum(layer_mass, axis=0)
    top_press = bottom - layer_mass
    thickness = GAS_CONST * theta_field * (jnp.log(bottom) - jnp.log(top_press))
    depth_sum = jnp.sum(thickness, axis=0)
    below_depth = prefix_over(depth_sum, "lev", False)
    inclusive = jnp.flip(jnp.cumsum(jnp.flip(thickness, 0), axis=0), 0)
    height_cols = (
        surface_height[None] + below_depth[None] + (inclusive - thickness) + 0.5 * thickness
    )
    lower_row = from_behind(height_cols[:, -1:], "lat", 1)
    height_south = jnp.concatenate([lower_row, height_cols[:, :-1]], axis=1)
    new_east = east_smooth - TIME_STEP * (height_cols - jnp.roll(height_cols, 1, -1))
    inside = (row_ids > 0).astype(jnp.float32)[None, :, None]
    new_north = (north_smooth - TIME_STEP * (height_cols - height_south)) * inside
    return (new_east, new_north, new_mass, new_heat, height_cols)


def solution(mesh):
    in_specs = (
        P("lev", "lat", None),
        P("lev", "lat", None),
        P("lev", "lat", None),
        P("lev", "lat", None),
        P("lat", None),
        P(),
    )
    out_specs = (
        P("lev", "lat", None),
        P("lev", "lat", None),
        P("lev", "lat", None),
        P("lev", "lat", None),
        P("lev", "lat", None),
    )
    return jax.shard_map(local, mesh=mesh, in_specs=in_specs, out_specs=out_specs, check_vma=False)
```

profile of v0, /device:TPU:256, one launch (start us, length us, event | category | flops | bytes accessed | tf_op | source)
XLA Modules:
  0.0 74.1 jit_solution(2055391764282271527)
XLA Ops:
  0.7 1.1 %fusion.52 = (f32[8,3,1151]{2,0,1:T(8,128)S(1)}, f32[8,3,1151]{2,0,1:T(8,128)S(1)}) fusion(f32[8,3,1152]{2,0,1:T(8,128)} %param.13), kind=kLoop, calls=%fused_computation.163 | loop fusion | bytes 441984 | tf_op jit(solution)/shard_map/jit(_roll_static)/slice | solution.py:38
  1.8 1.1 %fusion.50 = (f32[8,3,1150]{2,0,1:T(8,128)S(1)}, f32[8,3,1150]{2,0,1:T(8,128)S(1)}) fusion(f32[8,3,1152]{2,0,1:T(8,128)} %param.13), kind=kLoop, calls=%fused_computation.161 | loop fusion | bytes 441600 | tf_op jit(solution)/shard_map/jit(_roll_static)/slice | solution.py:39
  2.9 0.8 %fusion.53 = (f32[8,3,1]{2,0,1:T(8,128)S(1)}, f32[8,3,1]{2,0,1:T(8,128)S(1)}) fusion(f32[8,3,1152]{2,0,1:T(8,128)} %param.13), kind=kLoop, calls=%fused_computation.164 | loop fusion | bytes 384 | tf_op jit(solution)/shard_map/jit(_roll_static)/slice | solution.py:38
  3.7 0.8 %fusion.51 = (f32[8,3,2]{2,0,1:T(8,128)S(1)}, f32[8,3,2]{2,0,1:T(8,128)S(1)}) fusion(f32[8,3,1152]{2,0,1:T(8,128)} %param.13), kind=kLoop, calls=%fused_computation.162 | loop fusion | bytes 768 | tf_op jit(solution)/shard_map/jit(_roll_static)/slice | solution.py:39
  6.1 1.9 %collective-permute-start = (f32[2,8,3,1152]{3,2,1,0:T(4,128)S(1)}, f32[2,8,3,1152]{3,2,1,0:T(4,128)S(1)}, u32[]{:S(2)}, u32[]{:S(2)}) collective-permute-start(f32[2,8,3,1152]{3,2,1,0:T(4,128)S(1)} %pad_maximum_fusion.2), channel_id=1, source_target_pairs={{0,8},{8,16},{16,24},{24,32},{32,40},{40,48},{48,56},{56,64},{64,7... | collective-permute-start | bytes 663560 | tf_op jit(solution)/shard_map/ppermute | solution.py:20
  8.0 7.0 %collective-permute-start.1 = (f32[2,8,3,1152]{3,2,1,0:T(4,128)S(1)}, f32[2,8,3,1152]{3,2,1,0:T(4,128)S(1)}, u32[]{:S(2)}, u32[]{:S(2)}) collective-permute-start(f32[2,8,3,1152]{3,2,1,0:T(4,128)S(1)} %pad_maximum_fusion.2), channel_id=1, source_target_pairs={{8,0},{16,8},{24,16},{32,24},{40,32},{48,40},{56,48},{64,56},{72,6... | collective-permute-start | bytes 663560 | tf_op jit(solution)/shard_map/ppermute | solution.py:22
  15.0 3.5 %collective-permute-start.2 = (f32[3,1152]{1,0:T(4,128)S(1)}, f32[3,1152]{1,0:T(4,128)S(1)}, u32[]{:S(2)}, u32[]{:S(2)}) collective-permute-start(f32[3,1152]{1,0:T(4,128)S(1)} %reduce_sum.18), channel_id=1, source_target_pairs={{0,1},{1,2},{2,3},{3,4},{4,5},{5,6},{6,7},{8,9},{9,10},{10,11},{11... | collective-permute-start | bytes 41480 | tf_op jit(solution)/shard_map/ppermute | solution.py:134
  18.5 4.5 %collective-permute-start.3 = (f32[3,1152]{1,0:T(4,128)S(1)}, f32[3,1152]{1,0:T(4,128)S(1)}, u32[]{:S(2)}, u32[]{:S(2)}) collective-permute-start(f32[3,1152]{1,0:T(4,128)S(1)} %reduce_sum.18), channel_id=1, source_target_pairs={{0,2},{1,3},{2,4},{3,5},{4,6},{5,7},{8,10},{9,11},{10,12},{11,13},... | collective-permute-start | bytes 41480 | tf_op jit(solution)/shard_map/ppermute | solution.py:134
  23.0 4.9 %collective-permute-start.4 = (f32[3,1152]{1,0:T(4,128)S(1)}, f32[3,1152]{1,0:T(4,128)S(1)}, u32[]{:S(2)}, u32[]{:S(2)}) collective-permute-start(f32[3,1152]{1,0:T(4,128)S(1)} %reduce_sum.18), channel_id=1, source_target_pairs={{0,3},{1,4},{2,5},{3,6},{4,7},{8,11},{9,12},{10,13},{11,14},{12,15... | collective-permute-start | bytes 41480 | tf_op jit(solution)/shard_map/ppermute | solution.py:134
  29.2 2.0 %collective-permute-start.5 = (f32[3,1152]{1,0:T(4,128)S(1)}, f32[3,1152]{1,0:T(4,128)S(1)}, u32[]{:S(2)}, u32[]{:S(2)}) collective-permute-start(f32[3,1152]{1,0:T(4,128)S(1)} %reduce_sum.18), channel_id=1, source_target_pairs={{0,4},{1,5},{2,6},{3,7},{8,12},{9,13},{10,14},{11,15},{16,20},{17,... | collective-permute-start | bytes 41480 | tf_op jit(solution)/shard_map/ppermute | solution.py:134
  31.2 1.3 %collective-permute-start.6 = (f32[3,1152]{1,0:T(4,128)S(1)}, f32[3,1152]{1,0:T(4,128)S(1)}, u32[]{:S(2)}, u32[]{:S(2)}) collective-permute-start(f32[3,1152]{1,0:T(4,128)S(1)} %reduce_sum.18), channel_id=1, source_target_pairs={{0,5},{1,6},{2,7},{8,13},{9,14},{10,15},{16,21},{17,22},{18,23},{2... | collective-permute-start | bytes 41480 | tf_op jit(solution)/shard_map/ppermute | solution.py:134
  32.9 0.8 %copy-done.5 = f32[8,3,1152]{2,0,1:T(8,128)S(1)} copy-done((f32[8,3,1152]{2,0,1:T(8,128)S(1)}, f32[8,3,1152]{2,0,1:T(8,128)}, u32[]{:S(2)}) %copy-start.5) | copy-done | bytes 110616
  36.6 0.9 %convolution_select_fusion = f32[864,256]{1,0:T(8,128)S(1)} fusion(pred[864,256]{1,0:T(32,128)(4,1)S(1)} %bitcast_compare_fusion, f32[864,256]{1,0:T(8,128)S(1)} %constant_dynamic-update-slice_fusion.18, f32[256,256]{1,0:T(8,128)S(1)} %copy-done.2), kind=kOutput, calls=%fused_computation | convolution fusion | flops 679698432 | bytes 2252800 | tf_op jit(solution)/shard_map/dot_general | solution.py:105
  37.5 0.9 %fusion.55 = f32[864,256]{1,0:T(8,128)S(1)} fusion(f32[864,256]{1,0:T(8,128)S(1)} %convolution_select_fusion, f32[256,256]{1,0:T(8,128)S(1)} %copy-done.3), kind=kOutput, calls=%fused_computation.166 | convolution fusion | flops 679477248 | bytes 2031616 | tf_op jit(solution)/shard_map/dot_general | solution.py:107
  39.2 1.3 %collective-permute-start.7 = (f32[3,1152]{1,0:T(4,128)S(1)}, f32[3,1152]{1,0:T(4,128)S(1)}, u32[]{:S(2)}, u32[]{:S(2)}) collective-permute-start(f32[3,1152]{1,0:T(4,128)S(1)} %reduce_sum.18), channel_id=1, source_target_pairs={{0,6},{1,7},{8,14},{9,15},{16,22},{17,23},{24,30},{25,31},{32,38},... | collective-permute-start | bytes 41480 | tf_op jit(solution)/shard_map/ppermute | solution.py:134
  40.6 1.3 %collective-permute-start.8 = (f32[3,1152]{1,0:T(4,128)S(1)}, f32[3,1152]{1,0:T(4,128)S(1)}, u32[]{:S(2)}, u32[]{:S(2)}) collective-permute-start(f32[3,1152]{1,0:T(4,128)S(1)} %reduce_sum.18), channel_id=1, source_target_pairs={{0,7},{8,15},{16,23},{24,31},{32,39},{40,47},{48,55},{56,63},{64,7... | collective-permute-start | bytes 41480 | tf_op jit(solution)/shard_map/ppermute | solution.py:134
  42.0 1.9 %collective-permute-start.17 = (f32[8,1,1152]{2,1,0:T(1,128)S(1)}, f32[8,1,1152]{2,1,0:T(1,128)S(1)}, u32[]{:S(2)}, u32[]{:S(2)}) collective-permute-start(f32[8,1,1152]{2,1,0:T(1,128)S(1)} %slice.556), channel_id=1, source_target_pairs={{8,0},{16,8},{24,16},{32,24},{40,32},{48,40},{56,48},{64,56},{72,6... | collective-permute-start | bytes 110600 | tf_op jit(solution)/shard_map/ppermute | solution.py:32
  44.2 1.3 %collective-permute-done.17 = f32[8,1,1152]{2,1,0:T(1,128)S(1)} collective-permute-done((f32[8,1,1152]{2,1,0:T(1,128)S(1)}, f32[8,1,1152]{2,1,0:T(1,128)S(1)}, u32[]{:S(2)}, u32[]{:S(2)}) %collective-permute-start.17) | collective-permute-done | bytes 36896 | tf_op jit(solution)/shard_map/ppermute | solution.py:32
  46.6 1.3 %collective-permute-start.10 = (f32[3,1152]{1,0:T(4,128)S(1)}, f32[3,1152]{1,0:T(4,128)S(1)}, u32[]{:S(2)}, u32[]{:S(2)}) collective-permute-start(f32[3,1152]{1,0:T(4,128)S(1)} %get-tuple-element.10), channel_id=1, source_target_pairs={{2,0},{3,1},{4,2},{5,3},{6,4},{7,5},{10,8},{11,9},{12,10},{13,11},... | collective-permute-start | bytes 41480 | tf_op jit(solution)/shard_map/ppermute | solution.py:134
  47.9 1.3 %collective-permute-start.11 = (f32[3,1152]{1,0:T(4,128)S(1)}, f32[3,1152]{1,0:T(4,128)S(1)}, u32[]{:S(2)}, u32[]{:S(2)}) collective-permute-start(f32[3,1152]{1,0:T(4,128)S(1)} %get-tuple-element.10), channel_id=1, source_target_pairs={{3,0},{4,1},{5,2},{6,3},{7,4},{11,8},{12,9},{13,10},{14,11},{15,12... | collective-permute-start | bytes 41480 | tf_op jit(solution)/shard_map/ppermute | solution.py:134
  49.1 1.3 %collective-permute-start.12 = (f32[3,1152]{1,0:T(4,128)S(1)}, f32[3,1152]{1,0:T(4,128)S(1)}, u32[]{:S(2)}, u32[]{:S(2)}) collective-permute-start(f32[3,1152]{1,0:T(4,128)S(1)} %get-tuple-element.10), channel_id=1, source_target_pairs={{4,0},{5,1},{6,2},{7,3},{12,8},{13,9},{14,10},{15,11},{20,16},{21,... | collective-permute-start | bytes 41480 | tf_op jit(solution)/shard_map/ppermute | solution.py:134
  50.5 1.3 %collective-permute-start.13 = (f32[3,1152]{1,0:T(4,128)S(1)}, f32[3,1152]{1,0:T(4,128)S(1)}, u32[]{:S(2)}, u32[]{:S(2)}) collective-permute-start(f32[3,1152]{1,0:T(4,128)S(1)} %get-tuple-element.10), channel_id=1, source_target_pairs={{5,0},{6,1},{7,2},{13,8},{14,9},{15,10},{21,16},{22,17},{23,18},{2... | collective-permute-start | bytes 41480 | tf_op jit(solution)/shard_map/ppermute | solution.py:134
  51.8 1.3 %collective-permute-start.14 = (f32[3,1152]{1,0:T(4,128)S(1)}, f32[3,1152]{1,0:T(4,128)S(1)}, u32[]{:S(2)}, u32[]{:S(2)}) collective-permute-start(f32[3,1152]{1,0:T(4,128)S(1)} %get-tuple-element.10), channel_id=1, source_target_pairs={{6,0},{7,1},{14,8},{15,9},{22,16},{23,17},{30,24},{31,25},{38,32},... | collective-permute-start | bytes 41480 | tf_op jit(solution)/shard_map/ppermute | solution.py:134
  53.1 1.3 %collective-permute-start.15 = (f32[3,1152]{1,0:T(4,128)S(1)}, f32[3,1152]{1,0:T(4,128)S(1)}, u32[]{:S(2)}, u32[]{:S(2)}) collective-permute-start(f32[3,1152]{1,0:T(4,128)S(1)} %get-tuple-element.10), channel_id=1, source_target_pairs={{7,0},{15,8},{23,16},{31,24},{39,32},{47,40},{55,48},{63,56},{71,6... | collective-permute-start | bytes 41480 | tf_op jit(solution)/shard_map/ppermute | solution.py:134
  54.4 1.1 %collective-permute-done.11 = f32[3,1152]{1,0:T(4,128)S(1)} collective-permute-done((f32[3,1152]{1,0:T(4,128)S(1)}, f32[3,1152]{1,0:T(4,128)S(1)}, u32[]{:S(2)}, u32[]{:S(2)}) %collective-permute-start.11) | collective-permute-done | bytes 13856 | tf_op jit(solution)/shard_map/ppermute | solution.py:134
  55.4 1.3 %collective-permute-start.9 = (f32[3,1152]{1,0:T(4,128)S(1)}, f32[3,1152]{1,0:T(4,128)S(1)}, u32[]{:S(2)}, u32[]{:S(2)}) collective-permute-start(f32[3,1152]{1,0:T(4,128)S(1)} %get-tuple-element.10), channel_id=1, source_target_pairs={{1,0},{2,1},{3,2},{4,3},{5,4},{6,5},{7,6},{9,8},{10,9},{11,10},{12... | collective-permute-start | bytes 41480 | tf_op jit(solution)/shard_map/ppermute | solution.py:134
  56.8 1.9 %collective-permute-done.12 = f32[3,1152]{1,0:T(4,128)S(1)} collective-permute-done((f32[3,1152]{1,0:T(4,128)S(1)}, f32[3,1152]{1,0:T(4,128)S(1)}, u32[]{:S(2)}, u32[]{:S(2)}) %collective-permute-start.12) | collective-permute-done | bytes 13856 | tf_op jit(solution)/shard_map/ppermute | solution.py:134
  58.7 2.5 %collective-permute-done.13 = f32[3,1152]{1,0:T(4,128)S(1)} collective-permute-done((f32[3,1152]{1,0:T(4,128)S(1)}, f32[3,1152]{1,0:T(4,128)S(1)}, u32[]{:S(2)}, u32[]{:S(2)}) %collective-permute-start.13) | collective-permute-done | bytes 13856 | tf_op jit(solution)/shard_map/ppermute | solution.py:134
  61.2 1.3 %collective-permute-done.14 = f32[3,1152]{1,0:T(4,128)S(1)} collective-permute-done((f32[3,1152]{1,0:T(4,128)S(1)}, f32[3,1152]{1,0:T(4,128)S(1)}, u32[]{:S(2)}, u32[]{:S(2)}) %collective-permute-start.14) | collective-permute-done | bytes 13856 | tf_op jit(solution)/shard_map/ppermute | solution.py:134
  62.5 1.3 %collective-permute-done.15 = f32[3,1152]{1,0:T(4,128)S(1)} collective-permute-done((f32[3,1152]{1,0:T(4,128)S(1)}, f32[3,1152]{1,0:T(4,128)S(1)}, u32[]{:S(2)}, u32[]{:S(2)}) %collective-permute-start.15) | collective-permute-done | bytes 13856 | tf_op jit(solution)/shard_map/ppermute | solution.py:134
  64.0 1.9 %collective-permute-start.16 = (f32[8,1,1152]{2,1,0:T(1,128)S(1)}, f32[8,1,1152]{2,1,0:T(1,128)S(1)}, u32[]{:S(2)}, u32[]{:S(2)}) collective-permute-start(f32[8,1,1152]{2,1,0:T(1,128)S(1)} %slice.550), channel_id=1, source_target_pairs={{0,8},{8,16},{16,24},{24,32},{32,40},{40,48},{48,56},{56,64},{64,7... | collective-permute-start | bytes 110600 | tf_op jit(solution)/shard_map/ppermute | solution.py:32
  68.1 4.5 %collective-permute-done.16 = f32[8,1,1152]{2,1,0:T(1,128)S(1)} collective-permute-done((f32[8,1,1152]{2,1,0:T(1,128)S(1)}, f32[8,1,1152]{2,1,0:T(1,128)S(1)}, u32[]{:S(2)}, u32[]{:S(2)}) %collective-permute-start.16) | collective-permute-done | bytes 36896 | tf_op jit(solution)/shard_map/ppermute | solution.py:32
  (149 shorter events, 11.6 us)
Async XLA Ops:
  0.6 4.9 %copy-start = (f32[8,3,1152]{2,0,1:T(8,128)S(1)}, f32[8,3,1152]{2,0,1:T(8,128)}, u32[]{:S(2)}) copy-start(f32[8,3,1152]{2,0,1:T(8,128)} %param.13) | copy-start | bytes 331780
  0.6 4.9 %copy-start.1 = (f32[8,3,1152]{2,0,1:T(8,128)S(1)}, f32[8,3,1152]{2,0,1:T(8,128)}, u32[]{:S(2)}) copy-start(f32[8,3,1152]{2,0,1:T(8,128)} %param.14) | copy-start | bytes 331780
  1.8 3.8 %copy-start.4 = (f32[8,3,1152]{2,0,1:T(8,128)S(1)}, f32[8,3,1152]{2,0,1:T(8,128)}, u32[]{:S(2)}) copy-start(f32[8,3,1152]{2,0,1:T(8,128)} %param.11) | copy-start | bytes 331780
  6.0 22.4 %copy-start.10 = (s32[192]{0:T(256)S(1)}, s32[192]{0:T(256)}, u32[]{:S(2)}) copy-start(s32[192]{0:T(256)} %param.16) | copy-start | bytes 2308
  6.1 23.1 %collective-permute-start = (f32[2,8,3,1152]{3,2,1,0:T(4,128)S(1)}, f32[2,8,3,1152]{3,2,1,0:T(4,128)S(1)}, u32[]{:S(2)}, u32[]{:S(2)}) collective-permute-start(f32[2,8,3,1152]{3,2,1,0:T(4,128)S(1)} %pad_maximum_fusion.2), channel_id=1, source_target_pairs={{0,8},{8,16},{16,24},{24,32},{32,40},{40,48},{48,56},{56,64},{64,7... | collective-permute-start | bytes 663560 | tf_op jit(solution)/shard_map/ppermute | solution.py:20
  8.0 23.3 %collective-permute-start.1 = (f32[2,8,3,1152]{3,2,1,0:T(4,128)S(1)}, f32[2,8,3,1152]{3,2,1,0:T(4,128)S(1)}, u32[]{:S(2)}, u32[]{:S(2)}) collective-permute-start(f32[2,8,3,1152]{3,2,1,0:T(4,128)S(1)} %pad_maximum_fusion.2), channel_id=1, source_target_pairs={{8,0},{16,8},{24,16},{32,24},{40,32},{48,40},{56,48},{64,56},{72,6... | collective-permute-start | bytes 663560 | tf_op jit(solution)/shard_map/ppermute | solution.py:22
  15.0 13.9 %copy-start.9 = (s32[9,256]{1,0:T(8,128)S(1)}, s32[9,256]{1,0:T(8,128)}, u32[]{:S(2)}) copy-start(s32[9,256]{1,0:T(8,128)} %constant.129) | copy-start | bytes 27652
  15.0 24.2 %collective-permute-start.2 = (f32[3,1152]{1,0:T(4,128)S(1)}, f32[3,1152]{1,0:T(4,128)S(1)}, u32[]{:S(2)}, u32[]{:S(2)}) collective-permute-start(f32[3,1152]{1,0:T(4,128)S(1)} %reduce_sum.18), channel_id=1, source_target_pairs={{0,1},{1,2},{2,3},{3,4},{4,5},{5,6},{6,7},{8,9},{9,10},{10,11},{11... | collective-permute-start | bytes 41480 | tf_op jit(solution)/shard_map/ppermute | solution.py:134
  18.5 22.0 %collective-permute-start.3 = (f32[3,1152]{1,0:T(4,128)S(1)}, f32[3,1152]{1,0:T(4,128)S(1)}, u32[]{:S(2)}, u32[]{:S(2)}) collective-permute-start(f32[3,1152]{1,0:T(4,128)S(1)} %reduce_sum.18), channel_id=1, source_target_pairs={{0,2},{1,3},{2,4},{3,5},{4,6},{5,7},{8,10},{9,11},{10,12},{11,13},... | collective-permute-start | bytes 41480 | tf_op jit(solution)/shard_map/ppermute | solution.py:134
  23.0 19.0 %collective-permute-start.4 = (f32[3,1152]{1,0:T(4,128)S(1)}, f32[3,1152]{1,0:T(4,128)S(1)}, u32[]{:S(2)}, u32[]{:S(2)}) collective-permute-start(f32[3,1152]{1,0:T(4,128)S(1)} %reduce_sum.18), channel_id=1, source_target_pairs={{0,3},{1,4},{2,5},{3,6},{4,7},{8,11},{9,12},{10,13},{11,14},{12,15... | collective-permute-start | bytes 41480 | tf_op jit(solution)/shard_map/ppermute | solution.py:134
  29.2 14.7 %collective-permute-start.5 = (f32[3,1152]{1,0:T(4,128)S(1)}, f32[3,1152]{1,0:T(4,128)S(1)}, u32[]{:S(2)}, u32[]{:S(2)}) collective-permute-start(f32[3,1152]{1,0:T(4,128)S(1)} %reduce_sum.18), channel_id=1, source_target_pairs={{0,4},{1,5},{2,6},{3,7},{8,12},{9,13},{10,14},{11,15},{16,20},{17,... | collective-permute-start | bytes 41480 | tf_op jit(solution)/shard_map/ppermute | solution.py:134
  31.2 12.7 %collective-permute-start.6 = (f32[3,1152]{1,0:T(4,128)S(1)}, f32[3,1152]{1,0:T(4,128)S(1)}, u32[]{:S(2)}, u32[]{:S(2)}) collective-permute-start(f32[3,1152]{1,0:T(4,128)S(1)} %reduce_sum.18), channel_id=1, source_target_pairs={{0,5},{1,6},{2,7},{8,13},{9,14},{10,15},{16,21},{17,22},{18,23},{2... | collective-permute-start | bytes 41480 | tf_op jit(solution)/shard_map/ppermute | solution.py:134
  32.8 0.9 %copy-start.5 = (f32[8,3,1152]{2,0,1:T(8,128)S(1)}, f32[8,3,1152]{2,0,1:T(8,128)}, u32[]{:S(2)}) copy-start(f32[8,3,1152]{2,0,1:T(8,128)} %param.12) | copy-start | bytes 331780
  34.7 0.7 copy-start.6
  34.7 0.7 copy-start.7
  35.6 1.0 %copy-start.2 = (f32[256,256]{1,0:T(8,128)S(1)}, f32[256,256]{1,0:T(8,128)}, u32[]{:S(2)}) copy-start(f32[256,256]{1,0:T(8,128)} %constant.121.clone) | copy-start | bytes 786436
  35.8 1.7 %copy-start.3 = (f32[256,256]{1,0:T(8,128)S(1)}, f32[256,256]{1,0:T(8,128)}, u32[]{:S(2)}) copy-start(f32[256,256]{1,0:T(8,128)} %constant.123.clone) | copy-start | bytes 786436
  39.2 4.7 %collective-permute-start.7 = (f32[3,1152]{1,0:T(4,128)S(1)}, f32[3,1152]{1,0:T(4,128)S(1)}, u32[]{:S(2)}, u32[]{:S(2)}) collective-permute-start(f32[3,1152]{1,0:T(4,128)S(1)} %reduce_sum.18), channel_id=1, source_target_pairs={{0,6},{1,7},{8,14},{9,15},{16,22},{17,23},{24,30},{25,31},{32,38},... | collective-permute-start | bytes 41480 | tf_op jit(solution)/shard_map/ppermute | solution.py:134
  40.6 3.4 %collective-permute-start.8 = (f32[3,1152]{1,0:T(4,128)S(1)}, f32[3,1152]{1,0:T(4,128)S(1)}, u32[]{:S(2)}, u32[]{:S(2)}) collective-permute-start(f32[3,1152]{1,0:T(4,128)S(1)} %reduce_sum.18), channel_id=1, source_target_pairs={{0,7},{8,15},{16,23},{24,31},{32,39},{40,47},{48,55},{56,63},{64,7... | collective-permute-start | bytes 41480 | tf_op jit(solution)/shard_map/ppermute | solution.py:134
  42.0 3.5 %collective-permute-start.17 = (f32[8,1,1152]{2,1,0:T(1,128)S(1)}, f32[8,1,1152]{2,1,0:T(1,128)S(1)}, u32[]{:S(2)}, u32[]{:S(2)}) collective-permute-start(f32[8,1,1152]{2,1,0:T(1,128)S(1)} %slice.556), channel_id=1, source_target_pairs={{8,0},{16,8},{24,16},{32,24},{40,32},{48,40},{56,48},{64,56},{72,6... | collective-permute-start | bytes 110600 | tf_op jit(solution)/shard_map/ppermute | solution.py:32
  46.3 17.5 %copy-start.8 = (f32[3,1152]{1,0:T(4,128)S(1)}, f32[3,1152]{1,0:T(4,128)}, u32[]{:S(2)}) copy-start(f32[3,1152]{1,0:T(4,128)} %param.15) | copy-start | bytes 41476
  46.6 6.6 %collective-permute-start.10 = (f32[3,1152]{1,0:T(4,128)S(1)}, f32[3,1152]{1,0:T(4,128)S(1)}, u32[]{:S(2)}, u32[]{:S(2)}) collective-permute-start(f32[3,1152]{1,0:T(4,128)S(1)} %get-tuple-element.10), channel_id=1, source_target_pairs={{2,0},{3,1},{4,2},{5,3},{6,4},{7,5},{10,8},{11,9},{12,10},{13,11},... | collective-permute-start | bytes 41480 | tf_op jit(solution)/shard_map/ppermute | solution.py:134
  47.9 7.6 %collective-permute-start.11 = (f32[3,1152]{1,0:T(4,128)S(1)}, f32[3,1152]{1,0:T(4,128)S(1)}, u32[]{:S(2)}, u32[]{:S(2)}) collective-permute-start(f32[3,1152]{1,0:T(4,128)S(1)} %get-tuple-element.10), channel_id=1, source_target_pairs={{3,0},{4,1},{5,2},{6,3},{7,4},{11,8},{12,9},{13,10},{14,11},{15,12... | collective-permute-start | bytes 41480 | tf_op jit(solution)/shard_map/ppermute | solution.py:134
  49.1 9.6 %collective-permute-start.12 = (f32[3,1152]{1,0:T(4,128)S(1)}, f32[3,1152]{1,0:T(4,128)S(1)}, u32[]{:S(2)}, u32[]{:S(2)}) collective-permute-start(f32[3,1152]{1,0:T(4,128)S(1)} %get-tuple-element.10), channel_id=1, source_target_pairs={{4,0},{5,1},{6,2},{7,3},{12,8},{13,9},{14,10},{15,11},{20,16},{21,... | collective-permute-start | bytes 41480 | tf_op jit(solution)/shard_map/ppermute | solution.py:134
  50.5 10.8 %collective-permute-start.13 = (f32[3,1152]{1,0:T(4,128)S(1)}, f32[3,1152]{1,0:T(4,128)S(1)}, u32[]{:S(2)}, u32[]{:S(2)}) collective-permute-start(f32[3,1152]{1,0:T(4,128)S(1)} %get-tuple-element.10), channel_id=1, source_target_pairs={{5,0},{6,1},{7,2},{13,8},{14,9},{15,10},{21,16},{22,17},{23,18},{2... | collective-permute-start | bytes 41480 | tf_op jit(solution)/shard_map/ppermute | solution.py:134
  51.8 10.7 %collective-permute-start.14 = (f32[3,1152]{1,0:T(4,128)S(1)}, f32[3,1152]{1,0:T(4,128)S(1)}, u32[]{:S(2)}, u32[]{:S(2)}) collective-permute-start(f32[3,1152]{1,0:T(4,128)S(1)} %get-tuple-element.10), channel_id=1, source_target_pairs={{6,0},{7,1},{14,8},{15,9},{22,16},{23,17},{30,24},{31,25},{38,32},... | collective-permute-start | bytes 41480 | tf_op jit(solution)/shard_map/ppermute | solution.py:134
  53.1 10.7 %collective-permute-start.15 = (f32[3,1152]{1,0:T(4,128)S(1)}, f32[3,1152]{1,0:T(4,128)S(1)}, u32[]{:S(2)}, u32[]{:S(2)}) collective-permute-start(f32[3,1152]{1,0:T(4,128)S(1)} %get-tuple-element.10), channel_id=1, source_target_pairs={{7,0},{15,8},{23,16},{31,24},{39,32},{47,40},{55,48},{63,56},{71,6... | collective-permute-start | bytes 41480 | tf_op jit(solution)/shard_map/ppermute | solution.py:134
  55.4 8.4 %collective-permute-start.9 = (f32[3,1152]{1,0:T(4,128)S(1)}, f32[3,1152]{1,0:T(4,128)S(1)}, u32[]{:S(2)}, u32[]{:S(2)}) collective-permute-start(f32[3,1152]{1,0:T(4,128)S(1)} %get-tuple-element.10), channel_id=1, source_target_pairs={{1,0},{2,1},{3,2},{4,3},{5,4},{6,5},{7,6},{9,8},{10,9},{11,10},{12... | collective-permute-start | bytes 41480 | tf_op jit(solution)/shard_map/ppermute | solution.py:134
  64.0 8.6 %collective-permute-start.16 = (f32[8,1,1152]{2,1,0:T(1,128)S(1)}, f32[8,1,1152]{2,1,0:T(1,128)S(1)}, u32[]{:S(2)}, u32[]{:S(2)}) collective-permute-start(f32[8,1,1152]{2,1,0:T(1,128)S(1)} %slice.550), channel_id=1, source_target_pairs={{0,8},{8,16},{16,24},{24,32},{32,40},{40,48},{48,56},{56,64},{64,7... | collective-permute-start | bytes 110600 | tf_op jit(solution)/shard_map/ppermute | solution.py:32
where the time goes:
time: 74.9 us; the launch traced here: 74.1 us
  starting transfers between devices  40.6 us (54%)
  waiting for transfers between devices  14 us (19%)
  local copies, waits for them, and re-layouts  12.3 us (16%)
  other arithmetic  3.84 us (5%)
  matrix products  1.72 us (2%)
  between operations  1.71 us (2%)
    ppermute x14, starting transfers between devices, prefix_over(): total = total + lax.ppermute(value, axis, route)  27.8 us
    ppermute x14, waiting for transfers between devices, prefix_over(): total = total + lax.ppermute(value, axis, route)  8.15 us
    ppermute x1, starting transfers between devices, extended(): lax.ppermute(head, axis, [((i + 1) % count, i) for i in range(ends)])  6.96 us
    unnamed x59, local copies, waits for them, and re-layouts  5.96 us
    ppermute x2, waiting for transfers between devices, from_behind(): return lax.ppermute(block, axis, route)  5.81 us
    ppermute x2, starting transfers between devices, from_behind(): return lax.ppermute(block, axis, route)  3.84 us
    slice x4, local copies, waits for them, and re-layouts, face_lon(): jnp.roll(values, -1, -1)  2.07 us
    slice x4, local copies, waits for them, and re-layouts, face_lon(): jnp.roll(values, -2, -1)  2.03 us
  transfers between devices with their start and end apart: 18, of which 7 were waited for; matrix products, arithmetic and copies ran while one was open for 11% of the time, Pallas kernels for 0%

commit v1 on v0

--- a/solution.py
+++ b/solution.py
@@ -125,14 +125,24 @@
 
 def prefix_over(value, axis, before):
     count = lax.axis_size(axis)
-    total = jnp.zeros_like(value)
-    for step in range(1, count):
+    reach = max(1, count // 2)
+
+    def shifted(block, step):
         if before:
             route = [(i, i + step) for i in range(count - step)]
         else:
             route = [(i + step, i) for i in range(count - step)]
-        total = total + lax.ppermute(value, axis, route)
-    return total
+        return lax.ppermute(block, axis, route)
+
+    window = value
+    for step in range(1, min(reach, count)):
+        window = window + shifted(value, step)
+    total = window
+    step = reach
+    while step < count:
+        total = total + shifted(total, step)
+        step *= 2
+    return total - value
 
 
 def local(wind_east, wind_north, layer_mass, theta_field, surface_height, filter_cutoff):

time: 74.9 us -> 81.9 us (1.093)
  the two profiles are of different devices: /device:TPU:256 before, /device:TPU:280 now
where the time goes in v1:
time: 81.9 us; the launch traced here: 81.2 us
  starting transfers between devices  36.7 us (45%)
  waiting for transfers between devices  25 us (31%)
  local copies, waits for them, and re-layouts  12.3 us (15%)
  other arithmetic  3.84 us (5%)
  matrix products  1.72 us (2%)
  between operations  1.65 us (2%)
    ppermute x8, starting transfers between devices, shifted(): return lax.ppermute(block, axis, route)  24 us
    ppermute x8, waiting for transfers between devices, shifted(): return lax.ppermute(block, axis, route)  19.2 us
    ppermute x1, starting transfers between devices, extended(): lax.ppermute(head, axis, [((i + 1) % count, i) for i in range(ends)])  6.96 us
    unnamed x59, local copies, waits for them, and re-layouts  5.96 us
    ppermute x2, waiting for transfers between devices, from_behind(): return lax.ppermute(block, axis, route)  5.85 us
    ppermute x2, starting transfers between devices, from_behind(): return lax.ppermute(block, axis, route)  3.84 us
    slice x4, local copies, waits for them, and re-layouts, face_lon(): jnp.roll(values, -1, -1)  2.07 us
    slice x4, local copies, waits for them, and re-layouts, face_lon(): jnp.roll(values, -2, -1)  2.03 us
  transfers between devices with their start and end apart: 12, of which 7 were waited for; matrix products, arithmetic and copies ran while one was open for 10% of the time, Pallas kernels for 0%

profile of v1, /device:TPU:280, one launch (start us, length us, event | category | flops | bytes accessed | tf_op | source)
XLA Modules:
  0.0 81.2 jit_solution(11488219051509090911)
XLA Ops:
  0.7 1.1 %fusion.52 = (f32[8,3,1151]{2,0,1:T(8,128)S(1)}, f32[8,3,1151]{2,0,1:T(8,128)S(1)}) fusion(f32[8,3,1152]{2,0,1:T(8,128)} %param.13), kind=kLoop, calls=%fused_computation.165 | loop fusion | bytes 441984 | tf_op jit(solution)/shard_map/jit(_roll_static)/slice | solution.py:38
  1.8 1.1 %fusion.50 = (f32[8,3,1150]{2,0,1:T(8,128)S(1)}, f32[8,3,1150]{2,0,1:T(8,128)S(1)}) fusion(f32[8,3,1152]{2,0,1:T(8,128)} %param.13), kind=kLoop, calls=%fused_computation.163 | loop fusion | bytes 441600 | tf_op jit(solution)/shard_map/jit(_roll_static)/slice | solution.py:39
  2.9 0.8 fusion.53
  3.7 0.8 fusion.51
  4.5 0.8 slice.472
  6.1 1.9 %collective-permute-start = (f32[2,8,3,1152]{3,2,1,0:T(4,128)S(1)}, f32[2,8,3,1152]{3,2,1,0:T(4,128)S(1)}, u32[]{:S(2)}, u32[]{:S(2)}) collective-permute-start(f32[2,8,3,1152]{3,2,1,0:T(4,128)S(1)} %pad_maximum_fusion.2), channel_id=1, source_target_pairs={{0,8},{8,16},{16,24},{24,32},{32,40},{40,48},{48,56},{56,64},{64,7... | collective-permute-start | bytes 663560 | tf_op jit(solution)/shard_map/ppermute | solution.py:20
  8.0 7.0 %collective-permute-start.1 = (f32[2,8,3,1152]{3,2,1,0:T(4,128)S(1)}, f32[2,8,3,1152]{3,2,1,0:T(4,128)S(1)}, u32[]{:S(2)}, u32[]{:S(2)}) collective-permute-start(f32[2,8,3,1152]{3,2,1,0:T(4,128)S(1)} %pad_maximum_fusion.2), channel_id=1, source_target_pairs={{8,0},{16,8},{24,16},{32,24},{40,32},{48,40},{56,48},{64,56},{72,6... | collective-permute-start | bytes 663560 | tf_op jit(solution)/shard_map/ppermute | solution.py:22
  15.0 4.7 %collective-permute-start.2 = (f32[3,1152]{1,0:T(4,128)S(1)}, f32[3,1152]{1,0:T(4,128)S(1)}, u32[]{:S(2)}, u32[]{:S(2)}) collective-permute-start(f32[3,1152]{1,0:T(4,128)S(1)} %reduce_sum.18), channel_id=1, source_target_pairs={{0,1},{1,2},{2,3},{3,4},{4,5},{5,6},{6,7},{8,9},{9,10},{10,11},{11... | collective-permute-start | bytes 41480 | tf_op jit(solution)/shard_map/ppermute | solution.py:135
  19.7 2.7 %collective-permute-start.3 = (f32[3,1152]{1,0:T(4,128)S(1)}, f32[3,1152]{1,0:T(4,128)S(1)}, u32[]{:S(2)}, u32[]{:S(2)}) collective-permute-start(f32[3,1152]{1,0:T(4,128)S(1)} %reduce_sum.18), channel_id=1, source_target_pairs={{0,2},{1,3},{2,4},{3,5},{4,6},{5,7},{8,10},{9,11},{10,12},{11,13},... | collective-permute-start | bytes 41480 | tf_op jit(solution)/shard_map/ppermute | solution.py:135
  22.4 1.9 %collective-permute-start.4 = (f32[3,1152]{1,0:T(4,128)S(1)}, f32[3,1152]{1,0:T(4,128)S(1)}, u32[]{:S(2)}, u32[]{:S(2)}) collective-permute-start(f32[3,1152]{1,0:T(4,128)S(1)} %reduce_sum.18), channel_id=1, source_target_pairs={{0,3},{1,4},{2,5},{3,6},{4,7},{8,11},{9,12},{10,13},{11,14},{12,15... | collective-permute-start | bytes 41480 | tf_op jit(solution)/shard_map/ppermute | solution.py:135
  26.3 3.6 %collective-permute-done.4 = f32[3,1152]{1,0:T(4,128)S(1)} collective-permute-done((f32[3,1152]{1,0:T(4,128)S(1)}, f32[3,1152]{1,0:T(4,128)S(1)}, u32[]{:S(2)}, u32[]{:S(2)}) %collective-permute-start.4) | collective-permute-done | bytes 13856 | tf_op jit(solution)/shard_map/ppermute | solution.py:135
  29.9 2.2 %collective-permute-start.5 = (f32[3,1152]{1,0:T(4,128)S(1)}, f32[3,1152]{1,0:T(4,128)S(1)}, u32[]{:S(2)}, u32[]{:S(2)}) collective-permute-start(f32[3,1152]{1,0:T(4,128)S(1)} %add_add_fusion.1), channel_id=1, source_target_pairs={{0,4},{1,5},{2,6},{3,7},{8,12},{9,13},{10,14},{11,15},{16,20},{17,... | collective-permute-start | bytes 41480 | tf_op jit(solution)/shard_map/ppermute | solution.py:135
  32.5 0.8 copy-done.5
  35.4 0.8 copy-done.2
  36.2 0.9 %convolution_select_fusion = f32[864,256]{1,0:T(8,128)S(1)} fusion(pred[864,256]{1,0:T(32,128)(4,1)S(1)} %bitcast_compare_fusion, f32[864,256]{1,0:T(8,128)S(1)} %constant_dynamic-update-slice_fusion.18, f32[256,256]{1,0:T(8,128)S(1)} %copy-done.2), kind=kOutput, calls=%fused_computation | convolution fusion | flops 679698432 | bytes 2252800 | tf_op jit(solution)/shard_map/dot_general | solution.py:105
  37.0 0.9 %fusion.55 = f32[864,256]{1,0:T(8,128)S(1)} fusion(f32[864,256]{1,0:T(8,128)S(1)} %convolution_select_fusion, f32[256,256]{1,0:T(8,128)S(1)} %copy-done.3), kind=kOutput, calls=%fused_computation.168 | convolution fusion | flops 679477248 | bytes 2031616 | tf_op jit(solution)/shard_map/dot_general | solution.py:107
  38.9 1.9 %collective-permute-start.11 = (f32[8,1,1152]{2,1,0:T(1,128)S(1)}, f32[8,1,1152]{2,1,0:T(1,128)S(1)}, u32[]{:S(2)}, u32[]{:S(2)}) collective-permute-start(f32[8,1,1152]{2,1,0:T(1,128)S(1)} %slice.556), channel_id=1, source_target_pairs={{8,0},{16,8},{24,16},{32,24},{40,32},{48,40},{56,48},{64,56},{72,6... | collective-permute-start | bytes 110600 | tf_op jit(solution)/shard_map/ppermute | solution.py:32
  41.1 1.4 %collective-permute-done.11 = f32[8,1,1152]{2,1,0:T(1,128)S(1)} collective-permute-done((f32[8,1,1152]{2,1,0:T(1,128)S(1)}, f32[8,1,1152]{2,1,0:T(1,128)S(1)}, u32[]{:S(2)}, u32[]{:S(2)}) %collective-permute-start.11) | collective-permute-done | bytes 36896 | tf_op jit(solution)/shard_map/ppermute | solution.py:32
  43.5 4.3 %collective-permute-start.6 = (f32[3,1152]{1,0:T(4,128)S(1)}, f32[3,1152]{1,0:T(4,128)S(1)}, u32[]{:S(2)}, u32[]{:S(2)}) collective-permute-start(f32[3,1152]{1,0:T(4,128)S(1)} %get-tuple-element.10), channel_id=1, source_target_pairs={{1,0},{2,1},{3,2},{4,3},{5,4},{6,5},{7,6},{9,8},{10,9},{11,10},{12... | collective-permute-start | bytes 41480 | tf_op jit(solution)/shard_map/ppermute | solution.py:135
  47.8 4.9 %collective-permute-start.7 = (f32[3,1152]{1,0:T(4,128)S(1)}, f32[3,1152]{1,0:T(4,128)S(1)}, u32[]{:S(2)}, u32[]{:S(2)}) collective-permute-start(f32[3,1152]{1,0:T(4,128)S(1)} %get-tuple-element.10), channel_id=1, source_target_pairs={{2,0},{3,1},{4,2},{5,3},{6,4},{7,5},{10,8},{11,9},{12,10},{13,11},... | collective-permute-start | bytes 41480 | tf_op jit(solution)/shard_map/ppermute | solution.py:135
  52.7 1.9 %collective-permute-start.8 = (f32[3,1152]{1,0:T(4,128)S(1)}, f32[3,1152]{1,0:T(4,128)S(1)}, u32[]{:S(2)}, u32[]{:S(2)}) collective-permute-start(f32[3,1152]{1,0:T(4,128)S(1)} %get-tuple-element.10), channel_id=1, source_target_pairs={{3,0},{4,1},{5,2},{6,3},{7,4},{11,8},{12,9},{13,10},{14,11},{15,12... | collective-permute-start | bytes 41480 | tf_op jit(solution)/shard_map/ppermute | solution.py:135
  54.7 1.0 %collective-permute-done.7 = f32[3,1152]{1,0:T(4,128)S(1)} collective-permute-done((f32[3,1152]{1,0:T(4,128)S(1)}, f32[3,1152]{1,0:T(4,128)S(1)}, u32[]{:S(2)}, u32[]{:S(2)}) %collective-permute-start.7) | collective-permute-done | bytes 13856 | tf_op jit(solution)/shard_map/ppermute | solution.py:135
  55.6 5.7 %collective-permute-done.8 = f32[3,1152]{1,0:T(4,128)S(1)} collective-permute-done((f32[3,1152]{1,0:T(4,128)S(1)}, f32[3,1152]{1,0:T(4,128)S(1)}, u32[]{:S(2)}, u32[]{:S(2)}) %collective-permute-start.8) | collective-permute-done | bytes 13856 | tf_op jit(solution)/shard_map/ppermute | solution.py:135
  61.4 1.3 %collective-permute-start.9 = (f32[3,1152]{1,0:T(4,128)S(1)}, f32[3,1152]{1,0:T(4,128)S(1)}, u32[]{:S(2)}, u32[]{:S(2)}) collective-permute-start(f32[3,1152]{1,0:T(4,128)S(1)} %add_add_fusion), channel_id=1, source_target_pairs={{4,0},{5,1},{6,2},{7,3},{12,8},{13,9},{14,10},{15,11},{20,16},{21,... | collective-permute-start | bytes 41480 | tf_op jit(solution)/shard_map/ppermute | solution.py:135
  62.7 8.2 %collective-permute-done.9 = f32[3,1152]{1,0:T(4,128)S(1)} collective-permute-done((f32[3,1152]{1,0:T(4,128)S(1)}, f32[3,1152]{1,0:T(4,128)S(1)}, u32[]{:S(2)}, u32[]{:S(2)}) %collective-permute-start.9) | collective-permute-done | bytes 13856 | tf_op jit(solution)/shard_map/ppermute | solution.py:135
  71.1 1.9 %collective-permute-start.10 = (f32[8,1,1152]{2,1,0:T(1,128)S(1)}, f32[8,1,1152]{2,1,0:T(1,128)S(1)}, u32[]{:S(2)}, u32[]{:S(2)}) collective-permute-start(f32[8,1,1152]{2,1,0:T(1,128)S(1)} %slice.550), channel_id=1, source_target_pairs={{0,8},{8,16},{16,24},{24,32},{32,40},{40,48},{48,56},{56,64},{64,7... | collective-permute-start | bytes 110600 | tf_op jit(solution)/shard_map/ppermute | solution.py:32
  73.1 0.7 copy.63
  73.8 0.7 copy.62
  74.5 0.7 copy.64
  75.2 4.5 %collective-permute-done.10 = f32[8,1,1152]{2,1,0:T(1,128)S(1)} collective-permute-done((f32[8,1,1152]{2,1,0:T(1,128)S(1)}, f32[8,1,1152]{2,1,0:T(1,128)S(1)}, u32[]{:S(2)}, u32[]{:S(2)}) %collective-permute-start.10) | collective-permute-done | bytes 36896 | tf_op jit(solution)/shard_map/ppermute | solution.py:32
  79.9 0.7 copy.60
  80.5 0.7 copy.61
  (139 shorter events, 7.3 us)
Async XLA Ops:
  0.6 4.9 %copy-start = (f32[8,3,1152]{2,0,1:T(8,128)S(1)}, f32[8,3,1152]{2,0,1:T(8,128)}, u32[]{:S(2)}) copy-start(f32[8,3,1152]{2,0,1:T(8,128)} %param.13) | copy-start | bytes 331780
  0.6 4.9 %copy-start.1 = (f32[8,3,1152]{2,0,1:T(8,128)S(1)}, f32[8,3,1152]{2,0,1:T(8,128)}, u32[]{:S(2)}) copy-start(f32[8,3,1152]{2,0,1:T(8,128)} %param.14) | copy-start | bytes 331780
  1.8 3.8 %copy-start.4 = (f32[8,3,1152]{2,0,1:T(8,128)S(1)}, f32[8,3,1152]{2,0,1:T(8,128)}, u32[]{:S(2)}) copy-start(f32[8,3,1152]{2,0,1:T(8,128)} %param.11) | copy-start | bytes 331780
  6.0 18.9 %copy-start.10 = (s32[192]{0:T(256)S(1)}, s32[192]{0:T(256)}, u32[]{:S(2)}) copy-start(s32[192]{0:T(256)} %param.16) | copy-start | bytes 2308
  6.1 26.1 %collective-permute-start = (f32[2,8,3,1152]{3,2,1,0:T(4,128)S(1)}, f32[2,8,3,1152]{3,2,1,0:T(4,128)S(1)}, u32[]{:S(2)}, u32[]{:S(2)}) collective-permute-start(f32[2,8,3,1152]{3,2,1,0:T(4,128)S(1)} %pad_maximum_fusion.2), channel_id=1, source_target_pairs={{0,8},{8,16},{16,24},{24,32},{32,40},{40,48},{48,56},{56,64},{64,7... | collective-permute-start | bytes 663560 | tf_op jit(solution)/shard_map/ppermute | solution.py:20
  8.0 24.1 %collective-permute-start.1 = (f32[2,8,3,1152]{3,2,1,0:T(4,128)S(1)}, f32[2,8,3,1152]{3,2,1,0:T(4,128)S(1)}, u32[]{:S(2)}, u32[]{:S(2)}) collective-permute-start(f32[2,8,3,1152]{3,2,1,0:T(4,128)S(1)} %pad_maximum_fusion.2), channel_id=1, source_target_pairs={{8,0},{16,8},{24,16},{32,24},{40,32},{48,40},{56,48},{64,56},{72,6... | collective-permute-start | bytes 663560 | tf_op jit(solution)/shard_map/ppermute | solution.py:22
  15.0 10.6 %collective-permute-start.2 = (f32[3,1152]{1,0:T(4,128)S(1)}, f32[3,1152]{1,0:T(4,128)S(1)}, u32[]{:S(2)}, u32[]{:S(2)}) collective-permute-start(f32[3,1152]{1,0:T(4,128)S(1)} %reduce_sum.18), channel_id=1, source_target_pairs={{0,1},{1,2},{2,3},{3,4},{4,5},{5,6},{6,7},{8,9},{9,10},{10,11},{11... | collective-permute-start | bytes 41480 | tf_op jit(solution)/shard_map/ppermute | solution.py:135
  19.7 6.6 %collective-permute-start.3 = (f32[3,1152]{1,0:T(4,128)S(1)}, f32[3,1152]{1,0:T(4,128)S(1)}, u32[]{:S(2)}, u32[]{:S(2)}) collective-permute-start(f32[3,1152]{1,0:T(4,128)S(1)} %reduce_sum.18), channel_id=1, source_target_pairs={{0,2},{1,3},{2,4},{3,5},{4,6},{5,7},{8,10},{9,11},{10,12},{11,13},... | collective-permute-start | bytes 41480 | tf_op jit(solution)/shard_map/ppermute | solution.py:135
  22.4 7.5 %collective-permute-start.4 = (f32[3,1152]{1,0:T(4,128)S(1)}, f32[3,1152]{1,0:T(4,128)S(1)}, u32[]{:S(2)}, u32[]{:S(2)}) collective-permute-start(f32[3,1152]{1,0:T(4,128)S(1)} %reduce_sum.18), channel_id=1, source_target_pairs={{0,3},{1,4},{2,5},{3,6},{4,7},{8,11},{9,12},{10,13},{11,14},{12,15... | collective-permute-start | bytes 41480 | tf_op jit(solution)/shard_map/ppermute | solution.py:135
  24.3 1.1 %copy-start.9 = (s32[9,256]{1,0:T(8,128)S(1)}, s32[9,256]{1,0:T(8,128)}, u32[]{:S(2)}) copy-start(s32[9,256]{1,0:T(8,128)} %constant.129) | copy-start | bytes 27652
  29.9 11.0 %collective-permute-start.5 = (f32[3,1152]{1,0:T(4,128)S(1)}, f32[3,1152]{1,0:T(4,128)S(1)}, u32[]{:S(2)}, u32[]{:S(2)}) collective-permute-start(f32[3,1152]{1,0:T(4,128)S(1)} %add_add_fusion.1), channel_id=1, source_target_pairs={{0,4},{1,5},{2,6},{3,7},{8,12},{9,13},{10,14},{11,15},{16,20},{17,... | collective-permute-start | bytes 41480 | tf_op jit(solution)/shard_map/ppermute | solution.py:135
  32.4 0.9 %copy-start.5 = (f32[8,3,1152]{2,0,1:T(8,128)S(1)}, f32[8,3,1152]{2,0,1:T(8,128)}, u32[]{:S(2)}) copy-start(f32[8,3,1152]{2,0,1:T(8,128)} %param.12) | copy-start | bytes 331780
  34.3 0.7 copy-start.6
  34.3 0.7 copy-start.7
  35.2 1.0 %copy-start.2 = (f32[256,256]{1,0:T(8,128)S(1)}, f32[256,256]{1,0:T(8,128)}, u32[]{:S(2)}) copy-start(f32[256,256]{1,0:T(8,128)} %constant.121.clone) | copy-start | bytes 786436
  35.4 1.7 %copy-start.3 = (f32[256,256]{1,0:T(8,128)S(1)}, f32[256,256]{1,0:T(8,128)}, u32[]{:S(2)}) copy-start(f32[256,256]{1,0:T(8,128)} %constant.123.clone) | copy-start | bytes 786436
  38.9 3.5 %collective-permute-start.11 = (f32[8,1,1152]{2,1,0:T(1,128)S(1)}, f32[8,1,1152]{2,1,0:T(1,128)S(1)}, u32[]{:S(2)}, u32[]{:S(2)}) collective-permute-start(f32[8,1,1152]{2,1,0:T(1,128)S(1)} %slice.556), channel_id=1, source_target_pairs={{8,0},{16,8},{24,16},{32,24},{40,32},{48,40},{56,48},{64,56},{72,6... | collective-permute-start | bytes 110600 | tf_op jit(solution)/shard_map/ppermute | solution.py:32
  43.3 27.7 %copy-start.8 = (f32[3,1152]{1,0:T(4,128)S(1)}, f32[3,1152]{1,0:T(4,128)}, u32[]{:S(2)}) copy-start(f32[3,1152]{1,0:T(4,128)} %param.15) | copy-start | bytes 41476
  43.5 11.2 %collective-permute-start.6 = (f32[3,1152]{1,0:T(4,128)S(1)}, f32[3,1152]{1,0:T(4,128)S(1)}, u32[]{:S(2)}, u32[]{:S(2)}) collective-permute-start(f32[3,1152]{1,0:T(4,128)S(1)} %get-tuple-element.10), channel_id=1, source_target_pairs={{1,0},{2,1},{3,2},{4,3},{5,4},{6,5},{7,6},{9,8},{10,9},{11,10},{12... | collective-permute-start | bytes 41480 | tf_op jit(solution)/shard_map/ppermute | solution.py:135
  47.8 7.9 %collective-permute-start.7 = (f32[3,1152]{1,0:T(4,128)S(1)}, f32[3,1152]{1,0:T(4,128)S(1)}, u32[]{:S(2)}, u32[]{:S(2)}) collective-permute-start(f32[3,1152]{1,0:T(4,128)S(1)} %get-tuple-element.10), channel_id=1, source_target_pairs={{2,0},{3,1},{4,2},{5,3},{6,4},{7,5},{10,8},{11,9},{12,10},{13,11},... | collective-permute-start | bytes 41480 | tf_op jit(solution)/shard_map/ppermute | solution.py:135
  52.7 8.7 %collective-permute-start.8 = (f32[3,1152]{1,0:T(4,128)S(1)}, f32[3,1152]{1,0:T(4,128)S(1)}, u32[]{:S(2)}, u32[]{:S(2)}) collective-permute-start(f32[3,1152]{1,0:T(4,128)S(1)} %get-tuple-element.10), channel_id=1, source_target_pairs={{3,0},{4,1},{5,2},{6,3},{7,4},{11,8},{12,9},{13,10},{14,11},{15,12... | collective-permute-start | bytes 41480 | tf_op jit(solution)/shard_map/ppermute | solution.py:135
  61.4 9.6 %collective-permute-start.9 = (f32[3,1152]{1,0:T(4,128)S(1)}, f32[3,1152]{1,0:T(4,128)S(1)}, u32[]{:S(2)}, u32[]{:S(2)}) collective-permute-start(f32[3,1152]{1,0:T(4,128)S(1)} %add_add_fusion), channel_id=1, source_target_pairs={{4,0},{5,1},{6,2},{7,3},{12,8},{13,9},{14,10},{15,11},{20,16},{21,... | collective-permute-start | bytes 41480 | tf_op jit(solution)/shard_map/ppermute | solution.py:135
  71.1 8.6 %collective-permute-start.10 = (f32[8,1,1152]{2,1,0:T(1,128)S(1)}, f32[8,1,1152]{2,1,0:T(1,128)S(1)}, u32[]{:S(2)}, u32[]{:S(2)}) collective-permute-start(f32[8,1,1152]{2,1,0:T(1,128)S(1)} %slice.550), channel_id=1, source_target_pairs={{0,8},{8,16},{16,24},{24,32},{32,40},{40,48},{48,56},{56,64},{64,7... | collective-permute-start | bytes 110600 | tf_op jit(solution)/shard_map/ppermute | solution.py:32

commit v2 on v0

--- a/solution.py
+++ b/solution.py
@@ -42,9 +42,9 @@
 
 def face_lat(padded, count):
     return (
-        37.0 * (padded[..., 2 : 2 + count, :] + padded[..., 3 : 3 + count, :])
-        - 8.0 * (padded[..., 1 : 1 + count, :] + padded[..., 4 : 4 + count, :])
-        + (padded[..., 0:count, :] + padded[..., 5 : 5 + count, :])
+        37.0 * (padded[2 : 2 + count] + padded[3 : 3 + count])
+        - 8.0 * (padded[1 : 1 + count] + padded[4 : 4 + count])
+        + (padded[0:count] + padded[5 : 5 + count])
     ) / 60.0
 
 
@@ -137,53 +137,57 @@
 
 def local(wind_east, wind_north, layer_mass, theta_field, surface_height, filter_cutoff):
     levels, lat_rows, length = wind_east.shape
+    wind_east, wind_north, layer_mass, theta_field = (
+        jnp.transpose(v, (1, 0, 2)) for v in (wind_east, wind_north, layer_mass, theta_field)
+    )
     lat_count = lax.axis_size("lat")
     lat_rank = lax.axis_index("lat")
     nlat_all = lat_rows * lat_count
     first_row = lat_rank * lat_rows
     row_ids = first_row + jnp.arange(lat_rows, dtype=jnp.int32)
-    coslat = jnp.sin(jnp.pi * row_ids.astype(jnp.float32) / nlat_all)[None, :, None]
+    coslat = jnp.sin(jnp.pi * row_ids.astype(jnp.float32) / nlat_all)[:, None, None]
     stacked = jnp.stack([layer_mass, theta_field])
-    padded = extended(stacked, (("lat", 2),), 3)
+    padded = extended(stacked, (("lat", 1),), 3)
     mass_faces = face_lat(padded[0], lat_rows)
     theta_faces = face_lat(padded[1], lat_rows + 1)
     flux_east = wind_east * face_lon(layer_mass)
     flux_north = wind_north * mass_faces * coslat
     fields = jnp.stack([wind_east, wind_north, flux_east, flux_north])
     own_cuts = lax.dynamic_slice_in_dim(filter_cutoff, first_row, lat_rows)
-    row_cuts = jnp.broadcast_to(own_cuts, (4, levels, lat_rows)).reshape(-1)
+    row_cuts = jnp.broadcast_to(own_cuts[None, :, None], fields.shape[:3]).reshape(-1)
     smooth = filter_rows(fields.reshape(-1, length), row_cuts).reshape(fields.shape)
     east_smooth = smooth[0]
     north_smooth = smooth[1]
     east_flux = smooth[2]
     north_flux = smooth[3]
-    next_face = from_behind(north_flux[:, :1], "lat", -1)
-    north_full = jnp.concatenate([north_flux, next_face], axis=1)
+    next_face = from_behind(north_flux[:1], "lat", -1)
+    north_full = jnp.concatenate([north_flux, next_face], axis=0)
     new_mass = layer_mass - TIME_STEP * (
-        jnp.roll(east_flux, -1, -1) - east_flux + (north_full[:, 1:] - north_full[:, :-1])
+        jnp.roll(east_flux, -1, -1) - east_flux + (north_full[1:] - north_full[:-1])
     )
     heat_east = east_flux * face_lon(theta_field)
     heat_north = north_full * theta_faces
     new_heat = theta_field * layer_mass - TIME_STEP * (
-        jnp.roll(heat_east, -1, -1) - heat_east + (heat_north[:, 1:] - heat_north[:, :-1])
-    )
-    column = jnp.sum(layer_mass, axis=0)
+        jnp.roll(heat_east, -1, -1) - heat_east + (heat_north[1:] - heat_north[:-1])
+    )
+    column = jnp.sum(layer_mass, axis=1)
     above_mass = prefix_over(column, "lev", True)
-    bottom = TOP_PRESSURE + above_mass[None] + jnp.cumsum(layer_mass, axis=0)
+    bottom = TOP_PRESSURE + above_mass[:, None] + jnp.cumsum(layer_mass, axis=1)
     top_press = bottom - layer_mass
     thickness = GAS_CONST * theta_field * (jnp.log(bottom) - jnp.log(top_press))
-    depth_sum = jnp.sum(thickness, axis=0)
+    depth_sum = jnp.sum(thickness, axis=1)
     below_depth = prefix_over(depth_sum, "lev", False)
-    inclusive = jnp.flip(jnp.cumsum(jnp.flip(thickness, 0), axis=0), 0)
-    height_cols = (
-        surface_height[None] + below_depth[None] + (inclusive - thickness) + 0.5 * thickness
-    )
-    lower_row = from_behind(height_cols[:, -1:], "lat", 1)
-    height_south = jnp.concatenate([lower_row, height_cols[:, :-1]], axis=1)
-    new_east = east_smooth - TIME_STEP * (height_cols - jnp.roll(height_cols, 1, -1))
-    inside = (row_ids > 0).astype(jnp.float32)[None, :, None]
-    new_north = (north_smooth - TIME_STEP * (height_cols - height_south)) * inside
-    return (new_east, new_north, new_mass, new_heat, height_cols)
+    inclusive = jnp.flip(jnp.cumsum(jnp.flip(thickness, 1), axis=1), 1)
+    height = (
+        surface_height[:, None] + below_depth[:, None] + (inclusive - thickness) + 0.5 * thickness
+    )
+    lower_row = from_behind(height[-1:], "lat", 1)
+    height_south = jnp.concatenate([lower_row, height[:-1]], axis=0)
+    new_east = east_smooth - TIME_STEP * (height - jnp.roll(height, 1, -1))
+    inside = (row_ids > 0).astype(jnp.float32)[:, None, None]
+    new_north = (north_smooth - TIME_STEP * (height - height_south)) * inside
+    outputs = (new_east, new_north, new_mass, new_heat, height)
+    return tuple(jnp.transpose(v, (1, 0, 2)) for v in outputs)
 
 
 def solution(mesh):

time: 74.9 us -> 77.9 us (1.040)
  local copies, waits for them, and re-layouts: 12.3 us -> 6.31 us
  starting transfers between devices: 40.6 us -> 45 us
  waiting for transfers between devices: 14 us -> 17.1 us
  other arithmetic: 3.84 us -> 5.6 us
    ppermute x2, starting transfers between devices: 3.84 us -> 8.3 us  [from_behind(): return lax.ppermute(block, axis, route)]
    ppermute x2, waiting for transfers between devices: 5.81 us -> 8.05 us  [from_behind(): return lax.ppermute(block, axis, route)]
    slice x4, local copies, waits for them, and re-layouts: 2.07 us -> 0.33 us  [face_lon(): jnp.roll(values, -1, -1)]
    slice x4, local copies, waits for them, and re-layouts: 2.03 us -> 0.32 us  [face_lon(): jnp.roll(values, -2, -1)]
    unnamed x59 -> x35, local copies, waits for them, and re-layouts: 5.96 us -> 4.45 us
    another operation x1, other arithmetic: 0.07 us -> 1 us  [local(): stacked = jnp.stack([layer_mass, theta_field])]
    transpose x0 -> x1, other arithmetic: none -> 0.79 us  [local(): return tuple((jnp.transpose(v, (1, 0, 2)) for v in outputs))]
  transfers between devices with their start and end apart: 18 -> 18, of which waited for: 7 -> 10; matrix products, arithmetic and copies ran while one was open for 11% -> 3% of each run, Pallas kernels for 0% -> 0%
where the time goes in v2:
time: 77.9 us; the launch traced here: 77.1 us
  starting transfers between devices  45 us (58%)
  waiting for transfers between devices  17.1 us (22%)
  local copies, waits for them, and re-layouts  6.31 us (8%)
  other arithmetic  5.6 us (7%)
  matrix products  1.72 us (2%)
  between operations  1.4 us (2%)
    ppermute x14, starting transfers between devices, prefix_over(): total = total + lax.ppermute(value, axis, route)  27.8 us
    ppermute x14, waiting for transfers between devices, prefix_over(): total = total + lax.ppermute(value, axis, route)  8.91 us
    ppermute x2, starting transfers between devices, from_behind(): return lax.ppermute(block, axis, route)  8.3 us
    ppermute x2, waiting for transfers between devices, from_behind(): return lax.ppermute(block, axis, route)  8.05 us
    ppermute x1, starting transfers between devices, extended(): lax.ppermute(head, axis, [((i + 1) % count, i) for i in range(ends)])  6.96 us
    unnamed x35, local copies, waits for them, and re-layouts  4.45 us
    ppermute x1, starting transfers between devices, extended(): lax.ppermute(tail, axis, [(i, (i + 1) % count) for i in range(ends)])  1.92 us
  transfers between devices with their start and end apart: 18, of which 10 were waited for; matrix products, arithmetic and copies ran while one was open for 3% of the time, Pallas kernels for 0%

profile of v2, /device:TPU:256, one launch (start us, length us, event | category | flops | bytes accessed | tf_op | source)
XLA Modules:
  0.0 77.1 jit_solution(17483995507054644890)
XLA Ops:
  0.6 1.0 %pad_maximum_fusion.2 = f32[2,3,8,1152]{3,2,1,0:T(8,128)S(1)} fusion(f32[1,3,8,1152]{3,2,1,0:T(8,128)} %bitcast.124, f32[1,3,8,1152]{3,2,1,0:T(8,128)} %bitcast.115), kind=kLoop, calls=%fused_computation.9 | loop fusion | flops 55296 | bytes 442368 | tf_op jit(solution)/shard_map/stack | solution.py:149
  1.6 1.9 %collective-permute-start = (f32[2,3,8,1152]{3,2,1,0:T(8,128)S(1)}, f32[2,3,8,1152]{3,2,1,0:T(8,128)S(1)}, u32[]{:S(2)}, u32[]{:S(2)}) collective-permute-start(f32[2,3,8,1152]{3,2,1,0:T(8,128)S(1)} %pad_maximum_fusion.2), channel_id=1, source_target_pairs={{0,8},{8,16},{16,24},{24,32},{32,40},{40,48},{48,56},{56,64},{64,7... | collective-permute-start | bytes 663560 | tf_op jit(solution)/shard_map/ppermute | solution.py:20
  3.6 7.0 %collective-permute-start.1 = (f32[2,3,8,1152]{3,2,1,0:T(8,128)S(1)}, f32[2,3,8,1152]{3,2,1,0:T(8,128)S(1)}, u32[]{:S(2)}, u32[]{:S(2)}) collective-permute-start(f32[2,3,8,1152]{3,2,1,0:T(8,128)S(1)} %pad_maximum_fusion.2), channel_id=1, source_target_pairs={{8,0},{16,8},{24,16},{32,24},{40,32},{48,40},{56,48},{64,56},{72,6... | collective-permute-start | bytes 663560 | tf_op jit(solution)/shard_map/ppermute | solution.py:22
  16.7 0.9 %copy-done.5 = f32[256,256]{1,0:T(8,128)S(1)} copy-done((f32[256,256]{1,0:T(8,128)S(1)}, f32[256,256]{1,0:T(8,128)}, u32[]{:S(2)}) %copy-start.5) | copy-done | bytes 262168
  17.6 0.9 %convolution_select_fusion = f32[864,256]{1,0:T(8,128)S(1)} fusion(pred[864,256]{1,0:T(32,128)(4,1)S(1)} %bitcast_compare_fusion, f32[864,256]{1,0:T(8,128)S(1)} %constant_dynamic-update-slice_fusion.18, f32[256,256]{1,0:T(8,128)S(1)} %copy-done.5), kind=kOutput, calls=%fused_computation | convolution fusion | flops 679698432 | bytes 2252800 | tf_op jit(solution)/shard_map/dot_general | solution.py:105
  18.6 0.9 %fusion.61 = f32[864,256]{1,0:T(8,128)S(1)} fusion(f32[864,256]{1,0:T(8,128)S(1)} %convolution_select_fusion, f32[256,256]{1,0:T(8,128)S(1)} %copy-done.6), kind=kOutput, calls=%fused_computation.172 | convolution fusion | flops 679477248 | bytes 2031616 | tf_op jit(solution)/shard_map/dot_general | solution.py:107
  20.4 6.4 %collective-permute-start.17 = (f32[1,8,1152]{2,1,0:T(8,128)S(1)}, f32[1,8,1152]{2,1,0:T(8,128)S(1)}, u32[]{:S(2)}, u32[]{:S(2)}) collective-permute-start(f32[1,8,1152]{2,1,0:T(8,128)S(1)} %slice_bitcast_fusion.5), channel_id=1, source_target_pairs={{8,0},{16,8},{24,16},{32,24},{40,32},{48,40},{56,48},{64,56},{72,6... | collective-permute-start | bytes 110600 | tf_op jit(solution)/shard_map/ppermute | solution.py:32
  26.9 1.5 %collective-permute-done.17 = f32[1,8,1152]{2,1,0:T(8,128)S(1)} collective-permute-done((f32[1,8,1152]{2,1,0:T(8,128)S(1)}, f32[1,8,1152]{2,1,0:T(8,128)S(1)}, u32[]{:S(2)}, u32[]{:S(2)}) %collective-permute-start.17) | collective-permute-done | bytes 36896 | tf_op jit(solution)/shard_map/ppermute | solution.py:32
  28.4 0.8 %fusion.46 = (f32[3,8,1152]{2,1,0:T(8,128)S(1)}, f32[8,3,1152]{2,0,1:T(8,128)}, f32[3,1152]{1,0:T(4,128)S(1)}) fusion(f32[3,8,1151]{2,1,0:T(8,128)S(1)} %get-tuple-element.74, f32[3,8,1]{2,1,0:T(8,128)S(1)} %get-tuple-element.76, f32[3,8,1150]{2,1,0:T(8,128)S(1)} %get-tuple-element.70, f32[3,8,2]{2,1,0:T(8,128)S(1)} %get-tuple-element.72, ...), kind=kLoop, calls=%fused_computation.131 | loop fusion | flops 604800 | bytes 1377792 | tf_op jit(solution)/shard_map/mul | solution.py:168
  29.2 3.5 %collective-permute-start.2 = (f32[3,1152]{1,0:T(4,128)S(1)}, f32[3,1152]{1,0:T(4,128)S(1)}, u32[]{:S(2)}, u32[]{:S(2)}) collective-permute-start(f32[3,1152]{1,0:T(4,128)S(1)} %get-tuple-element.68), channel_id=1, source_target_pairs={{0,1},{1,2},{2,3},{3,4},{4,5},{5,6},{6,7},{8,9},{9,10},{10,11},{11... | collective-permute-start | bytes 41480 | tf_op jit(solution)/shard_map/ppermute | solution.py:134
  32.7 4.5 %collective-permute-start.3 = (f32[3,1152]{1,0:T(4,128)S(1)}, f32[3,1152]{1,0:T(4,128)S(1)}, u32[]{:S(2)}, u32[]{:S(2)}) collective-permute-start(f32[3,1152]{1,0:T(4,128)S(1)} %get-tuple-element.68), channel_id=1, source_target_pairs={{0,2},{1,3},{2,4},{3,5},{4,6},{5,7},{8,10},{9,11},{10,12},{11,13},... | collective-permute-start | bytes 41480 | tf_op jit(solution)/shard_map/ppermute | solution.py:134
  37.3 4.9 %collective-permute-start.4 = (f32[3,1152]{1,0:T(4,128)S(1)}, f32[3,1152]{1,0:T(4,128)S(1)}, u32[]{:S(2)}, u32[]{:S(2)}) collective-permute-start(f32[3,1152]{1,0:T(4,128)S(1)} %get-tuple-element.68), channel_id=1, source_target_pairs={{0,3},{1,4},{2,5},{3,6},{4,7},{8,11},{9,12},{10,13},{11,14},{12,15... | collective-permute-start | bytes 41480 | tf_op jit(solution)/shard_map/ppermute | solution.py:134
  42.2 2.0 %collective-permute-start.5 = (f32[3,1152]{1,0:T(4,128)S(1)}, f32[3,1152]{1,0:T(4,128)S(1)}, u32[]{:S(2)}, u32[]{:S(2)}) collective-permute-start(f32[3,1152]{1,0:T(4,128)S(1)} %get-tuple-element.68), channel_id=1, source_target_pairs={{0,4},{1,5},{2,6},{3,7},{8,12},{9,13},{10,14},{11,15},{16,20},{17,... | collective-permute-start | bytes 41480 | tf_op jit(solution)/shard_map/ppermute | solution.py:134
  44.2 1.3 %collective-permute-start.6 = (f32[3,1152]{1,0:T(4,128)S(1)}, f32[3,1152]{1,0:T(4,128)S(1)}, u32[]{:S(2)}, u32[]{:S(2)}) collective-permute-start(f32[3,1152]{1,0:T(4,128)S(1)} %get-tuple-element.68), channel_id=1, source_target_pairs={{0,5},{1,6},{2,7},{8,13},{9,14},{10,15},{16,21},{17,22},{18,23},{2... | collective-permute-start | bytes 41480 | tf_op jit(solution)/shard_map/ppermute | solution.py:134
  45.6 1.3 %collective-permute-start.7 = (f32[3,1152]{1,0:T(4,128)S(1)}, f32[3,1152]{1,0:T(4,128)S(1)}, u32[]{:S(2)}, u32[]{:S(2)}) collective-permute-start(f32[3,1152]{1,0:T(4,128)S(1)} %get-tuple-element.68), channel_id=1, source_target_pairs={{0,6},{1,7},{8,14},{9,15},{16,22},{17,23},{24,30},{25,31},{32,38},... | collective-permute-start | bytes 41480 | tf_op jit(solution)/shard_map/ppermute | solution.py:134
  46.9 1.3 %collective-permute-start.8 = (f32[3,1152]{1,0:T(4,128)S(1)}, f32[3,1152]{1,0:T(4,128)S(1)}, u32[]{:S(2)}, u32[]{:S(2)}) collective-permute-start(f32[3,1152]{1,0:T(4,128)S(1)} %get-tuple-element.68), channel_id=1, source_target_pairs={{0,7},{8,15},{16,23},{24,31},{32,39},{40,47},{48,55},{56,63},{64,7... | collective-permute-start | bytes 41480 | tf_op jit(solution)/shard_map/ppermute | solution.py:134
  48.4 1.2 %collective-permute-done.8 = f32[3,1152]{1,0:T(4,128)S(1)} collective-permute-done((f32[3,1152]{1,0:T(4,128)S(1)}, f32[3,1152]{1,0:T(4,128)S(1)}, u32[]{:S(2)}, u32[]{:S(2)}) %collective-permute-start.8) | collective-permute-done | bytes 13856 | tf_op jit(solution)/shard_map/ppermute | solution.py:134
  50.4 1.3 %collective-permute-start.10 = (f32[3,1152]{1,0:T(4,128)S(1)}, f32[3,1152]{1,0:T(4,128)S(1)}, u32[]{:S(2)}, u32[]{:S(2)}) collective-permute-start(f32[3,1152]{1,0:T(4,128)S(1)} %get-tuple-element.5), channel_id=1, source_target_pairs={{2,0},{3,1},{4,2},{5,3},{6,4},{7,5},{10,8},{11,9},{12,10},{13,11},... | collective-permute-start | bytes 41480 | tf_op jit(solution)/shard_map/ppermute | solution.py:134
  51.7 1.3 %collective-permute-start.11 = (f32[3,1152]{1,0:T(4,128)S(1)}, f32[3,1152]{1,0:T(4,128)S(1)}, u32[]{:S(2)}, u32[]{:S(2)}) collective-permute-start(f32[3,1152]{1,0:T(4,128)S(1)} %get-tuple-element.5), channel_id=1, source_target_pairs={{3,0},{4,1},{5,2},{6,3},{7,4},{11,8},{12,9},{13,10},{14,11},{15,12... | collective-permute-start | bytes 41480 | tf_op jit(solution)/shard_map/ppermute | solution.py:134
  53.0 1.3 %collective-permute-start.12 = (f32[3,1152]{1,0:T(4,128)S(1)}, f32[3,1152]{1,0:T(4,128)S(1)}, u32[]{:S(2)}, u32[]{:S(2)}) collective-permute-start(f32[3,1152]{1,0:T(4,128)S(1)} %get-tuple-element.5), channel_id=1, source_target_pairs={{4,0},{5,1},{6,2},{7,3},{12,8},{13,9},{14,10},{15,11},{20,16},{21,... | collective-permute-start | bytes 41480 | tf_op jit(solution)/shard_map/ppermute | solution.py:134
  54.3 1.3 %collective-permute-start.13 = (f32[3,1152]{1,0:T(4,128)S(1)}, f32[3,1152]{1,0:T(4,128)S(1)}, u32[]{:S(2)}, u32[]{:S(2)}) collective-permute-start(f32[3,1152]{1,0:T(4,128)S(1)} %get-tuple-element.5), channel_id=1, source_target_pairs={{5,0},{6,1},{7,2},{13,8},{14,9},{15,10},{21,16},{22,17},{23,18},{2... | collective-permute-start | bytes 41480 | tf_op jit(solution)/shard_map/ppermute | solution.py:134
  55.6 1.3 %collective-permute-start.14 = (f32[3,1152]{1,0:T(4,128)S(1)}, f32[3,1152]{1,0:T(4,128)S(1)}, u32[]{:S(2)}, u32[]{:S(2)}) collective-permute-start(f32[3,1152]{1,0:T(4,128)S(1)} %get-tuple-element.5), channel_id=1, source_target_pairs={{6,0},{7,1},{14,8},{15,9},{22,16},{23,17},{30,24},{31,25},{38,32},... | collective-permute-start | bytes 41480 | tf_op jit(solution)/shard_map/ppermute | solution.py:134
  56.9 1.3 %collective-permute-start.15 = (f32[3,1152]{1,0:T(4,128)S(1)}, f32[3,1152]{1,0:T(4,128)S(1)}, u32[]{:S(2)}, u32[]{:S(2)}) collective-permute-start(f32[3,1152]{1,0:T(4,128)S(1)} %get-tuple-element.5), channel_id=1, source_target_pairs={{7,0},{15,8},{23,16},{31,24},{39,32},{47,40},{55,48},{63,56},{71,6... | collective-permute-start | bytes 41480 | tf_op jit(solution)/shard_map/ppermute | solution.py:134
  58.2 0.9 %collective-permute-done.11 = f32[3,1152]{1,0:T(4,128)S(1)} collective-permute-done((f32[3,1152]{1,0:T(4,128)S(1)}, f32[3,1152]{1,0:T(4,128)S(1)}, u32[]{:S(2)}, u32[]{:S(2)}) %collective-permute-start.11) | collective-permute-done | bytes 13856 | tf_op jit(solution)/shard_map/ppermute | solution.py:134
  59.1 1.3 %collective-permute-start.9 = (f32[3,1152]{1,0:T(4,128)S(1)}, f32[3,1152]{1,0:T(4,128)S(1)}, u32[]{:S(2)}, u32[]{:S(2)}) collective-permute-start(f32[3,1152]{1,0:T(4,128)S(1)} %get-tuple-element.5), channel_id=1, source_target_pairs={{1,0},{2,1},{3,2},{4,3},{5,4},{6,5},{7,6},{9,8},{10,9},{11,10},{12... | collective-permute-start | bytes 41480 | tf_op jit(solution)/shard_map/ppermute | solution.py:134
  60.9 1.6 %collective-permute-done.12 = f32[3,1152]{1,0:T(4,128)S(1)} collective-permute-done((f32[3,1152]{1,0:T(4,128)S(1)}, f32[3,1152]{1,0:T(4,128)S(1)}, u32[]{:S(2)}, u32[]{:S(2)}) %collective-permute-start.12) | collective-permute-done | bytes 13856 | tf_op jit(solution)/shard_map/ppermute | solution.py:134
  62.5 2.5 %collective-permute-done.13 = f32[3,1152]{1,0:T(4,128)S(1)} collective-permute-done((f32[3,1152]{1,0:T(4,128)S(1)}, f32[3,1152]{1,0:T(4,128)S(1)}, u32[]{:S(2)}, u32[]{:S(2)}) %collective-permute-start.13) | collective-permute-done | bytes 13856 | tf_op jit(solution)/shard_map/ppermute | solution.py:134
  65.0 1.3 %collective-permute-done.14 = f32[3,1152]{1,0:T(4,128)S(1)} collective-permute-done((f32[3,1152]{1,0:T(4,128)S(1)}, f32[3,1152]{1,0:T(4,128)S(1)}, u32[]{:S(2)}, u32[]{:S(2)}) %collective-permute-start.14) | collective-permute-done | bytes 13856 | tf_op jit(solution)/shard_map/ppermute | solution.py:134
  66.3 1.3 %collective-permute-done.15 = f32[3,1152]{1,0:T(4,128)S(1)} collective-permute-done((f32[3,1152]{1,0:T(4,128)S(1)}, f32[3,1152]{1,0:T(4,128)S(1)}, u32[]{:S(2)}, u32[]{:S(2)}) %collective-permute-start.15) | collective-permute-done | bytes 13856 | tf_op jit(solution)/shard_map/ppermute | solution.py:134
  67.7 1.9 %collective-permute-start.16 = (f32[1,8,1152]{2,1,0:T(8,128)S(1)}, f32[1,8,1152]{2,1,0:T(8,128)S(1)}, u32[]{:S(2)}, u32[]{:S(2)}) collective-permute-start(f32[1,8,1152]{2,1,0:T(8,128)S(1)} %slice.583), channel_id=1, source_target_pairs={{0,8},{8,16},{16,24},{24,32},{32,40},{40,48},{48,56},{56,64},{64,7... | collective-permute-start | bytes 110600 | tf_op jit(solution)/shard_map/ppermute | solution.py:32
  69.7 6.6 %collective-permute-done.16 = f32[1,8,1152]{2,1,0:T(8,128)S(1)} collective-permute-done((f32[1,8,1152]{2,1,0:T(8,128)S(1)}, f32[1,8,1152]{2,1,0:T(8,128)S(1)}, u32[]{:S(2)}, u32[]{:S(2)}) %collective-permute-start.16) | collective-permute-done | bytes 36896 | tf_op jit(solution)/shard_map/ppermute | solution.py:32
  76.3 0.8 %fusion.19 = (f32[8,3,1152]{2,0,1:T(8,128)}, f32[8,3,1152]{2,0,1:T(8,128)}) fusion(f32[96,1152]{1,0:T(8,128)S(1)} %constant_dynamic-update-slice_fusion.45, f32[3,8,1152]{2,1,0:T(8,128)S(1)} %multiply_add_fusion.2, f32[2,8,1152]{2,1,0:T(8,128)S(1)} %slice.584, f32[1,8,1152]{2,1,0:T(8,128)S(1)} %collective-permute-done.16, f32[3]{0:T(128)S(1)} %compare_convert_fusion, ...), kind=kLoop, calls=%fused_computation.93 | loop fusion | flops 248832 | bytes 774156 | tf_op jit(solution)/shard_map/transpose | solution.py:190
  (119 shorter events, 8.6 us)
Async XLA Ops:
  0.6 9.9 %copy-start = (f32[8,3,1152]{2,0,1:T(8,128)S(1)}, f32[8,3,1152]{2,0,1:T(8,128)}, u32[]{:S(2)}) copy-start(f32[8,3,1152]{2,0,1:T(8,128)} %param.13) | copy-start | bytes 331780
  1.6 12.2 %collective-permute-start = (f32[2,3,8,1152]{3,2,1,0:T(8,128)S(1)}, f32[2,3,8,1152]{3,2,1,0:T(8,128)S(1)}, u32[]{:S(2)}, u32[]{:S(2)}) collective-permute-start(f32[2,3,8,1152]{3,2,1,0:T(8,128)S(1)} %pad_maximum_fusion.2), channel_id=1, source_target_pairs={{0,8},{8,16},{16,24},{24,32},{32,40},{40,48},{48,56},{56,64},{64,7... | collective-permute-start | bytes 663560 | tf_op jit(solution)/shard_map/ppermute | solution.py:20
  3.6 10.4 %collective-permute-start.1 = (f32[2,3,8,1152]{3,2,1,0:T(8,128)S(1)}, f32[2,3,8,1152]{3,2,1,0:T(8,128)S(1)}, u32[]{:S(2)}, u32[]{:S(2)}) collective-permute-start(f32[2,3,8,1152]{3,2,1,0:T(8,128)S(1)} %pad_maximum_fusion.2), channel_id=1, source_target_pairs={{8,0},{16,8},{24,16},{32,24},{40,32},{48,40},{56,48},{64,56},{72,6... | collective-permute-start | bytes 663560 | tf_op jit(solution)/shard_map/ppermute | solution.py:22
  10.7 0.9 %copy-start.1 = (f32[8,3,1152]{2,0,1:T(8,128)S(1)}, f32[8,3,1152]{2,0,1:T(8,128)}, u32[]{:S(2)}) copy-start(f32[8,3,1152]{2,0,1:T(8,128)} %param.14) | copy-start | bytes 331780
  12.0 0.7 copy-start.11
  12.9 0.7 copy-start.10
  13.9 0.9 %copy-start.3 = (f32[8,3,1152]{2,0,1:T(8,128)S(1)}, f32[8,3,1152]{2,0,1:T(8,128)}, u32[]{:S(2)}) copy-start(f32[8,3,1152]{2,0,1:T(8,128)} %param.11) | copy-start | bytes 331780
  13.9 0.9 %copy-start.4 = (f32[8,3,1152]{2,0,1:T(8,128)S(1)}, f32[8,3,1152]{2,0,1:T(8,128)}, u32[]{:S(2)}) copy-start(f32[8,3,1152]{2,0,1:T(8,128)} %param.12) | copy-start | bytes 331780
  15.7 0.7 copy-start.7
  15.7 0.7 copy-start.8
  16.7 1.0 %copy-start.5 = (f32[256,256]{1,0:T(8,128)S(1)}, f32[256,256]{1,0:T(8,128)}, u32[]{:S(2)}) copy-start(f32[256,256]{1,0:T(8,128)} %constant.121.clone) | copy-start | bytes 786436
  17.6 0.9 %copy-start.6 = (f32[256,256]{1,0:T(8,128)S(1)}, f32[256,256]{1,0:T(8,128)}, u32[]{:S(2)}) copy-start(f32[256,256]{1,0:T(8,128)} %constant.123.clone) | copy-start | bytes 786436
  20.4 8.0 %collective-permute-start.17 = (f32[1,8,1152]{2,1,0:T(8,128)S(1)}, f32[1,8,1152]{2,1,0:T(8,128)S(1)}, u32[]{:S(2)}, u32[]{:S(2)}) collective-permute-start(f32[1,8,1152]{2,1,0:T(8,128)S(1)} %slice_bitcast_fusion.5), channel_id=1, source_target_pairs={{8,0},{16,8},{24,16},{32,24},{40,32},{48,40},{56,48},{64,56},{72,6... | collective-permute-start | bytes 110600 | tf_op jit(solution)/shard_map/ppermute | solution.py:32
  29.2 16.4 %collective-permute-start.2 = (f32[3,1152]{1,0:T(4,128)S(1)}, f32[3,1152]{1,0:T(4,128)S(1)}, u32[]{:S(2)}, u32[]{:S(2)}) collective-permute-start(f32[3,1152]{1,0:T(4,128)S(1)} %get-tuple-element.68), channel_id=1, source_target_pairs={{0,1},{1,2},{2,3},{3,4},{4,5},{5,6},{6,7},{8,9},{9,10},{10,11},{11... | collective-permute-start | bytes 41480 | tf_op jit(solution)/shard_map/ppermute | solution.py:134
  32.7 14.2 %collective-permute-start.3 = (f32[3,1152]{1,0:T(4,128)S(1)}, f32[3,1152]{1,0:T(4,128)S(1)}, u32[]{:S(2)}, u32[]{:S(2)}) collective-permute-start(f32[3,1152]{1,0:T(4,128)S(1)} %get-tuple-element.68), channel_id=1, source_target_pairs={{0,2},{1,3},{2,4},{3,5},{4,6},{5,7},{8,10},{9,11},{10,12},{11,13},... | collective-permute-start | bytes 41480 | tf_op jit(solution)/shard_map/ppermute | solution.py:134
  37.3 11.1 %collective-permute-start.4 = (f32[3,1152]{1,0:T(4,128)S(1)}, f32[3,1152]{1,0:T(4,128)S(1)}, u32[]{:S(2)}, u32[]{:S(2)}) collective-permute-start(f32[3,1152]{1,0:T(4,128)S(1)} %get-tuple-element.68), channel_id=1, source_target_pairs={{0,3},{1,4},{2,5},{3,6},{4,7},{8,11},{9,12},{10,13},{11,14},{12,15... | collective-permute-start | bytes 41480 | tf_op jit(solution)/shard_map/ppermute | solution.py:134
  42.2 6.1 %collective-permute-start.5 = (f32[3,1152]{1,0:T(4,128)S(1)}, f32[3,1152]{1,0:T(4,128)S(1)}, u32[]{:S(2)}, u32[]{:S(2)}) collective-permute-start(f32[3,1152]{1,0:T(4,128)S(1)} %get-tuple-element.68), channel_id=1, source_target_pairs={{0,4},{1,5},{2,6},{3,7},{8,12},{9,13},{10,14},{11,15},{16,20},{17,... | collective-permute-start | bytes 41480 | tf_op jit(solution)/shard_map/ppermute | solution.py:134
  44.2 4.1 %collective-permute-start.6 = (f32[3,1152]{1,0:T(4,128)S(1)}, f32[3,1152]{1,0:T(4,128)S(1)}, u32[]{:S(2)}, u32[]{:S(2)}) collective-permute-start(f32[3,1152]{1,0:T(4,128)S(1)} %get-tuple-element.68), channel_id=1, source_target_pairs={{0,5},{1,6},{2,7},{8,13},{9,14},{10,15},{16,21},{17,22},{18,23},{2... | collective-permute-start | bytes 41480 | tf_op jit(solution)/shard_map/ppermute | solution.py:134
  45.6 2.8 %collective-permute-start.7 = (f32[3,1152]{1,0:T(4,128)S(1)}, f32[3,1152]{1,0:T(4,128)S(1)}, u32[]{:S(2)}, u32[]{:S(2)}) collective-permute-start(f32[3,1152]{1,0:T(4,128)S(1)} %get-tuple-element.68), channel_id=1, source_target_pairs={{0,6},{1,7},{8,14},{9,15},{16,22},{17,23},{24,30},{25,31},{32,38},... | collective-permute-start | bytes 41480 | tf_op jit(solution)/shard_map/ppermute | solution.py:134
  46.9 2.7 %collective-permute-start.8 = (f32[3,1152]{1,0:T(4,128)S(1)}, f32[3,1152]{1,0:T(4,128)S(1)}, u32[]{:S(2)}, u32[]{:S(2)}) collective-permute-start(f32[3,1152]{1,0:T(4,128)S(1)} %get-tuple-element.68), channel_id=1, source_target_pairs={{0,7},{8,15},{16,23},{24,31},{32,39},{40,47},{48,55},{56,63},{64,7... | collective-permute-start | bytes 41480 | tf_op jit(solution)/shard_map/ppermute | solution.py:134
  50.4 6.5 %collective-permute-start.10 = (f32[3,1152]{1,0:T(4,128)S(1)}, f32[3,1152]{1,0:T(4,128)S(1)}, u32[]{:S(2)}, u32[]{:S(2)}) collective-permute-start(f32[3,1152]{1,0:T(4,128)S(1)} %get-tuple-element.5), channel_id=1, source_target_pairs={{2,0},{3,1},{4,2},{5,3},{6,4},{7,5},{10,8},{11,9},{12,10},{13,11},... | collective-permute-start | bytes 41480 | tf_op jit(solution)/shard_map/ppermute | solution.py:134
  51.7 7.5 %collective-permute-start.11 = (f32[3,1152]{1,0:T(4,128)S(1)}, f32[3,1152]{1,0:T(4,128)S(1)}, u32[]{:S(2)}, u32[]{:S(2)}) collective-permute-start(f32[3,1152]{1,0:T(4,128)S(1)} %get-tuple-element.5), channel_id=1, source_target_pairs={{3,0},{4,1},{5,2},{6,3},{7,4},{11,8},{12,9},{13,10},{14,11},{15,12... | collective-permute-start | bytes 41480 | tf_op jit(solution)/shard_map/ppermute | solution.py:134
  53.0 9.6 %collective-permute-start.12 = (f32[3,1152]{1,0:T(4,128)S(1)}, f32[3,1152]{1,0:T(4,128)S(1)}, u32[]{:S(2)}, u32[]{:S(2)}) collective-permute-start(f32[3,1152]{1,0:T(4,128)S(1)} %get-tuple-element.5), channel_id=1, source_target_pairs={{4,0},{5,1},{6,2},{7,3},{12,8},{13,9},{14,10},{15,11},{20,16},{21,... | collective-permute-start | bytes 41480 | tf_op jit(solution)/shard_map/ppermute | solution.py:134
  54.3 10.8 %collective-permute-start.13 = (f32[3,1152]{1,0:T(4,128)S(1)}, f32[3,1152]{1,0:T(4,128)S(1)}, u32[]{:S(2)}, u32[]{:S(2)}) collective-permute-start(f32[3,1152]{1,0:T(4,128)S(1)} %get-tuple-element.5), channel_id=1, source_target_pairs={{5,0},{6,1},{7,2},{13,8},{14,9},{15,10},{21,16},{22,17},{23,18},{2... | collective-permute-start | bytes 41480 | tf_op jit(solution)/shard_map/ppermute | solution.py:134
  55.6 10.7 %collective-permute-start.14 = (f32[3,1152]{1,0:T(4,128)S(1)}, f32[3,1152]{1,0:T(4,128)S(1)}, u32[]{:S(2)}, u32[]{:S(2)}) collective-permute-start(f32[3,1152]{1,0:T(4,128)S(1)} %get-tuple-element.5), channel_id=1, source_target_pairs={{6,0},{7,1},{14,8},{15,9},{22,16},{23,17},{30,24},{31,25},{38,32},... | collective-permute-start | bytes 41480 | tf_op jit(solution)/shard_map/ppermute | solution.py:134
  56.9 10.7 %collective-permute-start.15 = (f32[3,1152]{1,0:T(4,128)S(1)}, f32[3,1152]{1,0:T(4,128)S(1)}, u32[]{:S(2)}, u32[]{:S(2)}) collective-permute-start(f32[3,1152]{1,0:T(4,128)S(1)} %get-tuple-element.5), channel_id=1, source_target_pairs={{7,0},{15,8},{23,16},{31,24},{39,32},{47,40},{55,48},{63,56},{71,6... | collective-permute-start | bytes 41480 | tf_op jit(solution)/shard_map/ppermute | solution.py:134
  59.1 8.5 %collective-permute-start.9 = (f32[3,1152]{1,0:T(4,128)S(1)}, f32[3,1152]{1,0:T(4,128)S(1)}, u32[]{:S(2)}, u32[]{:S(2)}) collective-permute-start(f32[3,1152]{1,0:T(4,128)S(1)} %get-tuple-element.5), channel_id=1, source_target_pairs={{1,0},{2,1},{3,2},{4,3},{5,4},{6,5},{7,6},{9,8},{10,9},{11,10},{12... | collective-permute-start | bytes 41480 | tf_op jit(solution)/shard_map/ppermute | solution.py:134
  60.7 6.9 %copy-start.9 = (f32[3,1152]{1,0:T(4,128)S(1)}, f32[3,1152]{1,0:T(4,128)}, u32[]{:S(2)}) copy-start(f32[3,1152]{1,0:T(4,128)} %param.15) | copy-start | bytes 41476
  67.7 8.6 %copy-start.2 = (f32[3,8,1152]{2,1,0:T(8,128)}, f32[3,8,1152]{2,1,0:T(8,128)S(1)}, u32[]{:S(2)}) copy-start(f32[3,8,1152]{2,1,0:T(8,128)S(1)} %multiply_add_fusion.2) | copy-start | bytes 331780
  67.7 8.6 %collective-permute-start.16 = (f32[1,8,1152]{2,1,0:T(8,128)S(1)}, f32[1,8,1152]{2,1,0:T(8,128)S(1)}, u32[]{:S(2)}, u32[]{:S(2)}) collective-permute-start(f32[1,8,1152]{2,1,0:T(8,128)S(1)} %slice.583), channel_id=1, source_target_pairs={{0,8},{8,16},{16,24},{24,32},{32,40},{40,48},{48,56},{56,64},{64,7... | collective-permute-start | bytes 110600 | tf_op jit(solution)/shard_map/ppermute | solution.py:32

commit v3 on v2

--- a/solution.py
+++ b/solution.py
@@ -125,14 +125,12 @@
 
 def prefix_over(value, axis, before):
     count = lax.axis_size(axis)
-    total = jnp.zeros_like(value)
-    for step in range(1, count):
-        if before:
-            route = [(i, i + step) for i in range(count - step)]
-        else:
-            route = [(i + step, i) for i in range(count - step)]
-        total = total + lax.ppermute(value, axis, route)
-    return total
+    rank = lax.axis_index(axis)
+    copies = jnp.broadcast_to(value, (count, *value.shape))
+    pieces = lax.all_to_all(copies, axis, split_axis=0, concat_axis=0, tiled=True)
+    owners = jnp.arange(count, dtype=jnp.int32)
+    chosen = owners < rank if before else owners > rank
+    return jnp.sum(jnp.where(chosen[:, None, None], pieces, 0.0), axis=0)
 
 
 def local(wind_east, wind_north, layer_mass, theta_field, surface_height, filter_cutoff):
@@ -152,7 +150,19 @@
     theta_faces = face_lat(padded[1], lat_rows + 1)
     flux_east = wind_east * face_lon(layer_mass)
     flux_north = wind_north * mass_faces * coslat
+    column = jnp.sum(layer_mass, axis=1)
+    above_mass = prefix_over(column, "lev", True)
+    bottom = TOP_PRESSURE + above_mass[:, None] + jnp.cumsum(layer_mass, axis=1)
+    top_press = bottom - layer_mass
+    thickness = GAS_CONST * theta_field * (jnp.log(bottom) - jnp.log(top_press))
+    depth_sum = jnp.sum(thickness, axis=1)
+    below_depth = prefix_over(depth_sum, "lev", False)
+    inclusive = jnp.flip(jnp.cumsum(jnp.flip(thickness, 1), axis=1), 1)
+    height = (
+        surface_height[:, None] + below_depth[:, None] + (inclusive - thickness) + 0.5 * thickness
+    )
     fields = jnp.stack([wind_east, wind_north, flux_east, flux_north])
+    fields, height = lax.optimization_barrier((fields, height))
     own_cuts = lax.dynamic_slice_in_dim(filter_cutoff, first_row, lat_rows)
     row_cuts = jnp.broadcast_to(own_cuts[None, :, None], fields.shape[:3]).reshape(-1)
     smooth = filter_rows(fields.reshape(-1, length), row_cuts).reshape(fields.shape)
@@ -170,17 +180,6 @@
     new_heat = theta_field * layer_mass - TIME_STEP * (
         jnp.roll(heat_east, -1, -1) - heat_east + (heat_north[1:] - heat_north[:-1])
     )
-    column = jnp.sum(layer_mass, axis=1)
-    above_mass = prefix_over(column, "lev", True)
-    bottom = TOP_PRESSURE + above_mass[:, None] + jnp.cumsum(layer_mass, axis=1)
-    top_press = bottom - layer_mass
-    thickness = GAS_CONST * theta_field * (jnp.log(bottom) - jnp.log(top_press))
-    depth_sum = jnp.sum(thickness, axis=1)
-    below_depth = prefix_over(depth_sum, "lev", False)
-    inclusive = jnp.flip(jnp.cumsum(jnp.flip(thickness, 1), axis=1), 1)
-    height = (
-        surface_height[:, None] + below_depth[:, None] + (inclusive - thickness) + 0.5 * thickness
-    )
     lower_row = from_behind(height[-1:], "lat", 1)
     height_south = jnp.concatenate([lower_row, height[:-1]], axis=0)
     new_east = east_smooth - TIME_STEP * (height - jnp.roll(height, 1, -1))

time: 77.9 us -> 65 us (0.83)
  starting transfers between devices: 45 us -> 25.1 us
  waiting for transfers between devices: 17.1 us -> 22.8 us
  local copies, waits for them, and re-layouts: 6.31 us -> 7.63 us
    ppermute x14 -> x0, starting transfers between devices: 27.8 us -> none  [prefix_over(): total = total + lax.ppermute(value, axis, route)]
    all_to_all x0 -> x2, waiting for transfers between devices: none -> 17.8 us  [prefix_over(): lax.all_to_all(copies, axis, split_axis=0, concat_axis=0, tiled=True)]
    all_to_all x0 -> x2, starting transfers between devices: none -> 10.5 us  [prefix_over(): lax.all_to_all(copies, axis, split_axis=0, concat_axis=0, tiled=True)]
    ppermute x14 -> x0, waiting for transfers between devices: 8.91 us -> none  [prefix_over(): total = total + lax.ppermute(value, axis, route)]
    ppermute x2, waiting for transfers between devices: 8.05 us -> 4.95 us  [from_behind(): return lax.ppermute(block, axis, route)]
    ppermute x2, starting transfers between devices: 8.3 us -> 5.7 us  [from_behind(): return lax.ppermute(block, axis, route)]
    broadcast_in_dim x0 -> x2, local copies, waits for them, and re-layouts: none -> 1.34 us  [prefix_over(): copies = jnp.broadcast_to(value, (count, *value.shape))]
  transfers between devices with their start and end apart: 18 -> 6, of which waited for: 10 -> 4; matrix products, arithmetic and copies ran while one was open for 3% -> 6% of each run, Pallas kernels for 0% -> 0%
where the time goes in v3:
time: 65 us; the launch traced here: 64.4 us
  starting transfers between devices  25.1 us (39%)
  waiting for transfers between devices  22.8 us (35%)
  local copies, waits for them, and re-layouts  7.63 us (12%)
  other arithmetic  5.88 us (9%)
  matrix products  1.72 us (3%)
  between operations  1.31 us (2%)
    all_to_all x2, waiting for transfers between devices, prefix_over(): lax.all_to_all(copies, axis, split_axis=0, concat_axis=0, tiled=True)  17.8 us
    all_to_all x2, starting transfers between devices, prefix_over(): lax.all_to_all(copies, axis, split_axis=0, concat_axis=0, tiled=True)  10.5 us
    ppermute x1, starting transfers between devices, extended(): lax.ppermute(head, axis, [((i + 1) % count, i) for i in range(ends)])  6.96 us
    ppermute x2, starting transfers between devices, from_behind(): return lax.ppermute(block, axis, route)  5.7 us
    ppermute x2, waiting for transfers between devices, from_behind(): return lax.ppermute(block, axis, route)  4.95 us
    unnamed x35, local copies, waits for them, and re-layouts  4.43 us
    ppermute x1, starting transfers between devices, extended(): lax.ppermute(tail, axis, [(i, (i + 1) % count) for i in range(ends)])  1.92 us
    transpose x2, other arithmetic, local(): return tuple((jnp.transpose(v, (1, 0, 2)) for v in outputs))  1.52 us
  transfers between devices with their start and end apart: 6, of which 4 were waited for; matrix products, arithmetic and copies ran while one was open for 6% of the time, Pallas kernels for 0%

profile of v3, /device:TPU:256, one launch (start us, length us, event | category | flops | bytes accessed | tf_op | source)
XLA Modules:
  0.0 64.4 jit_solution(9285625966521033398)
XLA Ops:
  0.6 1.0 %pad_maximum_fusion.2 = f32[2,3,8,1152]{3,2,1,0:T(8,128)S(1)} fusion(f32[1,3,8,1152]{3,2,1,0:T(8,128)} %bitcast.124, f32[1,3,8,1152]{3,2,1,0:T(8,128)} %bitcast.115), kind=kLoop, calls=%fused_computation.9 | loop fusion | flops 55296 | bytes 442368 | tf_op jit(solution)/shard_map/stack | solution.py:147
  1.6 1.9 %collective-permute-start = (f32[2,3,8,1152]{3,2,1,0:T(8,128)S(1)}, f32[2,3,8,1152]{3,2,1,0:T(8,128)S(1)}, u32[]{:S(2)}, u32[]{:S(2)}) collective-permute-start(f32[2,3,8,1152]{3,2,1,0:T(8,128)S(1)} %pad_maximum_fusion.2), channel_id=1, source_target_pairs={{0,8},{8,16},{16,24},{24,32},{32,40},{40,48},{48,56},{56,64},{64,7... | collective-permute-start | bytes 663560 | tf_op jit(solution)/shard_map/ppermute | solution.py:20
  3.6 7.0 %collective-permute-start.1 = (f32[2,3,8,1152]{3,2,1,0:T(8,128)S(1)}, f32[2,3,8,1152]{3,2,1,0:T(8,128)S(1)}, u32[]{:S(2)}, u32[]{:S(2)}) collective-permute-start(f32[2,3,8,1152]{3,2,1,0:T(8,128)S(1)} %pad_maximum_fusion.2), channel_id=1, source_target_pairs={{8,0},{16,8},{24,16},{32,24},{40,32},{48,40},{56,48},{64,56},{72,6... | collective-permute-start | bytes 663560 | tf_op jit(solution)/shard_map/ppermute | solution.py:22
  11.0 0.7 %copy-done.1 = f32[8,3,1152]{2,0,1:T(8,128)S(1)} copy-done((f32[8,3,1152]{2,0,1:T(8,128)S(1)}, f32[8,3,1152]{2,0,1:T(8,128)}, u32[]{:S(2)}) %copy-start.1) | copy-done | bytes 110616
  12.0 0.1 reduce_window_sum.17
  12.1 0.7 %copy-done.11 = s32[192]{0:T(256)S(1)} copy-done((s32[192]{0:T(256)S(1)}, s32[192]{0:T(256)}, u32[]{:S(2)}) %copy-start.11) | copy-done | bytes 792
  13.1 0.5 copy-done.10
  13.6 0.2 bitcast_compare_fusion
  14.0 0.8 %copy-done.4 = f32[8,3,1152]{2,0,1:T(8,128)S(1)} copy-done((f32[8,3,1152]{2,0,1:T(8,128)S(1)}, f32[8,3,1152]{2,0,1:T(8,128)}, u32[]{:S(2)}) %copy-start.4) | copy-done | bytes 110616
  14.9 0.7 %broadcast_in_dim.40 = f32[8,3,1152]{2,1,0:T(4,128)} broadcast(f32[3,1152]{1,0:T(4,128)S(1)} %get-tuple-element.80), dimensions={1,2} | broadcast | bytes 124416 | tf_op jit(solution)/shard_map/broadcast_in_dim | solution.py:129
  15.6 7.1 %all-to-all-start = ((f32[8,3,1152]{2,1,0:T(4,128)}), f32[8,3,1152]{2,1,0:T(4,128)S(1)}, u32[]{:S(2)}, u32[]{:S(2)}) async-start(f32[8,3,1152]{2,1,0:T(4,128)} %broadcast_in_dim.40), calls=%async_computation | async-start | bytes 294912 | tf_op jit(solution)/shard_map/all_to_all | solution.py:130
  22.8 9.2 %all-to-all-done = f32[8,3,1152]{2,1,0:T(4,128)S(1)} async-done(((f32[8,3,1152]{2,1,0:T(4,128)}), f32[8,3,1152]{2,1,0:T(4,128)S(1)}, u32[]{:S(2)}, u32[]{:S(2)}) %all-to-all-start) | async-done | bytes 110624 | tf_op jit(solution)/shard_map/all_to_all | solution.py:130
  31.9 0.1 select_reduce_fusion.1
  32.1 0.2 fusion.50
  32.3 0.7 %broadcast_in_dim.42 = f32[8,3,1152]{2,1,0:T(4,128)} broadcast(f32[3,1152]{1,0:T(4,128)S(1)} %get-tuple-element.19), dimensions={1,2} | broadcast | bytes 124416 | tf_op jit(solution)/shard_map/broadcast_in_dim | solution.py:129
  32.9 3.4 %all-to-all-start.1 = ((f32[8,3,1152]{2,1,0:T(4,128)}), f32[8,3,1152]{2,1,0:T(4,128)S(1)}, u32[]{:S(2)}, u32[]{:S(2)}) async-start(f32[8,3,1152]{2,1,0:T(4,128)} %broadcast_in_dim.42), calls=%async_computation.1 | async-start | bytes 294912 | tf_op jit(solution)/shard_map/all_to_all | solution.py:130
  36.3 0.2 rev.7
  36.5 0.1 reduce_window_sum.18
  36.6 0.2 rev.8
  36.9 8.6 %all-to-all-done.1 = f32[8,3,1152]{2,1,0:T(4,128)S(1)} async-done(((f32[8,3,1152]{2,1,0:T(4,128)}), f32[8,3,1152]{2,1,0:T(4,128)S(1)}, u32[]{:S(2)}, u32[]{:S(2)}) %all-to-all-start.1) | async-done | bytes 110624 | tf_op jit(solution)/shard_map/all_to_all | solution.py:130
  45.5 0.1 select_reduce_fusion
  46.3 0.7 %copy-done.7 = f32[1152]{0:T(1024)S(1)} copy-done((f32[1152]{0:T(1024)S(1)}, f32[1152]{0:T(1024)}, u32[]{:S(2)}) %copy-start.7) | copy-done | bytes 4632
  47.4 0.9 %copy-done.5 = f32[256,256]{1,0:T(8,128)S(1)} copy-done((f32[256,256]{1,0:T(8,128)S(1)}, f32[256,256]{1,0:T(8,128)}, u32[]{:S(2)}) %copy-start.5) | copy-done | bytes 262168
  48.3 0.9 %convolution_select_fusion = f32[864,256]{1,0:T(8,128)S(1)} fusion(pred[864,256]{1,0:T(32,128)(4,1)S(1)} %bitcast_compare_fusion, f32[864,256]{1,0:T(8,128)S(1)} %constant_dynamic-update-slice_fusion.18, f32[256,256]{1,0:T(8,128)S(1)} %copy-done.5), kind=kOutput, calls=%fused_computation | convolution fusion | flops 679698432 | bytes 2252800 | tf_op jit(solution)/shard_map/dot_general | solution.py:105
  49.2 0.9 %fusion.61 = f32[864,256]{1,0:T(8,128)S(1)} fusion(f32[864,256]{1,0:T(8,128)S(1)} %convolution_select_fusion, f32[256,256]{1,0:T(8,128)S(1)} %copy-done.6), kind=kOutput, calls=%fused_computation.175 | convolution fusion | flops 679477248 | bytes 2031616 | tf_op jit(solution)/shard_map/dot_general | solution.py:107
  50.2 0.1 multiply_add_fusion
  51.0 3.8 %collective-permute-start.3 = (f32[1,8,1152]{2,1,0:T(8,128)S(1)}, f32[1,8,1152]{2,1,0:T(8,128)S(1)}, u32[]{:S(2)}, u32[]{:S(2)}) collective-permute-start(f32[1,8,1152]{2,1,0:T(8,128)S(1)} %slice_bitcast_fusion.5), channel_id=1, source_target_pairs={{8,0},{16,8},{24,16},{32,24},{40,32},{48,40},{56,48},{64,56},{72,6... | collective-permute-start | bytes 110600 | tf_op jit(solution)/shard_map/ppermute | solution.py:32
  55.0 1.9 %collective-permute-start.2 = (f32[1,8,1152]{2,1,0:T(8,128)S(1)}, f32[1,8,1152]{2,1,0:T(8,128)S(1)}, u32[]{:S(2)}, u32[]{:S(2)}) collective-permute-start(f32[1,8,1152]{2,1,0:T(8,128)S(1)} %slice.472), channel_id=1, source_target_pairs={{0,8},{8,16},{16,24},{24,32},{32,40},{40,48},{48,56},{56,64},{64,7... | collective-permute-start | bytes 110600 | tf_op jit(solution)/shard_map/ppermute | solution.py:32
  56.9 0.8 %fusion.46 = (f32[3,8,1152]{2,1,0:T(8,128)S(1)}, f32[8,3,1152]{2,0,1:T(8,128)}) fusion(f32[3,8,1151]{2,1,0:T(8,128)S(1)} %get-tuple-element.76, f32[3,8,1]{2,1,0:T(8,128)S(1)} %get-tuple-element.78, f32[3,8,1150]{2,1,0:T(8,128)S(1)} %get-tuple-element.72, f32[3,8,2]{2,1,0:T(8,128)S(1)} %get-tuple-element.74, f32[3,8,1]{2,1,0:T(8,128)S(1)} %get-tuple-element.77, ...), kind=kLoop, calls=%fused_computation.133 | loop fusion | flops 580608 | bytes 1363968 | tf_op jit(solution)/shard_map/mul | solution.py:178
  57.9 0.7 %fusion.16 = f32[8,3,1152]{2,0,1:T(8,128)} fusion(f32[4,8,1152]{2,1,0:T(8,128)S(1)} %fusion, f32[3,8,1152]{2,1,0:T(8,128)S(1)} %get-tuple-element.45, f32[3,8,1]{2,1,0:T(8,128)S(1)} %slice.599, f32[3,8,1151]{2,1,0:T(8,128)S(1)} %slice.598, f32[8,3,1152]{2,0,1:T(8,128)S(1)} %copy-done.1, f32[8,3,1152]{2,0,1:T(8,128)S(1)} %copy-done), kind=kLoop, calls=%fused_computation.89 | loop fusion | flops 193536 | bytes 774144 | tf_op jit(solution)/shard_map/transpose | solution.py:189
  58.7 4.9 %collective-permute-done.2 = f32[1,8,1152]{2,1,0:T(8,128)S(1)} collective-permute-done((f32[1,8,1152]{2,1,0:T(8,128)S(1)}, f32[1,8,1152]{2,1,0:T(8,128)S(1)}, u32[]{:S(2)}, u32[]{:S(2)}) %collective-permute-start.2) | collective-permute-done | bytes 36896 | tf_op jit(solution)/shard_map/ppermute | solution.py:32
  63.6 0.8 %fusion.19 = (f32[8,3,1152]{2,0,1:T(8,128)}, f32[8,3,1152]{2,0,1:T(8,128)}) fusion(f32[96,1152]{1,0:T(8,128)S(1)} %constant_dynamic-update-slice_fusion.45, f32[3,8,1152]{2,1,0:T(8,128)S(1)} %multiply_add_fusion.2, f32[2,8,1152]{2,1,0:T(8,128)S(1)} %slice.473, f32[1,8,1152]{2,1,0:T(8,128)S(1)} %collective-permute-done.2, f32[3]{0:T(128)S(1)} %compare_convert_fusion, ...), kind=kLoop, calls=%fused_computation.95 | loop fusion | flops 248832 | bytes 774156 | tf_op jit(solution)/shard_map/transpose | solution.py:189
  (102 shorter events, 3.4 us)
Async XLA Ops:
  0.6 9.9 %copy-start = (f32[8,3,1152]{2,0,1:T(8,128)S(1)}, f32[8,3,1152]{2,0,1:T(8,128)}, u32[]{:S(2)}) copy-start(f32[8,3,1152]{2,0,1:T(8,128)} %param.13) | copy-start | bytes 331780
  1.6 12.3 %collective-permute-start = (f32[2,3,8,1152]{3,2,1,0:T(8,128)S(1)}, f32[2,3,8,1152]{3,2,1,0:T(8,128)S(1)}, u32[]{:S(2)}, u32[]{:S(2)}) collective-permute-start(f32[2,3,8,1152]{3,2,1,0:T(8,128)S(1)} %pad_maximum_fusion.2), channel_id=1, source_target_pairs={{0,8},{8,16},{16,24},{24,32},{32,40},{40,48},{48,56},{56,64},{64,7... | collective-permute-start | bytes 663560 | tf_op jit(solution)/shard_map/ppermute | solution.py:20
  3.6 10.4 %collective-permute-start.1 = (f32[2,3,8,1152]{3,2,1,0:T(8,128)S(1)}, f32[2,3,8,1152]{3,2,1,0:T(8,128)S(1)}, u32[]{:S(2)}, u32[]{:S(2)}) collective-permute-start(f32[2,3,8,1152]{3,2,1,0:T(8,128)S(1)} %pad_maximum_fusion.2), channel_id=1, source_target_pairs={{8,0},{16,8},{24,16},{32,24},{40,32},{48,40},{56,48},{64,56},{72,6... | collective-permute-start | bytes 663560 | tf_op jit(solution)/shard_map/ppermute | solution.py:22
  10.8 0.9 %copy-start.1 = (f32[8,3,1152]{2,0,1:T(8,128)S(1)}, f32[8,3,1152]{2,0,1:T(8,128)}, u32[]{:S(2)}) copy-start(f32[8,3,1152]{2,0,1:T(8,128)} %param.14) | copy-start | bytes 331780
  12.1 0.7 %copy-start.11 = (s32[192]{0:T(256)S(1)}, s32[192]{0:T(256)}, u32[]{:S(2)}) copy-start(s32[192]{0:T(256)} %param.16) | copy-start | bytes 2308
  12.9 0.7 %copy-start.10 = (s32[9,256]{1,0:T(8,128)S(1)}, s32[9,256]{1,0:T(8,128)}, u32[]{:S(2)}) copy-start(s32[9,256]{1,0:T(8,128)} %constant.132) | copy-start | bytes 27652
  13.9 0.9 %copy-start.4 = (f32[8,3,1152]{2,0,1:T(8,128)S(1)}, f32[8,3,1152]{2,0,1:T(8,128)}, u32[]{:S(2)}) copy-start(f32[8,3,1152]{2,0,1:T(8,128)} %param.12) | copy-start | bytes 331780
  15.6 16.4 %all-to-all-start = ((f32[8,3,1152]{2,1,0:T(4,128)}), f32[8,3,1152]{2,1,0:T(4,128)S(1)}, u32[]{:S(2)}, u32[]{:S(2)}) async-start(f32[8,3,1152]{2,1,0:T(4,128)} %broadcast_in_dim.40), calls=%async_computation | async-start | bytes 294912 | tf_op jit(solution)/shard_map/all_to_all | solution.py:130
  22.8 9.3 %copy-start.3 = (f32[8,3,1152]{2,0,1:T(8,128)S(1)}, f32[8,3,1152]{2,0,1:T(8,128)}, u32[]{:S(2)}) copy-start(f32[8,3,1152]{2,0,1:T(8,128)} %param.11) | copy-start | bytes 331780
  32.9 12.6 %all-to-all-start.1 = ((f32[8,3,1152]{2,1,0:T(4,128)}), f32[8,3,1152]{2,1,0:T(4,128)S(1)}, u32[]{:S(2)}, u32[]{:S(2)}) async-start(f32[8,3,1152]{2,1,0:T(4,128)} %broadcast_in_dim.42), calls=%async_computation.1 | async-start | bytes 294912 | tf_op jit(solution)/shard_map/all_to_all | solution.py:130
  36.9 8.7 %copy-start.9 = (f32[3,1152]{1,0:T(4,128)S(1)}, f32[3,1152]{1,0:T(4,128)}, u32[]{:S(2)}) copy-start(f32[3,1152]{1,0:T(4,128)} %param.15) | copy-start | bytes 41476
  45.7 17.9 %copy-start.2 = (f32[3,8,1152]{2,1,0:T(8,128)}, f32[3,8,1152]{2,1,0:T(8,128)S(1)}, u32[]{:S(2)}) copy-start(f32[3,8,1152]{2,1,0:T(8,128)S(1)} %multiply_add_fusion.2) | copy-start | bytes 331780
  46.3 0.7 %copy-start.7 = (f32[1152]{0:T(1024)S(1)}, f32[1152]{0:T(1024)}, u32[]{:S(2)}) copy-start(f32[1152]{0:T(1024)} %constant.133) | copy-start | bytes 13828
  46.3 0.7 %copy-start.8 = (f32[1152]{0:T(1024)S(1)}, f32[1152]{0:T(1024)}, u32[]{:S(2)}) copy-start(f32[1152]{0:T(1024)} %constant.134) | copy-start | bytes 13828
  47.3 1.0 %copy-start.5 = (f32[256,256]{1,0:T(8,128)S(1)}, f32[256,256]{1,0:T(8,128)}, u32[]{:S(2)}) copy-start(f32[256,256]{1,0:T(8,128)} %constant.124.clone) | copy-start | bytes 786436
  48.3 0.9 %copy-start.6 = (f32[256,256]{1,0:T(8,128)S(1)}, f32[256,256]{1,0:T(8,128)}, u32[]{:S(2)}) copy-start(f32[256,256]{1,0:T(8,128)} %constant.126.clone) | copy-start | bytes 786436
  51.0 5.9 %collective-permute-start.3 = (f32[1,8,1152]{2,1,0:T(8,128)S(1)}, f32[1,8,1152]{2,1,0:T(8,128)S(1)}, u32[]{:S(2)}, u32[]{:S(2)}) collective-permute-start(f32[1,8,1152]{2,1,0:T(8,128)S(1)} %slice_bitcast_fusion.5), channel_id=1, source_target_pairs={{8,0},{16,8},{24,16},{32,24},{40,32},{48,40},{56,48},{64,56},{72,6... | collective-permute-start | bytes 110600 | tf_op jit(solution)/shard_map/ppermute | solution.py:32
  55.0 8.6 %collective-permute-start.2 = (f32[1,8,1152]{2,1,0:T(8,128)S(1)}, f32[1,8,1152]{2,1,0:T(8,128)S(1)}, u32[]{:S(2)}, u32[]{:S(2)}) collective-permute-start(f32[1,8,1152]{2,1,0:T(8,128)S(1)} %slice.472), channel_id=1, source_target_pairs={{0,8},{8,16},{16,24},{24,32},{32,40},{40,48},{48,56},{56,64},{64,7... | collective-permute-start | bytes 110600 | tf_op jit(solution)/shard_map/ppermute | solution.py:32

commit v4 on v3

--- a/solution.py
+++ b/solution.py
@@ -7,29 +7,6 @@
 TIME_STEP = 0.25
 GAS_CONST = 1.0
 TOP_PRESSURE = 1.0
-
-
-def extended(cells, sides, width):
-    for axis, dim in sides:
-        count = lax.axis_size(axis)
-        ends = count - 1
-        head = lax.slice_in_dim(cells, 0, width, axis=dim)
-        tail = lax.slice_in_dim(cells, cells.shape[dim] - width, cells.shape[dim], axis=dim)
-        cells = jnp.concatenate(
-            [
-                lax.ppermute(tail, axis, [(i, (i + 1) % count) for i in range(ends)]),
-                cells,
-                lax.ppermute(head, axis, [((i + 1) % count, i) for i in range(ends)]),
-            ],
-            axis=dim,
-        )
-    return cells
-
-
-def from_behind(block, axis, distance):
-    devices = range(lax.axis_size(axis))
-    route = [(i - distance, i) for i in devices if i - distance in devices]
-    return lax.ppermute(block, axis, route)
 
 
 def face_lon(values):
@@ -142,36 +119,47 @@
     lat_rank = lax.axis_index("lat")
     nlat_all = lat_rows * lat_count
     first_row = lat_rank * lat_rows
-    row_ids = first_row + jnp.arange(lat_rows, dtype=jnp.int32)
-    coslat = jnp.sin(jnp.pi * row_ids.astype(jnp.float32) / nlat_all)[:, None, None]
-    stacked = jnp.stack([layer_mass, theta_field])
-    padded = extended(stacked, (("lat", 1),), 3)
-    mass_faces = face_lat(padded[0], lat_rows)
-    theta_faces = face_lat(padded[1], lat_rows + 1)
+    surface = jnp.broadcast_to(surface_height[:, None], (lat_rows, levels, length))
+    to_north = jnp.concatenate([layer_mass, theta_field, surface[-1:]], axis=0)
+    to_south = jnp.concatenate([layer_mass, theta_field, wind_north[:1]], axis=0)
+    count = lat_count
+    from_south = lax.ppermute(to_north, "lat", [(i, i + 1) for i in range(count - 1)])
+    from_north = lax.ppermute(to_south, "lat", [(i + 1, i) for i in range(count - 1)])
+    rows = lat_rows
+    mass_pad = jnp.concatenate([from_south[:rows], layer_mass, from_north[:rows]], axis=0)
+    theta_pad = jnp.concatenate(
+        [from_south[rows : 2 * rows], theta_field, from_north[rows : 2 * rows]], axis=0
+    )
+    face_rows = first_row + jnp.arange(lat_rows + 1, dtype=jnp.int32)
+    coslat = jnp.sin(jnp.pi * face_rows.astype(jnp.float32) / nlat_all)[:, None, None]
+    mass_faces = face_lat(mass_pad, lat_rows + 1)
+    theta_faces = face_lat(theta_pad, lat_rows + 1)
+    north_ext = jnp.concatenate([wind_north, from_north[2 * rows :]], axis=0)
     flux_east = wind_east * face_lon(layer_mass)
-    flux_north = wind_north * mass_faces * coslat
-    column = jnp.sum(layer_mass, axis=1)
+    flux_north = north_ext * mass_faces * coslat
+    mass_ext = jnp.concatenate([from_south[rows - 1 : rows], layer_mass], axis=0)
+    theta_ext = jnp.concatenate([from_south[2 * rows - 1 : 2 * rows], theta_field], axis=0)
+    surface_ext = jnp.concatenate([from_south[2 * rows :], surface], axis=0)
+    column = jnp.sum(mass_ext, axis=1)
     above_mass = prefix_over(column, "lev", True)
-    bottom = TOP_PRESSURE + above_mass[:, None] + jnp.cumsum(layer_mass, axis=1)
-    top_press = bottom - layer_mass
-    thickness = GAS_CONST * theta_field * (jnp.log(bottom) - jnp.log(top_press))
+    bottom = TOP_PRESSURE + above_mass[:, None] + jnp.cumsum(mass_ext, axis=1)
+    top_press = bottom - mass_ext
+    thickness = GAS_CONST * theta_ext * (jnp.log(bottom) - jnp.log(top_press))
     depth_sum = jnp.sum(thickness, axis=1)
     below_depth = prefix_over(depth_sum, "lev", False)
     inclusive = jnp.flip(jnp.cumsum(jnp.flip(thickness, 1), axis=1), 1)
-    height = (
-        surface_height[:, None] + below_depth[:, None] + (inclusive - thickness) + 0.5 * thickness
-    )
-    fields = jnp.stack([wind_east, wind_north, flux_east, flux_north])
-    fields, height = lax.optimization_barrier((fields, height))
-    own_cuts = lax.dynamic_slice_in_dim(filter_cutoff, first_row, lat_rows)
-    row_cuts = jnp.broadcast_to(own_cuts[None, :, None], fields.shape[:3]).reshape(-1)
+    height_ext = surface_ext + below_depth[:, None] + (inclusive - thickness) + 0.5 * thickness
+    fields = jnp.concatenate([wind_east, wind_north, flux_east, flux_north], axis=0)
+    fields, height_ext = lax.optimization_barrier((fields, height_ext))
+    cut_rows = jnp.concatenate([face_rows[:-1], face_rows[:-1], face_rows[:-1], face_rows])
+    row_cuts = jnp.broadcast_to(
+        filter_cutoff[jnp.minimum(cut_rows, nlat_all - 1)][:, None], fields.shape[:2]
+    ).reshape(-1)
     smooth = filter_rows(fields.reshape(-1, length), row_cuts).reshape(fields.shape)
-    east_smooth = smooth[0]
-    north_smooth = smooth[1]
-    east_flux = smooth[2]
-    north_flux = smooth[3]
-    next_face = from_behind(north_flux[:1], "lat", -1)
-    north_full = jnp.concatenate([north_flux, next_face], axis=0)
+    east_smooth = smooth[:rows]
+    north_smooth = smooth[rows : 2 * rows]
+    east_flux = smooth[2 * rows : 3 * rows]
+    north_full = smooth[3 * rows :]
     new_mass = layer_mass - TIME_STEP * (
         jnp.roll(east_flux, -1, -1) - east_flux + (north_full[1:] - north_full[:-1])
     )
@@ -180,11 +168,10 @@
     new_heat = theta_field * layer_mass - TIME_STEP * (
         jnp.roll(heat_east, -1, -1) - heat_east + (heat_north[1:] - heat_north[:-1])
     )
-    lower_row = from_behind(height[-1:], "lat", 1)
-    height_south = jnp.concatenate([lower_row, height[:-1]], axis=0)
+    height = height_ext[1:]
     new_east = east_smooth - TIME_STEP * (height - jnp.roll(height, 1, -1))
-    inside = (row_ids > 0).astype(jnp.float32)[:, None, None]
-    new_north = (north_smooth - TIME_STEP * (height - height_south)) * inside
+    inside = (face_rows[:-1] > 0).astype(jnp.float32)[:, None, None]
+    new_north = (north_smooth - TIME_STEP * (height - height_ext[:-1])) * inside
     outputs = (new_east, new_north, new_mass, new_heat, height)
     return tuple(jnp.transpose(v, (1, 0, 2)) for v in outputs)
 

time: 65 us -> 55.4 us (0.85)
  waiting for transfers between devices: 22.8 us -> 15.9 us
  starting transfers between devices: 25.1 us -> 19.4 us
  local copies, waits for them, and re-layouts: 7.63 us -> 10.1 us
    ppermute x4 -> x2, starting transfers between devices: 14.6 us -> 8.88 us  [the longest x1 6.96 us: local(): lax.ppermute(to_south, 'lat', [(i + 1, i) for i in range(count - 1)])]
    ppermute x4 -> x2, waiting for transfers between devices: 5.01 us -> 0.01 us  [the longest x1 0.01 us: local(): lax.ppermute(to_north, 'lat', [(i, i + 1) for i in range(count - 1)])]
    all_to_all x2, waiting for transfers between devices: 17.8 us -> 15.9 us  [prefix_over(): lax.all_to_all(copies, axis, split_axis=0, concat_axis=0, tiled=True)]
    slice x3 -> x7, local copies, waits for them, and re-layouts: 0.02 us -> 1.6 us  [the longest x1 0.81 us: local(): wind_north[:1]]
    another operation x3 -> x1, other arithmetic: 1.15 us -> 0.14 us  [local(): bottom = TOP_PRESSURE + above_mass[:, None] + jnp.cumsum(mass_ext, axis=1)]
    concatenate x1 -> x3, other arithmetic: 0.06 us -> 0.97 us  [the longest x1 0.93 us: local(): to_north = jnp.concatenate([layer_mass, theta_field, surface[-1:]], axis=0)]
    slice x2 -> x3, local copies, waits for them, and re-layouts: 0.09 us -> 0.79 us  [local(): jnp.roll(east_flux, -1, -1) - east_flux + (north_full[1:] - north_full[:-1])]
    gather x0 -> x1, local copies, waits for them, and re-layouts: none -> 0.66 us  [local(): filter_cutoff[jnp.minimum(cut_rows, nlat_all - 1)][:, None]]
  transfers between devices with their start and end apart: 6 -> 4, of which waited for: 4 -> 2; matrix products, arithmetic and copies ran while one was open for 6% -> 7% of each run, Pallas kernels for 0% -> 0%
where the time goes in v4:
time: 55.4 us; the launch traced here: 54.7 us
  starting transfers between devices  19.4 us (35%)
  waiting for transfers between devices  15.9 us (29%)
  local copies, waits for them, and re-layouts  10.1 us (18%)
  other arithmetic  6.2 us (11%)
  matrix products  1.84 us (3%)
  between operations  1.31 us (2%)
    all_to_all x2, waiting for transfers between devices, prefix_over(): lax.all_to_all(copies, axis, split_axis=0, concat_axis=0, tiled=True)  15.9 us
    all_to_all x2, starting transfers between devices, prefix_over(): lax.all_to_all(copies, axis, split_axis=0, concat_axis=0, tiled=True)  10.5 us
    ppermute x1, starting transfers between devices, local(): lax.ppermute(to_south, 'lat', [(i + 1, i) for i in range(count - 1)])  6.96 us
    unnamed x35, local copies, waits for them, and re-layouts  4.08 us
    ppermute x1, starting transfers between devices, local(): lax.ppermute(to_north, 'lat', [(i, i + 1) for i in range(count - 1)])  1.92 us
    transpose x2, other arithmetic, local(): return tuple((jnp.transpose(v, (1, 0, 2)) for v in outputs))  1.55 us
    broadcast_in_dim x2, local copies, waits for them, and re-layouts, prefix_over(): copies = jnp.broadcast_to(value, (count, *value.shape))  1.34 us
    unnamed x28, other arithmetic  1.15 us
  transfers between devices with their start and end apart: 4, of which 2 were waited for; matrix products, arithmetic and copies ran while one was open for 7% of the time, Pallas kernels for 0%

profile of v4, /device:TPU:256, one launch (start us, length us, event | category | flops | bytes accessed | tf_op | source)
XLA Modules:
  0.0 54.7 jit_solution(7779199882653321311)
XLA Ops:
  0.7 0.8 %slice.552 = f32[1,8,1152]{2,1,0:T(8,128)S(1)} slice(f32[3,8,1152]{2,1,0:T(8,128)} %bitcast.100), slice={[0:1], [0:8], [0:1152]} | slice | bytes 73728 | tf_op jit(solution)/shard_map/slice | solution.py:124
  1.5 0.7 %slice_reduce_fusion = f32[1152]{0:T(1024)S(1)} fusion(f32[3,1152]{1,0:T(4,128)} %param.15), kind=kLoop, calls=%fused_computation.179 | loop fusion | bytes 9216 | tf_op jit(solution)/shard_map/slice | solution.py:123
  2.2 0.9 %pad_maximum_fusion.3 = (f32[7,8,1152]{2,1,0:T(8,128)S(1)}, f32[7,8,1152]{2,1,0:T(8,128)S(1)}) fusion(f32[1,8,1152]{2,1,0:T(8,128)S(1)} %broadcast_in_dim.46, f32[3,8,1152]{2,1,0:T(8,128)} %bitcast.91, f32[3,8,1152]{2,1,0:T(8,128)S(1)} %bitcast.82, f32[1,8,1152]{2,1,0:T(8,128)S(1)} %slice.552), kind=kLoop, calls=%fused_computation.26 | loop fusion | flops 193536 | bytes 811008 | tf_op jit(solution)/shard_map/concatenate | solution.py:123
  3.2 1.9 %collective-permute-start.1 = (f32[7,8,1152]{2,1,0:T(8,128)S(1)}, f32[7,8,1152]{2,1,0:T(8,128)S(1)}, u32[]{:S(2)}, u32[]{:S(2)}) collective-permute-start(f32[7,8,1152]{2,1,0:T(8,128)S(1)} %get-tuple-element.74), channel_id=1, source_target_pairs={{0,8},{8,16},{16,24},{24,32},{32,40},{40,48},{48,56},{56,64},{64,7... | collective-permute-start | bytes 774152 | tf_op jit(solution)/shard_map/ppermute | solution.py:126
  5.1 7.0 %collective-permute-start = (f32[7,8,1152]{2,1,0:T(8,128)S(1)}, f32[7,8,1152]{2,1,0:T(8,128)S(1)}, u32[]{:S(2)}, u32[]{:S(2)}) collective-permute-start(f32[7,8,1152]{2,1,0:T(8,128)S(1)} %get-tuple-element.75), channel_id=1, source_target_pairs={{8,0},{16,8},{24,16},{32,24},{40,32},{48,40},{56,48},{64,56},{72,6... | collective-permute-start | bytes 774152 | tf_op jit(solution)/shard_map/ppermute | solution.py:127
  12.6 0.6 %copy-done.2 = f32[8,3,1152]{2,0,1:T(8,128)S(1)} copy-done((f32[8,3,1152]{2,0,1:T(8,128)S(1)}, f32[8,3,1152]{2,0,1:T(8,128)}, u32[]{:S(2)}) %copy-start.2) | copy-done | bytes 110616
  13.5 0.6 %copy-done.5 = f32[8,3,1152]{2,0,1:T(8,128)S(1)} copy-done((f32[8,3,1152]{2,0,1:T(8,128)S(1)}, f32[8,3,1152]{2,0,1:T(8,128)}, u32[]{:S(2)}) %copy-start.5) | copy-done | bytes 110616
  14.2 0.2 fusion.47
  14.5 0.7 %broadcast_in_dim.50 = f32[8,4,1152]{2,1,0:T(4,128)} broadcast(f32[4,1152]{1,0:T(4,128)S(1)} %get-tuple-element.77), dimensions={1,2} | broadcast | bytes 165888 | tf_op jit(solution)/shard_map/broadcast_in_dim | solution.py:106
  15.2 7.1 %all-to-all-start = ((f32[8,4,1152]{2,1,0:T(4,128)}), f32[8,4,1152]{2,1,0:T(4,128)S(1)}, u32[]{:S(2)}, u32[]{:S(2)}) async-start(f32[8,4,1152]{2,1,0:T(4,128)} %broadcast_in_dim.50), calls=%async_computation | async-start | bytes 294912 | tf_op jit(solution)/shard_map/all_to_all | solution.py:107
  22.3 0.1 reduce_window_sum.17
  22.5 9.0 %all-to-all-done = f32[8,4,1152]{2,1,0:T(4,128)S(1)} async-done(((f32[8,4,1152]{2,1,0:T(4,128)}), f32[8,4,1152]{2,1,0:T(4,128)S(1)}, u32[]{:S(2)}, u32[]{:S(2)}) %all-to-all-start) | async-done | bytes 147488 | tf_op jit(solution)/shard_map/all_to_all | solution.py:107
  31.7 0.2 fusion.61
  31.8 0.7 %broadcast_in_dim.52 = f32[8,4,1152]{2,1,0:T(4,128)} broadcast(f32[4,1152]{1,0:T(4,128)S(1)} %get-tuple-element.19), dimensions={1,2} | broadcast | bytes 165888 | tf_op jit(solution)/shard_map/broadcast_in_dim | solution.py:106
  32.5 3.4 %all-to-all-start.1 = ((f32[8,4,1152]{2,1,0:T(4,128)}), f32[8,4,1152]{2,1,0:T(4,128)S(1)}, u32[]{:S(2)}, u32[]{:S(2)}) async-start(f32[8,4,1152]{2,1,0:T(4,128)} %broadcast_in_dim.52), calls=%async_computation.1 | async-start | bytes 294912 | tf_op jit(solution)/shard_map/all_to_all | solution.py:107
  36.0 0.7 %gather_fusion = s32[13]{0:T(128)S(1)} fusion(s32[192]{0:T(256)S(1)} %copy-done, s32[1024]{0:T(1024)S(1)} %pad_clamp_fusion), kind=kCustom, calls=%fused_computation | custom fusion | bytes 156 | tf_op jit(solution)/shard_map/gather | solution.py:156
  36.9 0.5 copy-done.11
  37.4 0.2 bitcast_compare_fusion
  37.6 0.2 rev.7
  37.8 0.1 reduce_window_sum.18
  38.0 0.2 rev.8
  38.2 6.8 %all-to-all-done.1 = f32[8,4,1152]{2,1,0:T(4,128)S(1)} async-done(((f32[8,4,1152]{2,1,0:T(4,128)}), f32[8,4,1152]{2,1,0:T(4,128)S(1)}, u32[]{:S(2)}, u32[]{:S(2)}) %all-to-all-start.1) | async-done | bytes 147488 | tf_op jit(solution)/shard_map/all_to_all | solution.py:107
  45.9 0.7 %copy-done.8 = f32[1152]{0:T(1024)S(1)} copy-done((f32[1152]{0:T(1024)S(1)}, f32[1152]{0:T(1024)}, u32[]{:S(2)}) %copy-start.8) | copy-done | bytes 4632
  47.0 0.9 %copy-done.7 = f32[256,256]{1,0:T(8,128)S(1)} copy-done((f32[256,256]{1,0:T(8,128)S(1)}, f32[256,256]{1,0:T(8,128)}, u32[]{:S(2)}) %copy-start.7) | copy-done | bytes 262168
  47.9 0.9 %convolution_select_fusion = f32[936,256]{1,0:T(8,128)S(1)} fusion(pred[936,256]{1,0:T(8,128)(4,1)S(1)} %bitcast_compare_fusion, f32[936,256]{1,0:T(8,128)S(1)} %constant_dynamic-update-slice_fusion.18, f32[256,256]{1,0:T(8,128)S(1)} %copy-done.7), kind=kOutput, calls=%fused_computation.1 | convolution fusion | flops 736339968 | bytes 2418688 | tf_op jit(solution)/shard_map/dot_general | solution.py:82
  48.8 0.9 %fusion.75 = f32[936,256]{1,0:T(8,128)S(1)} fusion(f32[936,256]{1,0:T(8,128)S(1)} %convolution_select_fusion, f32[256,256]{1,0:T(8,128)S(1)} %copy-done.6), kind=kOutput, calls=%fused_computation.206 | convolution fusion | flops 736100352 | bytes 2179072 | tf_op jit(solution)/shard_map/dot_general | solution.py:84
  49.9 0.1 multiply_add_fusion
  50.9 0.5 copy-done.4
  51.4 0.7 %slice-done = f32[3,8,1]{2,1,0:T(8,128)S(1)} async-done(((f32[3,8,1152]{2,1,0:T(8,128)}), f32[3,8,1]{2,1,0:T(8,128)S(1)}, s32[]{:S(2)}) %slice-start) | async-done | bytes 120 | tf_op jit(solution)/shard_map/jit(_roll_static)/slice | solution.py:164
  52.1 0.8 %fusion.54 = (f32[3,8,1152]{2,1,0:T(8,128)S(1)}, f32[8,3,1152]{2,0,1:T(8,128)}) fusion(f32[3,8,1151]{2,1,0:T(8,128)S(1)} %get-tuple-element.84, f32[3,8,1]{2,1,0:T(8,128)S(1)} %get-tuple-element.86, f32[3,8,1150]{2,1,0:T(8,128)S(1)} %get-tuple-element.80, f32[3,8,2]{2,1,0:T(8,128)S(1)} %get-tuple-element.82, f32[3,8,1]{2,1,0:T(8,128)S(1)} %get-tuple-element.85, ...), kind=kLoop, calls=%fused_computation.156 | loop fusion | flops 552960 | bytes 1437696 | tf_op jit(solution)/shard_map/mul | solution.py:166
  53.2 0.7 %fusion.32 = f32[8,3,1152]{2,0,1:T(8,128)} fusion(f32[4,8,1152]{2,1,0:T(8,128)S(1)} %fusion.6, f32[3,8,1152]{2,1,0:T(8,128)S(1)} %get-tuple-element.45, f32[3,8,1]{2,1,0:T(8,128)S(1)} %slice.648, f32[3,8,1151]{2,1,0:T(8,128)S(1)} %slice.647, f32[8,3,1152]{2,0,1:T(8,128)S(1)} %copy-done.2, f32[8,3,1152]{2,0,1:T(8,128)S(1)} %copy-done.1), kind=kLoop, calls=%fused_computation.70 | loop fusion | flops 193536 | bytes 774144 | tf_op jit(solution)/shard_map/transpose | solution.py:176
  53.9 0.8 %fusion.40 = (f32[8,3,1152]{2,0,1:T(8,128)}, f32[8,3,1152]{2,0,1:T(8,128)}, f32[8,3,1152]{2,0,1:T(8,128)}) fusion(f32[104,1152]{1,0:T(8,128)S(1)} %constant_dynamic-update-slice_fusion.45, f32[4,8,1152]{2,1,0:T(8,128)S(1)} %fusion.28, f32[3]{0:T(128)S(1)} %compare_convert_fusion, f32[3,8,1151]{2,1,0:T(8,128)S(1)} %slice.506, f32[3,8,1]{2,1,0:T(8,128)S(1)} %slice.505), kind=kLoop, calls=%fused_computation.81 | loop fusion | flops 221184 | bytes 884748 | tf_op jit(solution)/shard_map/transpose | solution.py:176
  (109 shorter events, 3.6 us)
Async XLA Ops:
  0.6 35.3 %copy-start = (s32[192]{0:T(256)S(1)}, s32[192]{0:T(256)}, u32[]{:S(2)}) copy-start(s32[192]{0:T(256)} %param.16) | copy-start | bytes 2308
  0.6 1.6 %copy-start.1 = (f32[8,3,1152]{2,0,1:T(8,128)S(1)}, f32[8,3,1152]{2,0,1:T(8,128)}, u32[]{:S(2)}) copy-start(f32[8,3,1152]{2,0,1:T(8,128)} %param.13) | copy-start | bytes 331780
  3.2 11.3 %collective-permute-start.1 = (f32[7,8,1152]{2,1,0:T(8,128)S(1)}, f32[7,8,1152]{2,1,0:T(8,128)S(1)}, u32[]{:S(2)}, u32[]{:S(2)}) collective-permute-start(f32[7,8,1152]{2,1,0:T(8,128)S(1)} %get-tuple-element.74), channel_id=1, source_target_pairs={{0,8},{8,16},{16,24},{24,32},{32,40},{40,48},{48,56},{56,64},{64,7... | collective-permute-start | bytes 774152 | tf_op jit(solution)/shard_map/ppermute | solution.py:126
  5.1 17.3 %collective-permute-start = (f32[7,8,1152]{2,1,0:T(8,128)S(1)}, f32[7,8,1152]{2,1,0:T(8,128)S(1)}, u32[]{:S(2)}, u32[]{:S(2)}) collective-permute-start(f32[7,8,1152]{2,1,0:T(8,128)S(1)} %get-tuple-element.75), channel_id=1, source_target_pairs={{8,0},{16,8},{24,16},{32,24},{40,32},{48,40},{56,48},{64,56},{72,6... | collective-permute-start | bytes 774152 | tf_op jit(solution)/shard_map/ppermute | solution.py:127
  12.3 0.9 %copy-start.2 = (f32[8,3,1152]{2,0,1:T(8,128)S(1)}, f32[8,3,1152]{2,0,1:T(8,128)}, u32[]{:S(2)}) copy-start(f32[8,3,1152]{2,0,1:T(8,128)} %param.14) | copy-start | bytes 331780
  13.3 0.9 %copy-start.5 = (f32[8,3,1152]{2,0,1:T(8,128)S(1)}, f32[8,3,1152]{2,0,1:T(8,128)}, u32[]{:S(2)}) copy-start(f32[8,3,1152]{2,0,1:T(8,128)} %param.11) | copy-start | bytes 331780
  15.2 16.4 %all-to-all-start = ((f32[8,4,1152]{2,1,0:T(4,128)}), f32[8,4,1152]{2,1,0:T(4,128)S(1)}, u32[]{:S(2)}, u32[]{:S(2)}) async-start(f32[8,4,1152]{2,1,0:T(4,128)} %broadcast_in_dim.50), calls=%async_computation | async-start | bytes 294912 | tf_op jit(solution)/shard_map/all_to_all | solution.py:107
  22.5 9.2 %copy-start.3 = (f32[8,3,1152]{2,0,1:T(8,128)S(1)}, f32[8,3,1152]{2,0,1:T(8,128)}, u32[]{:S(2)}) copy-start(f32[8,3,1152]{2,0,1:T(8,128)} %param.12) | copy-start | bytes 331780
  32.5 12.6 %all-to-all-start.1 = ((f32[8,4,1152]{2,1,0:T(4,128)}), f32[8,4,1152]{2,1,0:T(4,128)S(1)}, u32[]{:S(2)}, u32[]{:S(2)}) async-start(f32[8,4,1152]{2,1,0:T(4,128)} %broadcast_in_dim.52), calls=%async_computation.1 | async-start | bytes 294912 | tf_op jit(solution)/shard_map/all_to_all | solution.py:107
  36.7 0.7 %copy-start.11 = (s32[9,256]{1,0:T(8,128)S(1)}, s32[9,256]{1,0:T(8,128)}, u32[]{:S(2)}) copy-start(s32[9,256]{1,0:T(8,128)} %constant.134) | copy-start | bytes 27652
  38.2 7.0 %copy-start.10 = (f32[3,1152]{1,0:T(4,128)S(1)}, f32[3,1152]{1,0:T(4,128)}, u32[]{:S(2)}) copy-start(f32[3,1152]{1,0:T(4,128)} %param.15) | copy-start | bytes 41476
  45.9 0.7 %copy-start.8 = (f32[1152]{0:T(1024)S(1)}, f32[1152]{0:T(1024)}, u32[]{:S(2)}) copy-start(f32[1152]{0:T(1024)} %constant.135) | copy-start | bytes 13828
  45.9 0.7 %copy-start.9 = (f32[1152]{0:T(1024)S(1)}, f32[1152]{0:T(1024)}, u32[]{:S(2)}) copy-start(f32[1152]{0:T(1024)} %constant.136) | copy-start | bytes 13828
  46.9 1.0 %copy-start.7 = (f32[256,256]{1,0:T(8,128)S(1)}, f32[256,256]{1,0:T(8,128)}, u32[]{:S(2)}) copy-start(f32[256,256]{1,0:T(8,128)} %constant.126.clone) | copy-start | bytes 786436
  47.9 0.9 %copy-start.6 = (f32[256,256]{1,0:T(8,128)S(1)}, f32[256,256]{1,0:T(8,128)}, u32[]{:S(2)}) copy-start(f32[256,256]{1,0:T(8,128)} %constant.128.clone) | copy-start | bytes 786436
  50.8 0.6 %copy-start.4 = (f32[3,8,1152]{2,1,0:T(8,128)}, f32[3,8,1152]{2,1,0:T(8,128)S(1)}, u32[]{:S(2)}) copy-start(f32[3,8,1152]{2,1,0:T(8,128)S(1)} %slice_bitcast_fusion.1) | copy-start | bytes 331780
  51.4 0.7 %slice-start = ((f32[3,8,1152]{2,1,0:T(8,128)}), f32[3,8,1]{2,1,0:T(8,128)S(1)}, s32[]{:S(2)}) async-start(f32[3,8,1152]{2,1,0:T(8,128)} %copy-done.4), calls=%async_computation.2 | async-start | bytes 24576 | tf_op jit(solution)/shard_map/jit(_roll_static)/slice | solution.py:164

commit v5 on v4

--- a/solution.py
+++ b/solution.py
@@ -2,6 +2,7 @@
 import jax
 import jax.numpy as jnp
 from jax import lax
+from jax.experimental import pallas as pl
 from jax.sharding import PartitionSpec as P
 
 TIME_STEP = 0.25
@@ -28,7 +29,6 @@
 FACTOR_ROWS = 9
 FACTOR_LANES = 128
 
-
 def fft_tables(length):
     rows, lanes = FACTOR_ROWS, FACTOR_LANES
     small = np.arange(rows)
@@ -43,62 +43,55 @@
     inverse = np.block([[wc, ws], [-ws, wc]]).astype(np.float32)
     number = np.arange(rows)[:, None] + rows * np.arange(lanes)[None, :]
     folded = np.minimum(number, length - number)
-    folded = np.concatenate([folded, folded], axis=1)[:, None, :].astype(np.int32)
-    return (
-        np.cos(small_phase),
-        np.sin(small_phase),
-        np.cos(twist).reshape(1, length).astype(np.float32),
-        np.sin(twist).reshape(1, length).astype(np.float32),
-        forward,
-        inverse,
-        folded,
-    )
+    folded = np.concatenate([folded, folded], axis=1).astype(np.int32)
+    return (np.cos(small_phase), np.sin(small_phase), np.cos(twist).astype(np.float32),
+            np.sin(twist).astype(np.float32), forward, inverse, folded)
 
+def filter_kernel(x_ref, cut_ref, twc_ref, tws_ref, fwd_ref, inv_ref, fold_ref, o_ref):
+    rows, lanes = FACTOR_ROWS, FACTOR_LANES
+    count, length = x_ref.shape
+    c9, s9 = fft_tables(length)[:2]
+    highest = lax.Precision.HIGHEST
+    parts = [x_ref[:, n * lanes:(n + 1) * lanes] for n in range(rows)]
+    half = rows // 2 + 1
+    real_a = [sum(float(c9[k, n]) * parts[n] for n in range(rows)) for k in range(half)]
+    imag_a = [sum(float(-s9[k, n]) * parts[n] for n in range(1, rows)) for k in range(half)]
+    real_a += [real_a[rows - k] for k in range(half, rows)]
+    imag_a += [-imag_a[rows - k] for k in range(half, rows)]
+    pieces = []
+    for k in range(rows):
+        twc = twc_ref[k:k + 1, :]
+        tws = tws_ref[k:k + 1, :]
+        pieces.append(jnp.concatenate(
+            [real_a[k] * twc + imag_a[k] * tws, imag_a[k] * twc - real_a[k] * tws], axis=1))
+    spectrum = jnp.dot(jnp.concatenate(pieces, axis=0), fwd_ref[...], precision=highest,
+                       preferred_element_type=jnp.float32)
+    cuts = cut_ref[...]
+    keep = jnp.concatenate(
+        [(fold_ref[k:k + 1, :] <= cuts).astype(jnp.float32) for k in range(rows)], axis=0)
+    back = jnp.dot(spectrum * keep, inv_ref[...], precision=highest,
+                   preferred_element_type=jnp.float32)
+    real_d, imag_d = [], []
+    for k in range(rows):
+        twc = twc_ref[k:k + 1, :]
+        tws = tws_ref[k:k + 1, :]
+        real_c = back[k * count:(k + 1) * count, :lanes]
+        imag_c = back[k * count:(k + 1) * count, lanes:]
+        real_d.append(real_c * twc - imag_c * tws)
+        imag_d.append(imag_c * twc + real_c * tws)
+    for n in range(rows):
+        o_ref[:, n * lanes:(n + 1) * lanes] = sum(
+            float(c9[k, n] / length) * real_d[k] - float(s9[k, n] / length) * imag_d[k]
+            for k in range(rows))
 
 def filter_rows(values, cuts):
-    rows, lanes = FACTOR_ROWS, FACTOR_LANES
     count, length = values.shape
-    c9, s9, twc, tws, forward, inverse, folded = fft_tables(length)
-    highest = lax.Precision.HIGHEST
-    parts = [values[:, n * lanes : (n + 1) * lanes] for n in range(rows)]
-    real_a = jnp.concatenate(
-        [sum(float(c9[k, n]) * parts[n] for n in range(rows)) for k in range(rows)], axis=1
-    )
-    imag_a = jnp.concatenate(
-        [sum(float(-s9[k, n]) * parts[n] for n in range(rows)) for k in range(rows)], axis=1
-    )
-    real_b = real_a * twc + imag_a * tws
-    imag_b = imag_a * twc - real_a * tws
-    stacked = jnp.concatenate(
-        [
-            jnp.concatenate(
-                [real_b[:, k * lanes : (k + 1) * lanes], imag_b[:, k * lanes : (k + 1) * lanes]],
-                axis=1,
-            )
-            for k in range(rows)
-        ],
-        axis=0,
-    )
-    spectrum = jnp.dot(stacked, forward, precision=highest)
-    keep = (folded <= cuts[None, :, None]).astype(jnp.float32).reshape(rows * count, 2 * lanes)
-    back = jnp.dot(spectrum * keep, inverse, precision=highest)
-    real_c = jnp.concatenate([back[k * count : (k + 1) * count, :lanes] for k in range(rows)], axis=1)
-    imag_c = jnp.concatenate([back[k * count : (k + 1) * count, lanes:] for k in range(rows)], axis=1)
-    real_d = real_c * twc - imag_c * tws
-    imag_d = imag_c * twc + real_c * tws
-    real_parts = [real_d[:, k * lanes : (k + 1) * lanes] for k in range(rows)]
-    imag_parts = [imag_d[:, k * lanes : (k + 1) * lanes] for k in range(rows)]
-    return jnp.concatenate(
-        [
-            sum(
-                float(c9[k, n] / length) * real_parts[k] - float(s9[k, n] / length) * imag_parts[k]
-                for k in range(rows)
-            )
-            for n in range(rows)
-        ],
-        axis=1,
-    )
-
+    _, _, twc, tws, forward, inverse, folded = fft_tables(length)
+    return pl.pallas_call(
+        filter_kernel,
+        out_shape=jax.ShapeDtypeStruct(values.shape, values.dtype),
+    )(values, cuts.reshape(count, 1), jnp.asarray(twc), jnp.asarray(tws), jnp.asarray(forward),
+      jnp.asarray(inverse), jnp.asarray(folded))
 
 def prefix_over(value, axis, before):
     count = lax.axis_size(axis)

time: 55.4 us -> 54.4 us (0.982)
  Pallas kernels: 0 us -> 5.62 us
  local copies, waits for them, and re-layouts: 10.1 us -> 7.99 us
  matrix products: 1.84 us -> 0 us
  other arithmetic: 6.2 us -> 4.53 us
    pallas_call x0 -> x1, Pallas kernels: none -> 5.62 us  [filter_rows(): pl.pallas_call(filter_kernel, out_shape=jax.ShapeDtypeStruct(values.shape...]
    unnamed x35 -> x14, local copies, waits for them, and re-layouts: 4.08 us -> 1.26 us
    dot_general x2 -> x0, matrix products: 1.84 us -> none  [the longest x1 0.93 us: filter_rows(): back = jnp.dot(spectrum * keep, inverse, precision=highest)]
    unnamed x28 -> x0, other arithmetic: 1.15 us -> none
    slice x1, local copies, waits for them, and re-layouts: 0.01 us -> 0.98 us  [local(): east_flux = smooth[2 * rows:3 * rows]]
    concatenate x1, other arithmetic: 0.04 us -> 0.81 us  [local(): jnp.concatenate([wind_east, wind_north, flux_east, flux_north], axis=0)]
    another operation x0 -> x1, local copies, waits for them, and re-layouts: none -> 0.71 us  [filter_rows(): cuts.reshape(count, 1)]
    slice x3 -> x2, local copies, waits for them, and re-layouts: 0.79 us -> 0.09 us  [local(): jnp.roll(east_flux, -1, -1) - east_flux + (north_full[1:] - north_full[:-1])]
  transfers between devices with their start and end apart: 4 -> 4, of which waited for: 2 -> 2; matrix products, arithmetic and copies ran while one was open for 7% -> 9% of each run, Pallas kernels for 0% -> 0%
where the time goes in v5:
time: 54.4 us; the launch traced here: 53.8 us
  starting transfers between devices  19.4 us (36%)
  waiting for transfers between devices  15.4 us (28%)
  local copies, waits for them, and re-layouts  7.99 us (15%)
  Pallas kernels  5.62 us (10%)
  other arithmetic  4.53 us (8%)
  between operations  0.96 us (2%)
    all_to_all x2, waiting for transfers between devices, prefix_over(): lax.all_to_all(copies, axis, split_axis=0, concat_axis=0, tiled=True)  15.4 us
    all_to_all x2, starting transfers between devices, prefix_over(): lax.all_to_all(copies, axis, split_axis=0, concat_axis=0, tiled=True)  10.5 us
    ppermute x1, starting transfers between devices, local(): lax.ppermute(to_south, 'lat', [(i + 1, i) for i in range(count - 1)])  6.96 us
    pallas_call x1, Pallas kernels, filter_rows(): pl.pallas_call(filter_kernel, out_shape=jax.ShapeDtypeStruct(values.shape...  5.62 us
    ppermute x1, starting transfers between devices, local(): lax.ppermute(to_north, 'lat', [(i, i + 1) for i in range(count - 1)])  1.92 us
    broadcast_in_dim x2, local copies, waits for them, and re-layouts, prefix_over(): copies = jnp.broadcast_to(value, (count, *value.shape))  1.33 us
    unnamed x14, local copies, waits for them, and re-layouts  1.26 us
  transfers between devices with their start and end apart: 4, of which 2 were waited for; matrix products, arithmetic and copies ran while one was open for 9% of the time, Pallas kernels for 0%

profile of v5, /device:TPU:256, one launch (start us, length us, event | category | flops | bytes accessed | tf_op | source)
XLA Modules:
  0.0 53.8 jit_solution(10421593755603601566)
XLA Ops:
  0.7 0.8 %slice.300 = f32[1,8,1152]{2,1,0:T(8,128)S(1)} slice(f32[3,8,1152]{2,1,0:T(8,128)} %bitcast.82), slice={[0:1], [0:8], [0:1152]} | slice | bytes 73728 | tf_op jit(solution)/shard_map/slice | solution.py:117
  1.5 0.7 %slice_reduce_fusion = f32[1152]{0:T(1024)S(1)} fusion(f32[3,1152]{1,0:T(4,128)} %param.15), kind=kLoop, calls=%fused_computation.103 | loop fusion | bytes 9216 | tf_op jit(solution)/shard_map/slice | solution.py:116
  2.2 0.9 %pad_maximum_fusion.3 = (f32[7,8,1152]{2,1,0:T(8,128)S(1)}, f32[7,8,1152]{2,1,0:T(8,128)S(1)}) fusion(f32[1,8,1152]{2,1,0:T(8,128)S(1)} %broadcast_in_dim.45, f32[3,8,1152]{2,1,0:T(8,128)} %bitcast.72, f32[3,8,1152]{2,1,0:T(8,128)S(1)} %bitcast.63, f32[1,8,1152]{2,1,0:T(8,128)S(1)} %slice.300), kind=kLoop, calls=%fused_computation.20 | loop fusion | flops 193536 | bytes 811008 | tf_op jit(solution)/shard_map/concatenate | solution.py:116
  3.2 1.9 %collective-permute-start.1 = (f32[7,8,1152]{2,1,0:T(8,128)S(1)}, f32[7,8,1152]{2,1,0:T(8,128)S(1)}, u32[]{:S(2)}, u32[]{:S(2)}) collective-permute-start(f32[7,8,1152]{2,1,0:T(8,128)S(1)} %get-tuple-element.22), channel_id=1, source_target_pairs={{0,8},{8,16},{16,24},{24,32},{32,40},{40,48},{48,56},{56,64},{64,7... | collective-permute-start | bytes 774152 | tf_op jit(solution)/shard_map/ppermute | solution.py:119
  5.1 7.0 %collective-permute-start = (f32[7,8,1152]{2,1,0:T(8,128)S(1)}, f32[7,8,1152]{2,1,0:T(8,128)S(1)}, u32[]{:S(2)}, u32[]{:S(2)}) collective-permute-start(f32[7,8,1152]{2,1,0:T(8,128)S(1)} %get-tuple-element.23), channel_id=1, source_target_pairs={{8,0},{16,8},{24,16},{32,24},{40,32},{48,40},{56,48},{64,56},{72,6... | collective-permute-start | bytes 774152 | tf_op jit(solution)/shard_map/ppermute | solution.py:120
  12.1 0.1 fusion.67
  12.2 0.1 fusion.69
  12.6 0.6 %copy-done.2 = f32[8,3,1152]{2,0,1:T(8,128)S(1)} copy-done((f32[8,3,1152]{2,0,1:T(8,128)S(1)}, f32[8,3,1152]{2,0,1:T(8,128)}, u32[]{:S(2)}) %copy-start.2) | copy-done | bytes 110616
  13.3 0.1 fusion.65
  13.5 0.6 %copy-done.5 = f32[8,3,1152]{2,0,1:T(8,128)S(1)} copy-done((f32[8,3,1152]{2,0,1:T(8,128)S(1)}, f32[8,3,1152]{2,0,1:T(8,128)}, u32[]{:S(2)}) %copy-start.5) | copy-done | bytes 110616
  14.2 0.2 fusion.47
  14.5 0.7 %broadcast_in_dim.49 = f32[8,4,1152]{2,1,0:T(4,128)} broadcast(f32[4,1152]{1,0:T(4,128)S(1)} %get-tuple-element.25), dimensions={1,2} | broadcast | bytes 165888 | tf_op jit(solution)/shard_map/broadcast_in_dim | solution.py:99
  15.2 7.1 %all-to-all-start = ((f32[8,4,1152]{2,1,0:T(4,128)}), f32[8,4,1152]{2,1,0:T(4,128)S(1)}, u32[]{:S(2)}, u32[]{:S(2)}) async-start(f32[8,4,1152]{2,1,0:T(4,128)} %broadcast_in_dim.49), calls=%async_computation | async-start | bytes 294912 | tf_op jit(solution)/shard_map/all_to_all | solution.py:100
  22.3 0.1 reduce_window_sum.17
  22.5 9.0 %all-to-all-done = f32[8,4,1152]{2,1,0:T(4,128)S(1)} async-done(((f32[8,4,1152]{2,1,0:T(4,128)}), f32[8,4,1152]{2,1,0:T(4,128)S(1)}, u32[]{:S(2)}, u32[]{:S(2)}) %all-to-all-start) | async-done | bytes 147488 | tf_op jit(solution)/shard_map/all_to_all | solution.py:100
  31.5 0.1 select_reduce_fusion.1
  31.7 0.2 fusion.59
  31.8 0.7 %broadcast_in_dim.51 = f32[8,4,1152]{2,1,0:T(4,128)} broadcast(f32[4,1152]{1,0:T(4,128)S(1)} %get-tuple-element.9), dimensions={1,2} | broadcast | bytes 165888 | tf_op jit(solution)/shard_map/broadcast_in_dim | solution.py:99
  32.5 3.4 %all-to-all-start.1 = ((f32[8,4,1152]{2,1,0:T(4,128)}), f32[8,4,1152]{2,1,0:T(4,128)S(1)}, u32[]{:S(2)}, u32[]{:S(2)}) async-start(f32[8,4,1152]{2,1,0:T(4,128)} %broadcast_in_dim.51), calls=%async_computation.1 | async-start | bytes 294912 | tf_op jit(solution)/shard_map/all_to_all | solution.py:100
  36.0 0.7 %gather_fusion = s32[13]{0:T(128)S(1)} fusion(s32[192]{0:T(256)S(1)} %copy-done, s32[1024]{0:T(1024)S(1)} %pad_clamp_fusion), kind=kCustom, calls=%fused_computation | custom fusion | bytes 156 | tf_op jit(solution)/shard_map/gather | solution.py:149
  36.7 0.7 %reshape_reshape.4.cut_ref = s32[104,1]{1,0:T(8,128)} reshape(s32[13,8]{1,0:T(8,128)S(1)} %broadcast_in_dim.52) | data formatting | bytes 832 | tf_op jit(solution)/shard_map/reshape;reshape | solution.py:93
  37.4 0.1 rev.7
  37.6 0.1 reduce_window_sum.18
  37.7 0.2 rev.8
  37.9 0.8 %pad_maximum_fusion = f32[13,8,1152]{2,1,0:T(8,128)} fusion(f32[4,8,1152]{2,1,0:T(8,128)S(1)} %get-tuple-element.35, f32[3,8,1152]{2,1,0:T(8,128)S(1)} %fusion.47, f32[3,8,1152]{2,1,0:T(8,128)S(1)} %bitcast.84, f32[3,8,1152]{2,1,0:T(8,128)S(1)} %bitcast.85), kind=kLoop, calls=%fused_computation.1 | loop fusion | flops 359424 | bytes 958464 | tf_op jit(solution)/shard_map/concatenate | solution.py:145
  38.7 6.3 %all-to-all-done.1 = f32[8,4,1152]{2,1,0:T(4,128)S(1)} async-done(((f32[8,4,1152]{2,1,0:T(4,128)}), f32[8,4,1152]{2,1,0:T(4,128)S(1)}, u32[]{:S(2)}, u32[]{:S(2)}) %all-to-all-start.1) | async-done | bytes 147488 | tf_op jit(solution)/shard_map/all_to_all | solution.py:100
  45.0 0.1 select_reduce_fusion
  45.2 5.6 %shard_map.146 = f32[104,1152]{1,0:T(8,128)} custom-call(f32[104,1152]{1,0:T(8,128)} %bitcast.81, s32[104,1]{1,0:T(8,128)} %reshape_reshape.4.cut_ref, f32[9,128]{1,0:T(8,128)} %constant.58.clone.twc_ref, f32[9,128]{1,0:T(8,128)} %constant.59.clone.tws_ref, f32[256,256]{1,0:T(8,128)} %constant.60.clone.fwd_ref, f32[256,256]{1,0:T(8,128)} %constant.61.clone.inv_ref, ...), custom_call_target="tpu_custom_call" | custom-call | tf_op jit(solution)/shard_map/pallas_call | solution.py:90
  50.8 1.0 %slice_bitcast_fusion.1 = f32[3,8,1152]{2,1,0:T(8,128)S(1)} fusion(f32[104,1152]{1,0:T(8,128)} %shard_map.146), kind=kLoop, calls=%fused_computation.71 | loop fusion | bytes 221184 | tf_op jit(solution)/shard_map/slice | solution.py:154
  51.9 0.8 %fusion.54 = (f32[3,8,1152]{2,1,0:T(8,128)S(1)}, f32[8,3,1152]{2,0,1:T(8,128)}) fusion(f32[3,8,1151]{2,1,0:T(8,128)S(1)} %get-tuple-element.32, f32[3,8,1]{2,1,0:T(8,128)S(1)} %get-tuple-element.34, f32[3,8,1150]{2,1,0:T(8,128)S(1)} %get-tuple-element.28, f32[3,8,2]{2,1,0:T(8,128)S(1)} %get-tuple-element.30, f32[3,8,1]{2,1,0:T(8,128)S(1)} %get-tuple-element.33, ...), kind=kLoop, calls=%fused_computation.96 | loop fusion | flops 552960 | bytes 1437696 | tf_op jit(solution)/shard_map/mul | solution.py:159
  52.8 0.1 slice.332
  53.0 0.8 %fusion.40 = (f32[8,3,1152]{2,0,1:T(8,128)}, f32[8,3,1152]{2,0,1:T(8,128)}, f32[8,3,1152]{2,0,1:T(8,128)}, f32[8,3,1152]{2,0,1:T(8,128)}) fusion(f32[104,1152]{1,0:T(8,128)S(1)} %copy-done.3, f32[4,8,1152]{2,1,0:T(8,128)S(1)} %fusion.28, f32[3]{0:T(128)S(1)} %compare_convert_fusion, f32[3,8,1151]{2,1,0:T(8,128)S(1)} %slice.254, f32[3,8,1]{2,1,0:T(8,128)S(1)} %slice.253, ...), kind=kLoop, calls=%fused_computation.75 | loop fusion | flops 414720 | bytes 1658892 | tf_op jit(solution)/shard_map/transpose | solution.py:169
  (46 shorter events, 1.2 us)
Async XLA Ops:
  0.6 35.3 %copy-start = (s32[192]{0:T(256)S(1)}, s32[192]{0:T(256)}, u32[]{:S(2)}) copy-start(s32[192]{0:T(256)} %param.16) | copy-start | bytes 2308
  0.6 1.6 %copy-start.1 = (f32[8,3,1152]{2,0,1:T(8,128)S(1)}, f32[8,3,1152]{2,0,1:T(8,128)}, u32[]{:S(2)}) copy-start(f32[8,3,1152]{2,0,1:T(8,128)} %param.13) | copy-start | bytes 331780
  3.2 11.3 %collective-permute-start.1 = (f32[7,8,1152]{2,1,0:T(8,128)S(1)}, f32[7,8,1152]{2,1,0:T(8,128)S(1)}, u32[]{:S(2)}, u32[]{:S(2)}) collective-permute-start(f32[7,8,1152]{2,1,0:T(8,128)S(1)} %get-tuple-element.22), channel_id=1, source_target_pairs={{0,8},{8,16},{16,24},{24,32},{32,40},{40,48},{48,56},{56,64},{64,7... | collective-permute-start | bytes 774152 | tf_op jit(solution)/shard_map/ppermute | solution.py:119
  5.1 17.3 %collective-permute-start = (f32[7,8,1152]{2,1,0:T(8,128)S(1)}, f32[7,8,1152]{2,1,0:T(8,128)S(1)}, u32[]{:S(2)}, u32[]{:S(2)}) collective-permute-start(f32[7,8,1152]{2,1,0:T(8,128)S(1)} %get-tuple-element.23), channel_id=1, source_target_pairs={{8,0},{16,8},{24,16},{32,24},{40,32},{48,40},{56,48},{64,56},{72,6... | collective-permute-start | bytes 774152 | tf_op jit(solution)/shard_map/ppermute | solution.py:120
  12.3 0.9 %copy-start.2 = (f32[8,3,1152]{2,0,1:T(8,128)S(1)}, f32[8,3,1152]{2,0,1:T(8,128)}, u32[]{:S(2)}) copy-start(f32[8,3,1152]{2,0,1:T(8,128)} %param.14) | copy-start | bytes 331780
  13.3 0.9 %copy-start.5 = (f32[8,3,1152]{2,0,1:T(8,128)S(1)}, f32[8,3,1152]{2,0,1:T(8,128)}, u32[]{:S(2)}) copy-start(f32[8,3,1152]{2,0,1:T(8,128)} %param.11) | copy-start | bytes 331780
  15.2 16.4 %all-to-all-start = ((f32[8,4,1152]{2,1,0:T(4,128)}), f32[8,4,1152]{2,1,0:T(4,128)S(1)}, u32[]{:S(2)}, u32[]{:S(2)}) async-start(f32[8,4,1152]{2,1,0:T(4,128)} %broadcast_in_dim.49), calls=%async_computation | async-start | bytes 294912 | tf_op jit(solution)/shard_map/all_to_all | solution.py:100
  22.5 9.2 %copy-start.4 = (f32[8,3,1152]{2,0,1:T(8,128)S(1)}, f32[8,3,1152]{2,0,1:T(8,128)}, u32[]{:S(2)}) copy-start(f32[8,3,1152]{2,0,1:T(8,128)} %param.12) | copy-start | bytes 331780
  32.5 12.6 %all-to-all-start.1 = ((f32[8,4,1152]{2,1,0:T(4,128)}), f32[8,4,1152]{2,1,0:T(4,128)S(1)}, u32[]{:S(2)}, u32[]{:S(2)}) async-start(f32[8,4,1152]{2,1,0:T(4,128)} %broadcast_in_dim.51), calls=%async_computation.1 | async-start | bytes 294912 | tf_op jit(solution)/shard_map/all_to_all | solution.py:100
  38.7 6.5 %copy-start.6 = (f32[3,1152]{1,0:T(4,128)S(1)}, f32[3,1152]{1,0:T(4,128)}, u32[]{:S(2)}) copy-start(f32[3,1152]{1,0:T(4,128)} %param.15) | copy-start | bytes 41476
  50.8 1.1 %copy-start.3 = (f32[104,1152]{1,0:T(8,128)S(1)}, f32[104,1152]{1,0:T(8,128)}, u32[]{:S(2)}) copy-start(f32[104,1152]{1,0:T(8,128)} %shard_map.146) | copy-start | bytes 1437700

commit v6 on v5

--- a/solution.py
+++ b/solution.py
@@ -52,37 +52,44 @@
     count, length = x_ref.shape
     c9, s9 = fft_tables(length)[:2]
     highest = lax.Precision.HIGHEST
-    parts = [x_ref[:, n * lanes:(n + 1) * lanes] for n in range(rows)]
     half = rows // 2 + 1
-    real_a = [sum(float(c9[k, n]) * parts[n] for n in range(rows)) for k in range(half)]
-    imag_a = [sum(float(-s9[k, n]) * parts[n] for n in range(1, rows)) for k in range(half)]
-    real_a += [real_a[rows - k] for k in range(half, rows)]
-    imag_a += [-imag_a[rows - k] for k in range(half, rows)]
+    parts = [x_ref[:, n * lanes : (n + 1) * lanes] for n in range(rows)]
     pieces = []
-    for k in range(rows):
-        twc = twc_ref[k:k + 1, :]
-        tws = tws_ref[k:k + 1, :]
-        pieces.append(jnp.concatenate(
-            [real_a[k] * twc + imag_a[k] * tws, imag_a[k] * twc - real_a[k] * tws], axis=1))
-    spectrum = jnp.dot(jnp.concatenate(pieces, axis=0), fwd_ref[...], precision=highest,
-                       preferred_element_type=jnp.float32)
+    for k in range(half):
+        real_a = sum(float(c9[k, n]) * parts[n] for n in range(rows))
+        imag_a = sum(float(-s9[k, n]) * parts[n] for n in range(1, rows))
+        twc = twc_ref[k : k + 1, :]
+        tws = tws_ref[k : k + 1, :]
+        pieces.append(
+            jnp.concatenate([real_a * twc + imag_a * tws, imag_a * twc - real_a * tws], axis=1)
+        )
+    spectrum = jnp.dot(
+        jnp.concatenate(pieces, axis=0),
+        fwd_ref[...],
+        precision=highest,
+        preferred_element_type=jnp.float32,
+    )
     cuts = cut_ref[...]
     keep = jnp.concatenate(
-        [(fold_ref[k:k + 1, :] <= cuts).astype(jnp.float32) for k in range(rows)], axis=0)
-    back = jnp.dot(spectrum * keep, inv_ref[...], precision=highest,
-                   preferred_element_type=jnp.float32)
+        [(fold_ref[k : k + 1, :] <= cuts).astype(jnp.float32) for k in range(half)], axis=0
+    )
+    back = jnp.dot(
+        spectrum * keep, inv_ref[...], precision=highest, preferred_element_type=jnp.float32
+    )
     real_d, imag_d = [], []
-    for k in range(rows):
-        twc = twc_ref[k:k + 1, :]
-        tws = tws_ref[k:k + 1, :]
-        real_c = back[k * count:(k + 1) * count, :lanes]
-        imag_c = back[k * count:(k + 1) * count, lanes:]
+    for k in range(half):
+        twc = twc_ref[k : k + 1, :]
+        tws = tws_ref[k : k + 1, :]
+        real_c = back[k * count : (k + 1) * count, :lanes]
+        imag_c = back[k * count : (k + 1) * count, lanes:]
         real_d.append(real_c * twc - imag_c * tws)
         imag_d.append(imag_c * twc + real_c * tws)
     for n in range(rows):
-        o_ref[:, n * lanes:(n + 1) * lanes] = sum(
-            float(c9[k, n] / length) * real_d[k] - float(s9[k, n] / length) * imag_d[k]
-            for k in range(rows))
+        o_ref[:, n * lanes : (n + 1) * lanes] = float(1.0 / length) * real_d[0] + sum(
+            float(2.0 * c9[k, n] / length) * real_d[k] - float(2.0 * s9[k, n] / length) * imag_d[k]
+            for k in range(1, half)
+        )
+
 
 def filter_rows(values, cuts):
     count, length = values.shape

time: 54.4 us -> 53 us (0.974)
  Pallas kernels: 5.62 us -> 4.26 us
    pallas_call x1, Pallas kernels: 5.62 us -> 4.26 us  [filter_rows(): pl.pallas_call(filter_kernel, out_shape=jax.ShapeDtypeStruct(values.shape...]
where the time goes in v6:
time: 53 us; the launch traced here: 52.5 us
  starting transfers between devices  19.4 us (37%)
  waiting for transfers between devices  15.4 us (29%)
  local copies, waits for them, and re-layouts  7.99 us (15%)
  other arithmetic  4.53 us (9%)
  Pallas kernels  4.26 us (8%)
  between operations  0.96 us (2%)
    all_to_all x2, waiting for transfers between devices, prefix_over(): lax.all_to_all(copies, axis, split_axis=0, concat_axis=0, tiled=True)  15.4 us
    all_to_all x2, starting transfers between devices, prefix_over(): lax.all_to_all(copies, axis, split_axis=0, concat_axis=0, tiled=True)  10.5 us
    ppermute x1, starting transfers between devices, local(): lax.ppermute(to_south, 'lat', [(i + 1, i) for i in range(count - 1)])  6.96 us
    pallas_call x1, Pallas kernels, filter_rows(): pl.pallas_call(filter_kernel, out_shape=jax.ShapeDtypeStruct(values.shape...  4.26 us
    ppermute x1, starting transfers between devices, local(): lax.ppermute(to_north, 'lat', [(i, i + 1) for i in range(count - 1)])  1.92 us
    broadcast_in_dim x2, local copies, waits for them, and re-layouts, prefix_over(): copies = jnp.broadcast_to(value, (count, *value.shape))  1.33 us
    unnamed x14, local copies, waits for them, and re-layouts  1.26 us
  transfers between devices with their start and end apart: 4, of which 2 were waited for; matrix products, arithmetic and copies ran while one was open for 9% of the time, Pallas kernels for 0%

profile of v6, /device:TPU:256, one launch (start us, length us, event | category | flops | bytes accessed | tf_op | source)
XLA Modules:
  0.0 52.5 jit_solution(18310732572309929131)
XLA Ops:
  0.7 0.8 %slice.300 = f32[1,8,1152]{2,1,0:T(8,128)S(1)} slice(f32[3,8,1152]{2,1,0:T(8,128)} %bitcast.82), slice={[0:1], [0:8], [0:1152]} | slice | bytes 73728 | tf_op jit(solution)/shard_map/slice | solution.py:124
  1.5 0.7 %slice_reduce_fusion = f32[1152]{0:T(1024)S(1)} fusion(f32[3,1152]{1,0:T(4,128)} %param.15), kind=kLoop, calls=%fused_computation.103 | loop fusion | bytes 9216 | tf_op jit(solution)/shard_map/slice | solution.py:123
  2.2 0.9 %pad_maximum_fusion.3 = (f32[7,8,1152]{2,1,0:T(8,128)S(1)}, f32[7,8,1152]{2,1,0:T(8,128)S(1)}) fusion(f32[1,8,1152]{2,1,0:T(8,128)S(1)} %broadcast_in_dim.45, f32[3,8,1152]{2,1,0:T(8,128)} %bitcast.72, f32[3,8,1152]{2,1,0:T(8,128)S(1)} %bitcast.63, f32[1,8,1152]{2,1,0:T(8,128)S(1)} %slice.300), kind=kLoop, calls=%fused_computation.20 | loop fusion | flops 193536 | bytes 811008 | tf_op jit(solution)/shard_map/concatenate | solution.py:123
  3.2 1.9 %collective-permute-start.1 = (f32[7,8,1152]{2,1,0:T(8,128)S(1)}, f32[7,8,1152]{2,1,0:T(8,128)S(1)}, u32[]{:S(2)}, u32[]{:S(2)}) collective-permute-start(f32[7,8,1152]{2,1,0:T(8,128)S(1)} %get-tuple-element.22), channel_id=1, source_target_pairs={{0,8},{8,16},{16,24},{24,32},{32,40},{40,48},{48,56},{56,64},{64,7... | collective-permute-start | bytes 774152 | tf_op jit(solution)/shard_map/ppermute | solution.py:126
  5.1 7.0 %collective-permute-start = (f32[7,8,1152]{2,1,0:T(8,128)S(1)}, f32[7,8,1152]{2,1,0:T(8,128)S(1)}, u32[]{:S(2)}, u32[]{:S(2)}) collective-permute-start(f32[7,8,1152]{2,1,0:T(8,128)S(1)} %get-tuple-element.23), channel_id=1, source_target_pairs={{8,0},{16,8},{24,16},{32,24},{40,32},{48,40},{56,48},{64,56},{72,6... | collective-permute-start | bytes 774152 | tf_op jit(solution)/shard_map/ppermute | solution.py:127
  12.1 0.1 fusion.67
  12.2 0.1 fusion.69
  12.6 0.6 %copy-done.2 = f32[8,3,1152]{2,0,1:T(8,128)S(1)} copy-done((f32[8,3,1152]{2,0,1:T(8,128)S(1)}, f32[8,3,1152]{2,0,1:T(8,128)}, u32[]{:S(2)}) %copy-start.2) | copy-done | bytes 110616
  13.3 0.1 fusion.65
  13.5 0.6 %copy-done.5 = f32[8,3,1152]{2,0,1:T(8,128)S(1)} copy-done((f32[8,3,1152]{2,0,1:T(8,128)S(1)}, f32[8,3,1152]{2,0,1:T(8,128)}, u32[]{:S(2)}) %copy-start.5) | copy-done | bytes 110616
  14.2 0.2 fusion.47
  14.5 0.7 %broadcast_in_dim.49 = f32[8,4,1152]{2,1,0:T(4,128)} broadcast(f32[4,1152]{1,0:T(4,128)S(1)} %get-tuple-element.25), dimensions={1,2} | broadcast | bytes 165888 | tf_op jit(solution)/shard_map/broadcast_in_dim | solution.py:106
  15.2 7.1 %all-to-all-start = ((f32[8,4,1152]{2,1,0:T(4,128)}), f32[8,4,1152]{2,1,0:T(4,128)S(1)}, u32[]{:S(2)}, u32[]{:S(2)}) async-start(f32[8,4,1152]{2,1,0:T(4,128)} %broadcast_in_dim.49), calls=%async_computation | async-start | bytes 294912 | tf_op jit(solution)/shard_map/all_to_all | solution.py:107
  22.3 0.1 reduce_window_sum.17
  22.5 9.0 %all-to-all-done = f32[8,4,1152]{2,1,0:T(4,128)S(1)} async-done(((f32[8,4,1152]{2,1,0:T(4,128)}), f32[8,4,1152]{2,1,0:T(4,128)S(1)}, u32[]{:S(2)}, u32[]{:S(2)}) %all-to-all-start) | async-done | bytes 147488 | tf_op jit(solution)/shard_map/all_to_all | solution.py:107
  31.5 0.1 select_reduce_fusion.1
  31.7 0.2 fusion.59
  31.8 0.7 %broadcast_in_dim.51 = f32[8,4,1152]{2,1,0:T(4,128)} broadcast(f32[4,1152]{1,0:T(4,128)S(1)} %get-tuple-element.9), dimensions={1,2} | broadcast | bytes 165888 | tf_op jit(solution)/shard_map/broadcast_in_dim | solution.py:106
  32.5 3.4 %all-to-all-start.1 = ((f32[8,4,1152]{2,1,0:T(4,128)}), f32[8,4,1152]{2,1,0:T(4,128)S(1)}, u32[]{:S(2)}, u32[]{:S(2)}) async-start(f32[8,4,1152]{2,1,0:T(4,128)} %broadcast_in_dim.51), calls=%async_computation.1 | async-start | bytes 294912 | tf_op jit(solution)/shard_map/all_to_all | solution.py:107
  36.0 0.7 %gather_fusion = s32[13]{0:T(128)S(1)} fusion(s32[192]{0:T(256)S(1)} %copy-done, s32[1024]{0:T(1024)S(1)} %pad_clamp_fusion), kind=kCustom, calls=%fused_computation | custom fusion | bytes 156 | tf_op jit(solution)/shard_map/gather | solution.py:156
  36.7 0.7 %reshape_reshape.4.cut_ref = s32[104,1]{1,0:T(8,128)} reshape(s32[13,8]{1,0:T(8,128)S(1)} %broadcast_in_dim.52) | data formatting | bytes 832 | tf_op jit(solution)/shard_map/reshape;reshape | solution.py:100
  37.4 0.1 rev.7
  37.6 0.1 reduce_window_sum.18
  37.7 0.2 rev.8
  37.9 0.8 %pad_maximum_fusion = f32[13,8,1152]{2,1,0:T(8,128)} fusion(f32[4,8,1152]{2,1,0:T(8,128)S(1)} %get-tuple-element.35, f32[3,8,1152]{2,1,0:T(8,128)S(1)} %fusion.47, f32[3,8,1152]{2,1,0:T(8,128)S(1)} %bitcast.84, f32[3,8,1152]{2,1,0:T(8,128)S(1)} %bitcast.85), kind=kLoop, calls=%fused_computation.1 | loop fusion | flops 359424 | bytes 958464 | tf_op jit(solution)/shard_map/concatenate | solution.py:152
  38.7 6.3 %all-to-all-done.1 = f32[8,4,1152]{2,1,0:T(4,128)S(1)} async-done(((f32[8,4,1152]{2,1,0:T(4,128)}), f32[8,4,1152]{2,1,0:T(4,128)S(1)}, u32[]{:S(2)}, u32[]{:S(2)}) %all-to-all-start.1) | async-done | bytes 147488 | tf_op jit(solution)/shard_map/all_to_all | solution.py:107
  45.0 0.1 select_reduce_fusion
  45.2 4.3 %shard_map.146 = f32[104,1152]{1,0:T(8,128)} custom-call(f32[104,1152]{1,0:T(8,128)} %bitcast.81, s32[104,1]{1,0:T(8,128)} %reshape_reshape.4.cut_ref, f32[9,128]{1,0:T(8,128)} %constant.58.clone.twc_ref, f32[9,128]{1,0:T(8,128)} %constant.59.clone.tws_ref, f32[256,256]{1,0:T(8,128)} %constant.60.clone.fwd_ref, f32[256,256]{1,0:T(8,128)} %constant.61.clone.inv_ref, ...), custom_call_target="tpu_custom_call" | custom-call | tf_op jit(solution)/shard_map/pallas_call | solution.py:97
  49.5 1.0 %slice_bitcast_fusion.1 = f32[3,8,1152]{2,1,0:T(8,128)S(1)} fusion(f32[104,1152]{1,0:T(8,128)} %shard_map.146), kind=kLoop, calls=%fused_computation.71 | loop fusion | bytes 221184 | tf_op jit(solution)/shard_map/slice | solution.py:161
  50.5 0.1 slice.318
  50.6 0.8 %fusion.54 = (f32[3,8,1152]{2,1,0:T(8,128)S(1)}, f32[8,3,1152]{2,0,1:T(8,128)}) fusion(f32[3,8,1151]{2,1,0:T(8,128)S(1)} %get-tuple-element.32, f32[3,8,1]{2,1,0:T(8,128)S(1)} %get-tuple-element.34, f32[3,8,1150]{2,1,0:T(8,128)S(1)} %get-tuple-element.28, f32[3,8,2]{2,1,0:T(8,128)S(1)} %get-tuple-element.30, f32[3,8,1]{2,1,0:T(8,128)S(1)} %get-tuple-element.33, ...), kind=kLoop, calls=%fused_computation.96 | loop fusion | flops 552960 | bytes 1437696 | tf_op jit(solution)/shard_map/mul | solution.py:166
  51.6 0.8 %fusion.40 = (f32[8,3,1152]{2,0,1:T(8,128)}, f32[8,3,1152]{2,0,1:T(8,128)}, f32[8,3,1152]{2,0,1:T(8,128)}, f32[8,3,1152]{2,0,1:T(8,128)}) fusion(f32[104,1152]{1,0:T(8,128)S(1)} %copy-done.3, f32[4,8,1152]{2,1,0:T(8,128)S(1)} %fusion.28, f32[3]{0:T(128)S(1)} %compare_convert_fusion, f32[3,8,1151]{2,1,0:T(8,128)S(1)} %slice.254, f32[3,8,1]{2,1,0:T(8,128)S(1)} %slice.253, ...), kind=kLoop, calls=%fused_computation.75 | loop fusion | flops 414720 | bytes 1658892 | tf_op jit(solution)/shard_map/transpose | solution.py:176
  (46 shorter events, 1.2 us)
Async XLA Ops:
  0.6 35.3 %copy-start = (s32[192]{0:T(256)S(1)}, s32[192]{0:T(256)}, u32[]{:S(2)}) copy-start(s32[192]{0:T(256)} %param.16) | copy-start | bytes 2308
  0.6 1.6 %copy-start.1 = (f32[8,3,1152]{2,0,1:T(8,128)S(1)}, f32[8,3,1152]{2,0,1:T(8,128)}, u32[]{:S(2)}) copy-start(f32[8,3,1152]{2,0,1:T(8,128)} %param.13) | copy-start | bytes 331780
  3.2 11.3 %collective-permute-start.1 = (f32[7,8,1152]{2,1,0:T(8,128)S(1)}, f32[7,8,1152]{2,1,0:T(8,128)S(1)}, u32[]{:S(2)}, u32[]{:S(2)}) collective-permute-start(f32[7,8,1152]{2,1,0:T(8,128)S(1)} %get-tuple-element.22), channel_id=1, source_target_pairs={{0,8},{8,16},{16,24},{24,32},{32,40},{40,48},{48,56},{56,64},{64,7... | collective-permute-start | bytes 774152 | tf_op jit(solution)/shard_map/ppermute | solution.py:126
  5.1 17.3 %collective-permute-start = (f32[7,8,1152]{2,1,0:T(8,128)S(1)}, f32[7,8,1152]{2,1,0:T(8,128)S(1)}, u32[]{:S(2)}, u32[]{:S(2)}) collective-permute-start(f32[7,8,1152]{2,1,0:T(8,128)S(1)} %get-tuple-element.23), channel_id=1, source_target_pairs={{8,0},{16,8},{24,16},{32,24},{40,32},{48,40},{56,48},{64,56},{72,6... | collective-permute-start | bytes 774152 | tf_op jit(solution)/shard_map/ppermute | solution.py:127
  12.3 0.9 %copy-start.2 = (f32[8,3,1152]{2,0,1:T(8,128)S(1)}, f32[8,3,1152]{2,0,1:T(8,128)}, u32[]{:S(2)}) copy-start(f32[8,3,1152]{2,0,1:T(8,128)} %param.14) | copy-start | bytes 331780
  13.3 0.9 %copy-start.5 = (f32[8,3,1152]{2,0,1:T(8,128)S(1)}, f32[8,3,1152]{2,0,1:T(8,128)}, u32[]{:S(2)}) copy-start(f32[8,3,1152]{2,0,1:T(8,128)} %param.11) | copy-start | bytes 331780
  15.2 16.4 %all-to-all-start = ((f32[8,4,1152]{2,1,0:T(4,128)}), f32[8,4,1152]{2,1,0:T(4,128)S(1)}, u32[]{:S(2)}, u32[]{:S(2)}) async-start(f32[8,4,1152]{2,1,0:T(4,128)} %broadcast_in_dim.49), calls=%async_computation | async-start | bytes 294912 | tf_op jit(solution)/shard_map/all_to_all | solution.py:107
  22.5 9.2 %copy-start.4 = (f32[8,3,1152]{2,0,1:T(8,128)S(1)}, f32[8,3,1152]{2,0,1:T(8,128)}, u32[]{:S(2)}) copy-start(f32[8,3,1152]{2,0,1:T(8,128)} %param.12) | copy-start | bytes 331780
  32.5 12.6 %all-to-all-start.1 = ((f32[8,4,1152]{2,1,0:T(4,128)}), f32[8,4,1152]{2,1,0:T(4,128)S(1)}, u32[]{:S(2)}, u32[]{:S(2)}) async-start(f32[8,4,1152]{2,1,0:T(4,128)} %broadcast_in_dim.51), calls=%async_computation.1 | async-start | bytes 294912 | tf_op jit(solution)/shard_map/all_to_all | solution.py:107
  38.7 6.5 %copy-start.6 = (f32[3,1152]{1,0:T(4,128)S(1)}, f32[3,1152]{1,0:T(4,128)}, u32[]{:S(2)}) copy-start(f32[3,1152]{1,0:T(4,128)} %param.15) | copy-start | bytes 41476
  49.5 1.1 %copy-start.3 = (f32[104,1152]{1,0:T(8,128)S(1)}, f32[104,1152]{1,0:T(8,128)}, u32[]{:S(2)}) copy-start(f32[104,1152]{1,0:T(8,128)} %shard_map.146) | copy-start | bytes 1437700

commit v7 on v6

--- a/solution.py
+++ b/solution.py
@@ -155,7 +155,14 @@
     row_cuts = jnp.broadcast_to(
         filter_cutoff[jnp.minimum(cut_rows, nlat_all - 1)][:, None], fields.shape[:2]
     ).reshape(-1)
-    smooth = filter_rows(fields.reshape(-1, length), row_cuts).reshape(fields.shape)
+    flat = fields.reshape(-1, length)
+    smooth = lax.cond(
+        jnp.any(row_cuts < length // 2),
+        filter_rows,
+        lambda values, cuts: values,
+        flat,
+        row_cuts,
+    ).reshape(fields.shape)
     east_smooth = smooth[:rows]
     north_smooth = smooth[rows : 2 * rows]
     east_flux = smooth[2 * rows : 3 * rows]

time: 53 us -> 53.6 us (1.011)
  the two profiles are of different devices: /device:TPU:256 before, /device:TPU:448 now
where the time goes in v7:
time: 53.6 us; the launch traced here: 53 us
  starting transfers between devices  18.1 us (34%)
  waiting for transfers between devices  16.9 us (32%)
  local copies, waits for them, and re-layouts  8.46 us (16%)
  other arithmetic  4.39 us (8%)
  Pallas kernels  3.46 us (6%)
  between operations  1.65 us (3%)
    all_to_all x2, waiting for transfers between devices, prefix_over(): lax.all_to_all(copies, axis, split_axis=0, concat_axis=0, tiled=True)  16.9 us
    all_to_all x2, starting transfers between devices, prefix_over(): lax.all_to_all(copies, axis, split_axis=0, concat_axis=0, tiled=True)  10.5 us
    ppermute x1, starting transfers between devices, local(): lax.ppermute(to_south, 'lat', [(i + 1, i) for i in range(count - 1)])  5.75 us
    pallas_call x1, Pallas kernels, filter_rows(): pl.pallas_call(filter_kernel, out_shape=jax.ShapeDtypeStruct(values.shape...  3.46 us
    ppermute x1, starting transfers between devices, local(): lax.ppermute(to_north, 'lat', [(i, i + 1) for i in range(count - 1)])  1.92 us
    broadcast_in_dim x2, local copies, waits for them, and re-layouts, prefix_over(): copies = jnp.broadcast_to(value, (count, *value.shape))  1.33 us
    unnamed x14, local copies, waits for them, and re-layouts  1.19 us
  transfers between devices with their start and end apart: 4, of which 2 were waited for; matrix products, arithmetic and copies ran while one was open for 7% of the time, Pallas kernels for 0%

profile of v7, /device:TPU:448, one launch (start us, length us, event | category | flops | bytes accessed | tf_op | source)
XLA Modules:
  0.0 53.0 jit_solution(2396823197784570813)
XLA Ops:
  0.7 0.8 %slice.300 = f32[1,8,1152]{2,1,0:T(8,128)S(1)} slice(f32[3,8,1152]{2,1,0:T(8,128)} %bitcast.83), slice={[0:1], [0:8], [0:1152]} | slice | bytes 73728 | tf_op jit(solution)/shard_map/slice | solution.py:124
  1.5 0.7 %slice_reduce_fusion = f32[1152]{0:T(1024)S(1)} fusion(f32[3,1152]{1,0:T(4,128)} %param.17), kind=kLoop, calls=%fused_computation.103 | loop fusion | bytes 9216 | tf_op jit(solution)/shard_map/slice | solution.py:123
  2.2 0.9 %pad_maximum_fusion.3 = (f32[7,8,1152]{2,1,0:T(8,128)S(1)}, f32[7,8,1152]{2,1,0:T(8,128)S(1)}) fusion(f32[1,8,1152]{2,1,0:T(8,128)S(1)} %broadcast_in_dim.49, f32[3,8,1152]{2,1,0:T(8,128)} %bitcast.72, f32[3,8,1152]{2,1,0:T(8,128)S(1)} %bitcast.63, f32[1,8,1152]{2,1,0:T(8,128)S(1)} %slice.300), kind=kLoop, calls=%fused_computation.20 | loop fusion | flops 193536 | bytes 811008 | tf_op jit(solution)/shard_map/concatenate | solution.py:123
  3.2 1.9 %collective-permute-start.1 = (f32[7,8,1152]{2,1,0:T(8,128)S(1)}, f32[7,8,1152]{2,1,0:T(8,128)S(1)}, u32[]{:S(2)}, u32[]{:S(2)}) collective-permute-start(f32[7,8,1152]{2,1,0:T(8,128)S(1)} %get-tuple-element.62), channel_id=1, source_target_pairs={{0,8},{8,16},{16,24},{24,32},{32,40},{40,48},{48,56},{56,64},{64,7... | collective-permute-start | bytes 774152 | tf_op jit(solution)/shard_map/ppermute | solution.py:126
  5.1 5.8 %collective-permute-start = (f32[7,8,1152]{2,1,0:T(8,128)S(1)}, f32[7,8,1152]{2,1,0:T(8,128)S(1)}, u32[]{:S(2)}, u32[]{:S(2)}) collective-permute-start(f32[7,8,1152]{2,1,0:T(8,128)S(1)} %get-tuple-element.63), channel_id=1, source_target_pairs={{8,0},{16,8},{24,16},{32,24},{40,32},{48,40},{56,48},{64,56},{72,6... | collective-permute-start | bytes 774152 | tf_op jit(solution)/shard_map/ppermute | solution.py:127
  11.0 0.1 fusion.69
  11.4 0.6 %copy-done.2 = f32[8,3,1152]{2,0,1:T(8,128)S(1)} copy-done((f32[8,3,1152]{2,0,1:T(8,128)S(1)}, f32[8,3,1152]{2,0,1:T(8,128)}, u32[]{:S(2)}) %copy-start.2) | copy-done | bytes 110616
  12.1 0.1 fusion.65
  12.4 0.7 %gather_fusion = s32[13]{0:T(128)S(1)} fusion(s32[192]{0:T(256)S(1)} %copy-done, s32[1024]{0:T(1024)S(1)} %pad_clamp_fusion), kind=kCustom, calls=%fused_computation | custom fusion | bytes 156 | tf_op jit(solution)/shard_map/gather | solution.py:156
  13.0 0.6 %broadcast_reduce_fusion = pred[]{:T(512)} fusion(pred[13]{0:T(512)(128)(4,1)S(1)} %broadcast_compare_fusion), kind=kLoop, calls=%fused_computation.107 | loop fusion | flops 103 | bytes 14 | tf_op jit(solution)/shard_map/reduce_or | solution.py:160
  13.7 0.2 fusion.47
  14.0 0.7 %broadcast_in_dim.53 = f32[8,4,1152]{2,1,0:T(4,128)} broadcast(f32[4,1152]{1,0:T(4,128)S(1)} %get-tuple-element.65), dimensions={1,2} | broadcast | bytes 165888 | tf_op jit(solution)/shard_map/broadcast_in_dim | solution.py:106
  14.7 7.1 %all-to-all-start = ((f32[8,4,1152]{2,1,0:T(4,128)}), f32[8,4,1152]{2,1,0:T(4,128)S(1)}, u32[]{:S(2)}, u32[]{:S(2)}) async-start(f32[8,4,1152]{2,1,0:T(4,128)} %broadcast_in_dim.53), calls=%async_computation | async-start | bytes 294912 | tf_op jit(solution)/shard_map/all_to_all | solution.py:107
  21.8 0.1 reduce_window_sum.17
  22.0 9.0 %all-to-all-done = f32[8,4,1152]{2,1,0:T(4,128)S(1)} async-done(((f32[8,4,1152]{2,1,0:T(4,128)}), f32[8,4,1152]{2,1,0:T(4,128)S(1)}, u32[]{:S(2)}, u32[]{:S(2)}) %all-to-all-start) | async-done | bytes 147488 | tf_op jit(solution)/shard_map/all_to_all | solution.py:107
  31.0 0.1 select_reduce_fusion.1
  31.2 0.1 fusion.59
  31.3 0.7 %broadcast_in_dim.55 = f32[8,4,1152]{2,1,0:T(4,128)} broadcast(f32[4,1152]{1,0:T(4,128)S(1)} %get-tuple-element.49), dimensions={1,2} | broadcast | bytes 165888 | tf_op jit(solution)/shard_map/broadcast_in_dim | solution.py:106
  32.0 3.4 %all-to-all-start.1 = ((f32[8,4,1152]{2,1,0:T(4,128)}), f32[8,4,1152]{2,1,0:T(4,128)S(1)}, u32[]{:S(2)}, u32[]{:S(2)}) async-start(f32[8,4,1152]{2,1,0:T(4,128)} %broadcast_in_dim.55), calls=%async_computation.1 | async-start | bytes 294912 | tf_op jit(solution)/shard_map/all_to_all | solution.py:107
  36.1 0.2 rev.7
  36.3 0.1 reduce_window_sum.18
  36.4 0.2 rev.8
  36.7 7.9 %all-to-all-done.1 = f32[8,4,1152]{2,1,0:T(4,128)S(1)} async-done(((f32[8,4,1152]{2,1,0:T(4,128)}), f32[8,4,1152]{2,1,0:T(4,128)S(1)}, u32[]{:S(2)}, u32[]{:S(2)}) %all-to-all-start.1) | async-done | bytes 147488 | tf_op jit(solution)/shard_map/all_to_all | solution.py:107
  44.5 0.1 select_reduce_fusion
  44.7 5.0 %conditional.1 = (f32[104,1152]{1,0:T(8,128)S(1)}) conditional(s32[]{:T(128)} %convert_element_type.13, f32[104,1152]{1,0:T(8,128)S(1)} %bitcast.81, (s32[13]{0:T(128)S(1)}, f32[104,1152]{1,0:T(8,128)S(1)}) %tuple.56), branch_computations={%region_7.8_spmd, %region_8.9_spmd.clone} | conditional | bytes 959772 | solution.py:159
  44.7 0.8 %copy.37.x_ref = f32[104,1152]{1,0:T(8,128)} copy(f32[104,1152]{1,0:T(8,128)S(1)} %get-tuple-element.45) | data formatting | bytes 958464 | tf_op jit(solution)/shard_map/cond
  45.6 0.7 %reshape_reshape.4.cut_ref = s32[104,1]{1,0:T(8,128)} reshape(s32[13,8]{1,0:T(8,128)S(1)} %broadcast_in_dim.56) | data formatting | bytes 832 | tf_op jit(solution)/shard_map/cond/branch_1_fun/reshape;reshape | solution.py:100
  46.3 3.5 %branch_1_fun.1 = f32[104,1152]{1,0:T(8,128)S(1)} custom-call(f32[104,1152]{1,0:T(8,128)} %copy.37.x_ref, s32[104,1]{1,0:T(8,128)} %reshape_reshape.4.cut_ref, f32[9,128]{1,0:T(8,128)} %constant.62.clone.2.twc_ref, f32[9,128]{1,0:T(8,128)} %constant.63.clone.2.tws_ref, f32[256,256]{1,0:T(8,128)} %constant.64.clone.2.fwd_ref, ...), custom_call_target="tpu_custom_call" | custom-call | tf_op jit(solution)/shard_map/cond/branch_1_fun/pallas_call | solution.py:97
  49.9 0.5 %copy-done.4 = f32[3,8,1152]{2,1,0:T(8,128)} copy-done((f32[3,8,1152]{2,1,0:T(8,128)}, f32[3,8,1152]{2,1,0:T(8,128)S(1)}, u32[]{:S(2)}) %copy-start.4) | copy-done | bytes 110616
  50.4 0.7 %slice-done = f32[3,8,1]{2,1,0:T(8,128)S(1)} async-done(((f32[3,8,1152]{2,1,0:T(8,128)}), f32[3,8,1]{2,1,0:T(8,128)S(1)}, s32[]{:S(2)}) %slice-start) | async-done | bytes 120 | tf_op jit(solution)/shard_map/jit(_roll_static)/slice | solution.py:171
  51.1 0.8 %fusion.54 = (f32[3,8,1152]{2,1,0:T(8,128)S(1)}, f32[8,3,1152]{2,0,1:T(8,128)}) fusion(f32[3,8,1151]{2,1,0:T(8,128)S(1)} %get-tuple-element.72, f32[3,8,1]{2,1,0:T(8,128)S(1)} %get-tuple-element.74, f32[3,8,1150]{2,1,0:T(8,128)S(1)} %get-tuple-element.68, f32[3,8,2]{2,1,0:T(8,128)S(1)} %get-tuple-element.70, f32[3,8,1]{2,1,0:T(8,128)S(1)} %get-tuple-element.73, ...), kind=kLoop, calls=%fused_computation.96 | loop fusion | flops 552960 | bytes 1437696 | tf_op jit(solution)/shard_map/mul | solution.py:173
  52.2 0.8 %fusion.40 = (f32[8,3,1152]{2,0,1:T(8,128)}, f32[8,3,1152]{2,0,1:T(8,128)}, f32[8,3,1152]{2,0,1:T(8,128)}, f32[8,3,1152]{2,0,1:T(8,128)}) fusion(f32[104,1152]{1,0:T(8,128)S(1)} %get-tuple-element.85, f32[4,8,1152]{2,1,0:T(8,128)S(1)} %fusion.28, f32[3]{0:T(128)S(1)} %compare_convert_fusion, f32[3,8,1151]{2,1,0:T(8,128)S(1)} %slice.254, ...), kind=kLoop, calls=%fused_computation.75 | loop fusion | flops 414720 | bytes 1658892 | tf_op jit(solution)/shard_map/transpose | solution.py:183
  (51 shorter events, 1.4 us)
Async XLA Ops:
  0.6 11.7 %copy-start = (s32[192]{0:T(256)S(1)}, s32[192]{0:T(256)}, u32[]{:S(2)}) copy-start(s32[192]{0:T(256)} %param.18) | copy-start | bytes 2308
  0.6 1.6 %copy-start.1 = (f32[8,3,1152]{2,0,1:T(8,128)S(1)}, f32[8,3,1152]{2,0,1:T(8,128)}, u32[]{:S(2)}) copy-start(f32[8,3,1152]{2,0,1:T(8,128)} %param.15) | copy-start | bytes 331780
  3.2 10.8 %collective-permute-start.1 = (f32[7,8,1152]{2,1,0:T(8,128)S(1)}, f32[7,8,1152]{2,1,0:T(8,128)S(1)}, u32[]{:S(2)}, u32[]{:S(2)}) collective-permute-start(f32[7,8,1152]{2,1,0:T(8,128)S(1)} %get-tuple-element.62), channel_id=1, source_target_pairs={{0,8},{8,16},{16,24},{24,32},{32,40},{40,48},{48,56},{56,64},{64,7... | collective-permute-start | bytes 774152 | tf_op jit(solution)/shard_map/ppermute | solution.py:126
  5.1 16.8 %collective-permute-start = (f32[7,8,1152]{2,1,0:T(8,128)S(1)}, f32[7,8,1152]{2,1,0:T(8,128)S(1)}, u32[]{:S(2)}, u32[]{:S(2)}) collective-permute-start(f32[7,8,1152]{2,1,0:T(8,128)S(1)} %get-tuple-element.63), channel_id=1, source_target_pairs={{8,0},{16,8},{24,16},{32,24},{40,32},{48,40},{56,48},{64,56},{72,6... | collective-permute-start | bytes 774152 | tf_op jit(solution)/shard_map/ppermute | solution.py:127
  11.1 0.9 %copy-start.2 = (f32[8,3,1152]{2,0,1:T(8,128)S(1)}, f32[8,3,1152]{2,0,1:T(8,128)}, u32[]{:S(2)}) copy-start(f32[8,3,1152]{2,0,1:T(8,128)} %param.16) | copy-start | bytes 331780
  12.3 1.3 %copy-start.5 = (f32[8,3,1152]{2,0,1:T(8,128)S(1)}, f32[8,3,1152]{2,0,1:T(8,128)}, u32[]{:S(2)}) copy-start(f32[8,3,1152]{2,0,1:T(8,128)} %param.13) | copy-start | bytes 331780
  14.7 16.4 %all-to-all-start = ((f32[8,4,1152]{2,1,0:T(4,128)}), f32[8,4,1152]{2,1,0:T(4,128)S(1)}, u32[]{:S(2)}, u32[]{:S(2)}) async-start(f32[8,4,1152]{2,1,0:T(4,128)} %broadcast_in_dim.53), calls=%async_computation | async-start | bytes 294912 | tf_op jit(solution)/shard_map/all_to_all | solution.py:107
  22.0 9.2 %copy-start.3 = (f32[8,3,1152]{2,0,1:T(8,128)S(1)}, f32[8,3,1152]{2,0,1:T(8,128)}, u32[]{:S(2)}) copy-start(f32[8,3,1152]{2,0,1:T(8,128)} %param.14) | copy-start | bytes 331780
  32.0 12.6 %all-to-all-start.1 = ((f32[8,4,1152]{2,1,0:T(4,128)}), f32[8,4,1152]{2,1,0:T(4,128)S(1)}, u32[]{:S(2)}, u32[]{:S(2)}) async-start(f32[8,4,1152]{2,1,0:T(4,128)} %broadcast_in_dim.55), calls=%async_computation.1 | async-start | bytes 294912 | tf_op jit(solution)/shard_map/all_to_all | solution.py:107
  36.7 8.0 %copy-start.6 = (f32[3,1152]{1,0:T(4,128)S(1)}, f32[3,1152]{1,0:T(4,128)}, u32[]{:S(2)}) copy-start(f32[3,1152]{1,0:T(4,128)} %param.17) | copy-start | bytes 41476
  49.8 0.6 %copy-start.4 = (f32[3,8,1152]{2,1,0:T(8,128)}, f32[3,8,1152]{2,1,0:T(8,128)S(1)}, u32[]{:S(2)}) copy-start(f32[3,8,1152]{2,1,0:T(8,128)S(1)} %slice_bitcast_fusion.1) | copy-start | bytes 331780
  50.4 0.7 %slice-start = ((f32[3,8,1152]{2,1,0:T(8,128)}), f32[3,8,1]{2,1,0:T(8,128)S(1)}, s32[]{:S(2)}) async-start(f32[3,8,1152]{2,1,0:T(8,128)} %copy-done.4), calls=%async_computation.2 | async-start | bytes 24576 | tf_op jit(solution)/shard_map/jit(_roll_static)/slice | solution.py:171

commit v8 on v7

--- a/solution.py
+++ b/solution.py
@@ -102,12 +102,16 @@
 
 def prefix_over(value, axis, before):
     count = lax.axis_size(axis)
-    rank = lax.axis_index(axis)
-    copies = jnp.broadcast_to(value, (count, *value.shape))
-    pieces = lax.all_to_all(copies, axis, split_axis=0, concat_axis=0, tiled=True)
-    owners = jnp.arange(count, dtype=jnp.int32)
-    chosen = owners < rank if before else owners > rank
-    return jnp.sum(jnp.where(chosen[:, None, None], pieces, 0.0), axis=0)
+    total = value
+    step = 1
+    while step < count:
+        if before:
+            route = [(i, i + step) for i in range(count - step)]
+        else:
+            route = [(i + step, i) for i in range(count - step)]
+        total = total + lax.ppermute(total, axis, route)
+        step *= 2
+    return total - value
 
 
 def local(wind_east, wind_north, layer_mass, theta_field, surface_height, filter_cutoff):

time: 53.6 us -> 70.4 us (1.31)
  the two profiles are of different devices: /device:TPU:448 before, /device:TPU:472 now
where the time goes in v8:
time: 70.4 us; the launch traced here: 69.8 us
  starting transfers between devices  28.1 us (40%)
  waiting for transfers between devices  23.9 us (34%)
  local copies, waits for them, and re-layouts  8.49 us (12%)
  other arithmetic  4.2 us (6%)
  Pallas kernels  3.46 us (5%)
  between operations  1.64 us (2%)
    ppermute x6, waiting for transfers between devices, prefix_over(): total = total + lax.ppermute(total, axis, route)  23.9 us
    ppermute x6, starting transfers between devices, prefix_over(): total = total + lax.ppermute(total, axis, route)  20.4 us
    ppermute x1, starting transfers between devices, local(): lax.ppermute(to_south, 'lat', [(i + 1, i) for i in range(count - 1)])  5.75 us
    pallas_call x1, Pallas kernels, filter_rows(): pl.pallas_call(filter_kernel, out_shape=jax.ShapeDtypeStruct(values.shape...  3.46 us
    unnamed x16, local copies, waits for them, and re-layouts  2.56 us
    ppermute x1, starting transfers between devices, local(): lax.ppermute(to_north, 'lat', [(i, i + 1) for i in range(count - 1)])  1.92 us
  transfers between devices with their start and end apart: 8, of which 6 were waited for; matrix products, arithmetic and copies ran while one was open for 5% of the time, Pallas kernels for 0%

profile of v8, /device:TPU:472, one launch (start us, length us, event | category | flops | bytes accessed | tf_op | source)
XLA Modules:
  0.0 69.8 jit_solution(160052168253790445)
XLA Ops:
  0.7 0.8 %slice.300 = f32[1,8,1152]{2,1,0:T(8,128)S(1)} slice(f32[3,8,1152]{2,1,0:T(8,128)} %bitcast.83), slice={[0:1], [0:8], [0:1152]} | slice | bytes 73728 | tf_op jit(solution)/shard_map/slice | solution.py:128
  1.5 0.7 %slice_reduce_fusion = f32[1152]{0:T(1024)S(1)} fusion(f32[3,1152]{1,0:T(4,128)} %param.17), kind=kLoop, calls=%fused_computation.102 | loop fusion | bytes 9216 | tf_op jit(solution)/shard_map/slice | solution.py:127
  2.2 0.9 %pad_maximum_fusion.3 = (f32[7,8,1152]{2,1,0:T(8,128)S(1)}, f32[7,8,1152]{2,1,0:T(8,128)S(1)}) fusion(f32[1,8,1152]{2,1,0:T(8,128)S(1)} %broadcast_in_dim.10, f32[3,8,1152]{2,1,0:T(8,128)} %bitcast.72, f32[3,8,1152]{2,1,0:T(8,128)S(1)} %bitcast.63, f32[1,8,1152]{2,1,0:T(8,128)S(1)} %slice.300), kind=kLoop, calls=%fused_computation.20 | loop fusion | flops 193536 | bytes 811008 | tf_op jit(solution)/shard_map/concatenate | solution.py:127
  3.2 1.9 %collective-permute-start.1 = (f32[7,8,1152]{2,1,0:T(8,128)S(1)}, f32[7,8,1152]{2,1,0:T(8,128)S(1)}, u32[]{:S(2)}, u32[]{:S(2)}) collective-permute-start(f32[7,8,1152]{2,1,0:T(8,128)S(1)} %get-tuple-element.62), channel_id=1, source_target_pairs={{0,8},{8,16},{16,24},{24,32},{32,40},{40,48},{48,56},{56,64},{64,7... | collective-permute-start | bytes 774152 | tf_op jit(solution)/shard_map/ppermute | solution.py:130
  5.1 5.8 %collective-permute-start = (f32[7,8,1152]{2,1,0:T(8,128)S(1)}, f32[7,8,1152]{2,1,0:T(8,128)S(1)}, u32[]{:S(2)}, u32[]{:S(2)}) collective-permute-start(f32[7,8,1152]{2,1,0:T(8,128)S(1)} %get-tuple-element.63), channel_id=1, source_target_pairs={{8,0},{16,8},{24,16},{32,24},{40,32},{48,40},{56,48},{64,56},{72,6... | collective-permute-start | bytes 774152 | tf_op jit(solution)/shard_map/ppermute | solution.py:131
  11.3 0.7 copy-done.2
  12.3 0.6 copy-done.5
  13.3 4.7 %collective-permute-start.2 = (f32[4,1152]{1,0:T(4,128)S(1)}, f32[4,1152]{1,0:T(4,128)S(1)}, u32[]{:S(2)}, u32[]{:S(2)}) collective-permute-start(f32[4,1152]{1,0:T(4,128)S(1)} %get-tuple-element.65), channel_id=1, source_target_pairs={{0,1},{1,2},{2,3},{3,4},{4,5},{5,6},{6,7},{8,9},{9,10},{10,11},{11... | collective-permute-start | bytes 55304 | tf_op jit(solution)/shard_map/ppermute | solution.py:112
  18.1 0.7 gather_fusion
  18.7 0.7 %collective-permute-done.2 = f32[4,1152]{1,0:T(4,128)S(1)} collective-permute-done((f32[4,1152]{1,0:T(4,128)S(1)}, f32[4,1152]{1,0:T(4,128)S(1)}, u32[]{:S(2)}, u32[]{:S(2)}) %collective-permute-start.2) | collective-permute-done | bytes 18464 | tf_op jit(solution)/shard_map/ppermute | solution.py:112
  19.4 4.3 %collective-permute-start.3 = (f32[4,1152]{1,0:T(4,128)S(1)}, f32[4,1152]{1,0:T(4,128)S(1)}, u32[]{:S(2)}, u32[]{:S(2)}) collective-permute-start(f32[4,1152]{1,0:T(4,128)S(1)} %add.138), channel_id=1, source_target_pairs={{0,2},{1,3},{2,4},{3,5},{4,6},{5,7},{8,10},{9,11},{10,12},{11,13},... | collective-permute-start | bytes 55304 | tf_op jit(solution)/shard_map/ppermute | solution.py:112
  23.8 2.2 %collective-permute-done.3 = f32[4,1152]{1,0:T(4,128)S(1)} collective-permute-done((f32[4,1152]{1,0:T(4,128)S(1)}, f32[4,1152]{1,0:T(4,128)S(1)}, u32[]{:S(2)}, u32[]{:S(2)}) %collective-permute-start.3) | collective-permute-done | bytes 18464 | tf_op jit(solution)/shard_map/ppermute | solution.py:112
  26.0 4.5 %collective-permute-start.4 = (f32[4,1152]{1,0:T(4,128)S(1)}, f32[4,1152]{1,0:T(4,128)S(1)}, u32[]{:S(2)}, u32[]{:S(2)}) collective-permute-start(f32[4,1152]{1,0:T(4,128)S(1)} %add.139), channel_id=1, source_target_pairs={{0,4},{1,5},{2,6},{3,7},{8,12},{9,13},{10,14},{11,15},{16,20},{17,... | collective-permute-start | bytes 55304 | tf_op jit(solution)/shard_map/ppermute | solution.py:112
  30.7 0.5 copy-done.6
  31.3 0.7 %collective-permute-done.4 = f32[4,1152]{1,0:T(4,128)S(1)} collective-permute-done((f32[4,1152]{1,0:T(4,128)S(1)}, f32[4,1152]{1,0:T(4,128)S(1)}, u32[]{:S(2)}, u32[]{:S(2)}) %collective-permute-start.4) | collective-permute-done | bytes 18464 | tf_op jit(solution)/shard_map/ppermute | solution.py:112
  32.3 3.7 %collective-permute-start.5 = (f32[4,1152]{1,0:T(4,128)S(1)}, f32[4,1152]{1,0:T(4,128)S(1)}, u32[]{:S(2)}, u32[]{:S(2)}) collective-permute-start(f32[4,1152]{1,0:T(4,128)S(1)} %get-tuple-element.49), channel_id=1, source_target_pairs={{1,0},{2,1},{3,2},{4,3},{5,4},{6,5},{7,6},{9,8},{10,9},{11,10},{12... | collective-permute-start | bytes 55304 | tf_op jit(solution)/shard_map/ppermute | solution.py:112
  36.0 8.1 %collective-permute-done.5 = f32[4,1152]{1,0:T(4,128)S(1)} collective-permute-done((f32[4,1152]{1,0:T(4,128)S(1)}, f32[4,1152]{1,0:T(4,128)S(1)}, u32[]{:S(2)}, u32[]{:S(2)}) %collective-permute-start.5) | collective-permute-done | bytes 18464 | tf_op jit(solution)/shard_map/ppermute | solution.py:112
  44.1 1.9 %collective-permute-start.6 = (f32[4,1152]{1,0:T(4,128)S(1)}, f32[4,1152]{1,0:T(4,128)S(1)}, u32[]{:S(2)}, u32[]{:S(2)}) collective-permute-start(f32[4,1152]{1,0:T(4,128)S(1)} %add.145), channel_id=1, source_target_pairs={{2,0},{3,1},{4,2},{5,3},{6,4},{7,5},{10,8},{11,9},{12,10},{13,11},... | collective-permute-start | bytes 55304 | tf_op jit(solution)/shard_map/ppermute | solution.py:112
  46.0 0.6 broadcast_reduce_fusion
  47.4 4.5 %collective-permute-done.6 = f32[4,1152]{1,0:T(4,128)S(1)} collective-permute-done((f32[4,1152]{1,0:T(4,128)S(1)}, f32[4,1152]{1,0:T(4,128)S(1)}, u32[]{:S(2)}, u32[]{:S(2)}) %collective-permute-start.6) | collective-permute-done | bytes 18464 | tf_op jit(solution)/shard_map/ppermute | solution.py:112
  51.9 1.3 %collective-permute-start.7 = (f32[4,1152]{1,0:T(4,128)S(1)}, f32[4,1152]{1,0:T(4,128)S(1)}, u32[]{:S(2)}, u32[]{:S(2)}) collective-permute-start(f32[4,1152]{1,0:T(4,128)S(1)} %add.146), channel_id=1, source_target_pairs={{4,0},{5,1},{6,2},{7,3},{12,8},{13,9},{14,10},{15,11},{20,16},{21,... | collective-permute-start | bytes 55304 | tf_op jit(solution)/shard_map/ppermute | solution.py:112
  53.2 0.2 rev.7
  53.5 0.2 rev.8
  53.7 7.7 %collective-permute-done.7 = f32[4,1152]{1,0:T(4,128)S(1)} collective-permute-done((f32[4,1152]{1,0:T(4,128)S(1)}, f32[4,1152]{1,0:T(4,128)S(1)}, u32[]{:S(2)}, u32[]{:S(2)}) %collective-permute-start.7) | collective-permute-done | bytes 18464 | tf_op jit(solution)/shard_map/ppermute | solution.py:112
  61.5 5.0 %conditional.1 = (f32[104,1152]{1,0:T(8,128)S(1)}) conditional(s32[]{:T(128)} %convert_element_type.13, f32[104,1152]{1,0:T(8,128)S(1)} %bitcast.81, (s32[13]{0:T(128)S(1)}, f32[104,1152]{1,0:T(8,128)S(1)}) %tuple.56), branch_computations={%region_5.6_spmd, %region_6.7_spmd.clone} | conditional | bytes 959772 | solution.py:163
  61.5 0.8 %copy.32.x_ref = f32[104,1152]{1,0:T(8,128)} copy(f32[104,1152]{1,0:T(8,128)S(1)} %get-tuple-element.45) | data formatting | bytes 958464 | tf_op jit(solution)/shard_map/cond
  62.4 0.7 %reshape_reshape.4.cut_ref = s32[104,1]{1,0:T(8,128)} reshape(s32[13,8]{1,0:T(8,128)S(1)} %broadcast_in_dim.12) | data formatting | bytes 832 | tf_op jit(solution)/shard_map/cond/branch_1_fun/reshape;reshape | solution.py:100
  63.1 3.5 %branch_1_fun.1 = f32[104,1152]{1,0:T(8,128)S(1)} custom-call(f32[104,1152]{1,0:T(8,128)} %copy.32.x_ref, s32[104,1]{1,0:T(8,128)} %reshape_reshape.4.cut_ref, f32[9,128]{1,0:T(8,128)} %constant.59.clone.2.twc_ref, f32[9,128]{1,0:T(8,128)} %constant.60.clone.2.tws_ref, f32[256,256]{1,0:T(8,128)} %constant.61.clone.2.fwd_ref, ...), custom_call_target="tpu_custom_call" | custom-call | tf_op jit(solution)/shard_map/cond/branch_1_fun/pallas_call | solution.py:97
  66.7 0.5 copy-done.4
  67.2 0.7 %slice-done = f32[3,8,1]{2,1,0:T(8,128)S(1)} async-done(((f32[3,8,1152]{2,1,0:T(8,128)}), f32[3,8,1]{2,1,0:T(8,128)S(1)}, s32[]{:S(2)}) %slice-start) | async-done | bytes 120 | tf_op jit(solution)/shard_map/jit(_roll_static)/slice | solution.py:175
  67.9 0.8 %fusion.54 = (f32[3,8,1152]{2,1,0:T(8,128)S(1)}, f32[8,3,1152]{2,0,1:T(8,128)}) fusion(f32[3,8,1151]{2,1,0:T(8,128)S(1)} %get-tuple-element.72, f32[3,8,1]{2,1,0:T(8,128)S(1)} %get-tuple-element.74, f32[3,8,1150]{2,1,0:T(8,128)S(1)} %get-tuple-element.68, f32[3,8,2]{2,1,0:T(8,128)S(1)} %get-tuple-element.70, f32[3,8,1]{2,1,0:T(8,128)S(1)} %get-tuple-element.73, ...), kind=kLoop, calls=%fused_computation.94 | loop fusion | flops 552960 | bytes 1437696 | tf_op jit(solution)/shard_map/mul | solution.py:177
  69.0 0.8 %fusion.40 = (f32[8,3,1152]{2,0,1:T(8,128)}, f32[8,3,1152]{2,0,1:T(8,128)}, f32[8,3,1152]{2,0,1:T(8,128)}, f32[8,3,1152]{2,0,1:T(8,128)}) fusion(f32[104,1152]{1,0:T(8,128)S(1)} %get-tuple-element.85, f32[4,8,1152]{2,1,0:T(8,128)S(1)} %fusion.28, f32[3]{0:T(128)S(1)} %compare_convert_fusion, f32[3,8,1151]{2,1,0:T(8,128)S(1)} %slice.254, ...), kind=kLoop, calls=%fused_computation.73 | loop fusion | flops 414720 | bytes 1658892 | tf_op jit(solution)/shard_map/transpose | solution.py:187
  (61 shorter events, 2.3 us)
Async XLA Ops:
  0.6 17.4 %copy-start = (s32[192]{0:T(256)S(1)}, s32[192]{0:T(256)}, u32[]{:S(2)}) copy-start(s32[192]{0:T(256)} %param.18) | copy-start | bytes 2308
  0.6 1.6 %copy-start.1 = (f32[8,3,1152]{2,0,1:T(8,128)S(1)}, f32[8,3,1152]{2,0,1:T(8,128)}, u32[]{:S(2)}) copy-start(f32[8,3,1152]{2,0,1:T(8,128)} %param.15) | copy-start | bytes 331780
  3.2 10.1 %collective-permute-start.1 = (f32[7,8,1152]{2,1,0:T(8,128)S(1)}, f32[7,8,1152]{2,1,0:T(8,128)S(1)}, u32[]{:S(2)}, u32[]{:S(2)}) collective-permute-start(f32[7,8,1152]{2,1,0:T(8,128)S(1)} %get-tuple-element.62), channel_id=1, source_target_pairs={{0,8},{8,16},{16,24},{24,32},{32,40},{40,48},{48,56},{56,64},{64,7... | collective-permute-start | bytes 774152 | tf_op jit(solution)/shard_map/ppermute | solution.py:130
  5.1 25.4 %collective-permute-start = (f32[7,8,1152]{2,1,0:T(8,128)S(1)}, f32[7,8,1152]{2,1,0:T(8,128)S(1)}, u32[]{:S(2)}, u32[]{:S(2)}) collective-permute-start(f32[7,8,1152]{2,1,0:T(8,128)S(1)} %get-tuple-element.63), channel_id=1, source_target_pairs={{8,0},{16,8},{24,16},{32,24},{40,32},{48,40},{56,48},{64,56},{72,6... | collective-permute-start | bytes 774152 | tf_op jit(solution)/shard_map/ppermute | solution.py:131
  11.1 0.9 %copy-start.2 = (f32[8,3,1152]{2,0,1:T(8,128)S(1)}, f32[8,3,1152]{2,0,1:T(8,128)}, u32[]{:S(2)}) copy-start(f32[8,3,1152]{2,0,1:T(8,128)} %param.16) | copy-start | bytes 331780
  12.1 0.9 %copy-start.5 = (f32[8,3,1152]{2,0,1:T(8,128)S(1)}, f32[8,3,1152]{2,0,1:T(8,128)}, u32[]{:S(2)}) copy-start(f32[8,3,1152]{2,0,1:T(8,128)} %param.13) | copy-start | bytes 331780
  13.3 6.1 %collective-permute-start.2 = (f32[4,1152]{1,0:T(4,128)S(1)}, f32[4,1152]{1,0:T(4,128)S(1)}, u32[]{:S(2)}, u32[]{:S(2)}) collective-permute-start(f32[4,1152]{1,0:T(4,128)S(1)} %get-tuple-element.65), channel_id=1, source_target_pairs={{0,1},{1,2},{2,3},{3,4},{4,5},{5,6},{6,7},{8,9},{9,10},{10,11},{11... | collective-permute-start | bytes 55304 | tf_op jit(solution)/shard_map/ppermute | solution.py:112
  19.4 6.5 %collective-permute-start.3 = (f32[4,1152]{1,0:T(4,128)S(1)}, f32[4,1152]{1,0:T(4,128)S(1)}, u32[]{:S(2)}, u32[]{:S(2)}) collective-permute-start(f32[4,1152]{1,0:T(4,128)S(1)} %add.138), channel_id=1, source_target_pairs={{0,2},{1,3},{2,4},{3,5},{4,6},{5,7},{8,10},{9,11},{10,12},{11,13},... | collective-permute-start | bytes 55304 | tf_op jit(solution)/shard_map/ppermute | solution.py:112
  26.0 6.0 %collective-permute-start.4 = (f32[4,1152]{1,0:T(4,128)S(1)}, f32[4,1152]{1,0:T(4,128)S(1)}, u32[]{:S(2)}, u32[]{:S(2)}) collective-permute-start(f32[4,1152]{1,0:T(4,128)S(1)} %add.139), channel_id=1, source_target_pairs={{0,4},{1,5},{2,6},{3,7},{8,12},{9,13},{10,14},{11,15},{16,20},{17,... | collective-permute-start | bytes 55304 | tf_op jit(solution)/shard_map/ppermute | solution.py:112
  30.5 0.7 %copy-start.6 = (f32[7,8,1152]{2,1,0:T(8,128)}, f32[7,8,1152]{2,1,0:T(8,128)S(1)}, u32[]{:S(2)}) copy-start(f32[7,8,1152]{2,1,0:T(8,128)S(1)} %collective-permute-done) | copy-start | bytes 774148
  31.2 0.9 %copy-start.3 = (f32[8,3,1152]{2,0,1:T(8,128)S(1)}, f32[8,3,1152]{2,0,1:T(8,128)}, u32[]{:S(2)}) copy-start(f32[8,3,1152]{2,0,1:T(8,128)} %param.14) | copy-start | bytes 331780
  31.3 0.9 %slice-start.1 = ((f32[7,8,1152]{2,1,0:T(8,128)}), f32[1,8,1152]{2,1,0:T(8,128)S(1)}, s32[]{:S(2)}) async-start(f32[7,8,1152]{2,1,0:T(8,128)} %copy-done.6), calls=%async_computation.1 | async-start | bytes 73728 | tf_op jit(solution)/shard_map/slice | solution.py:141
  32.3 11.8 %collective-permute-start.5 = (f32[4,1152]{1,0:T(4,128)S(1)}, f32[4,1152]{1,0:T(4,128)S(1)}, u32[]{:S(2)}, u32[]{:S(2)}) collective-permute-start(f32[4,1152]{1,0:T(4,128)S(1)} %get-tuple-element.49), channel_id=1, source_target_pairs={{1,0},{2,1},{3,2},{4,3},{5,4},{6,5},{7,6},{9,8},{10,9},{11,10},{12... | collective-permute-start | bytes 55304 | tf_op jit(solution)/shard_map/ppermute | solution.py:112
  44.1 7.8 %collective-permute-start.6 = (f32[4,1152]{1,0:T(4,128)S(1)}, f32[4,1152]{1,0:T(4,128)S(1)}, u32[]{:S(2)}, u32[]{:S(2)}) collective-permute-start(f32[4,1152]{1,0:T(4,128)S(1)} %add.145), channel_id=1, source_target_pairs={{2,0},{3,1},{4,2},{5,3},{6,4},{7,5},{10,8},{11,9},{12,10},{13,11},... | collective-permute-start | bytes 55304 | tf_op jit(solution)/shard_map/ppermute | solution.py:112
  51.9 9.6 %collective-permute-start.7 = (f32[4,1152]{1,0:T(4,128)S(1)}, f32[4,1152]{1,0:T(4,128)S(1)}, u32[]{:S(2)}, u32[]{:S(2)}) collective-permute-start(f32[4,1152]{1,0:T(4,128)S(1)} %add.146), channel_id=1, source_target_pairs={{4,0},{5,1},{6,2},{7,3},{12,8},{13,9},{14,10},{15,11},{20,16},{21,... | collective-permute-start | bytes 55304 | tf_op jit(solution)/shard_map/ppermute | solution.py:112
  53.7 7.7 %copy-start.7 = (f32[3,1152]{1,0:T(4,128)S(1)}, f32[3,1152]{1,0:T(4,128)}, u32[]{:S(2)}) copy-start(f32[3,1152]{1,0:T(4,128)} %param.17) | copy-start | bytes 41476
  66.5 0.6 copy-start.4
  67.2 0.7 %slice-start = ((f32[3,8,1152]{2,1,0:T(8,128)}), f32[3,8,1]{2,1,0:T(8,128)S(1)}, s32[]{:S(2)}) async-start(f32[3,8,1152]{2,1,0:T(8,128)} %copy-done.4), calls=%async_computation | async-start | bytes 24576 | tf_op jit(solution)/shard_map/jit(_roll_static)/slice | solution.py:175

commit v9 on v6

--- a/solution.py
+++ b/solution.py
@@ -149,17 +149,20 @@
     below_depth = prefix_over(depth_sum, "lev", False)
     inclusive = jnp.flip(jnp.cumsum(jnp.flip(thickness, 1), axis=1), 1)
     height_ext = surface_ext + below_depth[:, None] + (inclusive - thickness) + 0.5 * thickness
-    fields = jnp.concatenate([wind_east, wind_north, flux_east, flux_north], axis=0)
-    fields, height_ext = lax.optimization_barrier((fields, height_ext))
-    cut_rows = jnp.concatenate([face_rows[:-1], face_rows[:-1], face_rows[:-1], face_rows])
-    row_cuts = jnp.broadcast_to(
-        filter_cutoff[jnp.minimum(cut_rows, nlat_all - 1)][:, None], fields.shape[:2]
+    early = jnp.concatenate([wind_east, wind_north, flux_east], axis=0)
+    early_cuts = jnp.broadcast_to(
+        filter_cutoff[jnp.minimum(face_rows[:-1], nlat_all - 1)][None, :, None],
+        (3, lat_rows, levels),
     ).reshape(-1)
-    smooth = filter_rows(fields.reshape(-1, length), row_cuts).reshape(fields.shape)
+    smooth = filter_rows(early.reshape(-1, length), early_cuts).reshape(early.shape)
+    flux_north, height_ext = lax.optimization_barrier((flux_north, height_ext))
+    late_cuts = jnp.broadcast_to(
+        filter_cutoff[jnp.minimum(face_rows, nlat_all - 1)][:, None], flux_north.shape[:2]
+    ).reshape(-1)
+    north_full = filter_rows(flux_north.reshape(-1, length), late_cuts).reshape(flux_north.shape)
     east_smooth = smooth[:rows]
     north_smooth = smooth[rows : 2 * rows]
     east_flux = smooth[2 * rows : 3 * rows]
-    north_full = smooth[3 * rows :]
     new_mass = layer_mass - TIME_STEP * (
         jnp.roll(east_flux, -1, -1) - east_flux + (north_full[1:] - north_full[:-1])
     )

time: 53 us -> 61.2 us (1.15)
  local copies, waits for them, and re-layouts: 7.99 us -> 12.4 us
  Pallas kernels: 4.26 us -> 6.29 us
  other arithmetic: 4.53 us -> 5.99 us
    pallas_call x1 -> x2, Pallas kernels: 4.26 us -> 6.29 us  [filter_rows(): pl.pallas_call(filter_kernel, out_shape=jax.ShapeDtypeStruct(values.shape...]
    unnamed x14 -> x20, local copies, waits for them, and re-layouts: 1.26 us -> 2.9 us
    mul x1, other arithmetic: 0.82 us -> 1.79 us  [local(): heat_east = east_flux * face_lon(theta_field)]
    concatenate x2 -> x0, other arithmetic: 0.81 us -> none  [the longest x1 0.81 us: local(): jnp.concatenate([wind_east, wind_north, flux_east, flux_north], axis=0)]
    reshape x0 -> x1, other arithmetic: none -> 0.75 us  [local(): early.reshape(-1, length)]
    slice x1 -> x2, local copies, waits for them, and re-layouts: 0.01 us -> 0.75 us  [local(): north_ext = jnp.concatenate([wind_north, from_north[2 * rows:]], axis=0)]
    slice x2 -> x3, local copies, waits for them, and re-layouts: 0.09 us -> 0.79 us  [local(): jnp.roll(east_flux, -1, -1) - east_flux + (north_full[1:] - north_full[:-1])]
    another operation x1 -> x2, local copies, waits for them, and re-layouts: 0.71 us -> 1.4 us  [filter_rows(): cuts.reshape(count, 1)]
  transfers between devices with their start and end apart: 4 -> 4, of which waited for: 2 -> 2; matrix products, arithmetic and copies ran while one was open for 9% -> 12% of each run, Pallas kernels for 0% -> 6%
where the time goes in v9:
time: 61.2 us; the launch traced here: 60.5 us
  starting transfers between devices  19.4 us (32%)
  waiting for transfers between devices  15.4 us (25%)
  local copies, waits for them, and re-layouts  12.4 us (20%)
  Pallas kernels  6.29 us (10%)
  other arithmetic  5.99 us (10%)
  between operations  1 us (2%)
    all_to_all x2, waiting for transfers between devices, prefix_over(): lax.all_to_all(copies, axis, split_axis=0, concat_axis=0, tiled=True)  15.4 us
    all_to_all x2, starting transfers between devices, prefix_over(): lax.all_to_all(copies, axis, split_axis=0, concat_axis=0, tiled=True)  10.5 us
    ppermute x1, starting transfers between devices, local(): lax.ppermute(to_south, 'lat', [(i + 1, i) for i in range(count - 1)])  6.96 us
    pallas_call x2, Pallas kernels, filter_rows(): pl.pallas_call(filter_kernel, out_shape=jax.ShapeDtypeStruct(values.shape...  6.29 us
    unnamed x20, local copies, waits for them, and re-layouts  2.9 us
    ppermute x1, starting transfers between devices, local(): lax.ppermute(to_north, 'lat', [(i, i + 1) for i in range(count - 1)])  1.92 us
    mul x1, other arithmetic, local(): heat_east = east_flux * face_lon(theta_field)  1.79 us
    another operation x2, local copies, waits for them, and re-layouts, filter_rows(): cuts.reshape(count, 1)  1.4 us
  transfers between devices with their start and end apart: 4, of which 2 were waited for; matrix products, arithmetic and copies ran while one was open for 12% of the time, Pallas kernels for 6%

profile of v9, /device:TPU:256, one launch (start us, length us, event | category | flops | bytes accessed | tf_op | source)
XLA Modules:
  0.0 60.5 jit_solution(2577106143144292459)
XLA Ops:
  0.7 0.8 %slice.291 = f32[1,8,1152]{2,1,0:T(8,128)S(1)} slice(f32[3,8,1152]{2,1,0:T(8,128)} %bitcast.77), slice={[0:1], [0:8], [0:1152]} | slice | bytes 73728 | tf_op jit(solution)/shard_map/slice | solution.py:124
  1.5 0.7 %slice_reduce_fusion = f32[1152]{0:T(1024)S(1)} fusion(f32[3,1152]{1,0:T(4,128)} %param.20), kind=kLoop, calls=%fused_computation.103 | loop fusion | bytes 9216 | tf_op jit(solution)/shard_map/slice | solution.py:123
  2.2 0.9 %pad_maximum_fusion.2 = (f32[7,8,1152]{2,1,0:T(8,128)S(1)}, f32[7,8,1152]{2,1,0:T(8,128)S(1)}) fusion(f32[1,8,1152]{2,1,0:T(8,128)S(1)} %broadcast_in_dim.56, f32[3,8,1152]{2,1,0:T(8,128)} %bitcast.68, f32[3,8,1152]{2,1,0:T(8,128)S(1)} %bitcast.59, f32[1,8,1152]{2,1,0:T(8,128)S(1)} %slice.291), kind=kLoop, calls=%fused_computation.21 | loop fusion | flops 193536 | bytes 811008 | tf_op jit(solution)/shard_map/concatenate | solution.py:123
  3.2 1.9 %collective-permute-start.1 = (f32[7,8,1152]{2,1,0:T(8,128)S(1)}, f32[7,8,1152]{2,1,0:T(8,128)S(1)}, u32[]{:S(2)}, u32[]{:S(2)}) collective-permute-start(f32[7,8,1152]{2,1,0:T(8,128)S(1)} %get-tuple-element.22), channel_id=1, source_target_pairs={{0,8},{8,16},{16,24},{24,32},{32,40},{40,48},{48,56},{56,64},{64,7... | collective-permute-start | bytes 774152 | tf_op jit(solution)/shard_map/ppermute | solution.py:126
  5.1 7.0 %collective-permute-start = (f32[7,8,1152]{2,1,0:T(8,128)S(1)}, f32[7,8,1152]{2,1,0:T(8,128)S(1)}, u32[]{:S(2)}, u32[]{:S(2)}) collective-permute-start(f32[7,8,1152]{2,1,0:T(8,128)S(1)} %get-tuple-element.23), channel_id=1, source_target_pairs={{8,0},{16,8},{24,16},{32,24},{40,32},{48,40},{56,48},{64,56},{72,6... | collective-permute-start | bytes 774152 | tf_op jit(solution)/shard_map/ppermute | solution.py:127
  12.6 0.7 %copy-done.2 = f32[8,3,1152]{2,0,1:T(8,128)S(1)} copy-done((f32[8,3,1152]{2,0,1:T(8,128)S(1)}, f32[8,3,1152]{2,0,1:T(8,128)}, u32[]{:S(2)}) %copy-start.2) | copy-done | bytes 110616
  13.5 0.6 %gather_fusion = s32[3]{0:T(128)S(1)} fusion(s32[192]{0:T(256)S(1)} %copy-done, s32[1024]{0:T(1024)S(1)} %pad_clamp_fusion.1), kind=kCustom, calls=%fused_computation | custom fusion | bytes 36 | tf_op jit(solution)/shard_map/gather | solution.py:154
  14.2 0.7 %reshape_reshape.8.cut_ref = s32[72,1]{1,0:T(8,128)} reshape(s32[3,3,8]{2,1,0:T(4,128)S(1)} %broadcast_in_dim.55) | data formatting | bytes 576 | tf_op jit(solution)/shard_map/reshape;reshape | solution.py:100
  14.9 0.2 fusion.47
  15.1 0.7 %copy-done.5 = f32[8,3,1152]{2,0,1:T(8,128)S(1)} copy-done((f32[8,3,1152]{2,0,1:T(8,128)S(1)}, f32[8,3,1152]{2,0,1:T(8,128)}, u32[]{:S(2)}) %copy-start.5) | copy-done | bytes 110616
  15.8 0.8 %maximum_bitcast_fusion.x_ref = f32[72,1152]{1,0:T(8,128)} fusion(f32[3,8,1152]{2,1,0:T(8,128)S(1)} %fusion.47, f32[3,8,1152]{2,1,0:T(8,128)S(1)} %bitcast.78, f32[3,8,1152]{2,1,0:T(8,128)S(1)} %bitcast.81), kind=kLoop, calls=%fused_computation.2 | loop fusion | flops 165888 | bytes 663552 | tf_op jit(solution)/shard_map/reshape | solution.py:157
  16.6 3.5 %shard_map.191 = f32[72,1152]{1,0:T(8,128)} custom-call(f32[72,1152]{1,0:T(8,128)} %maximum_bitcast_fusion.x_ref, s32[72,1]{1,0:T(8,128)} %reshape_reshape.8.cut_ref, f32[9,128]{1,0:T(8,128)} %constant.60.clone.twc_ref, f32[9,128]{1,0:T(8,128)} %constant.61.clone.tws_ref, f32[256,256]{1,0:T(8,128)} %constant.62.clone.fwd_ref, ...), custom_call_target="tpu_custom_call" | custom-call | tf_op jit(solution)/shard_map/pallas_call | solution.py:97
  20.1 0.9 %slice_bitcast_fusion = f32[3,8,1152]{2,1,0:T(8,128)S(1)} fusion(f32[72,1152]{1,0:T(8,128)} %shard_map.191), kind=kLoop, calls=%fused_computation.71 | loop fusion | bytes 221184 | tf_op jit(solution)/shard_map/slice | solution.py:165
  21.2 0.7 %broadcast_in_dim.60 = f32[8,4,1152]{2,1,0:T(4,128)} broadcast(f32[4,1152]{1,0:T(4,128)S(1)} %get-tuple-element.25), dimensions={1,2} | broadcast | bytes 165888 | tf_op jit(solution)/shard_map/broadcast_in_dim | solution.py:106
  21.9 7.1 %all-to-all-start = ((f32[8,4,1152]{2,1,0:T(4,128)}), f32[8,4,1152]{2,1,0:T(4,128)S(1)}, u32[]{:S(2)}, u32[]{:S(2)}) async-start(f32[8,4,1152]{2,1,0:T(4,128)} %broadcast_in_dim.60), calls=%async_computation | async-start | bytes 294912 | tf_op jit(solution)/shard_map/all_to_all | solution.py:107
  29.2 0.7 %copy-done.8 = f32[7,8,1152]{2,1,0:T(8,128)} copy-done((f32[7,8,1152]{2,1,0:T(8,128)}, f32[7,8,1152]{2,1,0:T(8,128)S(1)}, u32[]{:S(2)}) %copy-start.8) | copy-done | bytes 258072
  29.8 8.4 %all-to-all-done = f32[8,4,1152]{2,1,0:T(4,128)S(1)} async-done(((f32[8,4,1152]{2,1,0:T(4,128)}), f32[8,4,1152]{2,1,0:T(4,128)S(1)}, u32[]{:S(2)}, u32[]{:S(2)}) %all-to-all-start) | async-done | bytes 147488 | tf_op jit(solution)/shard_map/all_to_all | solution.py:107
  38.3 0.7 %slice-done.1 = f32[1,8,1152]{2,1,0:T(8,128)S(1)} async-done(((f32[7,8,1152]{2,1,0:T(8,128)}), f32[1,8,1152]{2,1,0:T(8,128)S(1)}, s32[]{:S(2)}) %slice-start.1) | async-done | bytes 36888 | tf_op jit(solution)/shard_map/slice | solution.py:137
  39.1 0.8 %fusion.58 = (f32[4,1152]{1,0:T(4,128)S(1)}, f32[4,8,1152]{2,1,0:T(8,128)S(1)}, f32[4,8,1152]{2,1,0:T(8,128)}) fusion(f32[3,8,1152]{2,1,0:T(8,128)S(1)} %bitcast.67, f32[1,8,1152]{2,1,0:T(8,128)S(1)} %get-tuple-element.20, f32[4,8,1152]{2,1,0:T(8,128)S(1)} %reduce_window_sum.17, f32[4,1152]{1,0:T(4,128)S(1)} %broadcast_add_fusion, ...), kind=kLoop, calls=%fused_computation.115 | loop fusion | flops 880128 | bytes 1142800 | tf_op jit(solution)/shard_map/reduce_sum | solution.py:148
  39.9 0.7 %broadcast_in_dim.62 = f32[8,4,1152]{2,1,0:T(4,128)} broadcast(f32[4,1152]{1,0:T(4,128)S(1)} %get-tuple-element.9), dimensions={1,2} | broadcast | bytes 165888 | tf_op jit(solution)/shard_map/broadcast_in_dim | solution.py:106
  40.5 3.4 %all-to-all-start.1 = ((f32[8,4,1152]{2,1,0:T(4,128)}), f32[8,4,1152]{2,1,0:T(4,128)S(1)}, u32[]{:S(2)}, u32[]{:S(2)}) async-start(f32[8,4,1152]{2,1,0:T(4,128)} %broadcast_in_dim.62), calls=%async_computation.1 | async-start | bytes 294912 | tf_op jit(solution)/shard_map/all_to_all | solution.py:107
  44.1 0.6 %gather_fusion.1 = s32[4]{0:T(128)S(1)} fusion(s32[192]{0:T(256)S(1)} %copy-done, s32[1024]{0:T(1024)S(1)} %pad_clamp_fusion), kind=kCustom, calls=%fused_computation.1 | custom fusion | bytes 48 | tf_op jit(solution)/shard_map/gather | solution.py:160
  44.8 0.7 %reshape_reshape.9.cut_ref = s32[32,1]{1,0:T(8,128)} reshape(s32[4,8]{1,0:T(4,128)S(1)} %broadcast_in_dim.63) | data formatting | bytes 256 | tf_op jit(solution)/shard_map/reshape;reshape | solution.py:100
  45.6 0.1 rev.7
  45.7 0.1 reduce_window_sum.18
  45.9 0.2 rev.8
  46.1 7.0 %all-to-all-done.1 = f32[8,4,1152]{2,1,0:T(4,128)S(1)} async-done(((f32[8,4,1152]{2,1,0:T(4,128)}), f32[8,4,1152]{2,1,0:T(4,128)S(1)}, u32[]{:S(2)}, u32[]{:S(2)}) %all-to-all-start.1) | async-done | bytes 147488 | tf_op jit(solution)/shard_map/all_to_all | solution.py:107
  53.3 2.8 %shard_map.192 = f32[32,1152]{1,0:T(8,128)} custom-call(f32[32,1152]{1,0:T(8,128)} %bitcast.80, s32[32,1]{1,0:T(8,128)} %reshape_reshape.9.cut_ref, f32[9,128]{1,0:T(8,128)} %constant.60.clone.twc_ref, f32[9,128]{1,0:T(8,128)} %constant.61.clone.tws_ref, f32[256,256]{1,0:T(8,128)} %constant.62.clone.fwd_ref, f32[256,256]{1,0:T(8,128)} %constant.63.clone.inv_ref, ...), custom_call_target="tpu_custom_call" | custom-call | tf_op jit(solution)/shard_map/pallas_call | solution.py:97
  56.0 0.7 %slice-done = f32[3,8,1]{2,1,0:T(8,128)S(1)} async-done(((f32[3,8,1152]{2,1,0:T(8,128)}), f32[3,8,1]{2,1,0:T(8,128)S(1)}, s32[]{:S(2)}) %slice-start) | async-done | bytes 120 | tf_op jit(solution)/shard_map/jit(_roll_static)/slice | solution.py:167
  56.8 1.8 %fusion.54 = (f32[3,8,1152]{2,1,0:T(8,128)S(1)}, f32[8,3,1152]{2,0,1:T(8,128)}) fusion(f32[3,8,1151]{2,1,0:T(8,128)S(1)} %get-tuple-element.32, f32[3,8,1]{2,1,0:T(8,128)S(1)} %get-tuple-element.34, f32[3,8,1150]{2,1,0:T(8,128)S(1)} %get-tuple-element.28, f32[3,8,2]{2,1,0:T(8,128)S(1)} %get-tuple-element.30, f32[3,8,1]{2,1,0:T(8,128)S(1)} %get-tuple-element.33, ...), kind=kLoop, calls=%fused_computation.96 | loop fusion | flops 552960 | bytes 1437696 | tf_op jit(solution)/shard_map/mul | solution.py:169
  58.7 0.8 %copy-done.4 = f32[32,1152]{1,0:T(8,128)S(1)} copy-done((f32[32,1152]{1,0:T(8,128)S(1)}, f32[32,1152]{1,0:T(8,128)}, u32[]{:S(2)}) %copy-start.4) | copy-done | bytes 147480
  59.6 0.8 %fusion.40 = (f32[8,3,1152]{2,0,1:T(8,128)}, f32[8,3,1152]{2,0,1:T(8,128)}, f32[8,3,1152]{2,0,1:T(8,128)}, f32[8,3,1152]{2,0,1:T(8,128)}) fusion(f32[72,1152]{1,0:T(8,128)S(1)} %copy-done.3, f32[4,8,1152]{2,1,0:T(8,128)S(1)} %fusion.28, f32[3]{0:T(128)S(1)} %compare_convert_fusion, f32[3,8,1151]{2,1,0:T(8,128)S(1)} %slice.244, f32[3,8,1]{2,1,0:T(8,128)S(1)} %slice.243, ...), kind=kLoop, calls=%fused_computation.75 | loop fusion | flops 414720 | bytes 1658892 | tf_op jit(solution)/shard_map/transpose | solution.py:179
  (58 shorter events, 1.9 us)
Async XLA Ops:
  0.6 12.8 %copy-start = (s32[192]{0:T(256)S(1)}, s32[192]{0:T(256)}, u32[]{:S(2)}) copy-start(s32[192]{0:T(256)} %param.21) | copy-start | bytes 2308
  0.6 1.6 %copy-start.1 = (f32[8,3,1152]{2,0,1:T(8,128)S(1)}, f32[8,3,1152]{2,0,1:T(8,128)}, u32[]{:S(2)}) copy-start(f32[8,3,1152]{2,0,1:T(8,128)} %param.18) | copy-start | bytes 331780
  3.2 17.9 %collective-permute-start.1 = (f32[7,8,1152]{2,1,0:T(8,128)S(1)}, f32[7,8,1152]{2,1,0:T(8,128)S(1)}, u32[]{:S(2)}, u32[]{:S(2)}) collective-permute-start(f32[7,8,1152]{2,1,0:T(8,128)S(1)} %get-tuple-element.22), channel_id=1, source_target_pairs={{0,8},{8,16},{16,24},{24,32},{32,40},{40,48},{48,56},{56,64},{64,7... | collective-permute-start | bytes 774152 | tf_op jit(solution)/shard_map/ppermute | solution.py:126
  5.1 24.0 %collective-permute-start = (f32[7,8,1152]{2,1,0:T(8,128)S(1)}, f32[7,8,1152]{2,1,0:T(8,128)S(1)}, u32[]{:S(2)}, u32[]{:S(2)}) collective-permute-start(f32[7,8,1152]{2,1,0:T(8,128)S(1)} %get-tuple-element.23), channel_id=1, source_target_pairs={{8,0},{16,8},{24,16},{32,24},{40,32},{48,40},{56,48},{64,56},{72,6... | collective-permute-start | bytes 774152 | tf_op jit(solution)/shard_map/ppermute | solution.py:127
  12.3 0.9 %copy-start.2 = (f32[8,3,1152]{2,0,1:T(8,128)S(1)}, f32[8,3,1152]{2,0,1:T(8,128)}, u32[]{:S(2)}) copy-start(f32[8,3,1152]{2,0,1:T(8,128)} %param.19) | copy-start | bytes 331780
  13.5 1.4 %copy-start.7 = (f32[8,3,1152]{2,0,1:T(8,128)S(1)}, f32[8,3,1152]{2,0,1:T(8,128)}, u32[]{:S(2)}) copy-start(f32[8,3,1152]{2,0,1:T(8,128)} %param.16) | copy-start | bytes 331780
  14.9 0.9 %copy-start.5 = (f32[8,3,1152]{2,0,1:T(8,128)S(1)}, f32[8,3,1152]{2,0,1:T(8,128)}, u32[]{:S(2)}) copy-start(f32[8,3,1152]{2,0,1:T(8,128)} %param.17) | copy-start | bytes 331780
  21.0 23.0 %copy-start.6 = (f32[3,8,1152]{2,1,0:T(8,128)}, f32[3,8,1152]{2,1,0:T(8,128)S(1)}, u32[]{:S(2)}) copy-start(f32[3,8,1152]{2,1,0:T(8,128)S(1)} %slice_bitcast_fusion) | copy-start | bytes 331780
  21.9 16.4 %all-to-all-start = ((f32[8,4,1152]{2,1,0:T(4,128)}), f32[8,4,1152]{2,1,0:T(4,128)S(1)}, u32[]{:S(2)}, u32[]{:S(2)}) async-start(f32[8,4,1152]{2,1,0:T(4,128)} %broadcast_in_dim.60), calls=%async_computation | async-start | bytes 294912 | tf_op jit(solution)/shard_map/all_to_all | solution.py:107
  29.1 0.7 %copy-start.8 = (f32[7,8,1152]{2,1,0:T(8,128)}, f32[7,8,1152]{2,1,0:T(8,128)S(1)}, u32[]{:S(2)}) copy-start(f32[7,8,1152]{2,1,0:T(8,128)S(1)} %collective-permute-done) | copy-start | bytes 774148
  38.3 0.8 %slice-start.1 = ((f32[7,8,1152]{2,1,0:T(8,128)}), f32[1,8,1152]{2,1,0:T(8,128)S(1)}, s32[]{:S(2)}) async-start(f32[7,8,1152]{2,1,0:T(8,128)} %copy-done.8), calls=%async_computation.3 | async-start | bytes 73728 | tf_op jit(solution)/shard_map/slice | solution.py:137
  40.5 12.6 %all-to-all-start.1 = ((f32[8,4,1152]{2,1,0:T(4,128)}), f32[8,4,1152]{2,1,0:T(4,128)S(1)}, u32[]{:S(2)}, u32[]{:S(2)}) async-start(f32[8,4,1152]{2,1,0:T(4,128)} %broadcast_in_dim.62), calls=%async_computation.1 | async-start | bytes 294912 | tf_op jit(solution)/shard_map/all_to_all | solution.py:107
  46.1 7.1 %copy-start.9 = (f32[3,1152]{1,0:T(4,128)S(1)}, f32[3,1152]{1,0:T(4,128)}, u32[]{:S(2)}) copy-start(f32[3,1152]{1,0:T(4,128)} %param.20) | copy-start | bytes 41476
  53.3 2.8 %copy-start.3 = (f32[72,1152]{1,0:T(8,128)S(1)}, f32[72,1152]{1,0:T(8,128)}, u32[]{:S(2)}) copy-start(f32[72,1152]{1,0:T(8,128)} %shard_map.191) | copy-start | bytes 995332
  56.0 0.7 %slice-start = ((f32[3,8,1152]{2,1,0:T(8,128)}), f32[3,8,1]{2,1,0:T(8,128)S(1)}, s32[]{:S(2)}) async-start(f32[3,8,1152]{2,1,0:T(8,128)} %copy-done.6), calls=%async_computation.2 | async-start | bytes 24576 | tf_op jit(solution)/shard_map/jit(_roll_static)/slice | solution.py:167
  58.6 0.9 %copy-start.4 = (f32[32,1152]{1,0:T(8,128)S(1)}, f32[32,1152]{1,0:T(8,128)}, u32[]{:S(2)}) copy-start(f32[32,1152]{1,0:T(8,128)} %shard_map.192) | copy-start | bytes 442372

commit v10 on v6

--- a/solution.py
+++ b/solution.py
@@ -3,6 +3,7 @@
 import jax.numpy as jnp
 from jax import lax
 from jax.experimental import pallas as pl
+from jax.experimental.pallas import tpu as pltpu
 from jax.sharding import PartitionSpec as P
 
 TIME_STEP = 0.25
@@ -47,7 +48,11 @@
     return (np.cos(small_phase), np.sin(small_phase), np.cos(twist).astype(np.float32),
             np.sin(twist).astype(np.float32), forward, inverse, folded)
 
-def filter_kernel(x_ref, cut_ref, twc_ref, tws_ref, fwd_ref, inv_ref, fold_ref, o_ref):
+def filter_kernel(
+    x_ref, cut_ref, twc_ref, tws_ref, fwd_ref, inv_ref, fold_ref,
+    mass_ref, theta_ref, lon_ref, lat_ref, height_ref, inside_ref,
+    east_ref, north_ref, new_mass_ref, new_heat_ref, out_height_ref, y_ref,
+):
     rows, lanes = FACTOR_ROWS, FACTOR_LANES
     count, length = x_ref.shape
     c9, s9 = fft_tables(length)[:2]
@@ -85,20 +90,50 @@
         real_d.append(real_c * twc - imag_c * tws)
         imag_d.append(imag_c * twc + real_c * tws)
     for n in range(rows):
-        o_ref[:, n * lanes : (n + 1) * lanes] = float(1.0 / length) * real_d[0] + sum(
+        y_ref[:, n * lanes : (n + 1) * lanes] = float(1.0 / length) * real_d[0] + sum(
             float(2.0 * c9[k, n] / length) * real_d[k] - float(2.0 * s9[k, n] / length) * imag_d[k]
             for k in range(1, half)
         )
-
-
-def filter_rows(values, cuts):
+    block, _ = mass_ref.shape
+    step = count - 4 * block
+    east_smooth = y_ref[0:block, :]
+    north_smooth = y_ref[block : 2 * block, :]
+    east_flux = y_ref[2 * block : 3 * block, :]
+    north_low = y_ref[3 * block : 4 * block, :]
+    north_high = y_ref[3 * block + step : count, :]
+    mass = mass_ref[...]
+    theta = theta_ref[...]
+    new_mass_ref[...] = mass - TIME_STEP * (
+        pltpu.roll(east_flux, length - 1, 1) - east_flux + (north_high - north_low)
+    )
+    heat_east = east_flux * lon_ref[...]
+    heat_low = north_low * lat_ref[0:block, :]
+    heat_high = north_high * lat_ref[step : step + block, :]
+    new_heat_ref[...] = theta * mass - TIME_STEP * (
+        pltpu.roll(heat_east, length - 1, 1) - heat_east + (heat_high - heat_low)
+    )
+    height = height_ref[step : step + block, :]
+    south = height_ref[0:block, :]
+    out_height_ref[...] = height
+    east_ref[...] = east_smooth - TIME_STEP * (height - pltpu.roll(height, 1, 1))
+    north_ref[...] = (north_smooth - TIME_STEP * (height - south)) * inside_ref[...]
+
+
+def filter_rows(values, cuts, mass, theta, lon_theta, lat_theta, height_ext, inside):
     count, length = values.shape
     _, _, twc, tws, forward, inverse, folded = fft_tables(length)
+    block = mass.shape[0]
+    piece = jax.ShapeDtypeStruct((block, length), values.dtype)
     return pl.pallas_call(
         filter_kernel,
-        out_shape=jax.ShapeDtypeStruct(values.shape, values.dtype),
-    )(values, cuts.reshape(count, 1), jnp.asarray(twc), jnp.asarray(tws), jnp.asarray(forward),
-      jnp.asarray(inverse), jnp.asarray(folded))
+        out_shape=(piece, piece, piece, piece, piece),
+        scratch_shapes=[pltpu.VMEM((count, length), jnp.float32)],
+    )(
+        values, cuts.reshape(count, 1), jnp.asarray(twc), jnp.asarray(tws),
+        jnp.asarray(forward), jnp.asarray(inverse), jnp.asarray(folded),
+        mass, theta, lon_theta, lat_theta, height_ext, inside,
+    )
+
 
 def prefix_over(value, axis, before):
     count = lax.axis_size(axis)
@@ -150,28 +185,21 @@
     inclusive = jnp.flip(jnp.cumsum(jnp.flip(thickness, 1), axis=1), 1)
     height_ext = surface_ext + below_depth[:, None] + (inclusive - thickness) + 0.5 * thickness
     fields = jnp.concatenate([wind_east, wind_north, flux_east, flux_north], axis=0)
-    fields, height_ext = lax.optimization_barrier((fields, height_ext))
     cut_rows = jnp.concatenate([face_rows[:-1], face_rows[:-1], face_rows[:-1], face_rows])
     row_cuts = jnp.broadcast_to(
         filter_cutoff[jnp.minimum(cut_rows, nlat_all - 1)][:, None], fields.shape[:2]
     ).reshape(-1)
-    smooth = filter_rows(fields.reshape(-1, length), row_cuts).reshape(fields.shape)
-    east_smooth = smooth[:rows]
-    north_smooth = smooth[rows : 2 * rows]
-    east_flux = smooth[2 * rows : 3 * rows]
-    north_full = smooth[3 * rows :]
-    new_mass = layer_mass - TIME_STEP * (
-        jnp.roll(east_flux, -1, -1) - east_flux + (north_full[1:] - north_full[:-1])
-    )
-    heat_east = east_flux * face_lon(theta_field)
-    heat_north = north_full * theta_faces
-    new_heat = theta_field * layer_mass - TIME_STEP * (
-        jnp.roll(heat_east, -1, -1) - heat_east + (heat_north[1:] - heat_north[:-1])
-    )
-    height = height_ext[1:]
-    new_east = east_smooth - TIME_STEP * (height - jnp.roll(height, 1, -1))
-    inside = (face_rows[:-1] > 0).astype(jnp.float32)[:, None, None]
-    new_north = (north_smooth - TIME_STEP * (height - height_ext[:-1])) * inside
+    inside = jnp.broadcast_to(
+        (face_rows[:-1] > 0).astype(jnp.float32)[:, None, None], (lat_rows, levels, 1)
+    )
+    flat = lambda v: v.reshape(-1, v.shape[-1])
+    results = filter_rows(
+        flat(fields), row_cuts, flat(layer_mass), flat(theta_field),
+        flat(face_lon(theta_field)), flat(theta_faces), flat(height_ext), flat(inside),
+    )
+    new_east, new_north, new_mass, new_heat, height = (
+        v.reshape(lat_rows, levels, length) for v in results
+    )
     outputs = (new_east, new_north, new_mass, new_heat, height)
     return tuple(jnp.transpose(v, (1, 0, 2)) for v in outputs)
 

time: 53 us -> 55.4 us (1.045)
  the two profiles are of different devices: /device:TPU:256 before, /device:TPU:199 now
where the time goes in v10:
time: 55.4 us; the launch traced here: 54.9 us
  waiting for transfers between devices  19.3 us (35%)
  starting transfers between devices  17.8 us (32%)
  local copies, waits for them, and re-layouts  7.26 us (13%)
  other arithmetic  4.99 us (9%)
  Pallas kernels  4.57 us (8%)
  between operations  0.88 us (2%)
    all_to_all x2, waiting for transfers between devices, prefix_over(): lax.all_to_all(copies, axis, split_axis=0, concat_axis=0, tiled=True)  12.5 us
    all_to_all x2, starting transfers between devices, prefix_over(): lax.all_to_all(copies, axis, split_axis=0, concat_axis=0, tiled=True)  10.2 us
    ppermute x1, waiting for transfers between devices, local(): lax.ppermute(to_south, 'lat', [(i + 1, i) for i in range(count - 1)])  6.89 us
    ppermute x1, starting transfers between devices, local(): lax.ppermute(to_north, 'lat', [(i, i + 1) for i in range(count - 1)])  5.69 us
    pallas_call x1, Pallas kernels, filter_rows(): pl.pallas_call(filter_kernel, out_shape=(piece, piece, piece, piece, piec...  4.57 us
    reshape x3, other arithmetic, local(): flat = lambda v: v.reshape(-1, v.shape[-1])  2.32 us
    ppermute x1, starting transfers between devices, local(): lax.ppermute(to_south, 'lat', [(i + 1, i) for i in range(count - 1)])  1.92 us
    broadcast_in_dim x2, local copies, waits for them, and re-layouts, prefix_over(): copies = jnp.broadcast_to(value, (count, *value.shape))  1.36 us
  transfers between devices with their start and end apart: 4, of which 3 were waited for; matrix products, arithmetic and copies ran while one was open for 10% of the time, Pallas kernels for 0%

profile of v10, /device:TPU:199, one launch (start us, length us, event | category | flops | bytes accessed | tf_op | source)
XLA Modules:
  0.0 54.9 jit_solution(896535016192715901)
XLA Ops:
  0.7 0.8 %slice_reduce_fusion = f32[1152]{0:T(1024)S(1)} fusion(f32[3,1152]{1,0:T(4,128)} %param.15), kind=kLoop, calls=%fused_computation.79 | loop fusion | bytes 9216 | tf_op jit(solution)/shard_map/slice | solution.py:158
  1.4 0.8 %slice.214 = f32[1,8,1152]{2,1,0:T(8,128)S(1)} slice(f32[3,8,1152]{2,1,0:T(8,128)} %bitcast.61), slice={[0:1], [0:8], [0:1152]} | slice | bytes 73728 | tf_op jit(solution)/shard_map/slice | solution.py:159
  2.2 1.0 %pad_maximum_fusion.2 = (f32[7,8,1152]{2,1,0:T(8,128)S(1)}, f32[7,8,1152]{2,1,0:T(8,128)S(1)}) fusion(f32[1,8,1152]{2,1,0:T(8,128)S(1)} %broadcast_in_dim.52, f32[3,8,1152]{2,1,0:T(8,128)} %bitcast.52, f32[3,8,1152]{2,1,0:T(8,128)S(1)} %bitcast.43, f32[1,8,1152]{2,1,0:T(8,128)S(1)} %slice.214), kind=kLoop, calls=%fused_computation.20 | loop fusion | flops 193536 | bytes 811008 | tf_op jit(solution)/shard_map/concatenate | solution.py:158
  3.2 5.7 %collective-permute-start.1 = (f32[7,8,1152]{2,1,0:T(8,128)S(1)}, f32[7,8,1152]{2,1,0:T(8,128)S(1)}, u32[]{:S(2)}, u32[]{:S(2)}) collective-permute-start(f32[7,8,1152]{2,1,0:T(8,128)S(1)} %get-tuple-element.24), channel_id=1, source_target_pairs={{0,8},{8,16},{16,24},{24,32},{32,40},{40,48},{48,56},{56,64},{64,7... | collective-permute-start | bytes 774152 | tf_op jit(solution)/shard_map/ppermute | solution.py:161
  8.9 1.9 %collective-permute-start = (f32[7,8,1152]{2,1,0:T(8,128)S(1)}, f32[7,8,1152]{2,1,0:T(8,128)S(1)}, u32[]{:S(2)}, u32[]{:S(2)}) collective-permute-start(f32[7,8,1152]{2,1,0:T(8,128)S(1)} %get-tuple-element.25), channel_id=1, source_target_pairs={{8,0},{16,8},{24,16},{32,24},{40,32},{48,40},{56,48},{64,56},{72,6... | collective-permute-start | bytes 774152 | tf_op jit(solution)/shard_map/ppermute | solution.py:162
  11.4 0.1 fusion.55
  11.5 0.1 fusion.53
  11.6 0.1 fusion.51
  11.8 0.8 %fusion.40.lon_ref = f32[24,1152]{1,0:T(8,128)} fusion(f32[3,8,1151]{2,1,0:T(8,128)S(1)} %get-tuple-element.35, f32[3,8,1]{2,1,0:T(8,128)S(1)} %get-tuple-element.37, f32[3,8,1150]{2,1,0:T(8,128)S(1)} %get-tuple-element.31, f32[3,8,2]{2,1,0:T(8,128)S(1)} %get-tuple-element.33, f32[3,8,1]{2,1,0:T(8,128)S(1)} %get-tuple-element.36, ...), kind=kLoop, calls=%fused_computation.74 | loop fusion | flops 359424 | bytes 774144 | tf_op jit(solution)/shard_map/reshape | solution.py:195
  12.7 0.2 fusion.34
  13.0 6.9 %collective-permute-done = f32[7,8,1152]{2,1,0:T(8,128)S(1)} collective-permute-done((f32[7,8,1152]{2,1,0:T(8,128)S(1)}, f32[7,8,1152]{2,1,0:T(8,128)S(1)}, u32[]{:S(2)}, u32[]{:S(2)}) %collective-permute-start) | collective-permute-done | bytes 258080 | tf_op jit(solution)/shard_map/ppermute | solution.py:162
  19.9 0.9 %copy-done.3 = f32[8,3,1152]{2,0,1:T(8,128)S(1)} copy-done((f32[8,3,1152]{2,0,1:T(8,128)S(1)}, f32[8,3,1152]{2,0,1:T(8,128)}, u32[]{:S(2)}) %copy-start.3) | copy-done | bytes 110616
  20.8 0.1 fusion.44
  20.9 0.7 %broadcast_in_dim.57 = f32[8,4,1152]{2,1,0:T(4,128)} broadcast(f32[4,1152]{1,0:T(4,128)S(1)} %get-tuple-element.26), dimensions={1,2} | broadcast | bytes 165888 | tf_op jit(solution)/shard_map/broadcast_in_dim | solution.py:141
  21.6 6.8 %all-to-all-start = ((f32[8,4,1152]{2,1,0:T(4,128)}), f32[8,4,1152]{2,1,0:T(4,128)S(1)}, u32[]{:S(2)}, u32[]{:S(2)}) async-start(f32[8,4,1152]{2,1,0:T(4,128)} %broadcast_in_dim.57), calls=%async_computation | async-start | bytes 294912 | tf_op jit(solution)/shard_map/all_to_all | solution.py:142
  28.4 0.1 reduce_window_sum.17
  28.6 7.9 %all-to-all-done = f32[8,4,1152]{2,1,0:T(4,128)S(1)} async-done(((f32[8,4,1152]{2,1,0:T(4,128)}), f32[8,4,1152]{2,1,0:T(4,128)S(1)}, u32[]{:S(2)}, u32[]{:S(2)}) %all-to-all-start) | async-done | bytes 147488 | tf_op jit(solution)/shard_map/all_to_all | solution.py:142
  36.5 0.1 select_reduce_fusion.1
  36.6 0.8 %fusion.45 = (f32[4,1152]{1,0:T(4,128)S(1)}, f32[4,8,1152]{2,1,0:T(8,128)S(1)}, f32[32,1152]{1,0:T(8,128)}) fusion(f32[3,8,1152]{2,1,0:T(8,128)S(1)} %bitcast.51, f32[1,8,1152]{2,1,0:T(8,128)S(1)} %get-tuple-element.18, f32[4,8,1152]{2,1,0:T(8,128)S(1)} %reduce_window_sum.17, f32[4,1152]{1,0:T(4,128)S(1)} %broadcast_add_fusion, ...), kind=kLoop, calls=%fused_computation.92 | loop fusion | flops 769536 | bytes 995328 | tf_op jit(solution)/shard_map/reduce_sum | solution.py:183
  37.4 0.7 %broadcast_in_dim.59 = f32[8,4,1152]{2,1,0:T(4,128)} broadcast(f32[4,1152]{1,0:T(4,128)S(1)} %get-tuple-element.15), dimensions={1,2} | broadcast | bytes 165888 | tf_op jit(solution)/shard_map/broadcast_in_dim | solution.py:141
  38.1 3.4 %all-to-all-start.1 = ((f32[8,4,1152]{2,1,0:T(4,128)}), f32[8,4,1152]{2,1,0:T(4,128)S(1)}, u32[]{:S(2)}, u32[]{:S(2)}) async-start(f32[8,4,1152]{2,1,0:T(4,128)} %broadcast_in_dim.59), calls=%async_computation.1 | async-start | bytes 294912 | tf_op jit(solution)/shard_map/all_to_all | solution.py:142
  41.5 0.7 %broadcast_in_dim.62.inside_ref = f32[24,1]{1,0:T(8,128)} reshape(f32[3,8]{1,0:T(4,128)S(1)} %broadcast_in_dim.60) | data formatting | bytes 192 | tf_op jit(solution)/shard_map/broadcast_in_dim | solution.py:192
  42.2 0.7 %gather_fusion = s32[13]{0:T(128)S(1)} fusion(s32[192]{0:T(256)S(1)} %copy-done, s32[1024]{0:T(1024)S(1)} %pad_clamp_fusion), kind=kCustom, calls=%fused_computation | custom fusion | bytes 156 | tf_op jit(solution)/shard_map/gather | solution.py:190
  43.0 0.7 %reshape_reshape.4.cut_ref = s32[104,1]{1,0:T(8,128)} reshape(s32[13,8]{1,0:T(8,128)S(1)} %broadcast_in_dim.53) | data formatting | bytes 832 | tf_op jit(solution)/shard_map/reshape;reshape | solution.py:132
  43.7 0.8 %maximum_bitcast_fusion.x_ref = f32[104,1152]{1,0:T(8,128)} fusion(f32[4,8,1152]{2,1,0:T(8,128)S(1)} %get-tuple-element.29, f32[3,8,1152]{2,1,0:T(8,128)S(1)} %fusion.34, f32[3,8,1152]{2,1,0:T(8,128)S(1)} %bitcast.63, f32[3,8,1152]{2,1,0:T(8,128)S(1)} %bitcast.64), kind=kLoop, calls=%fused_computation.1 | loop fusion | flops 359424 | bytes 958464 | tf_op jit(solution)/shard_map/reshape | solution.py:195
  44.5 0.1 rev.7
  44.6 0.1 reduce_window_sum.18
  44.7 0.2 rev.8
  44.9 4.5 %all-to-all-done.1 = f32[8,4,1152]{2,1,0:T(4,128)S(1)} async-done(((f32[8,4,1152]{2,1,0:T(4,128)}), f32[8,4,1152]{2,1,0:T(4,128)S(1)}, u32[]{:S(2)}, u32[]{:S(2)}) %all-to-all-start.1) | async-done | bytes 147488 | tf_op jit(solution)/shard_map/all_to_all | solution.py:142
  49.5 0.1 select_reduce_fusion
  49.6 0.7 %fusion.29.height_ref = f32[32,1152]{1,0:T(8,128)} fusion(f32[3,8,1152]{2,1,0:T(8,128)S(1)} %broadcast_in_dim.54, f32[1,8,1152]{2,1,0:T(8,128)S(1)} %get-tuple-element.19, f32[4,8,1152]{2,1,0:T(8,128)S(1)} %get-tuple-element.16, f32[4,8,1152]{2,1,0:T(8,128)S(1)} %rev.8, f32[4,1152]{1,0:T(4,128)S(1)} %select_reduce_fusion), kind=kLoop, calls=%fused_computation.55 | loop fusion | flops 221184 | bytes 608256 | tf_op jit(solution)/shard_map/reshape | solution.py:195
  50.3 4.6 %shard_map.146 = (f32[24,1152]{1,0:T(8,128)}, f32[24,1152]{1,0:T(8,128)}, f32[24,1152]{1,0:T(8,128)}, f32[24,1152]{1,0:T(8,128)}, f32[24,1152]{1,0:T(8,128)}) custom-call(f32[104,1152]{1,0:T(8,128)} %maximum_bitcast_fusion.x_ref, s32[104,1]{1,0:T(8,128)} %reshape_reshape.4.cut_ref, f32[9,128]{1,0:T(8,128)} %constant.56.clone.twc_ref, ...), custom_call_target="tpu_custom_call" | custom-call | tf_op jit(solution)/shard_map/pallas_call | solution.py:127
  (37 shorter events, 1.0 us)
Async XLA Ops:
  0.6 41.6 %copy-start = (s32[192]{0:T(256)S(1)}, s32[192]{0:T(256)}, u32[]{:S(2)}) copy-start(s32[192]{0:T(256)} %param.16) | copy-start | bytes 2308
  0.6 1.6 %copy-start.1 = (f32[8,3,1152]{2,0,1:T(8,128)S(1)}, f32[8,3,1152]{2,0,1:T(8,128)}, u32[]{:S(2)}) copy-start(f32[8,3,1152]{2,0,1:T(8,128)} %param.13) | copy-start | bytes 331780
  2.2 8.8 %copy-start.2 = (f32[8,3,1152]{2,0,1:T(8,128)S(1)}, f32[8,3,1152]{2,0,1:T(8,128)}, u32[]{:S(2)}) copy-start(f32[8,3,1152]{2,0,1:T(8,128)} %param.14) | copy-start | bytes 331780
  3.2 9.7 %collective-permute-start.1 = (f32[7,8,1152]{2,1,0:T(8,128)S(1)}, f32[7,8,1152]{2,1,0:T(8,128)S(1)}, u32[]{:S(2)}, u32[]{:S(2)}) collective-permute-start(f32[7,8,1152]{2,1,0:T(8,128)S(1)} %get-tuple-element.24), channel_id=1, source_target_pairs={{0,8},{8,16},{16,24},{24,32},{32,40},{40,48},{48,56},{56,64},{64,7... | collective-permute-start | bytes 774152 | tf_op jit(solution)/shard_map/ppermute | solution.py:161
  8.9 11.0 %collective-permute-start = (f32[7,8,1152]{2,1,0:T(8,128)S(1)}, f32[7,8,1152]{2,1,0:T(8,128)S(1)}, u32[]{:S(2)}, u32[]{:S(2)}) collective-permute-start(f32[7,8,1152]{2,1,0:T(8,128)S(1)} %get-tuple-element.25), channel_id=1, source_target_pairs={{8,0},{16,8},{24,16},{32,24},{40,32},{48,40},{56,48},{64,56},{72,6... | collective-permute-start | bytes 774152 | tf_op jit(solution)/shard_map/ppermute | solution.py:162
  11.8 0.9 %copy-start.4 = (f32[8,3,1152]{2,0,1:T(8,128)S(1)}, f32[8,3,1152]{2,0,1:T(8,128)}, u32[]{:S(2)}) copy-start(f32[8,3,1152]{2,0,1:T(8,128)} %param.11) | copy-start | bytes 331780
  19.9 0.9 %copy-start.3 = (f32[8,3,1152]{2,0,1:T(8,128)S(1)}, f32[8,3,1152]{2,0,1:T(8,128)}, u32[]{:S(2)}) copy-start(f32[8,3,1152]{2,0,1:T(8,128)} %param.12) | copy-start | bytes 331780
  21.6 14.9 %all-to-all-start = ((f32[8,4,1152]{2,1,0:T(4,128)}), f32[8,4,1152]{2,1,0:T(4,128)S(1)}, u32[]{:S(2)}, u32[]{:S(2)}) async-start(f32[8,4,1152]{2,1,0:T(4,128)} %broadcast_in_dim.57), calls=%async_computation | async-start | bytes 294912 | tf_op jit(solution)/shard_map/all_to_all | solution.py:142
  38.1 11.4 %all-to-all-start.1 = ((f32[8,4,1152]{2,1,0:T(4,128)}), f32[8,4,1152]{2,1,0:T(4,128)S(1)}, u32[]{:S(2)}, u32[]{:S(2)}) async-start(f32[8,4,1152]{2,1,0:T(4,128)} %broadcast_in_dim.59), calls=%async_computation.1 | async-start | bytes 294912 | tf_op jit(solution)/shard_map/all_to_all | solution.py:142
  44.9 4.6 %copy-start.5 = (f32[3,1152]{1,0:T(4,128)S(1)}, f32[3,1152]{1,0:T(4,128)}, u32[]{:S(2)}) copy-start(f32[3,1152]{1,0:T(4,128)} %param.15) | copy-start | bytes 41476

commit v11 on v6

--- a/solution.py
+++ b/solution.py
@@ -47,11 +47,23 @@
     return (np.cos(small_phase), np.sin(small_phase), np.cos(twist).astype(np.float32),
             np.sin(twist).astype(np.float32), forward, inverse, folded)
 
+def split_table(table):
+    high = jnp.asarray(table, jnp.float32).astype(jnp.bfloat16)
+    low = (jnp.asarray(table, jnp.float32) - high.astype(jnp.float32)).astype(jnp.bfloat16)
+    return jnp.stack([high, low])
+
+
+def split_dot(values, table_high, table_low):
+    high = values.astype(jnp.bfloat16)
+    low = (values - high.astype(jnp.float32)).astype(jnp.bfloat16)
+    product = lambda a, b: jnp.dot(a, b, preferred_element_type=jnp.float32)
+    return product(high, table_high) + (product(high, table_low) + product(low, table_high))
+
+
 def filter_kernel(x_ref, cut_ref, twc_ref, tws_ref, fwd_ref, inv_ref, fold_ref, o_ref):
     rows, lanes = FACTOR_ROWS, FACTOR_LANES
     count, length = x_ref.shape
     c9, s9 = fft_tables(length)[:2]
-    highest = lax.Precision.HIGHEST
     half = rows // 2 + 1
     parts = [x_ref[:, n * lanes : (n + 1) * lanes] for n in range(rows)]
     pieces = []
@@ -63,19 +75,12 @@
         pieces.append(
             jnp.concatenate([real_a * twc + imag_a * tws, imag_a * twc - real_a * tws], axis=1)
         )
-    spectrum = jnp.dot(
-        jnp.concatenate(pieces, axis=0),
-        fwd_ref[...],
-        precision=highest,
-        preferred_element_type=jnp.float32,
-    )
+    spectrum = split_dot(jnp.concatenate(pieces, axis=0), fwd_ref[0], fwd_ref[1])
     cuts = cut_ref[...]
     keep = jnp.concatenate(
         [(fold_ref[k : k + 1, :] <= cuts).astype(jnp.float32) for k in range(half)], axis=0
     )
-    back = jnp.dot(
-        spectrum * keep, inv_ref[...], precision=highest, preferred_element_type=jnp.float32
-    )
+    back = split_dot(spectrum * keep, inv_ref[0], inv_ref[1])
     real_d, imag_d = [], []
     for k in range(half):
         twc = twc_ref[k : k + 1, :]
@@ -97,8 +102,8 @@
     return pl.pallas_call(
         filter_kernel,
         out_shape=jax.ShapeDtypeStruct(values.shape, values.dtype),
-    )(values, cuts.reshape(count, 1), jnp.asarray(twc), jnp.asarray(tws), jnp.asarray(forward),
-      jnp.asarray(inverse), jnp.asarray(folded))
+    )(values, cuts.reshape(count, 1), jnp.asarray(twc), jnp.asarray(tws), split_table(forward),
+      split_table(inverse), jnp.asarray(folded))
 
 def prefix_over(value, axis, before):
     count = lax.axis_size(axis)

time: 53 us -> 52.2 us (0.985)
  Pallas kernels: 4.26 us -> 3.36 us
    pallas_call x1, Pallas kernels: 4.26 us -> 3.36 us  [filter_rows(): pl.pallas_call(filter_kernel, out_shape=jax.ShapeDtypeStruct(values.shape...]
where the time goes in v11:
time: 52.2 us; the launch traced here: 51.6 us
  starting transfers between devices  19.4 us (37%)
  waiting for transfers between devices  15.4 us (30%)
  local copies, waits for them, and re-layouts  7.99 us (15%)
  other arithmetic  4.53 us (9%)
  Pallas kernels  3.36 us (6%)
  between operations  0.96 us (2%)
    all_to_all x2, waiting for transfers between devices, prefix_over(): lax.all_to_all(copies, axis, split_axis=0, concat_axis=0, tiled=True)  15.4 us
    all_to_all x2, starting transfers between devices, prefix_over(): lax.all_to_all(copies, axis, split_axis=0, concat_axis=0, tiled=True)  10.5 us
    ppermute x1, starting transfers between devices, local(): lax.ppermute(to_south, 'lat', [(i + 1, i) for i in range(count - 1)])  6.96 us
    pallas_call x1, Pallas kernels, filter_rows(): pl.pallas_call(filter_kernel, out_shape=jax.ShapeDtypeStruct(values.shape...  3.36 us
    ppermute x1, starting transfers between devices, local(): lax.ppermute(to_north, 'lat', [(i, i + 1) for i in range(count - 1)])  1.92 us
    broadcast_in_dim x2, local copies, waits for them, and re-layouts, prefix_over(): copies = jnp.broadcast_to(value, (count, *value.shape))  1.33 us
    unnamed x14, local copies, waits for them, and re-layouts  1.26 us
  transfers between devices with their start and end apart: 4, of which 2 were waited for; matrix products, arithmetic and copies ran while one was open for 9% of the time, Pallas kernels for 0%

profile of v11, /device:TPU:256, one launch (start us, length us, event | category | flops | bytes accessed | tf_op | source)
XLA Modules:
  0.0 51.6 jit_solution(6443137962421532621)
XLA Ops:
  0.7 0.8 %slice.300 = f32[1,8,1152]{2,1,0:T(8,128)S(1)} slice(f32[3,8,1152]{2,1,0:T(8,128)} %bitcast.82), slice={[0:1], [0:8], [0:1152]} | slice | bytes 73728 | tf_op jit(solution)/shard_map/slice | solution.py:129
  1.5 0.7 %slice_reduce_fusion = f32[1152]{0:T(1024)S(1)} fusion(f32[3,1152]{1,0:T(4,128)} %param.17), kind=kLoop, calls=%fused_computation.103 | loop fusion | bytes 9216 | tf_op jit(solution)/shard_map/slice | solution.py:128
  2.2 0.9 %pad_maximum_fusion.3 = (f32[7,8,1152]{2,1,0:T(8,128)S(1)}, f32[7,8,1152]{2,1,0:T(8,128)S(1)}) fusion(f32[1,8,1152]{2,1,0:T(8,128)S(1)} %broadcast_in_dim.45, f32[3,8,1152]{2,1,0:T(8,128)} %bitcast.72, f32[3,8,1152]{2,1,0:T(8,128)S(1)} %bitcast.63, f32[1,8,1152]{2,1,0:T(8,128)S(1)} %slice.300), kind=kLoop, calls=%fused_computation.20 | loop fusion | flops 193536 | bytes 811008 | tf_op jit(solution)/shard_map/concatenate | solution.py:128
  3.2 1.9 %collective-permute-start.1 = (f32[7,8,1152]{2,1,0:T(8,128)S(1)}, f32[7,8,1152]{2,1,0:T(8,128)S(1)}, u32[]{:S(2)}, u32[]{:S(2)}) collective-permute-start(f32[7,8,1152]{2,1,0:T(8,128)S(1)} %get-tuple-element.22), channel_id=1, source_target_pairs={{0,8},{8,16},{16,24},{24,32},{32,40},{40,48},{48,56},{56,64},{64,7... | collective-permute-start | bytes 774152 | tf_op jit(solution)/shard_map/ppermute | solution.py:131
  5.1 7.0 %collective-permute-start = (f32[7,8,1152]{2,1,0:T(8,128)S(1)}, f32[7,8,1152]{2,1,0:T(8,128)S(1)}, u32[]{:S(2)}, u32[]{:S(2)}) collective-permute-start(f32[7,8,1152]{2,1,0:T(8,128)S(1)} %get-tuple-element.23), channel_id=1, source_target_pairs={{8,0},{16,8},{24,16},{32,24},{40,32},{48,40},{56,48},{64,56},{72,6... | collective-permute-start | bytes 774152 | tf_op jit(solution)/shard_map/ppermute | solution.py:132
  12.1 0.1 fusion.67
  12.2 0.1 fusion.69
  12.6 0.6 %copy-done.2 = f32[8,3,1152]{2,0,1:T(8,128)S(1)} copy-done((f32[8,3,1152]{2,0,1:T(8,128)S(1)}, f32[8,3,1152]{2,0,1:T(8,128)}, u32[]{:S(2)}) %copy-start.2) | copy-done | bytes 110616
  13.3 0.1 fusion.65
  13.5 0.6 %copy-done.5 = f32[8,3,1152]{2,0,1:T(8,128)S(1)} copy-done((f32[8,3,1152]{2,0,1:T(8,128)S(1)}, f32[8,3,1152]{2,0,1:T(8,128)}, u32[]{:S(2)}) %copy-start.5) | copy-done | bytes 110616
  14.2 0.2 fusion.47
  14.5 0.7 %broadcast_in_dim.49 = f32[8,4,1152]{2,1,0:T(4,128)} broadcast(f32[4,1152]{1,0:T(4,128)S(1)} %get-tuple-element.25), dimensions={1,2} | broadcast | bytes 165888 | tf_op jit(solution)/shard_map/broadcast_in_dim | solution.py:111
  15.2 7.1 %all-to-all-start = ((f32[8,4,1152]{2,1,0:T(4,128)}), f32[8,4,1152]{2,1,0:T(4,128)S(1)}, u32[]{:S(2)}, u32[]{:S(2)}) async-start(f32[8,4,1152]{2,1,0:T(4,128)} %broadcast_in_dim.49), calls=%async_computation | async-start | bytes 294912 | tf_op jit(solution)/shard_map/all_to_all | solution.py:112
  22.3 0.1 reduce_window_sum.17
  22.5 9.0 %all-to-all-done = f32[8,4,1152]{2,1,0:T(4,128)S(1)} async-done(((f32[8,4,1152]{2,1,0:T(4,128)}), f32[8,4,1152]{2,1,0:T(4,128)S(1)}, u32[]{:S(2)}, u32[]{:S(2)}) %all-to-all-start) | async-done | bytes 147488 | tf_op jit(solution)/shard_map/all_to_all | solution.py:112
  31.5 0.1 select_reduce_fusion.1
  31.7 0.2 fusion.59
  31.8 0.7 %broadcast_in_dim.51 = f32[8,4,1152]{2,1,0:T(4,128)} broadcast(f32[4,1152]{1,0:T(4,128)S(1)} %get-tuple-element.9), dimensions={1,2} | broadcast | bytes 165888 | tf_op jit(solution)/shard_map/broadcast_in_dim | solution.py:111
  32.5 3.4 %all-to-all-start.1 = ((f32[8,4,1152]{2,1,0:T(4,128)}), f32[8,4,1152]{2,1,0:T(4,128)S(1)}, u32[]{:S(2)}, u32[]{:S(2)}) async-start(f32[8,4,1152]{2,1,0:T(4,128)} %broadcast_in_dim.51), calls=%async_computation.1 | async-start | bytes 294912 | tf_op jit(solution)/shard_map/all_to_all | solution.py:112
  36.0 0.7 %gather_fusion = s32[13]{0:T(128)S(1)} fusion(s32[192]{0:T(256)S(1)} %copy-done, s32[1024]{0:T(1024)S(1)} %pad_clamp_fusion), kind=kCustom, calls=%fused_computation | custom fusion | bytes 156 | tf_op jit(solution)/shard_map/gather | solution.py:161
  36.7 0.7 %reshape_reshape.4.cut_ref = s32[104,1]{1,0:T(8,128)} reshape(s32[13,8]{1,0:T(8,128)S(1)} %broadcast_in_dim.52) | data formatting | bytes 832 | tf_op jit(solution)/shard_map/reshape;reshape | solution.py:105
  37.4 0.1 rev.7
  37.6 0.1 reduce_window_sum.18
  37.7 0.2 rev.8
  37.9 0.8 %pad_maximum_fusion = f32[13,8,1152]{2,1,0:T(8,128)} fusion(f32[4,8,1152]{2,1,0:T(8,128)S(1)} %get-tuple-element.35, f32[3,8,1152]{2,1,0:T(8,128)S(1)} %fusion.47, f32[3,8,1152]{2,1,0:T(8,128)S(1)} %bitcast.84, f32[3,8,1152]{2,1,0:T(8,128)S(1)} %bitcast.85), kind=kLoop, calls=%fused_computation.1 | loop fusion | flops 359424 | bytes 958464 | tf_op jit(solution)/shard_map/concatenate | solution.py:157
  38.7 6.3 %all-to-all-done.1 = f32[8,4,1152]{2,1,0:T(4,128)S(1)} async-done(((f32[8,4,1152]{2,1,0:T(4,128)}), f32[8,4,1152]{2,1,0:T(4,128)S(1)}, u32[]{:S(2)}, u32[]{:S(2)}) %all-to-all-start.1) | async-done | bytes 147488 | tf_op jit(solution)/shard_map/all_to_all | solution.py:112
  45.0 0.1 select_reduce_fusion
  45.2 3.4 %shard_map.164 = f32[104,1152]{1,0:T(8,128)} custom-call(f32[104,1152]{1,0:T(8,128)} %bitcast.81, s32[104,1]{1,0:T(8,128)} %reshape_reshape.4.cut_ref, f32[9,128]{1,0:T(8,128)} %constant.58.clone.twc_ref, f32[9,128]{1,0:T(8,128)} %constant.59.clone.tws_ref, bf16[2,256,256]{2,1,0:T(8,128)(2,1)} %constant.74.fwd_ref, bf16[2,256,256]{2,1,0:T(8,128)(2,1)} %constant.81.inv_ref, ...), custom_call_target="tpu_custom_call" | custom-call | tf_op jit(solution)/shard_map/pallas_call | solution.py:102
  48.6 1.0 %slice_bitcast_fusion.1 = f32[3,8,1152]{2,1,0:T(8,128)S(1)} fusion(f32[104,1152]{1,0:T(8,128)} %shard_map.164), kind=kLoop, calls=%fused_computation.71 | loop fusion | bytes 221184 | tf_op jit(solution)/shard_map/slice | solution.py:166
  49.6 0.1 slice.318
  49.7 0.8 %fusion.54 = (f32[3,8,1152]{2,1,0:T(8,128)S(1)}, f32[8,3,1152]{2,0,1:T(8,128)}) fusion(f32[3,8,1151]{2,1,0:T(8,128)S(1)} %get-tuple-element.32, f32[3,8,1]{2,1,0:T(8,128)S(1)} %get-tuple-element.34, f32[3,8,1150]{2,1,0:T(8,128)S(1)} %get-tuple-element.28, f32[3,8,2]{2,1,0:T(8,128)S(1)} %get-tuple-element.30, f32[3,8,1]{2,1,0:T(8,128)S(1)} %get-tuple-element.33, ...), kind=kLoop, calls=%fused_computation.96 | loop fusion | flops 552960 | bytes 1437696 | tf_op jit(solution)/shard_map/mul | solution.py:171
  50.7 0.8 %fusion.40 = (f32[8,3,1152]{2,0,1:T(8,128)}, f32[8,3,1152]{2,0,1:T(8,128)}, f32[8,3,1152]{2,0,1:T(8,128)}, f32[8,3,1152]{2,0,1:T(8,128)}) fusion(f32[104,1152]{1,0:T(8,128)S(1)} %copy-done.3, f32[4,8,1152]{2,1,0:T(8,128)S(1)} %fusion.28, f32[3]{0:T(128)S(1)} %compare_convert_fusion, f32[3,8,1151]{2,1,0:T(8,128)S(1)} %slice.254, f32[3,8,1]{2,1,0:T(8,128)S(1)} %slice.253, ...), kind=kLoop, calls=%fused_computation.75 | loop fusion | flops 414720 | bytes 1658892 | tf_op jit(solution)/shard_map/transpose | solution.py:181
  (46 shorter events, 1.2 us)
Async XLA Ops:
  0.6 35.3 %copy-start = (s32[192]{0:T(256)S(1)}, s32[192]{0:T(256)}, u32[]{:S(2)}) copy-start(s32[192]{0:T(256)} %param.18) | copy-start | bytes 2308
  0.6 1.6 %copy-start.1 = (f32[8,3,1152]{2,0,1:T(8,128)S(1)}, f32[8,3,1152]{2,0,1:T(8,128)}, u32[]{:S(2)}) copy-start(f32[8,3,1152]{2,0,1:T(8,128)} %param.15) | copy-start | bytes 331780
  3.2 11.3 %collective-permute-start.1 = (f32[7,8,1152]{2,1,0:T(8,128)S(1)}, f32[7,8,1152]{2,1,0:T(8,128)S(1)}, u32[]{:S(2)}, u32[]{:S(2)}) collective-permute-start(f32[7,8,1152]{2,1,0:T(8,128)S(1)} %get-tuple-element.22), channel_id=1, source_target_pairs={{0,8},{8,16},{16,24},{24,32},{32,40},{40,48},{48,56},{56,64},{64,7... | collective-permute-start | bytes 774152 | tf_op jit(solution)/shard_map/ppermute | solution.py:131
  5.1 17.3 %collective-permute-start = (f32[7,8,1152]{2,1,0:T(8,128)S(1)}, f32[7,8,1152]{2,1,0:T(8,128)S(1)}, u32[]{:S(2)}, u32[]{:S(2)}) collective-permute-start(f32[7,8,1152]{2,1,0:T(8,128)S(1)} %get-tuple-element.23), channel_id=1, source_target_pairs={{8,0},{16,8},{24,16},{32,24},{40,32},{48,40},{56,48},{64,56},{72,6... | collective-permute-start | bytes 774152 | tf_op jit(solution)/shard_map/ppermute | solution.py:132
  12.3 0.9 %copy-start.2 = (f32[8,3,1152]{2,0,1:T(8,128)S(1)}, f32[8,3,1152]{2,0,1:T(8,128)}, u32[]{:S(2)}) copy-start(f32[8,3,1152]{2,0,1:T(8,128)} %param.16) | copy-start | bytes 331780
  13.3 0.9 %copy-start.5 = (f32[8,3,1152]{2,0,1:T(8,128)S(1)}, f32[8,3,1152]{2,0,1:T(8,128)}, u32[]{:S(2)}) copy-start(f32[8,3,1152]{2,0,1:T(8,128)} %param.13) | copy-start | bytes 331780
  15.2 16.4 %all-to-all-start = ((f32[8,4,1152]{2,1,0:T(4,128)}), f32[8,4,1152]{2,1,0:T(4,128)S(1)}, u32[]{:S(2)}, u32[]{:S(2)}) async-start(f32[8,4,1152]{2,1,0:T(4,128)} %broadcast_in_dim.49), calls=%async_computation | async-start | bytes 294912 | tf_op jit(solution)/shard_map/all_to_all | solution.py:112
  22.5 9.2 %copy-start.4 = (f32[8,3,1152]{2,0,1:T(8,128)S(1)}, f32[8,3,1152]{2,0,1:T(8,128)}, u32[]{:S(2)}) copy-start(f32[8,3,1152]{2,0,1:T(8,128)} %param.14) | copy-start | bytes 331780
  32.5 12.6 %all-to-all-start.1 = ((f32[8,4,1152]{2,1,0:T(4,128)}), f32[8,4,1152]{2,1,0:T(4,128)S(1)}, u32[]{:S(2)}, u32[]{:S(2)}) async-start(f32[8,4,1152]{2,1,0:T(4,128)} %broadcast_in_dim.51), calls=%async_computation.1 | async-start | bytes 294912 | tf_op jit(solution)/shard_map/all_to_all | solution.py:112
  38.7 6.5 %copy-start.6 = (f32[3,1152]{1,0:T(4,128)S(1)}, f32[3,1152]{1,0:T(4,128)}, u32[]{:S(2)}) copy-start(f32[3,1152]{1,0:T(4,128)} %param.17) | copy-start | bytes 41476
  48.6 1.1 %copy-start.3 = (f32[104,1152]{1,0:T(8,128)S(1)}, f32[104,1152]{1,0:T(8,128)}, u32[]{:S(2)}) copy-start(f32[104,1152]{1,0:T(8,128)} %shard_map.164) | copy-start | bytes 1437700

commit v12 on v11

--- a/solution.py
+++ b/solution.py
@@ -125,8 +125,8 @@
     nlat_all = lat_rows * lat_count
     first_row = lat_rank * lat_rows
     surface = jnp.broadcast_to(surface_height[:, None], (lat_rows, levels, length))
-    to_north = jnp.concatenate([layer_mass, theta_field, surface[-1:]], axis=0)
-    to_south = jnp.concatenate([layer_mass, theta_field, wind_north[:1]], axis=0)
+    to_north = jnp.concatenate([layer_mass, theta_field, surface], axis=0)
+    to_south = jnp.concatenate([layer_mass, theta_field, wind_north], axis=0)
     count = lat_count
     from_south = lax.ppermute(to_north, "lat", [(i, i + 1) for i in range(count - 1)])
     from_north = lax.ppermute(to_south, "lat", [(i + 1, i) for i in range(count - 1)])
@@ -139,12 +139,12 @@
     coslat = jnp.sin(jnp.pi * face_rows.astype(jnp.float32) / nlat_all)[:, None, None]
     mass_faces = face_lat(mass_pad, lat_rows + 1)
     theta_faces = face_lat(theta_pad, lat_rows + 1)
-    north_ext = jnp.concatenate([wind_north, from_north[2 * rows :]], axis=0)
+    north_ext = jnp.concatenate([wind_north, from_north[2 * rows : 2 * rows + 1]], axis=0)
     flux_east = wind_east * face_lon(layer_mass)
     flux_north = north_ext * mass_faces * coslat
     mass_ext = jnp.concatenate([from_south[rows - 1 : rows], layer_mass], axis=0)
     theta_ext = jnp.concatenate([from_south[2 * rows - 1 : 2 * rows], theta_field], axis=0)
-    surface_ext = jnp.concatenate([from_south[2 * rows :], surface], axis=0)
+    surface_ext = jnp.concatenate([from_south[3 * rows - 1 :], surface], axis=0)
     column = jnp.sum(mass_ext, axis=1)
     above_mass = prefix_over(column, "lev", True)
     bottom = TOP_PRESSURE + above_mass[:, None] + jnp.cumsum(mass_ext, axis=1)

time: 52.2 us -> 51.9 us (level)
  local copies, waits for them, and re-layouts: 7.99 us -> 7.34 us
    slice x3 -> x1, local copies, waits for them, and re-layouts: 1.55 us -> 0.01 us  [local(): from_north[2 * rows:2 * rows + 1]]
    broadcast_in_dim x2 -> x1, local copies, waits for them, and re-layouts: 0.01 us -> 0.77 us  [local(): jnp.broadcast_to(surface_height[:, None], (lat_rows, levels, length))]
    unnamed x14 -> x12, local copies, waits for them, and re-layouts: 1.26 us -> 1.4 us
  transfers between devices with their start and end apart: 4 -> 4, of which waited for: 2 -> 3; matrix products, arithmetic and copies ran while one was open for 9% -> 9% of each run, Pallas kernels for 0% -> 0%
where the time goes in v12:
time: 51.9 us; the launch traced here: 51.5 us
  starting transfers between devices  19.4 us (37%)
  waiting for transfers between devices  15.9 us (31%)
  local copies, waits for them, and re-layouts  7.34 us (14%)
  other arithmetic  4.61 us (9%)
  Pallas kernels  3.37 us (6%)
  between operations  0.93 us (2%)
    all_to_all x2, waiting for transfers between devices, prefix_over(): lax.all_to_all(copies, axis, split_axis=0, concat_axis=0, tiled=True)  15.4 us
    all_to_all x2, starting transfers between devices, prefix_over(): lax.all_to_all(copies, axis, split_axis=0, concat_axis=0, tiled=True)  10.5 us
    ppermute x1, starting transfers between devices, local(): lax.ppermute(to_south, 'lat', [(i + 1, i) for i in range(count - 1)])  6.96 us
    pallas_call x1, Pallas kernels, filter_rows(): pl.pallas_call(filter_kernel, out_shape=jax.ShapeDtypeStruct(values.shape...  3.37 us
    ppermute x1, starting transfers between devices, local(): lax.ppermute(to_north, 'lat', [(i, i + 1) for i in range(count - 1)])  1.92 us
    unnamed x12, local copies, waits for them, and re-layouts  1.4 us
    broadcast_in_dim x2, local copies, waits for them, and re-layouts, prefix_over(): copies = jnp.broadcast_to(value, (count, *value.shape))  1.35 us
  transfers between devices with their start and end apart: 4, of which 3 were waited for; matrix products, arithmetic and copies ran while one was open for 9% of the time, Pallas kernels for 0%

profile of v12, /device:TPU:256, one launch (start us, length us, event | category | flops | bytes accessed | tf_op | source)
XLA Modules:
  0.0 51.5 jit_solution(8557566756999501524)
XLA Ops:
  0.7 0.8 %broadcast_in_dim.43 = f32[3,8,1152]{2,1,0:T(8,128)S(1)} broadcast(f32[3,1152]{1,0:T(4,128)} %param.17), dimensions={0,2} | broadcast | bytes 124416 | tf_op jit(solution)/shard_map/broadcast_in_dim | solution.py:127
  1.4 0.1 copy-done.1
  1.6 1.0 %pad_maximum_fusion.3 = (f32[9,8,1152]{2,1,0:T(8,128)S(1)}, f32[9,8,1152]{2,1,0:T(8,128)S(1)}) fusion(f32[3,8,1152]{2,1,0:T(8,128)S(1)} %broadcast_in_dim.43, f32[3,8,1152]{2,1,0:T(8,128)} %bitcast.72, f32[3,8,1152]{2,1,0:T(8,128)S(1)} %bitcast.63, f32[3,8,1152]{2,1,0:T(8,128)} %bitcast.82), kind=kLoop, calls=%fused_computation.4 | loop fusion | flops 248832 | bytes 1105920 | tf_op jit(solution)/shard_map/concatenate | solution.py:128
  2.6 1.9 %collective-permute-start.1 = (f32[9,8,1152]{2,1,0:T(8,128)S(1)}, f32[9,8,1152]{2,1,0:T(8,128)S(1)}, u32[]{:S(2)}, u32[]{:S(2)}) collective-permute-start(f32[9,8,1152]{2,1,0:T(8,128)S(1)} %get-tuple-element.22), channel_id=1, source_target_pairs={{0,8},{8,16},{16,24},{24,32},{32,40},{40,48},{48,56},{56,64},{64,7... | collective-permute-start | bytes 995336 | tf_op jit(solution)/shard_map/ppermute | solution.py:131
  4.5 7.0 %collective-permute-start = (f32[9,8,1152]{2,1,0:T(8,128)S(1)}, f32[9,8,1152]{2,1,0:T(8,128)S(1)}, u32[]{:S(2)}, u32[]{:S(2)}) collective-permute-start(f32[9,8,1152]{2,1,0:T(8,128)S(1)} %get-tuple-element.23), channel_id=1, source_target_pairs={{8,0},{16,8},{24,16},{32,24},{40,32},{48,40},{56,48},{64,56},{72,6... | collective-permute-start | bytes 995336 | tf_op jit(solution)/shard_map/ppermute | solution.py:132
  11.5 0.1 fusion.67
  11.6 0.1 fusion.69
  12.0 0.6 %copy-done.2 = f32[8,3,1152]{2,0,1:T(8,128)S(1)} copy-done((f32[8,3,1152]{2,0,1:T(8,128)S(1)}, f32[8,3,1152]{2,0,1:T(8,128)}, u32[]{:S(2)}) %copy-start.2) | copy-done | bytes 110616
  12.7 0.1 fusion.65
  13.0 0.6 %copy-done.5 = f32[8,3,1152]{2,0,1:T(8,128)S(1)} copy-done((f32[8,3,1152]{2,0,1:T(8,128)S(1)}, f32[8,3,1152]{2,0,1:T(8,128)}, u32[]{:S(2)}) %copy-start.5) | copy-done | bytes 110616
  13.6 0.2 fusion.47
  13.8 0.5 collective-permute-done.1
  14.4 0.7 %broadcast_in_dim.46 = f32[8,4,1152]{2,1,0:T(4,128)} broadcast(f32[4,1152]{1,0:T(4,128)S(1)} %get-tuple-element.25), dimensions={1,2} | broadcast | bytes 165888 | tf_op jit(solution)/shard_map/broadcast_in_dim | solution.py:111
  15.1 7.1 %all-to-all-start = ((f32[8,4,1152]{2,1,0:T(4,128)}), f32[8,4,1152]{2,1,0:T(4,128)S(1)}, u32[]{:S(2)}, u32[]{:S(2)}) async-start(f32[8,4,1152]{2,1,0:T(4,128)} %broadcast_in_dim.46), calls=%async_computation | async-start | bytes 294912 | tf_op jit(solution)/shard_map/all_to_all | solution.py:112
  22.2 0.1 reduce_window_sum.17
  22.4 9.0 %all-to-all-done = f32[8,4,1152]{2,1,0:T(4,128)S(1)} async-done(((f32[8,4,1152]{2,1,0:T(4,128)}), f32[8,4,1152]{2,1,0:T(4,128)S(1)}, u32[]{:S(2)}, u32[]{:S(2)}) %all-to-all-start) | async-done | bytes 147488 | tf_op jit(solution)/shard_map/all_to_all | solution.py:112
  31.4 0.1 select_reduce_fusion.1
  31.6 0.1 fusion.59
  31.7 0.7 %broadcast_in_dim.48 = f32[8,4,1152]{2,1,0:T(4,128)} broadcast(f32[4,1152]{1,0:T(4,128)S(1)} %get-tuple-element.9), dimensions={1,2} | broadcast | bytes 165888 | tf_op jit(solution)/shard_map/broadcast_in_dim | solution.py:111
  32.4 3.4 %all-to-all-start.1 = ((f32[8,4,1152]{2,1,0:T(4,128)}), f32[8,4,1152]{2,1,0:T(4,128)S(1)}, u32[]{:S(2)}, u32[]{:S(2)}) async-start(f32[8,4,1152]{2,1,0:T(4,128)} %broadcast_in_dim.48), calls=%async_computation.1 | async-start | bytes 294912 | tf_op jit(solution)/shard_map/all_to_all | solution.py:112
  35.9 0.7 %gather_fusion = s32[13]{0:T(128)S(1)} fusion(s32[192]{0:T(256)S(1)} %copy-done, s32[1024]{0:T(1024)S(1)} %pad_clamp_fusion), kind=kCustom, calls=%fused_computation | custom fusion | bytes 156 | tf_op jit(solution)/shard_map/gather | solution.py:161
  36.6 0.7 %reshape_reshape.4.cut_ref = s32[104,1]{1,0:T(8,128)} reshape(s32[13,8]{1,0:T(8,128)S(1)} %broadcast_in_dim.49) | data formatting | bytes 832 | tf_op jit(solution)/shard_map/reshape;reshape | solution.py:105
  37.3 0.1 rev.7
  37.5 0.1 reduce_window_sum.18
  37.6 0.2 rev.8
  37.8 0.8 %pad_maximum_fusion = f32[13,8,1152]{2,1,0:T(8,128)} fusion(f32[4,8,1152]{2,1,0:T(8,128)S(1)} %get-tuple-element.35, f32[3,8,1152]{2,1,0:T(8,128)S(1)} %fusion.47, f32[3,8,1152]{2,1,0:T(8,128)S(1)} %bitcast.84, f32[3,8,1152]{2,1,0:T(8,128)S(1)} %bitcast.85), kind=kLoop, calls=%fused_computation.1 | loop fusion | flops 359424 | bytes 958464 | tf_op jit(solution)/shard_map/concatenate | solution.py:157
  38.6 6.3 %all-to-all-done.1 = f32[8,4,1152]{2,1,0:T(4,128)S(1)} async-done(((f32[8,4,1152]{2,1,0:T(4,128)}), f32[8,4,1152]{2,1,0:T(4,128)S(1)}, u32[]{:S(2)}, u32[]{:S(2)}) %all-to-all-start.1) | async-done | bytes 147488 | tf_op jit(solution)/shard_map/all_to_all | solution.py:112
  44.9 0.1 select_reduce_fusion
  45.1 3.4 %shard_map.164 = f32[104,1152]{1,0:T(8,128)} custom-call(f32[104,1152]{1,0:T(8,128)} %bitcast.81, s32[104,1]{1,0:T(8,128)} %reshape_reshape.4.cut_ref, f32[9,128]{1,0:T(8,128)} %constant.58.clone.twc_ref, f32[9,128]{1,0:T(8,128)} %constant.59.clone.tws_ref, bf16[2,256,256]{2,1,0:T(8,128)(2,1)} %constant.74.fwd_ref, bf16[2,256,256]{2,1,0:T(8,128)(2,1)} %constant.81.inv_ref, ...), custom_call_target="tpu_custom_call" | custom-call | tf_op jit(solution)/shard_map/pallas_call | solution.py:102
  48.5 1.0 %slice_bitcast_fusion.1 = f32[3,8,1152]{2,1,0:T(8,128)S(1)} fusion(f32[104,1152]{1,0:T(8,128)} %shard_map.164), kind=kLoop, calls=%fused_computation.71 | loop fusion | bytes 221184 | tf_op jit(solution)/shard_map/slice | solution.py:166
  49.6 0.8 %fusion.54 = (f32[3,8,1152]{2,1,0:T(8,128)S(1)}, f32[8,3,1152]{2,0,1:T(8,128)}) fusion(f32[3,8,1151]{2,1,0:T(8,128)S(1)} %get-tuple-element.32, f32[3,8,1]{2,1,0:T(8,128)S(1)} %get-tuple-element.34, f32[3,8,1150]{2,1,0:T(8,128)S(1)} %get-tuple-element.28, f32[3,8,2]{2,1,0:T(8,128)S(1)} %get-tuple-element.30, f32[3,8,1]{2,1,0:T(8,128)S(1)} %get-tuple-element.33, ...), kind=kLoop, calls=%fused_computation.96 | loop fusion | flops 552960 | bytes 1437696 | tf_op jit(solution)/shard_map/mul | solution.py:171
  50.6 0.8 %fusion.40 = (f32[8,3,1152]{2,0,1:T(8,128)}, f32[8,3,1152]{2,0,1:T(8,128)}, f32[8,3,1152]{2,0,1:T(8,128)}, f32[8,3,1152]{2,0,1:T(8,128)}) fusion(f32[104,1152]{1,0:T(8,128)S(1)} %copy-done.3, f32[4,8,1152]{2,1,0:T(8,128)S(1)} %fusion.28, f32[3]{0:T(128)S(1)} %compare_convert_fusion, f32[3,8,1151]{2,1,0:T(8,128)S(1)} %slice.241, f32[3,8,1]{2,1,0:T(8,128)S(1)} %slice.240, ...), kind=kLoop, calls=%fused_computation.75 | loop fusion | flops 414720 | bytes 1658892 | tf_op jit(solution)/shard_map/transpose | solution.py:181
  (41 shorter events, 1.3 us)
Async XLA Ops:
  0.6 35.2 %copy-start = (s32[192]{0:T(256)S(1)}, s32[192]{0:T(256)}, u32[]{:S(2)}) copy-start(s32[192]{0:T(256)} %param.18) | copy-start | bytes 2308
  0.6 0.9 %copy-start.1 = (f32[8,3,1152]{2,0,1:T(8,128)S(1)}, f32[8,3,1152]{2,0,1:T(8,128)}, u32[]{:S(2)}) copy-start(f32[8,3,1152]{2,0,1:T(8,128)} %param.15) | copy-start | bytes 331780
  2.6 11.8 %collective-permute-start.1 = (f32[9,8,1152]{2,1,0:T(8,128)S(1)}, f32[9,8,1152]{2,1,0:T(8,128)S(1)}, u32[]{:S(2)}, u32[]{:S(2)}) collective-permute-start(f32[9,8,1152]{2,1,0:T(8,128)S(1)} %get-tuple-element.22), channel_id=1, source_target_pairs={{0,8},{8,16},{16,24},{24,32},{32,40},{40,48},{48,56},{56,64},{64,7... | collective-permute-start | bytes 995336 | tf_op jit(solution)/shard_map/ppermute | solution.py:131
  4.5 17.8 %collective-permute-start = (f32[9,8,1152]{2,1,0:T(8,128)S(1)}, f32[9,8,1152]{2,1,0:T(8,128)S(1)}, u32[]{:S(2)}, u32[]{:S(2)}) collective-permute-start(f32[9,8,1152]{2,1,0:T(8,128)S(1)} %get-tuple-element.23), channel_id=1, source_target_pairs={{8,0},{16,8},{24,16},{32,24},{40,32},{48,40},{56,48},{64,56},{72,6... | collective-permute-start | bytes 995336 | tf_op jit(solution)/shard_map/ppermute | solution.py:132
  11.7 0.9 %copy-start.2 = (f32[8,3,1152]{2,0,1:T(8,128)S(1)}, f32[8,3,1152]{2,0,1:T(8,128)}, u32[]{:S(2)}) copy-start(f32[8,3,1152]{2,0,1:T(8,128)} %param.16) | copy-start | bytes 331780
  12.7 0.9 %copy-start.5 = (f32[8,3,1152]{2,0,1:T(8,128)S(1)}, f32[8,3,1152]{2,0,1:T(8,128)}, u32[]{:S(2)}) copy-start(f32[8,3,1152]{2,0,1:T(8,128)} %param.13) | copy-start | bytes 331780
  15.1 16.4 %all-to-all-start = ((f32[8,4,1152]{2,1,0:T(4,128)}), f32[8,4,1152]{2,1,0:T(4,128)S(1)}, u32[]{:S(2)}, u32[]{:S(2)}) async-start(f32[8,4,1152]{2,1,0:T(4,128)} %broadcast_in_dim.46), calls=%async_computation | async-start | bytes 294912 | tf_op jit(solution)/shard_map/all_to_all | solution.py:112
  22.4 9.2 %copy-start.4 = (f32[8,3,1152]{2,0,1:T(8,128)S(1)}, f32[8,3,1152]{2,0,1:T(8,128)}, u32[]{:S(2)}) copy-start(f32[8,3,1152]{2,0,1:T(8,128)} %param.14) | copy-start | bytes 331780
  32.4 12.6 %all-to-all-start.1 = ((f32[8,4,1152]{2,1,0:T(4,128)}), f32[8,4,1152]{2,1,0:T(4,128)S(1)}, u32[]{:S(2)}, u32[]{:S(2)}) async-start(f32[8,4,1152]{2,1,0:T(4,128)} %broadcast_in_dim.48), calls=%async_computation.1 | async-start | bytes 294912 | tf_op jit(solution)/shard_map/all_to_all | solution.py:112
  48.5 1.1 %copy-start.3 = (f32[104,1152]{1,0:T(8,128)S(1)}, f32[104,1152]{1,0:T(8,128)}, u32[]{:S(2)}) copy-start(f32[104,1152]{1,0:T(8,128)} %shard_map.164) | copy-start | bytes 1437700

commit v13 on v12

--- a/solution.py
+++ b/solution.py
@@ -124,7 +124,7 @@
     lat_rank = lax.axis_index("lat")
     nlat_all = lat_rows * lat_count
     first_row = lat_rank * lat_rows
-    surface = jnp.broadcast_to(surface_height[:, None], (lat_rows, levels, length))
+    surface = jnp.pad(surface_height[:, None], ((0, 0), (0, levels - 1), (0, 0)))
     to_north = jnp.concatenate([layer_mass, theta_field, surface], axis=0)
     to_south = jnp.concatenate([layer_mass, theta_field, wind_north], axis=0)
     count = lat_count
@@ -144,7 +144,9 @@
     flux_north = north_ext * mass_faces * coslat
     mass_ext = jnp.concatenate([from_south[rows - 1 : rows], layer_mass], axis=0)
     theta_ext = jnp.concatenate([from_south[2 * rows - 1 : 2 * rows], theta_field], axis=0)
-    surface_ext = jnp.concatenate([from_south[3 * rows - 1 :], surface], axis=0)
+    surface_ext = jnp.concatenate(
+        [from_south[3 * rows - 1 :, :1], surface_height[:, None]], axis=0
+    )
     column = jnp.sum(mass_ext, axis=1)
     above_mass = prefix_over(column, "lev", True)
     bottom = TOP_PRESSURE + above_mass[:, None] + jnp.cumsum(mass_ext, axis=1)

time: 51.9 us -> 52.3 us (level)
  waiting for transfers between devices: 15.9 us -> 16.9 us
  local copies, waits for them, and re-layouts: 7.34 us -> 6.6 us
    all_to_all x2, waiting for transfers between devices: 15.4 us -> 16.9 us  [prefix_over(): lax.all_to_all(copies, axis, split_axis=0, concat_axis=0, tiled=True)]
    unnamed x12 -> x14, local copies, waits for them, and re-layouts: 1.4 us -> 0.64 us
  transfers between devices with their start and end apart: 4 -> 4, of which waited for: 3 -> 2; matrix products, arithmetic and copies ran while one was open for 9% -> 9% of each run, Pallas kernels for 0% -> 0%
where the time goes in v13:
time: 52.3 us; the launch traced here: 51.8 us
  starting transfers between devices  19.4 us (37%)
  waiting for transfers between devices  16.9 us (32%)
  local copies, waits for them, and re-layouts  6.6 us (13%)
  other arithmetic  4.69 us (9%)
  Pallas kernels  3.36 us (6%)
  between operations  0.97 us (2%)
    all_to_all x2, waiting for transfers between devices, prefix_over(): lax.all_to_all(copies, axis, split_axis=0, concat_axis=0, tiled=True)  16.9 us
    all_to_all x2, starting transfers between devices, prefix_over(): lax.all_to_all(copies, axis, split_axis=0, concat_axis=0, tiled=True)  10.5 us
    ppermute x1, starting transfers between devices, local(): lax.ppermute(to_south, 'lat', [(i + 1, i) for i in range(count - 1)])  6.96 us
    pallas_call x1, Pallas kernels, filter_rows(): pl.pallas_call(filter_kernel, out_shape=jax.ShapeDtypeStruct(values.shape...  3.36 us
    ppermute x1, starting transfers between devices, local(): lax.ppermute(to_north, 'lat', [(i, i + 1) for i in range(count - 1)])  1.92 us
    broadcast_in_dim x2, local copies, waits for them, and re-layouts, prefix_over(): copies = jnp.broadcast_to(value, (count, *value.shape))  1.34 us
    concatenate x1, other arithmetic, local(): to_north = jnp.concatenate([layer_mass, theta_field, surface], axis=0)  1.08 us
  transfers between devices with their start and end apart: 4, of which 2 were waited for; matrix products, arithmetic and copies ran while one was open for 9% of the time, Pallas kernels for 0%

profile of v13, /device:TPU:256, one launch (start us, length us, event | category | flops | bytes accessed | tf_op | source)
XLA Modules:
  0.0 51.8 jit_solution(4573471478415560103)
XLA Ops:
  0.6 0.7 %broadcast_in_dim.41 = f32[3,1,1152]{2,1,0:T(1,128)S(1)} reshape(f32[3,1152]{1,0:T(4,128)} %param.17) | data formatting | bytes 27648 | tf_op jit(solution)/shard_map/broadcast_in_dim | solution.py:127
  1.4 1.1 %select_maximum_fusion = (f32[9,8,1152]{2,1,0:T(8,128)S(1)}, f32[9,8,1152]{2,1,0:T(8,128)S(1)}) fusion(f32[3,1,1152]{2,1,0:T(1,128)S(1)} %broadcast_in_dim.41, f32[3,8,1152]{2,1,0:T(8,128)} %bitcast.74, f32[3,8,1152]{2,1,0:T(8,128)} %bitcast.65, f32[3,8,1152]{2,1,0:T(8,128)} %bitcast.84), kind=kLoop, calls=%fused_computation.2 | loop fusion | flops 414720 | bytes 1009152 | tf_op jit(solution)/shard_map/concatenate | solution.py:128
  2.5 1.9 %collective-permute-start.1 = (f32[9,8,1152]{2,1,0:T(8,128)S(1)}, f32[9,8,1152]{2,1,0:T(8,128)S(1)}, u32[]{:S(2)}, u32[]{:S(2)}) collective-permute-start(f32[9,8,1152]{2,1,0:T(8,128)S(1)} %get-tuple-element.21), channel_id=1, source_target_pairs={{0,8},{8,16},{16,24},{24,32},{32,40},{40,48},{48,56},{56,64},{64,7... | collective-permute-start | bytes 995336 | tf_op jit(solution)/shard_map/ppermute | solution.py:131
  4.4 7.0 %collective-permute-start = (f32[9,8,1152]{2,1,0:T(8,128)S(1)}, f32[9,8,1152]{2,1,0:T(8,128)S(1)}, u32[]{:S(2)}, u32[]{:S(2)}) collective-permute-start(f32[9,8,1152]{2,1,0:T(8,128)S(1)} %get-tuple-element.22), channel_id=1, source_target_pairs={{8,0},{16,8},{24,16},{32,24},{40,32},{48,40},{56,48},{64,56},{72,6... | collective-permute-start | bytes 995336 | tf_op jit(solution)/shard_map/ppermute | solution.py:132
  11.4 0.1 fusion.65
  11.5 0.1 fusion.67
  11.9 0.6 %copy-done.2 = f32[8,3,1152]{2,0,1:T(8,128)S(1)} copy-done((f32[8,3,1152]{2,0,1:T(8,128)S(1)}, f32[8,3,1152]{2,0,1:T(8,128)}, u32[]{:S(2)}) %copy-start.2) | copy-done | bytes 110616
  12.5 0.1 fusion.61
  12.6 0.1 fusion.63
  13.0 0.7 %gather_fusion = s32[13]{0:T(128)S(1)} fusion(s32[192]{0:T(256)S(1)} %copy-done, s32[1024]{0:T(1024)S(1)} %pad_clamp_fusion), kind=kCustom, calls=%fused_computation | custom fusion | bytes 156 | tf_op jit(solution)/shard_map/gather | solution.py:163
  13.7 0.7 %reshape_reshape.4.cut_ref = s32[104,1]{1,0:T(8,128)} reshape(s32[13,8]{1,0:T(8,128)S(1)} %broadcast_in_dim.47) | data formatting | bytes 832 | tf_op jit(solution)/shard_map/reshape;reshape | solution.py:105
  14.4 0.2 fusion.45
  14.8 0.7 %broadcast_in_dim.44 = f32[8,4,1152]{2,1,0:T(4,128)} broadcast(f32[4,1152]{1,0:T(4,128)S(1)} %get-tuple-element.24), dimensions={1,2} | broadcast | bytes 165888 | tf_op jit(solution)/shard_map/broadcast_in_dim | solution.py:111
  15.4 7.1 %all-to-all-start = ((f32[8,4,1152]{2,1,0:T(4,128)}), f32[8,4,1152]{2,1,0:T(4,128)S(1)}, u32[]{:S(2)}, u32[]{:S(2)}) async-start(f32[8,4,1152]{2,1,0:T(4,128)} %broadcast_in_dim.44), calls=%async_computation | async-start | bytes 294912 | tf_op jit(solution)/shard_map/all_to_all | solution.py:112
  22.5 0.1 reduce_window_sum.17
  22.8 9.0 %all-to-all-done = f32[8,4,1152]{2,1,0:T(4,128)S(1)} async-done(((f32[8,4,1152]{2,1,0:T(4,128)}), f32[8,4,1152]{2,1,0:T(4,128)S(1)}, u32[]{:S(2)}, u32[]{:S(2)}) %all-to-all-start) | async-done | bytes 147488 | tf_op jit(solution)/shard_map/all_to_all | solution.py:112
  31.8 0.1 select_reduce_fusion.1
  31.9 0.1 fusion.57
  32.1 0.7 %broadcast_in_dim.46 = f32[8,4,1152]{2,1,0:T(4,128)} broadcast(f32[4,1152]{1,0:T(4,128)S(1)} %get-tuple-element.9), dimensions={1,2} | broadcast | bytes 165888 | tf_op jit(solution)/shard_map/broadcast_in_dim | solution.py:111
  32.7 3.4 %all-to-all-start.1 = ((f32[8,4,1152]{2,1,0:T(4,128)}), f32[8,4,1152]{2,1,0:T(4,128)S(1)}, u32[]{:S(2)}, u32[]{:S(2)}) async-start(f32[8,4,1152]{2,1,0:T(4,128)} %broadcast_in_dim.46), calls=%async_computation.1 | async-start | bytes 294912 | tf_op jit(solution)/shard_map/all_to_all | solution.py:112
  36.1 0.2 rev.7
  36.3 0.1 reduce_window_sum.18
  36.5 0.2 rev.8
  36.6 0.8 %pad_maximum_fusion = f32[13,8,1152]{2,1,0:T(8,128)} fusion(f32[4,8,1152]{2,1,0:T(8,128)S(1)} %get-tuple-element.34, f32[3,8,1152]{2,1,0:T(8,128)S(1)} %fusion.45, f32[3,8,1152]{2,1,0:T(8,128)S(1)} %bitcast.86, f32[3,8,1152]{2,1,0:T(8,128)S(1)} %bitcast.87), kind=kLoop, calls=%fused_computation.1 | loop fusion | flops 359424 | bytes 958464 | tf_op jit(solution)/shard_map/concatenate | solution.py:159
  37.5 7.8 %all-to-all-done.1 = f32[8,4,1152]{2,1,0:T(4,128)S(1)} async-done(((f32[8,4,1152]{2,1,0:T(4,128)}), f32[8,4,1152]{2,1,0:T(4,128)S(1)}, u32[]{:S(2)}, u32[]{:S(2)}) %all-to-all-start.1) | async-done | bytes 147488 | tf_op jit(solution)/shard_map/all_to_all | solution.py:112
  45.3 0.1 select_reduce_fusion
  45.5 3.4 %shard_map.164 = f32[104,1152]{1,0:T(8,128)} custom-call(f32[104,1152]{1,0:T(8,128)} %bitcast.83, s32[104,1]{1,0:T(8,128)} %reshape_reshape.4.cut_ref, f32[9,128]{1,0:T(8,128)} %constant.60.clone.twc_ref, f32[9,128]{1,0:T(8,128)} %constant.61.clone.tws_ref, bf16[2,256,256]{2,1,0:T(8,128)(2,1)} %constant.78.fwd_ref, bf16[2,256,256]{2,1,0:T(8,128)(2,1)} %constant.85.inv_ref, ...), custom_call_target="tpu_custom_call" | custom-call | tf_op jit(solution)/shard_map/pallas_call | solution.py:102
  48.8 1.0 %slice_bitcast_fusion.1 = f32[3,8,1152]{2,1,0:T(8,128)S(1)} fusion(f32[104,1152]{1,0:T(8,128)} %shard_map.164), kind=kLoop, calls=%fused_computation.70 | loop fusion | bytes 221184 | tf_op jit(solution)/shard_map/slice | solution.py:168
  49.8 0.1 slice.304
  49.9 0.8 %fusion.52 = (f32[3,8,1152]{2,1,0:T(8,128)S(1)}, f32[8,3,1152]{2,0,1:T(8,128)}) fusion(f32[3,8,1151]{2,1,0:T(8,128)S(1)} %get-tuple-element.31, f32[3,8,1]{2,1,0:T(8,128)S(1)} %get-tuple-element.33, f32[3,8,1150]{2,1,0:T(8,128)S(1)} %get-tuple-element.27, f32[3,8,2]{2,1,0:T(8,128)S(1)} %get-tuple-element.29, f32[3,8,1]{2,1,0:T(8,128)S(1)} %get-tuple-element.32, ...), kind=kLoop, calls=%fused_computation.95 | loop fusion | flops 552960 | bytes 1437696 | tf_op jit(solution)/shard_map/mul | solution.py:173
  50.7 0.1 slice.318
  51.0 0.8 %fusion.38 = (f32[8,3,1152]{2,0,1:T(8,128)}, f32[8,3,1152]{2,0,1:T(8,128)}, f32[8,3,1152]{2,0,1:T(8,128)}, f32[8,3,1152]{2,0,1:T(8,128)}) fusion(f32[104,1152]{1,0:T(8,128)S(1)} %copy-done.3, f32[4,8,1152]{2,1,0:T(8,128)S(1)} %multiply_add_fusion, f32[3]{0:T(128)S(1)} %compare_convert_fusion, f32[3,8,1151]{2,1,0:T(8,128)S(1)} %slice.241, ...), kind=kLoop, calls=%fused_computation.74 | loop fusion | flops 414720 | bytes 1658892 | tf_op jit(solution)/shard_map/transpose | solution.py:183
  (45 shorter events, 1.0 us)
Async XLA Ops:
  0.6 12.3 %copy-start = (s32[192]{0:T(256)S(1)}, s32[192]{0:T(256)}, u32[]{:S(2)}) copy-start(s32[192]{0:T(256)} %param.18) | copy-start | bytes 2308
  1.4 10.0 %copy-start.1 = (f32[8,3,1152]{2,0,1:T(8,128)S(1)}, f32[8,3,1152]{2,0,1:T(8,128)}, u32[]{:S(2)}) copy-start(f32[8,3,1152]{2,0,1:T(8,128)} %param.15) | copy-start | bytes 331780
  2.5 12.2 %collective-permute-start.1 = (f32[9,8,1152]{2,1,0:T(8,128)S(1)}, f32[9,8,1152]{2,1,0:T(8,128)S(1)}, u32[]{:S(2)}, u32[]{:S(2)}) collective-permute-start(f32[9,8,1152]{2,1,0:T(8,128)S(1)} %get-tuple-element.21), channel_id=1, source_target_pairs={{0,8},{8,16},{16,24},{24,32},{32,40},{40,48},{48,56},{56,64},{64,7... | collective-permute-start | bytes 995336 | tf_op jit(solution)/shard_map/ppermute | solution.py:131
  4.4 18.3 %collective-permute-start = (f32[9,8,1152]{2,1,0:T(8,128)S(1)}, f32[9,8,1152]{2,1,0:T(8,128)S(1)}, u32[]{:S(2)}, u32[]{:S(2)}) collective-permute-start(f32[9,8,1152]{2,1,0:T(8,128)S(1)} %get-tuple-element.22), channel_id=1, source_target_pairs={{8,0},{16,8},{24,16},{32,24},{40,32},{48,40},{56,48},{64,56},{72,6... | collective-permute-start | bytes 995336 | tf_op jit(solution)/shard_map/ppermute | solution.py:132
  11.6 0.9 %copy-start.2 = (f32[8,3,1152]{2,0,1:T(8,128)S(1)}, f32[8,3,1152]{2,0,1:T(8,128)}, u32[]{:S(2)}) copy-start(f32[8,3,1152]{2,0,1:T(8,128)} %param.16) | copy-start | bytes 331780
  13.0 1.5 %copy-start.5 = (f32[8,3,1152]{2,0,1:T(8,128)S(1)}, f32[8,3,1152]{2,0,1:T(8,128)}, u32[]{:S(2)}) copy-start(f32[8,3,1152]{2,0,1:T(8,128)} %param.13) | copy-start | bytes 331780
  15.4 16.4 %all-to-all-start = ((f32[8,4,1152]{2,1,0:T(4,128)}), f32[8,4,1152]{2,1,0:T(4,128)S(1)}, u32[]{:S(2)}, u32[]{:S(2)}) async-start(f32[8,4,1152]{2,1,0:T(4,128)} %broadcast_in_dim.44), calls=%async_computation | async-start | bytes 294912 | tf_op jit(solution)/shard_map/all_to_all | solution.py:112
  22.7 9.2 %copy-start.4 = (f32[8,3,1152]{2,0,1:T(8,128)S(1)}, f32[8,3,1152]{2,0,1:T(8,128)}, u32[]{:S(2)}) copy-start(f32[8,3,1152]{2,0,1:T(8,128)} %param.14) | copy-start | bytes 331780
  32.7 12.6 %all-to-all-start.1 = ((f32[8,4,1152]{2,1,0:T(4,128)}), f32[8,4,1152]{2,1,0:T(4,128)S(1)}, u32[]{:S(2)}, u32[]{:S(2)}) async-start(f32[8,4,1152]{2,1,0:T(4,128)} %broadcast_in_dim.46), calls=%async_computation.1 | async-start | bytes 294912 | tf_op jit(solution)/shard_map/all_to_all | solution.py:112
  37.5 7.9 %copy-start.6 = (f32[3,1152]{1,0:T(4,128)S(1)}, f32[3,1152]{1,0:T(4,128)}, u32[]{:S(2)}) copy-start(f32[3,1152]{1,0:T(4,128)} %param.17) | copy-start | bytes 41476
  48.8 1.1 %copy-start.3 = (f32[104,1152]{1,0:T(8,128)S(1)}, f32[104,1152]{1,0:T(8,128)}, u32[]{:S(2)}) copy-start(f32[104,1152]{1,0:T(8,128)} %shard_map.164) | copy-start | bytes 1437700

commit v14 on v12

--- a/solution.py
+++ b/solution.py
@@ -66,10 +66,12 @@
     c9, s9 = fft_tables(length)[:2]
     half = rows // 2 + 1
     parts = [x_ref[:, n * lanes : (n + 1) * lanes] for n in range(rows)]
+    pairs = [parts[n] + parts[rows - n] for n in range(1, half)]
+    gaps = [parts[n] - parts[rows - n] for n in range(1, half)]
     pieces = []
     for k in range(half):
-        real_a = sum(float(c9[k, n]) * parts[n] for n in range(rows))
-        imag_a = sum(float(-s9[k, n]) * parts[n] for n in range(1, rows))
+        real_a = parts[0] + sum(float(c9[k, n]) * pairs[n - 1] for n in range(1, half))
+        imag_a = sum(float(-s9[k, n]) * gaps[n - 1] for n in range(1, half))
         twc = twc_ref[k : k + 1, :]
         tws = tws_ref[k : k + 1, :]
         pieces.append(
@@ -89,11 +91,16 @@
         imag_c = back[k * count : (k + 1) * count, lanes:]
         real_d.append(real_c * twc - imag_c * tws)
         imag_d.append(imag_c * twc + real_c * tws)
-    for n in range(rows):
-        o_ref[:, n * lanes : (n + 1) * lanes] = float(1.0 / length) * real_d[0] + sum(
-            float(2.0 * c9[k, n] / length) * real_d[k] - float(2.0 * s9[k, n] / length) * imag_d[k]
-            for k in range(1, half)
+    base = float(1.0 / length) * real_d[0]
+    for n in range(half):
+        even = base + sum(float(2.0 * c9[k, n] / length) * real_d[k] for k in range(1, half))
+        o_ref[:, n * lanes : (n + 1) * lanes] = even - sum(
+            float(2.0 * s9[k, n] / length) * imag_d[k] for k in range(1, half)
         )
+        if n > 0:
+            o_ref[:, (rows - n) * lanes : (rows - n + 1) * lanes] = even + sum(
+                float(2.0 * s9[k, n] / length) * imag_d[k] for k in range(1, half)
+            )
 
 
 def filter_rows(values, cuts):

time: 51.9 us -> 51.8 us (level)
  no operation moved by 1% of the time
where the time goes in v14:
time: 51.8 us; the launch traced here: 51.3 us
  starting transfers between devices  19.4 us (37%)
  waiting for transfers between devices  15.9 us (31%)
  local copies, waits for them, and re-layouts  7.34 us (14%)
  other arithmetic  4.61 us (9%)
  Pallas kernels  3.19 us (6%)
  between operations  0.93 us (2%)
    all_to_all x2, waiting for transfers between devices, prefix_over(): lax.all_to_all(copies, axis, split_axis=0, concat_axis=0, tiled=True)  15.4 us
    all_to_all x2, starting transfers between devices, prefix_over(): lax.all_to_all(copies, axis, split_axis=0, concat_axis=0, tiled=True)  10.5 us
    ppermute x1, starting transfers between devices, local(): lax.ppermute(to_south, 'lat', [(i + 1, i) for i in range(count - 1)])  6.96 us
    pallas_call x1, Pallas kernels, filter_rows(): pl.pallas_call(filter_kernel, out_shape=jax.ShapeDtypeStruct(values.shape...  3.19 us
    ppermute x1, starting transfers between devices, local(): lax.ppermute(to_north, 'lat', [(i, i + 1) for i in range(count - 1)])  1.92 us
    unnamed x12, local copies, waits for them, and re-layouts  1.4 us
    broadcast_in_dim x2, local copies, waits for them, and re-layouts, prefix_over(): copies = jnp.broadcast_to(value, (count, *value.shape))  1.35 us
  transfers between devices with their start and end apart: 4, of which 3 were waited for; matrix products, arithmetic and copies ran while one was open for 9% of the time, Pallas kernels for 0%

profile of v14, /device:TPU:256, one launch (start us, length us, event | category | flops | bytes accessed | tf_op | source)
XLA Modules:
  0.0 51.3 jit_solution(13650322061540504606)
XLA Ops:
  0.7 0.8 %broadcast_in_dim.43 = f32[3,8,1152]{2,1,0:T(8,128)S(1)} broadcast(f32[3,1152]{1,0:T(4,128)} %param.17), dimensions={0,2} | broadcast | bytes 124416 | tf_op jit(solution)/shard_map/broadcast_in_dim | solution.py:134
  1.4 0.1 copy-done.1
  1.6 1.0 %pad_maximum_fusion.3 = (f32[9,8,1152]{2,1,0:T(8,128)S(1)}, f32[9,8,1152]{2,1,0:T(8,128)S(1)}) fusion(f32[3,8,1152]{2,1,0:T(8,128)S(1)} %broadcast_in_dim.43, f32[3,8,1152]{2,1,0:T(8,128)} %bitcast.72, f32[3,8,1152]{2,1,0:T(8,128)S(1)} %bitcast.63, f32[3,8,1152]{2,1,0:T(8,128)} %bitcast.82), kind=kLoop, calls=%fused_computation.4 | loop fusion | flops 248832 | bytes 1105920 | tf_op jit(solution)/shard_map/concatenate | solution.py:135
  2.6 1.9 %collective-permute-start.1 = (f32[9,8,1152]{2,1,0:T(8,128)S(1)}, f32[9,8,1152]{2,1,0:T(8,128)S(1)}, u32[]{:S(2)}, u32[]{:S(2)}) collective-permute-start(f32[9,8,1152]{2,1,0:T(8,128)S(1)} %get-tuple-element.22), channel_id=1, source_target_pairs={{0,8},{8,16},{16,24},{24,32},{32,40},{40,48},{48,56},{56,64},{64,7... | collective-permute-start | bytes 995336 | tf_op jit(solution)/shard_map/ppermute | solution.py:138
  4.5 7.0 %collective-permute-start = (f32[9,8,1152]{2,1,0:T(8,128)S(1)}, f32[9,8,1152]{2,1,0:T(8,128)S(1)}, u32[]{:S(2)}, u32[]{:S(2)}) collective-permute-start(f32[9,8,1152]{2,1,0:T(8,128)S(1)} %get-tuple-element.23), channel_id=1, source_target_pairs={{8,0},{16,8},{24,16},{32,24},{40,32},{48,40},{56,48},{64,56},{72,6... | collective-permute-start | bytes 995336 | tf_op jit(solution)/shard_map/ppermute | solution.py:139
  11.5 0.1 fusion.67
  11.6 0.1 fusion.69
  12.0 0.6 %copy-done.2 = f32[8,3,1152]{2,0,1:T(8,128)S(1)} copy-done((f32[8,3,1152]{2,0,1:T(8,128)S(1)}, f32[8,3,1152]{2,0,1:T(8,128)}, u32[]{:S(2)}) %copy-start.2) | copy-done | bytes 110616
  12.7 0.1 fusion.65
  13.0 0.6 %copy-done.5 = f32[8,3,1152]{2,0,1:T(8,128)S(1)} copy-done((f32[8,3,1152]{2,0,1:T(8,128)S(1)}, f32[8,3,1152]{2,0,1:T(8,128)}, u32[]{:S(2)}) %copy-start.5) | copy-done | bytes 110616
  13.6 0.2 fusion.47
  13.8 0.5 collective-permute-done.1
  14.4 0.7 %broadcast_in_dim.46 = f32[8,4,1152]{2,1,0:T(4,128)} broadcast(f32[4,1152]{1,0:T(4,128)S(1)} %get-tuple-element.25), dimensions={1,2} | broadcast | bytes 165888 | tf_op jit(solution)/shard_map/broadcast_in_dim | solution.py:118
  15.1 7.1 %all-to-all-start = ((f32[8,4,1152]{2,1,0:T(4,128)}), f32[8,4,1152]{2,1,0:T(4,128)S(1)}, u32[]{:S(2)}, u32[]{:S(2)}) async-start(f32[8,4,1152]{2,1,0:T(4,128)} %broadcast_in_dim.46), calls=%async_computation | async-start | bytes 294912 | tf_op jit(solution)/shard_map/all_to_all | solution.py:119
  22.2 0.1 reduce_window_sum.17
  22.4 9.0 %all-to-all-done = f32[8,4,1152]{2,1,0:T(4,128)S(1)} async-done(((f32[8,4,1152]{2,1,0:T(4,128)}), f32[8,4,1152]{2,1,0:T(4,128)S(1)}, u32[]{:S(2)}, u32[]{:S(2)}) %all-to-all-start) | async-done | bytes 147488 | tf_op jit(solution)/shard_map/all_to_all | solution.py:119
  31.4 0.1 select_reduce_fusion.1
  31.6 0.1 fusion.59
  31.7 0.7 %broadcast_in_dim.48 = f32[8,4,1152]{2,1,0:T(4,128)} broadcast(f32[4,1152]{1,0:T(4,128)S(1)} %get-tuple-element.9), dimensions={1,2} | broadcast | bytes 165888 | tf_op jit(solution)/shard_map/broadcast_in_dim | solution.py:118
  32.4 3.4 %all-to-all-start.1 = ((f32[8,4,1152]{2,1,0:T(4,128)}), f32[8,4,1152]{2,1,0:T(4,128)S(1)}, u32[]{:S(2)}, u32[]{:S(2)}) async-start(f32[8,4,1152]{2,1,0:T(4,128)} %broadcast_in_dim.48), calls=%async_computation.1 | async-start | bytes 294912 | tf_op jit(solution)/shard_map/all_to_all | solution.py:119
  35.9 0.7 %gather_fusion = s32[13]{0:T(128)S(1)} fusion(s32[192]{0:T(256)S(1)} %copy-done, s32[1024]{0:T(1024)S(1)} %pad_clamp_fusion), kind=kCustom, calls=%fused_computation | custom fusion | bytes 156 | tf_op jit(solution)/shard_map/gather | solution.py:168
  36.6 0.7 %reshape_reshape.4.cut_ref = s32[104,1]{1,0:T(8,128)} reshape(s32[13,8]{1,0:T(8,128)S(1)} %broadcast_in_dim.49) | data formatting | bytes 832 | tf_op jit(solution)/shard_map/reshape;reshape | solution.py:112
  37.3 0.1 rev.7
  37.5 0.1 reduce_window_sum.18
  37.6 0.2 rev.8
  37.8 0.8 %pad_maximum_fusion = f32[13,8,1152]{2,1,0:T(8,128)} fusion(f32[4,8,1152]{2,1,0:T(8,128)S(1)} %get-tuple-element.35, f32[3,8,1152]{2,1,0:T(8,128)S(1)} %fusion.47, f32[3,8,1152]{2,1,0:T(8,128)S(1)} %bitcast.84, f32[3,8,1152]{2,1,0:T(8,128)S(1)} %bitcast.85), kind=kLoop, calls=%fused_computation.1 | loop fusion | flops 359424 | bytes 958464 | tf_op jit(solution)/shard_map/concatenate | solution.py:164
  38.6 6.3 %all-to-all-done.1 = f32[8,4,1152]{2,1,0:T(4,128)S(1)} async-done(((f32[8,4,1152]{2,1,0:T(4,128)}), f32[8,4,1152]{2,1,0:T(4,128)S(1)}, u32[]{:S(2)}, u32[]{:S(2)}) %all-to-all-start.1) | async-done | bytes 147488 | tf_op jit(solution)/shard_map/all_to_all | solution.py:119
  44.9 0.1 select_reduce_fusion
  45.1 3.2 %shard_map.164 = f32[104,1152]{1,0:T(8,128)} custom-call(f32[104,1152]{1,0:T(8,128)} %bitcast.81, s32[104,1]{1,0:T(8,128)} %reshape_reshape.4.cut_ref, f32[9,128]{1,0:T(8,128)} %constant.58.clone.twc_ref, f32[9,128]{1,0:T(8,128)} %constant.59.clone.tws_ref, bf16[2,256,256]{2,1,0:T(8,128)(2,1)} %constant.74.fwd_ref, bf16[2,256,256]{2,1,0:T(8,128)(2,1)} %constant.81.inv_ref, ...), custom_call_target="tpu_custom_call" | custom-call | tf_op jit(solution)/shard_map/pallas_call | solution.py:109
  48.3 1.0 %slice_bitcast_fusion.1 = f32[3,8,1152]{2,1,0:T(8,128)S(1)} fusion(f32[104,1152]{1,0:T(8,128)} %shard_map.164), kind=kLoop, calls=%fused_computation.71 | loop fusion | bytes 221184 | tf_op jit(solution)/shard_map/slice | solution.py:173
  49.4 0.8 %fusion.54 = (f32[3,8,1152]{2,1,0:T(8,128)S(1)}, f32[8,3,1152]{2,0,1:T(8,128)}) fusion(f32[3,8,1151]{2,1,0:T(8,128)S(1)} %get-tuple-element.32, f32[3,8,1]{2,1,0:T(8,128)S(1)} %get-tuple-element.34, f32[3,8,1150]{2,1,0:T(8,128)S(1)} %get-tuple-element.28, f32[3,8,2]{2,1,0:T(8,128)S(1)} %get-tuple-element.30, f32[3,8,1]{2,1,0:T(8,128)S(1)} %get-tuple-element.33, ...), kind=kLoop, calls=%fused_computation.96 | loop fusion | flops 552960 | bytes 1437696 | tf_op jit(solution)/shard_map/mul | solution.py:178
  50.5 0.8 %fusion.40 = (f32[8,3,1152]{2,0,1:T(8,128)}, f32[8,3,1152]{2,0,1:T(8,128)}, f32[8,3,1152]{2,0,1:T(8,128)}, f32[8,3,1152]{2,0,1:T(8,128)}) fusion(f32[104,1152]{1,0:T(8,128)S(1)} %copy-done.3, f32[4,8,1152]{2,1,0:T(8,128)S(1)} %fusion.28, f32[3]{0:T(128)S(1)} %compare_convert_fusion, f32[3,8,1151]{2,1,0:T(8,128)S(1)} %slice.241, f32[3,8,1]{2,1,0:T(8,128)S(1)} %slice.240, ...), kind=kLoop, calls=%fused_computation.75 | loop fusion | flops 414720 | bytes 1658892 | tf_op jit(solution)/shard_map/transpose | solution.py:188
  (41 shorter events, 1.3 us)
Async XLA Ops:
  0.6 35.2 %copy-start = (s32[192]{0:T(256)S(1)}, s32[192]{0:T(256)}, u32[]{:S(2)}) copy-start(s32[192]{0:T(256)} %param.18) | copy-start | bytes 2308
  0.6 0.9 %copy-start.1 = (f32[8,3,1152]{2,0,1:T(8,128)S(1)}, f32[8,3,1152]{2,0,1:T(8,128)}, u32[]{:S(2)}) copy-start(f32[8,3,1152]{2,0,1:T(8,128)} %param.15) | copy-start | bytes 331780
  2.6 11.8 %collective-permute-start.1 = (f32[9,8,1152]{2,1,0:T(8,128)S(1)}, f32[9,8,1152]{2,1,0:T(8,128)S(1)}, u32[]{:S(2)}, u32[]{:S(2)}) collective-permute-start(f32[9,8,1152]{2,1,0:T(8,128)S(1)} %get-tuple-element.22), channel_id=1, source_target_pairs={{0,8},{8,16},{16,24},{24,32},{32,40},{40,48},{48,56},{56,64},{64,7... | collective-permute-start | bytes 995336 | tf_op jit(solution)/shard_map/ppermute | solution.py:138
  4.5 17.8 %collective-permute-start = (f32[9,8,1152]{2,1,0:T(8,128)S(1)}, f32[9,8,1152]{2,1,0:T(8,128)S(1)}, u32[]{:S(2)}, u32[]{:S(2)}) collective-permute-start(f32[9,8,1152]{2,1,0:T(8,128)S(1)} %get-tuple-element.23), channel_id=1, source_target_pairs={{8,0},{16,8},{24,16},{32,24},{40,32},{48,40},{56,48},{64,56},{72,6... | collective-permute-start | bytes 995336 | tf_op jit(solution)/shard_map/ppermute | solution.py:139
  11.7 0.9 %copy-start.2 = (f32[8,3,1152]{2,0,1:T(8,128)S(1)}, f32[8,3,1152]{2,0,1:T(8,128)}, u32[]{:S(2)}) copy-start(f32[8,3,1152]{2,0,1:T(8,128)} %param.16) | copy-start | bytes 331780
  12.7 0.9 %copy-start.5 = (f32[8,3,1152]{2,0,1:T(8,128)S(1)}, f32[8,3,1152]{2,0,1:T(8,128)}, u32[]{:S(2)}) copy-start(f32[8,3,1152]{2,0,1:T(8,128)} %param.13) | copy-start | bytes 331780
  15.1 16.4 %all-to-all-start = ((f32[8,4,1152]{2,1,0:T(4,128)}), f32[8,4,1152]{2,1,0:T(4,128)S(1)}, u32[]{:S(2)}, u32[]{:S(2)}) async-start(f32[8,4,1152]{2,1,0:T(4,128)} %broadcast_in_dim.46), calls=%async_computation | async-start | bytes 294912 | tf_op jit(solution)/shard_map/all_to_all | solution.py:119
  22.4 9.2 %copy-start.4 = (f32[8,3,1152]{2,0,1:T(8,128)S(1)}, f32[8,3,1152]{2,0,1:T(8,128)}, u32[]{:S(2)}) copy-start(f32[8,3,1152]{2,0,1:T(8,128)} %param.14) | copy-start | bytes 331780
  32.4 12.6 %all-to-all-start.1 = ((f32[8,4,1152]{2,1,0:T(4,128)}), f32[8,4,1152]{2,1,0:T(4,128)S(1)}, u32[]{:S(2)}, u32[]{:S(2)}) async-start(f32[8,4,1152]{2,1,0:T(4,128)} %broadcast_in_dim.48), calls=%async_computation.1 | async-start | bytes 294912 | tf_op jit(solution)/shard_map/all_to_all | solution.py:119
  48.3 1.1 %copy-start.3 = (f32[104,1152]{1,0:T(8,128)S(1)}, f32[104,1152]{1,0:T(8,128)}, u32[]{:S(2)}) copy-start(f32[104,1152]{1,0:T(8,128)} %shard_map.164) | copy-start | bytes 1437700

commit v15 on v14

--- a/solution.py
+++ b/solution.py
@@ -60,7 +60,7 @@
     return product(high, table_high) + (product(high, table_low) + product(low, table_high))
 
 
-def filter_kernel(x_ref, cut_ref, twc_ref, tws_ref, fwd_ref, inv_ref, fold_ref, o_ref):
+def filter_kernel(x_ref, cut_ref, twc_ref, tws_ref, fwd_ref, inv_ref, fold_ref, *out_refs):
     rows, lanes = FACTOR_ROWS, FACTOR_LANES
     count, length = x_ref.shape
     c9, s9 = fft_tables(length)[:2]
@@ -92,23 +92,30 @@
         real_d.append(real_c * twc - imag_c * tws)
         imag_d.append(imag_c * twc + real_c * tws)
     base = float(1.0 / length) * real_d[0]
+
+    def store(n, value):
+        start = 0
+        for ref in out_refs:
+            size = ref.shape[0]
+            ref[:, n * lanes : (n + 1) * lanes] = value[start : start + size]
+            start += size
+
     for n in range(half):
         even = base + sum(float(2.0 * c9[k, n] / length) * real_d[k] for k in range(1, half))
-        o_ref[:, n * lanes : (n + 1) * lanes] = even - sum(
-            float(2.0 * s9[k, n] / length) * imag_d[k] for k in range(1, half)
-        )
+        store(n, even - sum(float(2.0 * s9[k, n] / length) * imag_d[k] for k in range(1, half)))
         if n > 0:
-            o_ref[:, (rows - n) * lanes : (rows - n + 1) * lanes] = even + sum(
-                float(2.0 * s9[k, n] / length) * imag_d[k] for k in range(1, half)
+            store(
+                rows - n,
+                even + sum(float(2.0 * s9[k, n] / length) * imag_d[k] for k in range(1, half)),
             )
 
 
-def filter_rows(values, cuts):
+def filter_rows(values, cuts, sizes):
     count, length = values.shape
     _, _, twc, tws, forward, inverse, folded = fft_tables(length)
     return pl.pallas_call(
         filter_kernel,
-        out_shape=jax.ShapeDtypeStruct(values.shape, values.dtype),
+        out_shape=tuple(jax.ShapeDtypeStruct((size, length), values.dtype) for size in sizes),
     )(values, cuts.reshape(count, 1), jnp.asarray(twc), jnp.asarray(tws), split_table(forward),
       split_table(inverse), jnp.asarray(folded))
 
@@ -167,11 +174,11 @@
     row_cuts = jnp.broadcast_to(
         filter_cutoff[jnp.minimum(cut_rows, nlat_all - 1)][:, None], fields.shape[:2]
     ).reshape(-1)
-    smooth = filter_rows(fields.reshape(-1, length), row_cuts).reshape(fields.shape)
-    east_smooth = smooth[:rows]
-    north_smooth = smooth[rows : 2 * rows]
-    east_flux = smooth[2 * rows : 3 * rows]
-    north_full = smooth[3 * rows :]
+    sizes = (rows * levels, rows * levels, rows * levels, (rows + 1) * levels)
+    east_smooth, north_smooth, east_flux, north_full = (
+        v.reshape(-1, levels, length)
+        for v in filter_rows(fields.reshape(-1, length), row_cuts, sizes)
+    )
     new_mass = layer_mass - TIME_STEP * (
         jnp.roll(east_flux, -1, -1) - east_flux + (north_full[1:] - north_full[:-1])
     )

time: 51.8 us -> 54.5 us (1.052)
  local copies, waits for them, and re-layouts: 7.34 us -> 8.47 us
  other arithmetic: 4.61 us -> 5.58 us
  waiting for transfers between devices: 15.9 us -> 16.5 us
    unnamed x12 -> x22, local copies, waits for them, and re-layouts: 1.4 us -> 3.47 us
    slice x1 -> x0, local copies, waits for them, and re-layouts: 0.98 us -> none  [local(): east_flux = smooth[2 * rows:3 * rows]]
    transpose x1 -> x2, other arithmetic: 0.85 us -> 1.56 us  [local(): return tuple((jnp.transpose(v, (1, 0, 2)) for v in outputs))]
    ppermute x1, waiting for transfers between devices: 0.49 us -> 1.09 us  [local(): lax.ppermute(to_north, 'lat', [(i, i + 1) for i in range(count - 1)])]
where the time goes in v15:
time: 54.5 us; the launch traced here: 53.9 us
  starting transfers between devices  19.4 us (36%)
  waiting for transfers between devices  16.5 us (30%)
  local copies, waits for them, and re-layouts  8.47 us (16%)
  other arithmetic  5.58 us (10%)
  Pallas kernels  3.12 us (6%)
  between operations  0.95 us (2%)
    all_to_all x2, waiting for transfers between devices, prefix_over(): lax.all_to_all(copies, axis, split_axis=0, concat_axis=0, tiled=True)  15.4 us
    all_to_all x2, starting transfers between devices, prefix_over(): lax.all_to_all(copies, axis, split_axis=0, concat_axis=0, tiled=True)  10.5 us
    ppermute x1, starting transfers between devices, local(): lax.ppermute(to_south, 'lat', [(i + 1, i) for i in range(count - 1)])  6.96 us
    unnamed x22, local copies, waits for them, and re-layouts  3.47 us
    pallas_call x1, Pallas kernels, filter_rows(): pl.pallas_call(filter_kernel, out_shape=tuple((jax.ShapeDtypeStruct((size...  3.12 us
    ppermute x1, starting transfers between devices, local(): lax.ppermute(to_north, 'lat', [(i, i + 1) for i in range(count - 1)])  1.92 us
    transpose x2, other arithmetic, local(): return tuple((jnp.transpose(v, (1, 0, 2)) for v in outputs))  1.56 us
    broadcast_in_dim x2, local copies, waits for them, and re-layouts, prefix_over(): copies = jnp.broadcast_to(value, (count, *value.shape))  1.38 us
  transfers between devices with their start and end apart: 4, of which 3 were waited for; matrix products, arithmetic and copies ran while one was open for 9% of the time, Pallas kernels for 0%

profile of v15, /device:TPU:256, one launch (start us, length us, event | category | flops | bytes accessed | tf_op | source)
XLA Modules:
  0.0 53.9 jit_solution(7990918803548248924)
XLA Ops:
  0.7 0.8 %broadcast_in_dim.43 = f32[3,8,1152]{2,1,0:T(8,128)S(1)} broadcast(f32[3,1152]{1,0:T(4,128)} %param.17), dimensions={0,2} | broadcast | bytes 124416 | tf_op jit(solution)/shard_map/broadcast_in_dim | solution.py:141
  1.4 0.1 copy-done.1
  1.6 1.0 %pad_maximum_fusion.3 = (f32[9,8,1152]{2,1,0:T(8,128)S(1)}, f32[9,8,1152]{2,1,0:T(8,128)S(1)}) fusion(f32[3,8,1152]{2,1,0:T(8,128)S(1)} %broadcast_in_dim.43, f32[3,8,1152]{2,1,0:T(8,128)S(1)} %bitcast.44, f32[3,8,1152]{2,1,0:T(8,128)} %bitcast.53, f32[3,8,1152]{2,1,0:T(8,128)} %bitcast.65), kind=kLoop, calls=%fused_computation.4 | loop fusion | flops 248832 | bytes 1105920 | tf_op jit(solution)/shard_map/concatenate | solution.py:142
  2.6 1.9 %collective-permute-start.1 = (f32[9,8,1152]{2,1,0:T(8,128)S(1)}, f32[9,8,1152]{2,1,0:T(8,128)S(1)}, u32[]{:S(2)}, u32[]{:S(2)}) collective-permute-start(f32[9,8,1152]{2,1,0:T(8,128)S(1)} %get-tuple-element.26), channel_id=1, source_target_pairs={{0,8},{8,16},{16,24},{24,32},{32,40},{40,48},{48,56},{56,64},{64,7... | collective-permute-start | bytes 995336 | tf_op jit(solution)/shard_map/ppermute | solution.py:145
  4.5 7.0 %collective-permute-start = (f32[9,8,1152]{2,1,0:T(8,128)S(1)}, f32[9,8,1152]{2,1,0:T(8,128)S(1)}, u32[]{:S(2)}, u32[]{:S(2)}) collective-permute-start(f32[9,8,1152]{2,1,0:T(8,128)S(1)} %get-tuple-element.27), channel_id=1, source_target_pairs={{8,0},{16,8},{24,16},{32,24},{40,32},{48,40},{56,48},{64,56},{72,6... | collective-permute-start | bytes 995336 | tf_op jit(solution)/shard_map/ppermute | solution.py:146
  12.4 0.6 %copy-done.8 = f32[8,3,1152]{2,0,1:T(8,128)S(1)} copy-done((f32[8,3,1152]{2,0,1:T(8,128)S(1)}, f32[8,3,1152]{2,0,1:T(8,128)}, u32[]{:S(2)}) %copy-start.8) | copy-done | bytes 110616
  13.0 0.2 fusion.37
  13.3 1.1 %collective-permute-done.1 = f32[9,8,1152]{2,1,0:T(8,128)S(1)} collective-permute-done((f32[9,8,1152]{2,1,0:T(8,128)S(1)}, f32[9,8,1152]{2,1,0:T(8,128)S(1)}, u32[]{:S(2)}, u32[]{:S(2)}) %collective-permute-start.1) | collective-permute-done | bytes 331808 | tf_op jit(solution)/shard_map/ppermute | solution.py:145
  14.4 0.7 %broadcast_in_dim.46 = f32[8,4,1152]{2,1,0:T(4,128)} broadcast(f32[4,1152]{1,0:T(4,128)S(1)} %get-tuple-element.31), dimensions={1,2} | broadcast | bytes 165888 | tf_op jit(solution)/shard_map/broadcast_in_dim | solution.py:125
  15.1 7.1 %all-to-all-start = ((f32[8,4,1152]{2,1,0:T(4,128)}), f32[8,4,1152]{2,1,0:T(4,128)S(1)}, u32[]{:S(2)}, u32[]{:S(2)}) async-start(f32[8,4,1152]{2,1,0:T(4,128)} %broadcast_in_dim.46), calls=%async_computation | async-start | bytes 294912 | tf_op jit(solution)/shard_map/all_to_all | solution.py:126
  22.2 0.1 reduce_window_sum.17
  22.4 9.0 %all-to-all-done = f32[8,4,1152]{2,1,0:T(4,128)S(1)} async-done(((f32[8,4,1152]{2,1,0:T(4,128)}), f32[8,4,1152]{2,1,0:T(4,128)S(1)}, u32[]{:S(2)}, u32[]{:S(2)}) %all-to-all-start) | async-done | bytes 147488 | tf_op jit(solution)/shard_map/all_to_all | solution.py:126
  31.5 0.1 select_reduce_fusion.1
  31.6 0.1 fusion.57
  31.7 0.7 %broadcast_in_dim.48 = f32[8,4,1152]{2,1,0:T(4,128)} broadcast(f32[4,1152]{1,0:T(4,128)S(1)} %get-tuple-element.17), dimensions={1,2} | broadcast | bytes 165888 | tf_op jit(solution)/shard_map/broadcast_in_dim | solution.py:125
  32.4 3.4 %all-to-all-start.1 = ((f32[8,4,1152]{2,1,0:T(4,128)}), f32[8,4,1152]{2,1,0:T(4,128)S(1)}, u32[]{:S(2)}, u32[]{:S(2)}) async-start(f32[8,4,1152]{2,1,0:T(4,128)} %broadcast_in_dim.48), calls=%async_computation.1 | async-start | bytes 294912 | tf_op jit(solution)/shard_map/all_to_all | solution.py:126
  35.9 0.7 %gather_fusion = s32[13]{0:T(128)S(1)} fusion(s32[192]{0:T(256)S(1)} %copy-done, s32[1024]{0:T(1024)S(1)} %pad_clamp_fusion), kind=kCustom, calls=%fused_computation | custom fusion | bytes 156 | tf_op jit(solution)/shard_map/gather | solution.py:175
  36.6 0.7 %reshape_reshape.4.cut_ref = s32[104,1]{1,0:T(8,128)} reshape(s32[13,8]{1,0:T(8,128)S(1)} %broadcast_in_dim.49) | data formatting | bytes 832 | tf_op jit(solution)/shard_map/reshape;reshape | solution.py:119
  37.4 0.1 rev.7
  37.5 0.1 reduce_window_sum.18
  37.6 0.2 rev.8
  37.8 0.8 %pad_maximum_fusion = f32[13,8,1152]{2,1,0:T(8,128)} fusion(f32[4,8,1152]{2,1,0:T(8,128)S(1)} %get-tuple-element.43, f32[3,8,1152]{2,1,0:T(8,128)S(1)} %fusion.37, f32[3,8,1152]{2,1,0:T(8,128)S(1)} %bitcast.67, f32[3,8,1152]{2,1,0:T(8,128)S(1)} %bitcast.68), kind=kLoop, calls=%fused_computation.1 | loop fusion | flops 359424 | bytes 958464 | tf_op jit(solution)/shard_map/concatenate | solution.py:171
  38.6 6.3 %all-to-all-done.1 = f32[8,4,1152]{2,1,0:T(4,128)S(1)} async-done(((f32[8,4,1152]{2,1,0:T(4,128)}), f32[8,4,1152]{2,1,0:T(4,128)S(1)}, u32[]{:S(2)}, u32[]{:S(2)}) %all-to-all-start.1) | async-done | bytes 147488 | tf_op jit(solution)/shard_map/all_to_all | solution.py:126
  45.1 3.1 %shard_map.164 = (f32[24,1152]{1,0:T(8,128)}, f32[24,1152]{1,0:T(8,128)}, f32[24,1152]{1,0:T(8,128)}, f32[32,1152]{1,0:T(8,128)}) custom-call(f32[104,1152]{1,0:T(8,128)} %bitcast.62, s32[104,1]{1,0:T(8,128)} %reshape_reshape.4.cut_ref, f32[9,128]{1,0:T(8,128)} %constant.58.clone.twc_ref, f32[9,128]{1,0:T(8,128)} %constant.59.clone.tws_ref, ...), custom_call_target="tpu_custom_call" | custom-call | tf_op jit(solution)/shard_map/pallas_call | solution.py:116
  48.3 1.1 %fusion.50 = f32[3,8,1152]{2,1,0:T(8,128)S(1)} fusion(f32[3,8,1151]{2,1,0:T(8,128)S(1)} %get-tuple-element.40, f32[3,8,1]{2,1,0:T(8,128)S(1)} %get-tuple-element.42, f32[3,8,1150]{2,1,0:T(8,128)S(1)} %get-tuple-element.36, f32[3,8,2]{2,1,0:T(8,128)S(1)} %get-tuple-element.38, f32[3,8,1]{2,1,0:T(8,128)S(1)} %get-tuple-element.41, ...), kind=kLoop, calls=%fused_computation.87 | loop fusion | flops 387072 | bytes 884736 | tf_op jit(solution)/shard_map/mul | solution.py:185
  49.5 0.5 copy-done.4
  50.0 0.3 copy-done.3
  50.5 0.8 %copy-done.7 = f32[32,1152]{1,0:T(8,128)S(1)} copy-done((f32[32,1152]{1,0:T(8,128)S(1)}, f32[32,1152]{1,0:T(8,128)}, u32[]{:S(2)}) %copy-start.7) | copy-done | bytes 147480
  51.4 0.8 %copy-done.5 = f32[3,8,1152]{2,1,0:T(8,128)S(1)} copy-done((f32[3,8,1152]{2,1,0:T(8,128)S(1)}, f32[3,8,1152]{2,1,0:T(8,128)}, u32[]{:S(2)}) %copy-start.5) | copy-done | bytes 110616
  52.2 0.8 %fusion.32 = (f32[8,3,1152]{2,0,1:T(8,128)}, f32[8,3,1152]{2,0,1:T(8,128)}) fusion(f32[4,8,1152]{2,1,0:T(8,128)S(1)} %fusion.6, f32[3,8,1152]{2,1,0:T(8,128)S(1)} %copy-done.5, f32[3,8,1]{2,1,0:T(8,128)S(1)} %slice-done, f32[3,8,1151]{2,1,0:T(8,128)S(1)} %slice.279, f32[8,3,1152]{2,0,1:T(8,128)S(1)} %copy-done.1, f32[8,3,1152]{2,0,1:T(8,128)S(1)} %copy-done.2, ...), kind=kLoop, calls=%fused_computation.63 | loop fusion | flops 359424 | bytes 1327104 | tf_op jit(solution)/shard_map/transpose | solution.py:195
  53.0 0.1 copy-done.9
  53.2 0.8 %slice_bitcast_fusion = (f32[8,3,1152]{2,0,1:T(8,128)}, f32[8,3,1152]{2,0,1:T(8,128)}, f32[8,3,1152]{2,0,1:T(8,128)}) fusion(f32[4,8,1152]{2,1,0:T(8,128)S(1)} %fusion.28, f32[3]{0:T(128)S(1)} %compare_convert_fusion, f32[24,1152]{1,0:T(8,128)S(1)} %copy-done.10, f32[3,8,1151]{2,1,0:T(8,128)S(1)} %slice.213, f32[3,8,1]{2,1,0:T(8,128)S(1)} %slice.212, ...), kind=kLoop, calls=%fused_computation.95 | loop fusion | flops 221184 | bytes 884748 | tf_op jit(solution)/shard_map/transpose | solution.py:195
  (52 shorter events, 1.7 us)
Async XLA Ops:
  0.6 35.3 %copy-start = (s32[192]{0:T(256)S(1)}, s32[192]{0:T(256)}, u32[]{:S(2)}) copy-start(s32[192]{0:T(256)} %param.18) | copy-start | bytes 2308
  0.6 0.9 %copy-start.1 = (f32[8,3,1152]{2,0,1:T(8,128)S(1)}, f32[8,3,1152]{2,0,1:T(8,128)}, u32[]{:S(2)}) copy-start(f32[8,3,1152]{2,0,1:T(8,128)} %param.16) | copy-start | bytes 331780
  1.6 9.9 %copy-start.2 = (f32[8,3,1152]{2,0,1:T(8,128)S(1)}, f32[8,3,1152]{2,0,1:T(8,128)}, u32[]{:S(2)}) copy-start(f32[8,3,1152]{2,0,1:T(8,128)} %param.15) | copy-start | bytes 331780
  2.6 11.8 %collective-permute-start.1 = (f32[9,8,1152]{2,1,0:T(8,128)S(1)}, f32[9,8,1152]{2,1,0:T(8,128)S(1)}, u32[]{:S(2)}, u32[]{:S(2)}) collective-permute-start(f32[9,8,1152]{2,1,0:T(8,128)S(1)} %get-tuple-element.26), channel_id=1, source_target_pairs={{0,8},{8,16},{16,24},{24,32},{32,40},{40,48},{48,56},{56,64},{64,7... | collective-permute-start | bytes 995336 | tf_op jit(solution)/shard_map/ppermute | solution.py:145
  4.5 17.9 %collective-permute-start = (f32[9,8,1152]{2,1,0:T(8,128)S(1)}, f32[9,8,1152]{2,1,0:T(8,128)S(1)}, u32[]{:S(2)}, u32[]{:S(2)}) collective-permute-start(f32[9,8,1152]{2,1,0:T(8,128)S(1)} %get-tuple-element.27), channel_id=1, source_target_pairs={{8,0},{16,8},{24,16},{32,24},{40,32},{48,40},{56,48},{64,56},{72,6... | collective-permute-start | bytes 995336 | tf_op jit(solution)/shard_map/ppermute | solution.py:146
  12.1 0.9 %copy-start.8 = (f32[8,3,1152]{2,0,1:T(8,128)S(1)}, f32[8,3,1152]{2,0,1:T(8,128)}, u32[]{:S(2)}) copy-start(f32[8,3,1152]{2,0,1:T(8,128)} %param.13) | copy-start | bytes 331780
  15.1 16.4 %all-to-all-start = ((f32[8,4,1152]{2,1,0:T(4,128)}), f32[8,4,1152]{2,1,0:T(4,128)S(1)}, u32[]{:S(2)}, u32[]{:S(2)}) async-start(f32[8,4,1152]{2,1,0:T(4,128)} %broadcast_in_dim.46), calls=%async_computation | async-start | bytes 294912 | tf_op jit(solution)/shard_map/all_to_all | solution.py:126
  22.4 9.2 %copy-start.6 = (f32[8,3,1152]{2,0,1:T(8,128)S(1)}, f32[8,3,1152]{2,0,1:T(8,128)}, u32[]{:S(2)}) copy-start(f32[8,3,1152]{2,0,1:T(8,128)} %param.14) | copy-start | bytes 331780
  32.4 12.6 %all-to-all-start.1 = ((f32[8,4,1152]{2,1,0:T(4,128)}), f32[8,4,1152]{2,1,0:T(4,128)S(1)}, u32[]{:S(2)}, u32[]{:S(2)}) async-start(f32[8,4,1152]{2,1,0:T(4,128)} %broadcast_in_dim.48), calls=%async_computation.1 | async-start | bytes 294912 | tf_op jit(solution)/shard_map/all_to_all | solution.py:126
  49.3 0.6 %copy-start.4 = (f32[3,8,1152]{2,1,0:T(8,128)}, f32[3,8,1152]{2,1,0:T(8,128)S(1)}, u32[]{:S(2)}) copy-start(f32[3,8,1152]{2,1,0:T(8,128)S(1)} %fusion.50) | copy-start | bytes 331780
  49.4 0.9 %copy-start.3 = (f32[24,1152]{1,0:T(8,128)S(1)}, f32[24,1152]{1,0:T(8,128)}, u32[]{:S(2)}) copy-start(f32[24,1152]{1,0:T(8,128)} %get-tuple-element.15) | copy-start | bytes 331780
  50.4 0.9 %copy-start.7 = (f32[32,1152]{1,0:T(8,128)S(1)}, f32[32,1152]{1,0:T(8,128)}, u32[]{:S(2)}) copy-start(f32[32,1152]{1,0:T(8,128)} %get-tuple-element.16) | copy-start | bytes 442372
  51.3 0.9 %copy-start.5 = (f32[3,8,1152]{2,1,0:T(8,128)S(1)}, f32[3,8,1152]{2,1,0:T(8,128)}, u32[]{:S(2)}) copy-start(f32[3,8,1152]{2,1,0:T(8,128)} %copy-done.4) | copy-start | bytes 331780
  51.3 0.9 %slice-start = ((f32[3,8,1152]{2,1,0:T(8,128)}), f32[3,8,1]{2,1,0:T(8,128)S(1)}, s32[]{:S(2)}) async-start(f32[3,8,1152]{2,1,0:T(8,128)} %copy-done.4), calls=%async_computation.2 | async-start | bytes 24576 | tf_op jit(solution)/shard_map/jit(_roll_static)/slice | solution.py:188
  52.2 0.9 %copy-start.9 = (f32[24,1152]{1,0:T(8,128)S(1)}, f32[24,1152]{1,0:T(8,128)}, u32[]{:S(2)}) copy-start(f32[24,1152]{1,0:T(8,128)} %get-tuple-element.12) | copy-start | bytes 331780
  52.2 0.9 %copy-start.10 = (f32[24,1152]{1,0:T(8,128)S(1)}, f32[24,1152]{1,0:T(8,128)}, u32[]{:S(2)}) copy-start(f32[24,1152]{1,0:T(8,128)} %get-tuple-element.14) | copy-start | bytes 331780

commit v16 on v14

--- a/solution.py
+++ b/solution.py
@@ -3,6 +3,7 @@
 import jax.numpy as jnp
 from jax import lax
 from jax.experimental import pallas as pl
+from jax.experimental.pallas import tpu as pltpu
 from jax.sharding import PartitionSpec as P
 
 TIME_STEP = 0.25
@@ -60,7 +61,7 @@
     return product(high, table_high) + (product(high, table_low) + product(low, table_high))
 
 
-def filter_kernel(x_ref, cut_ref, twc_ref, tws_ref, fwd_ref, inv_ref, fold_ref, o_ref):
+def filter_kernel(x_ref, cut_ref, twc_ref, tws_ref, fwd_ref, inv_ref, fold_ref, o_ref, roll_ref):
     rows, lanes = FACTOR_ROWS, FACTOR_LANES
     count, length = x_ref.shape
     c9, s9 = fft_tables(length)[:2]
@@ -101,14 +102,19 @@
             o_ref[:, (rows - n) * lanes : (rows - n + 1) * lanes] = even + sum(
                 float(2.0 * s9[k, n] / length) * imag_d[k] for k in range(1, half)
             )
-
-
-def filter_rows(values, cuts):
+    block = roll_ref.shape[0]
+    roll_ref[...] = pltpu.roll(o_ref[2 * block : 3 * block, :], length - 1, 1)
+
+
+def filter_rows(values, cuts, block):
     count, length = values.shape
     _, _, twc, tws, forward, inverse, folded = fft_tables(length)
     return pl.pallas_call(
         filter_kernel,
-        out_shape=jax.ShapeDtypeStruct(values.shape, values.dtype),
+        out_shape=(
+            jax.ShapeDtypeStruct(values.shape, values.dtype),
+            jax.ShapeDtypeStruct((block, length), values.dtype),
+        ),
     )(values, cuts.reshape(count, 1), jnp.asarray(twc), jnp.asarray(tws), split_table(forward),
       split_table(inverse), jnp.asarray(folded))
 
@@ -167,18 +173,22 @@
     row_cuts = jnp.broadcast_to(
         filter_cutoff[jnp.minimum(cut_rows, nlat_all - 1)][:, None], fields.shape[:2]
     ).reshape(-1)
-    smooth = filter_rows(fields.reshape(-1, length), row_cuts).reshape(fields.shape)
+    smooth, east_next = filter_rows(fields.reshape(-1, length), row_cuts, rows * levels)
+    smooth = smooth.reshape(fields.shape)
+    east_next = east_next.reshape(rows, levels, length)
     east_smooth = smooth[:rows]
     north_smooth = smooth[rows : 2 * rows]
     east_flux = smooth[2 * rows : 3 * rows]
     north_full = smooth[3 * rows :]
     new_mass = layer_mass - TIME_STEP * (
-        jnp.roll(east_flux, -1, -1) - east_flux + (north_full[1:] - north_full[:-1])
-    )
-    heat_east = east_flux * face_lon(theta_field)
+        east_next - east_flux + (north_full[1:] - north_full[:-1])
+    )
+    lon_theta = face_lon(theta_field)
+    heat_east = east_flux * lon_theta
+    heat_next = east_next * jnp.roll(lon_theta, -1, -1)
     heat_north = north_full * theta_faces
     new_heat = theta_field * layer_mass - TIME_STEP * (
-        jnp.roll(heat_east, -1, -1) - heat_east + (heat_north[1:] - heat_north[:-1])
+        heat_next - heat_east + (heat_north[1:] - heat_north[:-1])
     )
     height = height_ext[1:]
     new_east = east_smooth - TIME_STEP * (height - jnp.roll(height, 1, -1))

time: 51.8 us -> 51.7 us (level)
  local copies, waits for them, and re-layouts: 7.34 us -> 5.97 us
  other arithmetic: 4.61 us -> 5.7 us
    slice x5 -> x3, local copies, waits for them, and re-layouts: 1.15 us -> 0.09 us  [local(): heat_next = east_next * jnp.roll(lon_theta, -1, -1)]
    mul x1, other arithmetic: 0.06 us -> 1.03 us  [local(): heat_north = north_full * theta_faces]
    mul x1 -> x0, other arithmetic: 0.82 us -> none  [local(): heat_east = east_flux * face_lon(theta_field)]
    transpose x1 -> x2, other arithmetic: 0.85 us -> 1.58 us  [local(): return tuple((jnp.transpose(v, (1, 0, 2)) for v in outputs))]
    unnamed x12 -> x18, local copies, waits for them, and re-layouts: 1.4 us -> 1.07 us
  transfers between devices with their start and end apart: 4 -> 4, of which waited for: 3 -> 3; matrix products, arithmetic and copies ran while one was open for 9% -> 10% of each run, Pallas kernels for 0% -> 0%
where the time goes in v16:
time: 51.7 us; the launch traced here: 51.2 us
  starting transfers between devices  19.4 us (38%)
  waiting for transfers between devices  16.1 us (31%)
  local copies, waits for them, and re-layouts  5.97 us (12%)
  other arithmetic  5.7 us (11%)
  Pallas kernels  3.2 us (6%)
  between operations  0.94 us (2%)
    all_to_all x2, waiting for transfers between devices, prefix_over(): lax.all_to_all(copies, axis, split_axis=0, concat_axis=0, tiled=True)  15.3 us
    all_to_all x2, starting transfers between devices, prefix_over(): lax.all_to_all(copies, axis, split_axis=0, concat_axis=0, tiled=True)  10.5 us
    ppermute x1, starting transfers between devices, local(): lax.ppermute(to_south, 'lat', [(i + 1, i) for i in range(count - 1)])  6.96 us
    pallas_call x1, Pallas kernels, filter_rows(): pl.pallas_call(filter_kernel, out_shape=(jax.ShapeDtypeStruct(values.shap...  3.2 us
    ppermute x1, starting transfers between devices, local(): lax.ppermute(to_north, 'lat', [(i, i + 1) for i in range(count - 1)])  1.92 us
    transpose x2, other arithmetic, local(): return tuple((jnp.transpose(v, (1, 0, 2)) for v in outputs))  1.58 us
    broadcast_in_dim x2, local copies, waits for them, and re-layouts, prefix_over(): copies = jnp.broadcast_to(value, (count, *value.shape))  1.35 us
    unnamed x18, local copies, waits for them, and re-layouts  1.07 us
  transfers between devices with their start and end apart: 4, of which 3 were waited for; matrix products, arithmetic and copies ran while one was open for 10% of the time, Pallas kernels for 0%

profile of v16, /device:TPU:256, one launch (start us, length us, event | category | flops | bytes accessed | tf_op | source)
XLA Modules:
  0.0 51.2 jit_solution(11260781434541025503)
XLA Ops:
  0.7 0.8 %broadcast_in_dim.43 = f32[3,8,1152]{2,1,0:T(8,128)S(1)} broadcast(f32[3,1152]{1,0:T(4,128)} %param.17), dimensions={0,2} | broadcast | bytes 124416 | tf_op jit(solution)/shard_map/broadcast_in_dim | solution.py:140
  1.4 0.1 copy-done.1
  1.6 1.0 %pad_maximum_fusion.3 = (f32[9,8,1152]{2,1,0:T(8,128)S(1)}, f32[9,8,1152]{2,1,0:T(8,128)S(1)}) fusion(f32[3,8,1152]{2,1,0:T(8,128)S(1)} %broadcast_in_dim.43, f32[3,8,1152]{2,1,0:T(8,128)S(1)} %bitcast.57, f32[3,8,1152]{2,1,0:T(8,128)} %bitcast.66, f32[3,8,1152]{2,1,0:T(8,128)} %bitcast.76), kind=kLoop, calls=%fused_computation.4 | loop fusion | flops 248832 | bytes 1105920 | tf_op jit(solution)/shard_map/concatenate | solution.py:141
  2.6 1.9 %collective-permute-start.1 = (f32[9,8,1152]{2,1,0:T(8,128)S(1)}, f32[9,8,1152]{2,1,0:T(8,128)S(1)}, u32[]{:S(2)}, u32[]{:S(2)}) collective-permute-start(f32[9,8,1152]{2,1,0:T(8,128)S(1)} %get-tuple-element.26), channel_id=1, source_target_pairs={{0,8},{8,16},{16,24},{24,32},{32,40},{40,48},{48,56},{56,64},{64,7... | collective-permute-start | bytes 995336 | tf_op jit(solution)/shard_map/ppermute | solution.py:144
  4.5 7.0 %collective-permute-start = (f32[9,8,1152]{2,1,0:T(8,128)S(1)}, f32[9,8,1152]{2,1,0:T(8,128)S(1)}, u32[]{:S(2)}, u32[]{:S(2)}) collective-permute-start(f32[9,8,1152]{2,1,0:T(8,128)S(1)} %get-tuple-element.27), channel_id=1, source_target_pairs={{8,0},{16,8},{24,16},{32,24},{40,32},{48,40},{56,48},{64,56},{72,6... | collective-permute-start | bytes 995336 | tf_op jit(solution)/shard_map/ppermute | solution.py:145
  11.5 0.1 fusion.64
  11.6 0.1 fusion.66
  12.1 0.1 fusion.62
  12.5 0.2 fusion.45
  12.7 0.7 %copy-done.7 = f32[8,3,1152]{2,0,1:T(8,128)S(1)} copy-done((f32[8,3,1152]{2,0,1:T(8,128)S(1)}, f32[8,3,1152]{2,0,1:T(8,128)}, u32[]{:S(2)}) %copy-start.7) | copy-done | bytes 110616
  13.4 0.2 fusion.37
  13.6 0.7 %collective-permute-done.1 = f32[9,8,1152]{2,1,0:T(8,128)S(1)} collective-permute-done((f32[9,8,1152]{2,1,0:T(8,128)S(1)}, f32[9,8,1152]{2,1,0:T(8,128)S(1)}, u32[]{:S(2)}, u32[]{:S(2)}) %collective-permute-start.1) | collective-permute-done | bytes 331808 | tf_op jit(solution)/shard_map/ppermute | solution.py:144
  14.4 0.7 %broadcast_in_dim.46 = f32[8,4,1152]{2,1,0:T(4,128)} broadcast(f32[4,1152]{1,0:T(4,128)S(1)} %get-tuple-element.29), dimensions={1,2} | broadcast | bytes 165888 | tf_op jit(solution)/shard_map/broadcast_in_dim | solution.py:124
  15.1 7.1 %all-to-all-start = ((f32[8,4,1152]{2,1,0:T(4,128)}), f32[8,4,1152]{2,1,0:T(4,128)S(1)}, u32[]{:S(2)}, u32[]{:S(2)}) async-start(f32[8,4,1152]{2,1,0:T(4,128)} %broadcast_in_dim.46), calls=%async_computation | async-start | bytes 294912 | tf_op jit(solution)/shard_map/all_to_all | solution.py:125
  22.2 0.1 reduce_window_sum.17
  22.4 9.0 %all-to-all-done = f32[8,4,1152]{2,1,0:T(4,128)S(1)} async-done(((f32[8,4,1152]{2,1,0:T(4,128)}), f32[8,4,1152]{2,1,0:T(4,128)S(1)}, u32[]{:S(2)}, u32[]{:S(2)}) %all-to-all-start) | async-done | bytes 147488 | tf_op jit(solution)/shard_map/all_to_all | solution.py:125
  31.5 0.1 select_reduce_fusion.1
  31.6 0.2 fusion.56
  31.7 0.7 %broadcast_in_dim.48 = f32[8,4,1152]{2,1,0:T(4,128)} broadcast(f32[4,1152]{1,0:T(4,128)S(1)} %get-tuple-element.13), dimensions={1,2} | broadcast | bytes 165888 | tf_op jit(solution)/shard_map/broadcast_in_dim | solution.py:124
  32.4 3.4 %all-to-all-start.1 = ((f32[8,4,1152]{2,1,0:T(4,128)}), f32[8,4,1152]{2,1,0:T(4,128)S(1)}, u32[]{:S(2)}, u32[]{:S(2)}) async-start(f32[8,4,1152]{2,1,0:T(4,128)} %broadcast_in_dim.48), calls=%async_computation.1 | async-start | bytes 294912 | tf_op jit(solution)/shard_map/all_to_all | solution.py:125
  35.9 0.7 %gather_fusion = s32[13]{0:T(128)S(1)} fusion(s32[192]{0:T(256)S(1)} %copy-done, s32[1024]{0:T(1024)S(1)} %pad_clamp_fusion), kind=kCustom, calls=%fused_computation | custom fusion | bytes 156 | tf_op jit(solution)/shard_map/gather | solution.py:174
  36.7 0.7 %reshape_reshape.4.cut_ref = s32[104,1]{1,0:T(8,128)} reshape(s32[13,8]{1,0:T(8,128)S(1)} %broadcast_in_dim.49) | data formatting | bytes 832 | tf_op jit(solution)/shard_map/reshape;reshape | solution.py:118
  37.4 0.1 rev.7
  37.5 0.1 reduce_window_sum.18
  37.7 0.2 rev.8
  37.9 0.8 %pad_maximum_fusion = f32[13,8,1152]{2,1,0:T(8,128)} fusion(f32[4,8,1152]{2,1,0:T(8,128)S(1)} %get-tuple-element.39, f32[3,8,1152]{2,1,0:T(8,128)S(1)} %fusion.37, f32[3,8,1152]{2,1,0:T(8,128)S(1)} %bitcast.78, f32[3,8,1152]{2,1,0:T(8,128)S(1)} %bitcast.79), kind=kLoop, calls=%fused_computation.1 | loop fusion | flops 359424 | bytes 958464 | tf_op jit(solution)/shard_map/concatenate | solution.py:170
  38.7 6.3 %all-to-all-done.1 = f32[8,4,1152]{2,1,0:T(4,128)S(1)} async-done(((f32[8,4,1152]{2,1,0:T(4,128)}), f32[8,4,1152]{2,1,0:T(4,128)S(1)}, u32[]{:S(2)}, u32[]{:S(2)}) %all-to-all-start.1) | async-done | bytes 147488 | tf_op jit(solution)/shard_map/all_to_all | solution.py:125
  45.0 0.1 select_reduce_fusion
  45.2 3.2 %shard_map.164 = (f32[104,1152]{1,0:T(8,128)}, f32[24,1152]{1,0:T(8,128)}) custom-call(f32[104,1152]{1,0:T(8,128)} %bitcast.75, s32[104,1]{1,0:T(8,128)} %reshape_reshape.4.cut_ref, f32[9,128]{1,0:T(8,128)} %constant.58.clone.twc_ref, f32[9,128]{1,0:T(8,128)} %constant.59.clone.tws_ref, bf16[2,256,256]{2,1,0:T(8,128)(2,1)} %constant.74.fwd_ref, ...), custom_call_target="tpu_custom_call" | custom-call | tf_op jit(solution)/shard_map/pallas_call | solution.py:112
  48.4 1.0 %fusion.6 = f32[4,8,1152]{2,1,0:T(8,128)S(1)} fusion(f32[3,8,1152]{2,1,0:T(8,128)S(1)} %bitcast.65, f32[3,8,1152]{2,1,0:T(8,128)S(1)} %get-tuple-element.21, f32[3,8,1152]{2,1,0:T(8,128)S(1)} %get-tuple-element.19, f32[104,1152]{1,0:T(8,128)} %get-tuple-element.10), kind=kLoop, calls=%fused_computation.27 | loop fusion | flops 552960 | bytes 626688 | tf_op jit(solution)/shard_map/mul | solution.py:189
  49.5 0.8 %fusion.52 = (f32[8,3,1152]{2,0,1:T(8,128)}, f32[8,3,1152]{2,0,1:T(8,128)}, f32[8,3,1152]{2,0,1:T(8,128)}) fusion(f32[4,8,1152]{2,1,0:T(8,128)S(1)} %fusion.28, f32[104,1152]{1,0:T(8,128)S(1)} %copy-done.5, f32[3]{0:T(128)S(1)} %compare_convert_fusion, f32[3,8,1151]{2,1,0:T(8,128)S(1)} %slice.235, f32[3,8,1]{2,1,0:T(8,128)S(1)} %slice.234), kind=kLoop, calls=%fused_computation.95 | loop fusion | flops 221184 | bytes 884748 | tf_op jit(solution)/shard_map/transpose | solution.py:198
  50.5 0.8 %fusion.32 = (f32[8,3,1152]{2,0,1:T(8,128)}, f32[8,3,1152]{2,0,1:T(8,128)}) fusion(f32[4,8,1152]{2,1,0:T(8,128)S(1)} %fusion.6, f32[3,8,1]{2,1,0:T(8,128)S(1)} %slice-done, f32[3,8,1151]{2,1,0:T(8,128)S(1)} %slice.303, f32[3,8,1152]{2,1,0:T(8,128)S(1)} %copy-done.4, f32[24,1152]{1,0:T(8,128)S(1)} %copy-done.8, f32[104,1152]{1,0:T(8,128)S(1)} %copy-done.5, ...), kind=kLoop, calls=%fused_computation.63 | loop fusion | flops 387072 | bytes 1327104 | tf_op jit(solution)/shard_map/transpose | solution.py:198
  (46 shorter events, 1.3 us)
Async XLA Ops:
  0.6 35.3 %copy-start = (s32[192]{0:T(256)S(1)}, s32[192]{0:T(256)}, u32[]{:S(2)}) copy-start(s32[192]{0:T(256)} %param.18) | copy-start | bytes 2308
  0.6 0.9 %copy-start.1 = (f32[8,3,1152]{2,0,1:T(8,128)S(1)}, f32[8,3,1152]{2,0,1:T(8,128)}, u32[]{:S(2)}) copy-start(f32[8,3,1152]{2,0,1:T(8,128)} %param.16) | copy-start | bytes 331780
  1.6 9.9 %copy-start.2 = (f32[8,3,1152]{2,0,1:T(8,128)S(1)}, f32[8,3,1152]{2,0,1:T(8,128)}, u32[]{:S(2)}) copy-start(f32[8,3,1152]{2,0,1:T(8,128)} %param.15) | copy-start | bytes 331780
  2.6 11.8 %collective-permute-start.1 = (f32[9,8,1152]{2,1,0:T(8,128)S(1)}, f32[9,8,1152]{2,1,0:T(8,128)S(1)}, u32[]{:S(2)}, u32[]{:S(2)}) collective-permute-start(f32[9,8,1152]{2,1,0:T(8,128)S(1)} %get-tuple-element.26), channel_id=1, source_target_pairs={{0,8},{8,16},{16,24},{24,32},{32,40},{40,48},{48,56},{56,64},{64,7... | collective-permute-start | bytes 995336 | tf_op jit(solution)/shard_map/ppermute | solution.py:144
  4.5 17.8 %collective-permute-start = (f32[9,8,1152]{2,1,0:T(8,128)S(1)}, f32[9,8,1152]{2,1,0:T(8,128)S(1)}, u32[]{:S(2)}, u32[]{:S(2)}) collective-permute-start(f32[9,8,1152]{2,1,0:T(8,128)S(1)} %get-tuple-element.27), channel_id=1, source_target_pairs={{8,0},{16,8},{24,16},{32,24},{40,32},{48,40},{56,48},{64,56},{72,6... | collective-permute-start | bytes 995336 | tf_op jit(solution)/shard_map/ppermute | solution.py:145
  12.5 0.9 %copy-start.7 = (f32[8,3,1152]{2,0,1:T(8,128)S(1)}, f32[8,3,1152]{2,0,1:T(8,128)}, u32[]{:S(2)}) copy-start(f32[8,3,1152]{2,0,1:T(8,128)} %param.13) | copy-start | bytes 331780
  12.7 23.2 %copy-start.3 = (f32[3,8,1152]{2,1,0:T(8,128)}, f32[3,8,1152]{2,1,0:T(8,128)S(1)}, u32[]{:S(2)}) copy-start(f32[3,8,1152]{2,1,0:T(8,128)S(1)} %fusion.45) | copy-start | bytes 331780
  15.1 16.4 %all-to-all-start = ((f32[8,4,1152]{2,1,0:T(4,128)}), f32[8,4,1152]{2,1,0:T(4,128)S(1)}, u32[]{:S(2)}, u32[]{:S(2)}) async-start(f32[8,4,1152]{2,1,0:T(4,128)} %broadcast_in_dim.46), calls=%async_computation | async-start | bytes 294912 | tf_op jit(solution)/shard_map/all_to_all | solution.py:125
  22.4 9.2 %copy-start.6 = (f32[8,3,1152]{2,0,1:T(8,128)S(1)}, f32[8,3,1152]{2,0,1:T(8,128)}, u32[]{:S(2)}) copy-start(f32[8,3,1152]{2,0,1:T(8,128)} %param.14) | copy-start | bytes 331780
  32.4 12.6 %all-to-all-start.1 = ((f32[8,4,1152]{2,1,0:T(4,128)}), f32[8,4,1152]{2,1,0:T(4,128)S(1)}, u32[]{:S(2)}, u32[]{:S(2)}) async-start(f32[8,4,1152]{2,1,0:T(4,128)} %broadcast_in_dim.48), calls=%async_computation.1 | async-start | bytes 294912 | tf_op jit(solution)/shard_map/all_to_all | solution.py:125
  48.4 1.1 %copy-start.5 = (f32[104,1152]{1,0:T(8,128)S(1)}, f32[104,1152]{1,0:T(8,128)}, u32[]{:S(2)}) copy-start(f32[104,1152]{1,0:T(8,128)} %get-tuple-element.10) | copy-start | bytes 1437700
  49.5 0.9 %copy-start.4 = (f32[3,8,1152]{2,1,0:T(8,128)S(1)}, f32[3,8,1152]{2,1,0:T(8,128)}, u32[]{:S(2)}) copy-start(f32[3,8,1152]{2,1,0:T(8,128)} %copy-done.3) | copy-start | bytes 331780
  49.5 0.9 %slice-start = ((f32[3,8,1152]{2,1,0:T(8,128)}), f32[3,8,1]{2,1,0:T(8,128)S(1)}, s32[]{:S(2)}) async-start(f32[3,8,1152]{2,1,0:T(8,128)} %copy-done.3), calls=%async_computation.2 | async-start | bytes 24576 | tf_op jit(solution)/shard_map/jit(_roll_static)/slice | solution.py:188
  49.5 1.0 %copy-start.8 = (f32[24,1152]{1,0:T(8,128)S(1)}, f32[24,1152]{1,0:T(8,128)}, u32[]{:S(2)}) copy-start(f32[24,1152]{1,0:T(8,128)} %get-tuple-element.12) | copy-start | bytes 331780

commit v17 on v16

--- a/solution.py
+++ b/solution.py
@@ -186,9 +186,8 @@
     lon_theta = face_lon(theta_field)
     heat_east = east_flux * lon_theta
     heat_next = east_next * jnp.roll(lon_theta, -1, -1)
-    heat_north = north_full * theta_faces
     new_heat = theta_field * layer_mass - TIME_STEP * (
-        heat_next - heat_east + (heat_north[1:] - heat_north[:-1])
+        heat_next - heat_east + (north_full[1:] * theta_faces[1:] - north_full[:-1] * theta_faces[:-1])
     )
     height = height_ext[1:]
     new_east = east_smooth - TIME_STEP * (height - jnp.roll(height, 1, -1))

time: 51.7 us -> 55.5 us (1.074)
  the two profiles are of different devices: /device:TPU:256 before, /device:TPU:199 now
where the time goes in v17:
time: 55.5 us; the launch traced here: 55 us
  waiting for transfers between devices  20.3 us (37%)
  starting transfers between devices  17.8 us (32%)
  local copies, waits for them, and re-layouts  7.12 us (13%)
  other arithmetic  5.69 us (10%)
  Pallas kernels  3.2 us (6%)
  between operations  0.93 us (2%)
    all_to_all x2, waiting for transfers between devices, prefix_over(): lax.all_to_all(copies, axis, split_axis=0, concat_axis=0, tiled=True)  13.1 us
    all_to_all x2, starting transfers between devices, prefix_over(): lax.all_to_all(copies, axis, split_axis=0, concat_axis=0, tiled=True)  10.2 us
    ppermute x1, waiting for transfers between devices, local(): lax.ppermute(to_south, 'lat', [(i + 1, i) for i in range(count - 1)])  7.21 us
    ppermute x1, starting transfers between devices, local(): lax.ppermute(to_north, 'lat', [(i, i + 1) for i in range(count - 1)])  5.69 us
    pallas_call x1, Pallas kernels, filter_rows(): pl.pallas_call(filter_kernel, out_shape=(jax.ShapeDtypeStruct(values.shap...  3.2 us
    transpose x2, other arithmetic, local(): return tuple((jnp.transpose(v, (1, 0, 2)) for v in outputs))  2.61 us
    unnamed x18, local copies, waits for them, and re-layouts  2.23 us
    ppermute x1, starting transfers between devices, local(): lax.ppermute(to_south, 'lat', [(i + 1, i) for i in range(count - 1)])  1.92 us
  transfers between devices with their start and end apart: 4, of which 3 were waited for; matrix products, arithmetic and copies ran while one was open for 8% of the time, Pallas kernels for 0%

profile of v17, /device:TPU:199, one launch (start us, length us, event | category | flops | bytes accessed | tf_op | source)
XLA Modules:
  0.0 55.0 jit_solution(16481048671247776825)
XLA Ops:
  0.7 0.8 %broadcast_in_dim.43 = f32[3,8,1152]{2,1,0:T(8,128)S(1)} broadcast(f32[3,1152]{1,0:T(4,128)} %param.17), dimensions={0,2} | broadcast | bytes 124416 | tf_op jit(solution)/shard_map/broadcast_in_dim | solution.py:140
  1.4 0.1 copy-done.1
  1.6 1.0 %pad_maximum_fusion.3 = (f32[9,8,1152]{2,1,0:T(8,128)S(1)}, f32[9,8,1152]{2,1,0:T(8,128)S(1)}) fusion(f32[3,8,1152]{2,1,0:T(8,128)S(1)} %broadcast_in_dim.43, f32[3,8,1152]{2,1,0:T(8,128)} %bitcast.70, f32[3,8,1152]{2,1,0:T(8,128)S(1)} %bitcast.61, f32[3,8,1152]{2,1,0:T(8,128)} %bitcast.79), kind=kLoop, calls=%fused_computation.4 | loop fusion | flops 248832 | bytes 1105920 | tf_op jit(solution)/shard_map/concatenate | solution.py:141
  2.6 5.7 %collective-permute-start.1 = (f32[9,8,1152]{2,1,0:T(8,128)S(1)}, f32[9,8,1152]{2,1,0:T(8,128)S(1)}, u32[]{:S(2)}, u32[]{:S(2)}) collective-permute-start(f32[9,8,1152]{2,1,0:T(8,128)S(1)} %get-tuple-element.26), channel_id=1, source_target_pairs={{0,8},{8,16},{16,24},{24,32},{32,40},{40,48},{48,56},{56,64},{64,7... | collective-permute-start | bytes 995336 | tf_op jit(solution)/shard_map/ppermute | solution.py:144
  8.3 1.9 %collective-permute-start = (f32[9,8,1152]{2,1,0:T(8,128)S(1)}, f32[9,8,1152]{2,1,0:T(8,128)S(1)}, u32[]{:S(2)}, u32[]{:S(2)}) collective-permute-start(f32[9,8,1152]{2,1,0:T(8,128)S(1)} %get-tuple-element.27), channel_id=1, source_target_pairs={{8,0},{16,8},{24,16},{32,24},{40,32},{48,40},{56,48},{64,56},{72,6... | collective-permute-start | bytes 995336 | tf_op jit(solution)/shard_map/ppermute | solution.py:145
  10.3 0.1 fusion.67
  10.7 0.6 %copy-done.2 = f32[8,3,1152]{2,0,1:T(8,128)S(1)} copy-done((f32[8,3,1152]{2,0,1:T(8,128)S(1)}, f32[8,3,1152]{2,0,1:T(8,128)}, u32[]{:S(2)}) %copy-start.2) | copy-done | bytes 110616
  11.8 0.6 %copy-done.7 = f32[8,3,1152]{2,0,1:T(8,128)S(1)} copy-done((f32[8,3,1152]{2,0,1:T(8,128)S(1)}, f32[8,3,1152]{2,0,1:T(8,128)}, u32[]{:S(2)}) %copy-start.7) | copy-done | bytes 110616
  12.4 0.2 fusion.37
  12.6 0.2 fusion.45
  12.8 7.2 %collective-permute-done = f32[9,8,1152]{2,1,0:T(8,128)S(1)} collective-permute-done((f32[9,8,1152]{2,1,0:T(8,128)S(1)}, f32[9,8,1152]{2,1,0:T(8,128)S(1)}, u32[]{:S(2)}, u32[]{:S(2)}) %collective-permute-start) | collective-permute-done | bytes 331808 | tf_op jit(solution)/shard_map/ppermute | solution.py:145
  20.1 0.9 %copy-done.5 = f32[8,3,1152]{2,0,1:T(8,128)S(1)} copy-done((f32[8,3,1152]{2,0,1:T(8,128)S(1)}, f32[8,3,1152]{2,0,1:T(8,128)}, u32[]{:S(2)}) %copy-start.5) | copy-done | bytes 110616
  20.9 0.1 fusion.56
  21.0 0.7 %broadcast_in_dim.46 = f32[8,4,1152]{2,1,0:T(4,128)} broadcast(f32[4,1152]{1,0:T(4,128)S(1)} %get-tuple-element.29), dimensions={1,2} | broadcast | bytes 165888 | tf_op jit(solution)/shard_map/broadcast_in_dim | solution.py:124
  21.7 6.8 %all-to-all-start = ((f32[8,4,1152]{2,1,0:T(4,128)}), f32[8,4,1152]{2,1,0:T(4,128)S(1)}, u32[]{:S(2)}, u32[]{:S(2)}) async-start(f32[8,4,1152]{2,1,0:T(4,128)} %broadcast_in_dim.46), calls=%async_computation | async-start | bytes 294912 | tf_op jit(solution)/shard_map/all_to_all | solution.py:125
  28.5 0.1 reduce_window_sum.17
  28.7 7.9 %all-to-all-done = f32[8,4,1152]{2,1,0:T(4,128)S(1)} async-done(((f32[8,4,1152]{2,1,0:T(4,128)}), f32[8,4,1152]{2,1,0:T(4,128)S(1)}, u32[]{:S(2)}, u32[]{:S(2)}) %all-to-all-start) | async-done | bytes 147488 | tf_op jit(solution)/shard_map/all_to_all | solution.py:125
  36.6 0.1 select_reduce_fusion.1
  36.7 0.1 fusion.57
  36.9 0.7 %broadcast_in_dim.48 = f32[8,4,1152]{2,1,0:T(4,128)} broadcast(f32[4,1152]{1,0:T(4,128)S(1)} %get-tuple-element.13), dimensions={1,2} | broadcast | bytes 165888 | tf_op jit(solution)/shard_map/broadcast_in_dim | solution.py:124
  37.6 3.4 %all-to-all-start.1 = ((f32[8,4,1152]{2,1,0:T(4,128)}), f32[8,4,1152]{2,1,0:T(4,128)S(1)}, u32[]{:S(2)}, u32[]{:S(2)}) async-start(f32[8,4,1152]{2,1,0:T(4,128)} %broadcast_in_dim.48), calls=%async_computation.1 | async-start | bytes 294912 | tf_op jit(solution)/shard_map/all_to_all | solution.py:125
  41.1 0.7 %gather_fusion = s32[13]{0:T(128)S(1)} fusion(s32[192]{0:T(256)S(1)} %copy-done, s32[1024]{0:T(1024)S(1)} %pad_clamp_fusion), kind=kCustom, calls=%fused_computation | custom fusion | bytes 156 | tf_op jit(solution)/shard_map/gather | solution.py:174
  41.8 0.7 %reshape_reshape.4.cut_ref = s32[104,1]{1,0:T(8,128)} reshape(s32[13,8]{1,0:T(8,128)S(1)} %broadcast_in_dim.49) | data formatting | bytes 832 | tf_op jit(solution)/shard_map/reshape;reshape | solution.py:118
  42.5 0.8 %pad_maximum_fusion = f32[13,8,1152]{2,1,0:T(8,128)} fusion(f32[4,8,1152]{2,1,0:T(8,128)S(1)} %get-tuple-element.40, f32[3,8,1152]{2,1,0:T(8,128)S(1)} %fusion.37, f32[3,8,1152]{2,1,0:T(8,128)S(1)} %bitcast.81, f32[3,8,1152]{2,1,0:T(8,128)S(1)} %bitcast.82), kind=kLoop, calls=%fused_computation.1 | loop fusion | flops 359424 | bytes 958464 | tf_op jit(solution)/shard_map/concatenate | solution.py:170
  43.3 0.1 rev.7
  43.5 0.1 reduce_window_sum.18
  43.6 0.2 rev.8
  43.8 5.1 %all-to-all-done.1 = f32[8,4,1152]{2,1,0:T(4,128)S(1)} async-done(((f32[8,4,1152]{2,1,0:T(4,128)}), f32[8,4,1152]{2,1,0:T(4,128)S(1)}, u32[]{:S(2)}, u32[]{:S(2)}) %all-to-all-start.1) | async-done | bytes 147488 | tf_op jit(solution)/shard_map/all_to_all | solution.py:125
  48.9 0.1 select_reduce_fusion
  49.2 3.2 %shard_map.164 = (f32[104,1152]{1,0:T(8,128)}, f32[24,1152]{1,0:T(8,128)}) custom-call(f32[104,1152]{1,0:T(8,128)} %bitcast.78, s32[104,1]{1,0:T(8,128)} %reshape_reshape.4.cut_ref, f32[9,128]{1,0:T(8,128)} %constant.58.clone.twc_ref, f32[9,128]{1,0:T(8,128)} %constant.59.clone.tws_ref, bf16[2,256,256]{2,1,0:T(8,128)(2,1)} %constant.74.fwd_ref, ...), custom_call_target="tpu_custom_call" | custom-call | tf_op jit(solution)/shard_map/pallas_call | solution.py:112
  52.4 1.8 %fusion.53 = (f32[8,3,1152]{2,0,1:T(8,128)}, f32[8,3,1152]{2,0,1:T(8,128)}, f32[8,3,1152]{2,0,1:T(8,128)}) fusion(f32[4,8,1152]{2,1,0:T(8,128)S(1)} %fusion.27, f32[104,1152]{1,0:T(8,128)} %get-tuple-element.10, f32[3]{0:T(128)S(1)} %compare_convert_fusion, f32[3,8,1151]{2,1,0:T(8,128)S(1)} %slice.237, f32[3,8,1]{2,1,0:T(8,128)S(1)} %slice.236), kind=kLoop, calls=%fused_computation.97 | loop fusion | flops 221184 | bytes 884748 | tf_op jit(solution)/shard_map/transpose | solution.py:197
  54.3 0.8 %fusion.32 = (f32[8,3,1152]{2,0,1:T(8,128)}, f32[8,3,1152]{2,0,1:T(8,128)}) fusion(f32[4,8,1152]{2,1,0:T(8,128)S(1)} %get-tuple-element.39, f32[3,8,1]{2,1,0:T(8,128)S(1)} %slice-done, f32[3,8,1151]{2,1,0:T(8,128)S(1)} %slice.305, f32[3,8,1152]{2,1,0:T(8,128)S(1)} %copy-done.4, f32[24,1152]{1,0:T(8,128)S(1)} %copy-done.8, f32[104,1152]{1,0:T(8,128)S(1)} %copy-done.6, ...), kind=kLoop, calls=%fused_computation.63 | loop fusion | flops 442368 | bytes 1327104 | tf_op jit(solution)/shard_map/transpose | solution.py:197
  (45 shorter events, 1.2 us)
Async XLA Ops:
  0.6 40.4 %copy-start = (s32[192]{0:T(256)S(1)}, s32[192]{0:T(256)}, u32[]{:S(2)}) copy-start(s32[192]{0:T(256)} %param.18) | copy-start | bytes 2308
  0.6 0.9 %copy-start.1 = (f32[8,3,1152]{2,0,1:T(8,128)S(1)}, f32[8,3,1152]{2,0,1:T(8,128)}, u32[]{:S(2)}) copy-start(f32[8,3,1152]{2,0,1:T(8,128)} %param.15) | copy-start | bytes 331780
  2.6 10.2 %collective-permute-start.1 = (f32[9,8,1152]{2,1,0:T(8,128)S(1)}, f32[9,8,1152]{2,1,0:T(8,128)S(1)}, u32[]{:S(2)}, u32[]{:S(2)}) collective-permute-start(f32[9,8,1152]{2,1,0:T(8,128)S(1)} %get-tuple-element.26), channel_id=1, source_target_pairs={{0,8},{8,16},{16,24},{24,32},{32,40},{40,48},{48,56},{56,64},{64,7... | collective-permute-start | bytes 995336 | tf_op jit(solution)/shard_map/ppermute | solution.py:144
  8.3 11.8 %collective-permute-start = (f32[9,8,1152]{2,1,0:T(8,128)S(1)}, f32[9,8,1152]{2,1,0:T(8,128)S(1)}, u32[]{:S(2)}, u32[]{:S(2)}) collective-permute-start(f32[9,8,1152]{2,1,0:T(8,128)S(1)} %get-tuple-element.27), channel_id=1, source_target_pairs={{8,0},{16,8},{24,16},{32,24},{40,32},{48,40},{56,48},{64,56},{72,6... | collective-permute-start | bytes 995336 | tf_op jit(solution)/shard_map/ppermute | solution.py:145
  10.4 0.9 %copy-start.2 = (f32[8,3,1152]{2,0,1:T(8,128)S(1)}, f32[8,3,1152]{2,0,1:T(8,128)}, u32[]{:S(2)}) copy-start(f32[8,3,1152]{2,0,1:T(8,128)} %param.16) | copy-start | bytes 331780
  11.5 0.9 %copy-start.7 = (f32[8,3,1152]{2,0,1:T(8,128)S(1)}, f32[8,3,1152]{2,0,1:T(8,128)}, u32[]{:S(2)}) copy-start(f32[8,3,1152]{2,0,1:T(8,128)} %param.13) | copy-start | bytes 331780
  12.7 28.3 %copy-start.3 = (f32[3,8,1152]{2,1,0:T(8,128)}, f32[3,8,1152]{2,1,0:T(8,128)S(1)}, u32[]{:S(2)}) copy-start(f32[3,8,1152]{2,1,0:T(8,128)S(1)} %fusion.45) | copy-start | bytes 331780
  20.0 0.9 %copy-start.5 = (f32[8,3,1152]{2,0,1:T(8,128)S(1)}, f32[8,3,1152]{2,0,1:T(8,128)}, u32[]{:S(2)}) copy-start(f32[8,3,1152]{2,0,1:T(8,128)} %param.14) | copy-start | bytes 331780
  21.7 14.9 %all-to-all-start = ((f32[8,4,1152]{2,1,0:T(4,128)}), f32[8,4,1152]{2,1,0:T(4,128)S(1)}, u32[]{:S(2)}, u32[]{:S(2)}) async-start(f32[8,4,1152]{2,1,0:T(4,128)} %broadcast_in_dim.46), calls=%async_computation | async-start | bytes 294912 | tf_op jit(solution)/shard_map/all_to_all | solution.py:125
  37.6 11.4 %all-to-all-start.1 = ((f32[8,4,1152]{2,1,0:T(4,128)}), f32[8,4,1152]{2,1,0:T(4,128)S(1)}, u32[]{:S(2)}, u32[]{:S(2)}) async-start(f32[8,4,1152]{2,1,0:T(4,128)} %broadcast_in_dim.48), calls=%async_computation.1 | async-start | bytes 294912 | tf_op jit(solution)/shard_map/all_to_all | solution.py:125
  52.4 1.9 %copy-start.6 = (f32[104,1152]{1,0:T(8,128)S(1)}, f32[104,1152]{1,0:T(8,128)}, u32[]{:S(2)}) copy-start(f32[104,1152]{1,0:T(8,128)} %get-tuple-element.10) | copy-start | bytes 1437700
  52.4 1.9 %copy-start.4 = (f32[3,8,1152]{2,1,0:T(8,128)S(1)}, f32[3,8,1152]{2,1,0:T(8,128)}, u32[]{:S(2)}) copy-start(f32[3,8,1152]{2,1,0:T(8,128)} %copy-done.3) | copy-start | bytes 331780
  52.4 1.9 %slice-start = ((f32[3,8,1152]{2,1,0:T(8,128)}), f32[3,8,1]{2,1,0:T(8,128)S(1)}, s32[]{:S(2)}) async-start(f32[3,8,1152]{2,1,0:T(8,128)} %copy-done.3), calls=%async_computation.2 | async-start | bytes 24576 | tf_op jit(solution)/shard_map/jit(_roll_static)/slice | solution.py:188
  52.4 1.9 %copy-start.8 = (f32[24,1152]{1,0:T(8,128)S(1)}, f32[24,1152]{1,0:T(8,128)}, u32[]{:S(2)}) copy-start(f32[24,1152]{1,0:T(8,128)} %get-tuple-element.12) | copy-start | bytes 331780

commit v18 on v16

--- a/solution.py
+++ b/solution.py
@@ -118,12 +118,13 @@
     )(values, cuts.reshape(count, 1), jnp.asarray(twc), jnp.asarray(tws), split_table(forward),
       split_table(inverse), jnp.asarray(folded))
 
-def prefix_over(value, axis, before):
+def prefix_over(field, axis, before):
     count = lax.axis_size(axis)
     rank = lax.axis_index(axis)
-    copies = jnp.broadcast_to(value, (count, *value.shape))
+    owners = jnp.arange(count, dtype=jnp.int32)
+    live = (owners < count + rank).astype(field.dtype)
+    copies = jnp.sum(field[None] * live[:, None, None, None], axis=2)
     pieces = lax.all_to_all(copies, axis, split_axis=0, concat_axis=0, tiled=True)
-    owners = jnp.arange(count, dtype=jnp.int32)
     chosen = owners < rank if before else owners > rank
     return jnp.sum(jnp.where(chosen[:, None, None], pieces, 0.0), axis=0)
 
@@ -158,13 +159,11 @@
     mass_ext = jnp.concatenate([from_south[rows - 1 : rows], layer_mass], axis=0)
     theta_ext = jnp.concatenate([from_south[2 * rows - 1 : 2 * rows], theta_field], axis=0)
     surface_ext = jnp.concatenate([from_south[3 * rows - 1 :], surface], axis=0)
-    column = jnp.sum(mass_ext, axis=1)
-    above_mass = prefix_over(column, "lev", True)
+    above_mass = prefix_over(mass_ext, "lev", True)
     bottom = TOP_PRESSURE + above_mass[:, None] + jnp.cumsum(mass_ext, axis=1)
     top_press = bottom - mass_ext
     thickness = GAS_CONST * theta_ext * (jnp.log(bottom) - jnp.log(top_press))
-    depth_sum = jnp.sum(thickness, axis=1)
-    below_depth = prefix_over(depth_sum, "lev", False)
+    below_depth = prefix_over(thickness, "lev", False)
     inclusive = jnp.flip(jnp.cumsum(jnp.flip(thickness, 1), axis=1), 1)
     height_ext = surface_ext + below_depth[:, None] + (inclusive - thickness) + 0.5 * thickness
     fields = jnp.concatenate([wind_east, wind_north, flux_east, flux_north], axis=0)

time: 51.7 us -> 52.5 us (1.015)
  other arithmetic: 5.7 us -> 7.93 us
  local copies, waits for them, and re-layouts: 5.97 us -> 4.6 us
    reduce_sum x2, other arithmetic: 0.21 us -> 2.23 us  [prefix_over(): copies = jnp.sum(field[None] * live[:, None, None, None], axis=2)]
    broadcast_in_dim x2 -> x0, local copies, waits for them, and re-layouts: 1.35 us -> none  [prefix_over(): copies = jnp.broadcast_to(value, (count, *value.shape))]
where the time goes in v18:
time: 52.5 us; the launch traced here: 51.9 us
  starting transfers between devices  19.4 us (37%)
  waiting for transfers between devices  15.9 us (30%)
  other arithmetic  7.93 us (15%)
  local copies, waits for them, and re-layouts  4.6 us (9%)
  Pallas kernels  3.2 us (6%)
  between operations  0.94 us (2%)
    all_to_all x2, waiting for transfers between devices, prefix_over(): lax.all_to_all(copies, axis, split_axis=0, concat_axis=0, tiled=True)  15.3 us
    all_to_all x2, starting transfers between devices, prefix_over(): lax.all_to_all(copies, axis, split_axis=0, concat_axis=0, tiled=True)  10.5 us
    ppermute x1, starting transfers between devices, local(): lax.ppermute(to_south, 'lat', [(i + 1, i) for i in range(count - 1)])  6.96 us
    pallas_call x1, Pallas kernels, filter_rows(): pl.pallas_call(filter_kernel, out_shape=(jax.ShapeDtypeStruct(values.shap...  3.2 us
    reduce_sum x2, other arithmetic, prefix_over(): copies = jnp.sum(field[None] * live[:, None, None, None], axis=2)  2.23 us
    ppermute x1, starting transfers between devices, local(): lax.ppermute(to_north, 'lat', [(i, i + 1) for i in range(count - 1)])  1.92 us
    transpose x2, other arithmetic, local(): return tuple((jnp.transpose(v, (1, 0, 2)) for v in outputs))  1.58 us
    unnamed x18, local copies, waits for them, and re-layouts  1.09 us
  transfers between devices with their start and end apart: 4, of which 3 were waited for; matrix products, arithmetic and copies ran while one was open for 10% of the time, Pallas kernels for 0%

profile of v18, /device:TPU:256, one launch (start us, length us, event | category | flops | bytes accessed | tf_op | source)
XLA Modules:
  0.0 51.9 jit_solution(3850794412581826591)
XLA Ops:
  0.6 0.7 %broadcast_in_dim.22 = f32[3,8,1152]{2,1,0:T(8,128)S(1)} broadcast(f32[3,1152]{1,0:T(4,128)} %param.17), dimensions={0,2} | broadcast | bytes 124416 | tf_op jit(solution)/shard_map/broadcast_in_dim | solution.py:141
  1.4 1.1 %pad_maximum_fusion.3 = (f32[9,8,1152]{2,1,0:T(8,128)S(1)}, f32[9,8,1152]{2,1,0:T(8,128)S(1)}) fusion(f32[3,8,1152]{2,1,0:T(8,128)S(1)} %broadcast_in_dim.22, f32[3,8,1152]{2,1,0:T(8,128)} %bitcast.57, f32[3,8,1152]{2,1,0:T(8,128)} %bitcast.66, f32[3,8,1152]{2,1,0:T(8,128)} %bitcast.76), kind=kLoop, calls=%fused_computation.6 | loop fusion | flops 248832 | bytes 1105920 | tf_op jit(solution)/shard_map/concatenate | solution.py:142
  2.5 1.9 %collective-permute-start.1 = (f32[9,8,1152]{2,1,0:T(8,128)S(1)}, f32[9,8,1152]{2,1,0:T(8,128)S(1)}, u32[]{:S(2)}, u32[]{:S(2)}) collective-permute-start(f32[9,8,1152]{2,1,0:T(8,128)S(1)} %get-tuple-element.24), channel_id=1, source_target_pairs={{0,8},{8,16},{16,24},{24,32},{32,40},{40,48},{48,56},{56,64},{64,7... | collective-permute-start | bytes 995336 | tf_op jit(solution)/shard_map/ppermute | solution.py:145
  4.4 7.0 %collective-permute-start = (f32[9,8,1152]{2,1,0:T(8,128)S(1)}, f32[9,8,1152]{2,1,0:T(8,128)S(1)}, u32[]{:S(2)}, u32[]{:S(2)}) collective-permute-start(f32[9,8,1152]{2,1,0:T(8,128)S(1)} %get-tuple-element.25), channel_id=1, source_target_pairs={{8,0},{16,8},{24,16},{32,24},{40,32},{48,40},{56,48},{64,56},{72,6... | collective-permute-start | bytes 995336 | tf_op jit(solution)/shard_map/ppermute | solution.py:146
  11.4 0.1 fusion.62
  11.5 0.1 fusion.64
  11.9 0.4 copy-done.1
  12.4 0.1 fusion.60
  12.8 0.2 fusion.45
  13.0 0.5 copy-done.7
  13.5 0.2 fusion.37
  13.7 0.6 %collective-permute-done.1 = f32[9,8,1152]{2,1,0:T(8,128)S(1)} collective-permute-done((f32[9,8,1152]{2,1,0:T(8,128)S(1)}, f32[9,8,1152]{2,1,0:T(8,128)S(1)}, u32[]{:S(2)}, u32[]{:S(2)}) %collective-permute-start.1) | collective-permute-done | bytes 331808 | tf_op jit(solution)/shard_map/ppermute | solution.py:145
  14.3 1.1 %multiply_reduce_fusion.1 = f32[8,4,1152]{2,1,0:T(4,128)} fusion(f32[8]{0:T(128)S(1)} %compare_convert_fusion.1, f32[4,8,1152]{2,1,0:T(8,128)S(1)} %pad_maximum_fusion.8), kind=kLoop, calls=%fused_computation.2 | loop fusion | flops 552960 | bytes 294944 | tf_op jit(solution)/shard_map/reduce_sum | solution.py:126
  15.4 7.1 %all-to-all-start = ((f32[8,4,1152]{2,1,0:T(4,128)}), f32[8,4,1152]{2,1,0:T(4,128)S(1)}, u32[]{:S(2)}, u32[]{:S(2)}) async-start(f32[8,4,1152]{2,1,0:T(4,128)} %multiply_reduce_fusion.1), calls=%async_computation | async-start | bytes 294912 | tf_op jit(solution)/shard_map/all_to_all | solution.py:127
  22.5 0.1 reduce_window_sum.17
  22.7 9.0 %all-to-all-done = f32[8,4,1152]{2,1,0:T(4,128)S(1)} async-done(((f32[8,4,1152]{2,1,0:T(4,128)}), f32[8,4,1152]{2,1,0:T(4,128)S(1)}, u32[]{:S(2)}, u32[]{:S(2)}) %all-to-all-start) | async-done | bytes 147488 | tf_op jit(solution)/shard_map/all_to_all | solution.py:127
  31.7 0.1 select_reduce_fusion.1
  31.9 0.1 maximum_multiply_fusion
  32.0 1.1 %multiply_reduce_fusion = f32[8,4,1152]{2,1,0:T(4,128)} fusion(f32[4,8,1152]{2,1,0:T(8,128)S(1)} %get-tuple-element.35, f32[8]{0:T(128)S(1)} %compare_convert_fusion.1), kind=kLoop, calls=%fused_computation.1 | loop fusion | flops 552960 | bytes 294944 | tf_op jit(solution)/shard_map/reduce_sum | solution.py:126
  33.1 3.4 %all-to-all-start.1 = ((f32[8,4,1152]{2,1,0:T(4,128)}), f32[8,4,1152]{2,1,0:T(4,128)S(1)}, u32[]{:S(2)}, u32[]{:S(2)}) async-start(f32[8,4,1152]{2,1,0:T(4,128)} %multiply_reduce_fusion), calls=%async_computation.1 | async-start | bytes 294912 | tf_op jit(solution)/shard_map/all_to_all | solution.py:127
  36.6 0.7 %gather_fusion = s32[13]{0:T(128)S(1)} fusion(s32[192]{0:T(256)S(1)} %copy-done, s32[1024]{0:T(1024)S(1)} %pad_clamp_fusion), kind=kCustom, calls=%fused_computation | custom fusion | bytes 156 | tf_op jit(solution)/shard_map/gather | solution.py:173
  37.4 0.7 %reshape_reshape.4.cut_ref = s32[104,1]{1,0:T(8,128)} reshape(s32[13,8]{1,0:T(8,128)S(1)} %broadcast_in_dim.26) | data formatting | bytes 832 | tf_op jit(solution)/shard_map/reshape;reshape | solution.py:118
  38.1 0.1 rev.7
  38.2 0.1 reduce_window_sum.18
  38.4 0.2 rev.8
  38.5 0.8 %pad_maximum_fusion = f32[13,8,1152]{2,1,0:T(8,128)} fusion(f32[4,8,1152]{2,1,0:T(8,128)S(1)} %get-tuple-element.36, f32[3,8,1152]{2,1,0:T(8,128)S(1)} %fusion.37, f32[3,8,1152]{2,1,0:T(8,128)S(1)} %bitcast.78, f32[3,8,1152]{2,1,0:T(8,128)S(1)} %bitcast.79), kind=kLoop, calls=%fused_computation.3 | loop fusion | flops 359424 | bytes 958464 | tf_op jit(solution)/shard_map/concatenate | solution.py:169
  39.4 6.3 %all-to-all-done.1 = f32[8,4,1152]{2,1,0:T(4,128)S(1)} async-done(((f32[8,4,1152]{2,1,0:T(4,128)}), f32[8,4,1152]{2,1,0:T(4,128)S(1)}, u32[]{:S(2)}, u32[]{:S(2)}) %all-to-all-start.1) | async-done | bytes 147488 | tf_op jit(solution)/shard_map/all_to_all | solution.py:127
  45.7 0.1 select_reduce_fusion
  45.9 3.2 %shard_map.164 = (f32[104,1152]{1,0:T(8,128)}, f32[24,1152]{1,0:T(8,128)}) custom-call(f32[104,1152]{1,0:T(8,128)} %bitcast.75, s32[104,1]{1,0:T(8,128)} %reshape_reshape.4.cut_ref, f32[9,128]{1,0:T(8,128)} %constant.60.clone.twc_ref, f32[9,128]{1,0:T(8,128)} %constant.61.clone.tws_ref, bf16[2,256,256]{2,1,0:T(8,128)(2,1)} %constant.76.fwd_ref, ...), custom_call_target="tpu_custom_call" | custom-call | tf_op jit(solution)/shard_map/pallas_call | solution.py:112
  49.1 1.0 %fusion.6 = f32[4,8,1152]{2,1,0:T(8,128)S(1)} fusion(f32[3,8,1152]{2,1,0:T(8,128)S(1)} %bitcast.65, f32[3,8,1152]{2,1,0:T(8,128)S(1)} %get-tuple-element.19, f32[3,8,1152]{2,1,0:T(8,128)S(1)} %get-tuple-element.17, f32[104,1152]{1,0:T(8,128)} %get-tuple-element.10), kind=kLoop, calls=%fused_computation.29 | loop fusion | flops 552960 | bytes 626688 | tf_op jit(solution)/shard_map/mul | solution.py:188
  50.2 0.8 %fusion.52 = (f32[8,3,1152]{2,0,1:T(8,128)}, f32[8,3,1152]{2,0,1:T(8,128)}, f32[8,3,1152]{2,0,1:T(8,128)}) fusion(f32[4,8,1152]{2,1,0:T(8,128)S(1)} %fusion.28, f32[104,1152]{1,0:T(8,128)S(1)} %copy-done.5, f32[3]{0:T(128)S(1)} %compare_convert_fusion, f32[3,8,1151]{2,1,0:T(8,128)S(1)} %slice.235, f32[3,8,1]{2,1,0:T(8,128)S(1)} %slice.234), kind=kLoop, calls=%fused_computation.97 | loop fusion | flops 221184 | bytes 884748 | tf_op jit(solution)/shard_map/transpose | solution.py:197
  51.2 0.8 %fusion.32 = (f32[8,3,1152]{2,0,1:T(8,128)}, f32[8,3,1152]{2,0,1:T(8,128)}) fusion(f32[4,8,1152]{2,1,0:T(8,128)S(1)} %fusion.6, f32[3,8,1]{2,1,0:T(8,128)S(1)} %slice-done, f32[3,8,1151]{2,1,0:T(8,128)S(1)} %slice.303, f32[3,8,1152]{2,1,0:T(8,128)S(1)} %copy-done.4, f32[24,1152]{1,0:T(8,128)S(1)} %copy-done.8, f32[104,1152]{1,0:T(8,128)S(1)} %copy-done.5, ...), kind=kLoop, calls=%fused_computation.65 | loop fusion | flops 387072 | bytes 1327104 | tf_op jit(solution)/shard_map/transpose | solution.py:197
  (47 shorter events, 1.3 us)
Async XLA Ops:
  0.6 36.0 %copy-start = (s32[192]{0:T(256)S(1)}, s32[192]{0:T(256)}, u32[]{:S(2)}) copy-start(s32[192]{0:T(256)} %param.18) | copy-start | bytes 2308
  1.4 10.0 %copy-start.2 = (f32[8,3,1152]{2,0,1:T(8,128)S(1)}, f32[8,3,1152]{2,0,1:T(8,128)}, u32[]{:S(2)}) copy-start(f32[8,3,1152]{2,0,1:T(8,128)} %param.15) | copy-start | bytes 331780
  2.5 11.8 %collective-permute-start.1 = (f32[9,8,1152]{2,1,0:T(8,128)S(1)}, f32[9,8,1152]{2,1,0:T(8,128)S(1)}, u32[]{:S(2)}, u32[]{:S(2)}) collective-permute-start(f32[9,8,1152]{2,1,0:T(8,128)S(1)} %get-tuple-element.24), channel_id=1, source_target_pairs={{0,8},{8,16},{16,24},{24,32},{32,40},{40,48},{48,56},{56,64},{64,7... | collective-permute-start | bytes 995336 | tf_op jit(solution)/shard_map/ppermute | solution.py:145
  4.4 18.3 %collective-permute-start = (f32[9,8,1152]{2,1,0:T(8,128)S(1)}, f32[9,8,1152]{2,1,0:T(8,128)S(1)}, u32[]{:S(2)}, u32[]{:S(2)}) collective-permute-start(f32[9,8,1152]{2,1,0:T(8,128)S(1)} %get-tuple-element.25), channel_id=1, source_target_pairs={{8,0},{16,8},{24,16},{32,24},{40,32},{48,40},{56,48},{64,56},{72,6... | collective-permute-start | bytes 995336 | tf_op jit(solution)/shard_map/ppermute | solution.py:146
  11.4 0.9 %copy-start.1 = (f32[8,3,1152]{2,0,1:T(8,128)S(1)}, f32[8,3,1152]{2,0,1:T(8,128)}, u32[]{:S(2)}) copy-start(f32[8,3,1152]{2,0,1:T(8,128)} %param.16) | copy-start | bytes 331780
  12.6 0.9 %copy-start.7 = (f32[8,3,1152]{2,0,1:T(8,128)S(1)}, f32[8,3,1152]{2,0,1:T(8,128)}, u32[]{:S(2)}) copy-start(f32[8,3,1152]{2,0,1:T(8,128)} %param.13) | copy-start | bytes 331780
  13.0 23.6 %copy-start.3 = (f32[3,8,1152]{2,1,0:T(8,128)}, f32[3,8,1152]{2,1,0:T(8,128)S(1)}, u32[]{:S(2)}) copy-start(f32[3,8,1152]{2,1,0:T(8,128)S(1)} %fusion.45) | copy-start | bytes 331780
  15.4 16.4 %all-to-all-start = ((f32[8,4,1152]{2,1,0:T(4,128)}), f32[8,4,1152]{2,1,0:T(4,128)S(1)}, u32[]{:S(2)}, u32[]{:S(2)}) async-start(f32[8,4,1152]{2,1,0:T(4,128)} %multiply_reduce_fusion.1), calls=%async_computation | async-start | bytes 294912 | tf_op jit(solution)/shard_map/all_to_all | solution.py:127
  22.6 9.2 %copy-start.6 = (f32[8,3,1152]{2,0,1:T(8,128)S(1)}, f32[8,3,1152]{2,0,1:T(8,128)}, u32[]{:S(2)}) copy-start(f32[8,3,1152]{2,0,1:T(8,128)} %param.14) | copy-start | bytes 331780
  33.1 12.6 %all-to-all-start.1 = ((f32[8,4,1152]{2,1,0:T(4,128)}), f32[8,4,1152]{2,1,0:T(4,128)S(1)}, u32[]{:S(2)}, u32[]{:S(2)}) async-start(f32[8,4,1152]{2,1,0:T(4,128)} %multiply_reduce_fusion), calls=%async_computation.1 | async-start | bytes 294912 | tf_op jit(solution)/shard_map/all_to_all | solution.py:127
  49.1 1.1 %copy-start.5 = (f32[104,1152]{1,0:T(8,128)S(1)}, f32[104,1152]{1,0:T(8,128)}, u32[]{:S(2)}) copy-start(f32[104,1152]{1,0:T(8,128)} %get-tuple-element.10) | copy-start | bytes 1437700
  50.2 0.9 %copy-start.4 = (f32[3,8,1152]{2,1,0:T(8,128)S(1)}, f32[3,8,1152]{2,1,0:T(8,128)}, u32[]{:S(2)}) copy-start(f32[3,8,1152]{2,1,0:T(8,128)} %copy-done.3) | copy-start | bytes 331780
  50.2 0.9 %slice-start = ((f32[3,8,1152]{2,1,0:T(8,128)}), f32[3,8,1]{2,1,0:T(8,128)S(1)}, s32[]{:S(2)}) async-start(f32[3,8,1152]{2,1,0:T(8,128)} %copy-done.3), calls=%async_computation.2 | async-start | bytes 24576 | tf_op jit(solution)/shard_map/jit(_roll_static)/slice | solution.py:187
  50.2 1.0 %copy-start.8 = (f32[24,1152]{1,0:T(8,128)S(1)}, f32[24,1152]{1,0:T(8,128)}, u32[]{:S(2)}) copy-start(f32[24,1152]{1,0:T(8,128)} %get-tuple-element.12) | copy-start | bytes 331780

commit v19 on v16

--- a/solution.py
+++ b/solution.py
@@ -61,7 +61,9 @@
     return product(high, table_high) + (product(high, table_low) + product(low, table_high))
 
 
-def filter_kernel(x_ref, cut_ref, twc_ref, tws_ref, fwd_ref, inv_ref, fold_ref, o_ref, roll_ref):
+def filter_kernel(
+    x_ref, cut_ref, twc_ref, tws_ref, fwd_ref, inv_ref, fold_ref, face_ref, o_ref, roll_ref, heat_ref
+):
     rows, lanes = FACTOR_ROWS, FACTOR_LANES
     count, length = x_ref.shape
     c9, s9 = fft_tables(length)[:2]
@@ -104,9 +106,10 @@
             )
     block = roll_ref.shape[0]
     roll_ref[...] = pltpu.roll(o_ref[2 * block : 3 * block, :], length - 1, 1)
-
-
-def filter_rows(values, cuts, block):
+    heat_ref[...] = o_ref[3 * block : count, :] * face_ref[...]
+
+
+def filter_rows(values, cuts, block, faces):
     count, length = values.shape
     _, _, twc, tws, forward, inverse, folded = fft_tables(length)
     return pl.pallas_call(
@@ -114,9 +117,10 @@
         out_shape=(
             jax.ShapeDtypeStruct(values.shape, values.dtype),
             jax.ShapeDtypeStruct((block, length), values.dtype),
+            jax.ShapeDtypeStruct(faces.shape, values.dtype),
         ),
     )(values, cuts.reshape(count, 1), jnp.asarray(twc), jnp.asarray(tws), split_table(forward),
-      split_table(inverse), jnp.asarray(folded))
+      split_table(inverse), jnp.asarray(folded), faces)
 
 def prefix_over(value, axis, before):
     count = lax.axis_size(axis)
@@ -173,7 +177,10 @@
     row_cuts = jnp.broadcast_to(
         filter_cutoff[jnp.minimum(cut_rows, nlat_all - 1)][:, None], fields.shape[:2]
     ).reshape(-1)
-    smooth, east_next = filter_rows(fields.reshape(-1, length), row_cuts, rows * levels)
+    smooth, east_next, heat_north = filter_rows(
+        fields.reshape(-1, length), row_cuts, rows * levels, theta_faces.reshape(-1, length)
+    )
+    heat_north = heat_north.reshape(rows + 1, levels, length)
     smooth = smooth.reshape(fields.shape)
     east_next = east_next.reshape(rows, levels, length)
     east_smooth = smooth[:rows]
@@ -186,7 +193,6 @@
     lon_theta = face_lon(theta_field)
     heat_east = east_flux * lon_theta
     heat_next = east_next * jnp.roll(lon_theta, -1, -1)
-    heat_north = north_full * theta_faces
     new_heat = theta_field * layer_mass - TIME_STEP * (
         heat_next - heat_east + (heat_north[1:] - heat_north[:-1])
     )

time: 51.7 us -> 56.3 us (1.089)
  the two profiles are of different devices: /device:TPU:256 before, /device:TPU:199 now
where the time goes in v19:
time: 56.3 us; the launch traced here: 55.8 us
  waiting for transfers between devices  20.3 us (36%)
  starting transfers between devices  17.8 us (32%)
  local copies, waits for them, and re-layouts  7.15 us (13%)
  other arithmetic  6.32 us (11%)
  Pallas kernels  3.31 us (6%)
  between operations  0.95 us (2%)
    all_to_all x2, waiting for transfers between devices, prefix_over(): lax.all_to_all(copies, axis, split_axis=0, concat_axis=0, tiled=True)  13.1 us
    all_to_all x2, starting transfers between devices, prefix_over(): lax.all_to_all(copies, axis, split_axis=0, concat_axis=0, tiled=True)  10.2 us
    ppermute x1, waiting for transfers between devices, local(): lax.ppermute(to_south, 'lat', [(i + 1, i) for i in range(count - 1)])  7.21 us
    ppermute x1, starting transfers between devices, local(): lax.ppermute(to_north, 'lat', [(i, i + 1) for i in range(count - 1)])  5.69 us
    pallas_call x1, Pallas kernels, filter_rows(): pl.pallas_call(filter_kernel, out_shape=(jax.ShapeDtypeStruct(values.shap...  3.31 us
    transpose x2, other arithmetic, local(): return tuple((jnp.transpose(v, (1, 0, 2)) for v in outputs))  2.61 us
    unnamed x20, local copies, waits for them, and re-layouts  2.23 us
    ppermute x1, starting transfers between devices, local(): lax.ppermute(to_south, 'lat', [(i + 1, i) for i in range(count - 1)])  1.92 us
  transfers between devices with their start and end apart: 4, of which 3 were waited for; matrix products, arithmetic and copies ran while one was open for 8% of the time, Pallas kernels for 0%

profile of v19, /device:TPU:199, one launch (start us, length us, event | category | flops | bytes accessed | tf_op | source)
XLA Modules:
  0.0 55.8 jit_solution(14965872572020125438)
XLA Ops:
  0.7 0.8 %broadcast_in_dim.43 = f32[3,8,1152]{2,1,0:T(8,128)S(1)} broadcast(f32[3,1152]{1,0:T(4,128)} %param.17), dimensions={0,2} | broadcast | bytes 124416 | tf_op jit(solution)/shard_map/broadcast_in_dim | solution.py:144
  1.4 0.1 copy-done.1
  1.6 1.0 %pad_maximum_fusion.3 = (f32[9,8,1152]{2,1,0:T(8,128)S(1)}, f32[9,8,1152]{2,1,0:T(8,128)S(1)}) fusion(f32[3,8,1152]{2,1,0:T(8,128)S(1)} %broadcast_in_dim.43, f32[3,8,1152]{2,1,0:T(8,128)} %bitcast.68, f32[3,8,1152]{2,1,0:T(8,128)S(1)} %bitcast.59, f32[3,8,1152]{2,1,0:T(8,128)} %bitcast.77), kind=kLoop, calls=%fused_computation.4 | loop fusion | flops 248832 | bytes 1105920 | tf_op jit(solution)/shard_map/concatenate | solution.py:145
  2.6 5.7 %collective-permute-start.1 = (f32[9,8,1152]{2,1,0:T(8,128)S(1)}, f32[9,8,1152]{2,1,0:T(8,128)S(1)}, u32[]{:S(2)}, u32[]{:S(2)}) collective-permute-start(f32[9,8,1152]{2,1,0:T(8,128)S(1)} %get-tuple-element.28), channel_id=1, source_target_pairs={{0,8},{8,16},{16,24},{24,32},{32,40},{40,48},{48,56},{56,64},{64,7... | collective-permute-start | bytes 995336 | tf_op jit(solution)/shard_map/ppermute | solution.py:148
  8.3 1.9 %collective-permute-start = (f32[9,8,1152]{2,1,0:T(8,128)S(1)}, f32[9,8,1152]{2,1,0:T(8,128)S(1)}, u32[]{:S(2)}, u32[]{:S(2)}) collective-permute-start(f32[9,8,1152]{2,1,0:T(8,128)S(1)} %get-tuple-element.29), channel_id=1, source_target_pairs={{8,0},{16,8},{24,16},{32,24},{40,32},{48,40},{56,48},{64,56},{72,6... | collective-permute-start | bytes 995336 | tf_op jit(solution)/shard_map/ppermute | solution.py:149
  10.3 0.1 fusion.66
  10.7 0.6 %copy-done.2 = f32[8,3,1152]{2,0,1:T(8,128)S(1)} copy-done((f32[8,3,1152]{2,0,1:T(8,128)S(1)}, f32[8,3,1152]{2,0,1:T(8,128)}, u32[]{:S(2)}) %copy-start.2) | copy-done | bytes 110616
  11.8 0.6 %copy-done.7 = f32[8,3,1152]{2,0,1:T(8,128)S(1)} copy-done((f32[8,3,1152]{2,0,1:T(8,128)S(1)}, f32[8,3,1152]{2,0,1:T(8,128)}, u32[]{:S(2)}) %copy-start.7) | copy-done | bytes 110616
  12.4 0.2 fusion.33
  12.6 0.2 fusion.41
  12.8 7.2 %collective-permute-done = f32[9,8,1152]{2,1,0:T(8,128)S(1)} collective-permute-done((f32[9,8,1152]{2,1,0:T(8,128)S(1)}, f32[9,8,1152]{2,1,0:T(8,128)S(1)}, u32[]{:S(2)}, u32[]{:S(2)}) %collective-permute-start) | collective-permute-done | bytes 331808 | tf_op jit(solution)/shard_map/ppermute | solution.py:149
  20.1 0.9 %copy-done.5 = f32[8,3,1152]{2,0,1:T(8,128)S(1)} copy-done((f32[8,3,1152]{2,0,1:T(8,128)S(1)}, f32[8,3,1152]{2,0,1:T(8,128)}, u32[]{:S(2)}) %copy-start.5) | copy-done | bytes 110616
  20.9 0.1 fusion.55
  21.0 0.7 %broadcast_in_dim.46 = f32[8,4,1152]{2,1,0:T(4,128)} broadcast(f32[4,1152]{1,0:T(4,128)S(1)} %get-tuple-element.31), dimensions={1,2} | broadcast | bytes 165888 | tf_op jit(solution)/shard_map/broadcast_in_dim | solution.py:128
  21.7 6.8 %all-to-all-start = ((f32[8,4,1152]{2,1,0:T(4,128)}), f32[8,4,1152]{2,1,0:T(4,128)S(1)}, u32[]{:S(2)}, u32[]{:S(2)}) async-start(f32[8,4,1152]{2,1,0:T(4,128)} %broadcast_in_dim.46), calls=%async_computation | async-start | bytes 294912 | tf_op jit(solution)/shard_map/all_to_all | solution.py:129
  28.5 0.1 reduce_window_sum.17
  28.7 7.9 %all-to-all-done = f32[8,4,1152]{2,1,0:T(4,128)S(1)} async-done(((f32[8,4,1152]{2,1,0:T(4,128)}), f32[8,4,1152]{2,1,0:T(4,128)S(1)}, u32[]{:S(2)}, u32[]{:S(2)}) %all-to-all-start) | async-done | bytes 147488 | tf_op jit(solution)/shard_map/all_to_all | solution.py:129
  36.6 0.1 select_reduce_fusion.1
  36.8 0.8 %fusion.56 = (f32[4,1152]{1,0:T(4,128)S(1)}, f32[4,8,1152]{2,1,0:T(8,128)S(1)}, f32[32,1152]{1,0:T(8,128)}) fusion(f32[3,8,1152]{2,1,0:T(8,128)S(1)} %bitcast.67, f32[1,8,1152]{2,1,0:T(8,128)S(1)} %get-tuple-element.26, f32[4,8,1152]{2,1,0:T(8,128)S(1)} %reduce_window_sum.17, f32[4,1152]{1,0:T(4,128)S(1)} %broadcast_add_fusion, ...), kind=kLoop, calls=%fused_computation.109 | loop fusion | flops 769536 | bytes 995328 | tf_op jit(solution)/shard_map/reduce_sum | solution.py:170
  37.5 0.7 %broadcast_in_dim.48 = f32[8,4,1152]{2,1,0:T(4,128)} broadcast(f32[4,1152]{1,0:T(4,128)S(1)} %get-tuple-element.15), dimensions={1,2} | broadcast | bytes 165888 | tf_op jit(solution)/shard_map/broadcast_in_dim | solution.py:128
  38.2 3.4 %all-to-all-start.1 = ((f32[8,4,1152]{2,1,0:T(4,128)}), f32[8,4,1152]{2,1,0:T(4,128)S(1)}, u32[]{:S(2)}, u32[]{:S(2)}) async-start(f32[8,4,1152]{2,1,0:T(4,128)} %broadcast_in_dim.48), calls=%async_computation.1 | async-start | bytes 294912 | tf_op jit(solution)/shard_map/all_to_all | solution.py:129
  41.7 0.7 %gather_fusion = s32[13]{0:T(128)S(1)} fusion(s32[192]{0:T(256)S(1)} %copy-done, s32[1024]{0:T(1024)S(1)} %pad_clamp_fusion), kind=kCustom, calls=%fused_computation | custom fusion | bytes 156 | tf_op jit(solution)/shard_map/gather | solution.py:178
  42.5 0.7 %reshape_reshape.4.cut_ref = s32[104,1]{1,0:T(8,128)} reshape(s32[13,8]{1,0:T(8,128)S(1)} %broadcast_in_dim.49) | data formatting | bytes 832 | tf_op jit(solution)/shard_map/reshape;reshape | solution.py:122
  43.2 0.8 %pad_maximum_fusion = f32[13,8,1152]{2,1,0:T(8,128)} fusion(f32[4,8,1152]{2,1,0:T(8,128)S(1)} %get-tuple-element.42, f32[3,8,1152]{2,1,0:T(8,128)S(1)} %fusion.33, f32[3,8,1152]{2,1,0:T(8,128)S(1)} %bitcast.79, f32[3,8,1152]{2,1,0:T(8,128)S(1)} %bitcast.80), kind=kLoop, calls=%fused_computation.1 | loop fusion | flops 359424 | bytes 958464 | tf_op jit(solution)/shard_map/concatenate | solution.py:174
  44.0 0.1 rev.7
  44.1 0.1 reduce_window_sum.18
  44.3 0.2 rev.8
  44.5 5.1 %all-to-all-done.1 = f32[8,4,1152]{2,1,0:T(4,128)S(1)} async-done(((f32[8,4,1152]{2,1,0:T(4,128)}), f32[8,4,1152]{2,1,0:T(4,128)S(1)}, u32[]{:S(2)}, u32[]{:S(2)}) %all-to-all-start.1) | async-done | bytes 147488 | tf_op jit(solution)/shard_map/all_to_all | solution.py:129
  49.6 0.1 select_reduce_fusion
  49.8 3.3 %shard_map.164 = (f32[104,1152]{1,0:T(8,128)}, f32[24,1152]{1,0:T(8,128)}, f32[32,1152]{1,0:T(8,128)}) custom-call(f32[104,1152]{1,0:T(8,128)} %bitcast.76, s32[104,1]{1,0:T(8,128)} %reshape_reshape.4.cut_ref, f32[9,128]{1,0:T(8,128)} %constant.58.clone.twc_ref, f32[9,128]{1,0:T(8,128)} %constant.59.clone.tws_ref, bf16[2,256,256]{2,1,0:T(8,128)(2,1)} %constant.74.fwd_ref, ...), custom_call_target="tpu_custom_call" | custom-call | tf_op jit(solution)/shard_map/pallas_call | solution.py:115
  53.2 1.8 %fusion.52 = (f32[8,3,1152]{2,0,1:T(8,128)}, f32[8,3,1152]{2,0,1:T(8,128)}, f32[8,3,1152]{2,0,1:T(8,128)}) fusion(f32[4,8,1152]{2,1,0:T(8,128)S(1)} %fusion.28, f32[104,1152]{1,0:T(8,128)} %get-tuple-element.11, f32[3]{0:T(128)S(1)} %compare_convert_fusion, f32[3,8,1151]{2,1,0:T(8,128)S(1)} %slice.241, f32[3,8,1]{2,1,0:T(8,128)S(1)} %slice.240), kind=kLoop, calls=%fused_computation.94 | loop fusion | flops 221184 | bytes 884748 | tf_op jit(solution)/shard_map/transpose | solution.py:204
  55.1 0.8 %fusion.47 = (f32[8,3,1152]{2,0,1:T(8,128)}, f32[8,3,1152]{2,0,1:T(8,128)}) fusion(f32[3,8,1]{2,1,0:T(8,128)S(1)} %slice-done, f32[3,8,1151]{2,1,0:T(8,128)S(1)} %slice.309, f32[3,8,1152]{2,1,0:T(8,128)S(1)} %copy-done.4, f32[24,1152]{1,0:T(8,128)S(1)} %copy-done.9, f32[32,1152]{1,0:T(8,128)S(1)} %copy-done.8, f32[104,1152]{1,0:T(8,128)S(1)} %copy-done.6, ...), kind=kLoop, calls=%fused_computation.85 | loop fusion | flops 387072 | bytes 1327104 | tf_op jit(solution)/shard_map/transpose | solution.py:204
  (47 shorter events, 1.2 us)
Async XLA Ops:
  0.6 41.1 %copy-start = (s32[192]{0:T(256)S(1)}, s32[192]{0:T(256)}, u32[]{:S(2)}) copy-start(s32[192]{0:T(256)} %param.18) | copy-start | bytes 2308
  0.6 0.9 %copy-start.1 = (f32[8,3,1152]{2,0,1:T(8,128)S(1)}, f32[8,3,1152]{2,0,1:T(8,128)}, u32[]{:S(2)}) copy-start(f32[8,3,1152]{2,0,1:T(8,128)} %param.15) | copy-start | bytes 331780
  2.6 10.2 %collective-permute-start.1 = (f32[9,8,1152]{2,1,0:T(8,128)S(1)}, f32[9,8,1152]{2,1,0:T(8,128)S(1)}, u32[]{:S(2)}, u32[]{:S(2)}) collective-permute-start(f32[9,8,1152]{2,1,0:T(8,128)S(1)} %get-tuple-element.28), channel_id=1, source_target_pairs={{0,8},{8,16},{16,24},{24,32},{32,40},{40,48},{48,56},{56,64},{64,7... | collective-permute-start | bytes 995336 | tf_op jit(solution)/shard_map/ppermute | solution.py:148
  8.3 11.8 %collective-permute-start = (f32[9,8,1152]{2,1,0:T(8,128)S(1)}, f32[9,8,1152]{2,1,0:T(8,128)S(1)}, u32[]{:S(2)}, u32[]{:S(2)}) collective-permute-start(f32[9,8,1152]{2,1,0:T(8,128)S(1)} %get-tuple-element.29), channel_id=1, source_target_pairs={{8,0},{16,8},{24,16},{32,24},{40,32},{48,40},{56,48},{64,56},{72,6... | collective-permute-start | bytes 995336 | tf_op jit(solution)/shard_map/ppermute | solution.py:149
  10.4 0.9 %copy-start.2 = (f32[8,3,1152]{2,0,1:T(8,128)S(1)}, f32[8,3,1152]{2,0,1:T(8,128)}, u32[]{:S(2)}) copy-start(f32[8,3,1152]{2,0,1:T(8,128)} %param.16) | copy-start | bytes 331780
  11.5 0.9 %copy-start.7 = (f32[8,3,1152]{2,0,1:T(8,128)S(1)}, f32[8,3,1152]{2,0,1:T(8,128)}, u32[]{:S(2)}) copy-start(f32[8,3,1152]{2,0,1:T(8,128)} %param.13) | copy-start | bytes 331780
  12.7 29.0 %copy-start.3 = (f32[3,8,1152]{2,1,0:T(8,128)}, f32[3,8,1152]{2,1,0:T(8,128)S(1)}, u32[]{:S(2)}) copy-start(f32[3,8,1152]{2,1,0:T(8,128)S(1)} %fusion.41) | copy-start | bytes 331780
  20.0 0.9 %copy-start.5 = (f32[8,3,1152]{2,0,1:T(8,128)S(1)}, f32[8,3,1152]{2,0,1:T(8,128)}, u32[]{:S(2)}) copy-start(f32[8,3,1152]{2,0,1:T(8,128)} %param.14) | copy-start | bytes 331780
  21.7 14.9 %all-to-all-start = ((f32[8,4,1152]{2,1,0:T(4,128)}), f32[8,4,1152]{2,1,0:T(4,128)S(1)}, u32[]{:S(2)}, u32[]{:S(2)}) async-start(f32[8,4,1152]{2,1,0:T(4,128)} %broadcast_in_dim.46), calls=%async_computation | async-start | bytes 294912 | tf_op jit(solution)/shard_map/all_to_all | solution.py:129
  38.2 11.4 %all-to-all-start.1 = ((f32[8,4,1152]{2,1,0:T(4,128)}), f32[8,4,1152]{2,1,0:T(4,128)S(1)}, u32[]{:S(2)}, u32[]{:S(2)}) async-start(f32[8,4,1152]{2,1,0:T(4,128)} %broadcast_in_dim.48), calls=%async_computation.1 | async-start | bytes 294912 | tf_op jit(solution)/shard_map/all_to_all | solution.py:129
  53.2 1.9 %copy-start.6 = (f32[104,1152]{1,0:T(8,128)S(1)}, f32[104,1152]{1,0:T(8,128)}, u32[]{:S(2)}) copy-start(f32[104,1152]{1,0:T(8,128)} %get-tuple-element.11) | copy-start | bytes 1437700
  53.2 1.9 %copy-start.4 = (f32[3,8,1152]{2,1,0:T(8,128)S(1)}, f32[3,8,1152]{2,1,0:T(8,128)}, u32[]{:S(2)}) copy-start(f32[3,8,1152]{2,1,0:T(8,128)} %copy-done.3) | copy-start | bytes 331780
  53.2 1.9 %slice-start = ((f32[3,8,1152]{2,1,0:T(8,128)}), f32[3,8,1]{2,1,0:T(8,128)S(1)}, s32[]{:S(2)}) async-start(f32[3,8,1152]{2,1,0:T(8,128)} %copy-done.3), calls=%async_computation.2 | async-start | bytes 24576 | tf_op jit(solution)/shard_map/jit(_roll_static)/slice | solution.py:195
  53.2 1.9 %copy-start.8 = (f32[32,1152]{1,0:T(8,128)S(1)}, f32[32,1152]{1,0:T(8,128)}, u32[]{:S(2)}) copy-start(f32[32,1152]{1,0:T(8,128)} %get-tuple-element.14) | copy-start | bytes 442372
  53.2 1.9 %copy-start.9 = (f32[24,1152]{1,0:T(8,128)S(1)}, f32[24,1152]{1,0:T(8,128)}, u32[]{:S(2)}) copy-start(f32[24,1152]{1,0:T(8,128)} %get-tuple-element.13) | copy-start | bytes 331780

commit v20 on v16

--- a/solution.py
+++ b/solution.py
@@ -72,6 +72,9 @@
     pieces = []
     for k in range(half):
         real_a = parts[0] + sum(float(c9[k, n]) * pairs[n - 1] for n in range(1, half))
+        if k == 0:
+            pieces.append(jnp.concatenate([real_a, jnp.zeros_like(real_a)], axis=1))
+            continue
         imag_a = sum(float(-s9[k, n]) * gaps[n - 1] for n in range(1, half))
         twc = twc_ref[k : k + 1, :]
         tws = tws_ref[k : k + 1, :]
@@ -90,6 +93,10 @@
         tws = tws_ref[k : k + 1, :]
         real_c = back[k * count : (k + 1) * count, :lanes]
         imag_c = back[k * count : (k + 1) * count, lanes:]
+        if k == 0:
+            real_d.append(real_c)
+            imag_d.append(imag_c)
+            continue
         real_d.append(real_c * twc - imag_c * tws)
         imag_d.append(imag_c * twc + real_c * tws)
     base = float(1.0 / length) * real_d[0]

time: 51.7 us -> 51.7 us (level)
  no operation moved by 1% of the time
where the time goes in v20:
time: 51.7 us; the launch traced here: 51.2 us
  starting transfers between devices  19.4 us (38%)
  waiting for transfers between devices  16.1 us (31%)
  local copies, waits for them, and re-layouts  5.97 us (12%)
  other arithmetic  5.7 us (11%)
  Pallas kernels  3.18 us (6%)
  between operations  0.94 us (2%)
    all_to_all x2, waiting for transfers between devices, prefix_over(): lax.all_to_all(copies, axis, split_axis=0, concat_axis=0, tiled=True)  15.3 us
    all_to_all x2, starting transfers between devices, prefix_over(): lax.all_to_all(copies, axis, split_axis=0, concat_axis=0, tiled=True)  10.5 us
    ppermute x1, starting transfers between devices, local(): lax.ppermute(to_south, 'lat', [(i + 1, i) for i in range(count - 1)])  6.96 us
    pallas_call x1, Pallas kernels, filter_rows(): pl.pallas_call(filter_kernel, out_shape=(jax.ShapeDtypeStruct(values.shap...  3.18 us
    ppermute x1, starting transfers between devices, local(): lax.ppermute(to_north, 'lat', [(i, i + 1) for i in range(count - 1)])  1.92 us
    transpose x2, other arithmetic, local(): return tuple((jnp.transpose(v, (1, 0, 2)) for v in outputs))  1.58 us
    broadcast_in_dim x2, local copies, waits for them, and re-layouts, prefix_over(): copies = jnp.broadcast_to(value, (count, *value.shape))  1.35 us
    unnamed x18, local copies, waits for them, and re-layouts  1.07 us
  transfers between devices with their start and end apart: 4, of which 3 were waited for; matrix products, arithmetic and copies ran while one was open for 10% of the time, Pallas kernels for 0%

profile of v20, /device:TPU:256, one launch (start us, length us, event | category | flops | bytes accessed | tf_op | source)
XLA Modules:
  0.0 51.2 jit_solution(10057690044550243733)
XLA Ops:
  0.7 0.8 %broadcast_in_dim.43 = f32[3,8,1152]{2,1,0:T(8,128)S(1)} broadcast(f32[3,1152]{1,0:T(4,128)} %param.17), dimensions={0,2} | broadcast | bytes 124416 | tf_op jit(solution)/shard_map/broadcast_in_dim | solution.py:147
  1.4 0.1 copy-done.1
  1.6 1.0 %pad_maximum_fusion.3 = (f32[9,8,1152]{2,1,0:T(8,128)S(1)}, f32[9,8,1152]{2,1,0:T(8,128)S(1)}) fusion(f32[3,8,1152]{2,1,0:T(8,128)S(1)} %broadcast_in_dim.43, f32[3,8,1152]{2,1,0:T(8,128)S(1)} %bitcast.57, f32[3,8,1152]{2,1,0:T(8,128)} %bitcast.66, f32[3,8,1152]{2,1,0:T(8,128)} %bitcast.76), kind=kLoop, calls=%fused_computation.4 | loop fusion | flops 248832 | bytes 1105920 | tf_op jit(solution)/shard_map/concatenate | solution.py:148
  2.6 1.9 %collective-permute-start.1 = (f32[9,8,1152]{2,1,0:T(8,128)S(1)}, f32[9,8,1152]{2,1,0:T(8,128)S(1)}, u32[]{:S(2)}, u32[]{:S(2)}) collective-permute-start(f32[9,8,1152]{2,1,0:T(8,128)S(1)} %get-tuple-element.26), channel_id=1, source_target_pairs={{0,8},{8,16},{16,24},{24,32},{32,40},{40,48},{48,56},{56,64},{64,7... | collective-permute-start | bytes 995336 | tf_op jit(solution)/shard_map/ppermute | solution.py:151
  4.5 7.0 %collective-permute-start = (f32[9,8,1152]{2,1,0:T(8,128)S(1)}, f32[9,8,1152]{2,1,0:T(8,128)S(1)}, u32[]{:S(2)}, u32[]{:S(2)}) collective-permute-start(f32[9,8,1152]{2,1,0:T(8,128)S(1)} %get-tuple-element.27), channel_id=1, source_target_pairs={{8,0},{16,8},{24,16},{32,24},{40,32},{48,40},{56,48},{64,56},{72,6... | collective-permute-start | bytes 995336 | tf_op jit(solution)/shard_map/ppermute | solution.py:152
  11.5 0.1 fusion.64
  11.6 0.1 fusion.66
  12.1 0.1 fusion.62
  12.5 0.2 fusion.45
  12.7 0.7 %copy-done.7 = f32[8,3,1152]{2,0,1:T(8,128)S(1)} copy-done((f32[8,3,1152]{2,0,1:T(8,128)S(1)}, f32[8,3,1152]{2,0,1:T(8,128)}, u32[]{:S(2)}) %copy-start.7) | copy-done | bytes 110616
  13.4 0.2 fusion.37
  13.6 0.7 %collective-permute-done.1 = f32[9,8,1152]{2,1,0:T(8,128)S(1)} collective-permute-done((f32[9,8,1152]{2,1,0:T(8,128)S(1)}, f32[9,8,1152]{2,1,0:T(8,128)S(1)}, u32[]{:S(2)}, u32[]{:S(2)}) %collective-permute-start.1) | collective-permute-done | bytes 331808 | tf_op jit(solution)/shard_map/ppermute | solution.py:151
  14.4 0.7 %broadcast_in_dim.46 = f32[8,4,1152]{2,1,0:T(4,128)} broadcast(f32[4,1152]{1,0:T(4,128)S(1)} %get-tuple-element.29), dimensions={1,2} | broadcast | bytes 165888 | tf_op jit(solution)/shard_map/broadcast_in_dim | solution.py:131
  15.1 7.1 %all-to-all-start = ((f32[8,4,1152]{2,1,0:T(4,128)}), f32[8,4,1152]{2,1,0:T(4,128)S(1)}, u32[]{:S(2)}, u32[]{:S(2)}) async-start(f32[8,4,1152]{2,1,0:T(4,128)} %broadcast_in_dim.46), calls=%async_computation | async-start | bytes 294912 | tf_op jit(solution)/shard_map/all_to_all | solution.py:132
  22.2 0.1 reduce_window_sum.17
  22.4 9.0 %all-to-all-done = f32[8,4,1152]{2,1,0:T(4,128)S(1)} async-done(((f32[8,4,1152]{2,1,0:T(4,128)}), f32[8,4,1152]{2,1,0:T(4,128)S(1)}, u32[]{:S(2)}, u32[]{:S(2)}) %all-to-all-start) | async-done | bytes 147488 | tf_op jit(solution)/shard_map/all_to_all | solution.py:132
  31.5 0.1 select_reduce_fusion.1
  31.6 0.2 fusion.56
  31.7 0.7 %broadcast_in_dim.48 = f32[8,4,1152]{2,1,0:T(4,128)} broadcast(f32[4,1152]{1,0:T(4,128)S(1)} %get-tuple-element.13), dimensions={1,2} | broadcast | bytes 165888 | tf_op jit(solution)/shard_map/broadcast_in_dim | solution.py:131
  32.4 3.4 %all-to-all-start.1 = ((f32[8,4,1152]{2,1,0:T(4,128)}), f32[8,4,1152]{2,1,0:T(4,128)S(1)}, u32[]{:S(2)}, u32[]{:S(2)}) async-start(f32[8,4,1152]{2,1,0:T(4,128)} %broadcast_in_dim.48), calls=%async_computation.1 | async-start | bytes 294912 | tf_op jit(solution)/shard_map/all_to_all | solution.py:132
  35.9 0.7 %gather_fusion = s32[13]{0:T(128)S(1)} fusion(s32[192]{0:T(256)S(1)} %copy-done, s32[1024]{0:T(1024)S(1)} %pad_clamp_fusion), kind=kCustom, calls=%fused_computation | custom fusion | bytes 156 | tf_op jit(solution)/shard_map/gather | solution.py:181
  36.7 0.7 %reshape_reshape.4.cut_ref = s32[104,1]{1,0:T(8,128)} reshape(s32[13,8]{1,0:T(8,128)S(1)} %broadcast_in_dim.49) | data formatting | bytes 832 | tf_op jit(solution)/shard_map/reshape;reshape | solution.py:125
  37.4 0.1 rev.7
  37.5 0.1 reduce_window_sum.18
  37.7 0.2 rev.8
  37.9 0.8 %pad_maximum_fusion = f32[13,8,1152]{2,1,0:T(8,128)} fusion(f32[4,8,1152]{2,1,0:T(8,128)S(1)} %get-tuple-element.39, f32[3,8,1152]{2,1,0:T(8,128)S(1)} %fusion.37, f32[3,8,1152]{2,1,0:T(8,128)S(1)} %bitcast.78, f32[3,8,1152]{2,1,0:T(8,128)S(1)} %bitcast.79), kind=kLoop, calls=%fused_computation.1 | loop fusion | flops 359424 | bytes 958464 | tf_op jit(solution)/shard_map/concatenate | solution.py:177
  38.7 6.3 %all-to-all-done.1 = f32[8,4,1152]{2,1,0:T(4,128)S(1)} async-done(((f32[8,4,1152]{2,1,0:T(4,128)}), f32[8,4,1152]{2,1,0:T(4,128)S(1)}, u32[]{:S(2)}, u32[]{:S(2)}) %all-to-all-start.1) | async-done | bytes 147488 | tf_op jit(solution)/shard_map/all_to_all | solution.py:132
  45.0 0.1 select_reduce_fusion
  45.2 3.2 %shard_map.164 = (f32[104,1152]{1,0:T(8,128)}, f32[24,1152]{1,0:T(8,128)}) custom-call(f32[104,1152]{1,0:T(8,128)} %bitcast.75, s32[104,1]{1,0:T(8,128)} %reshape_reshape.4.cut_ref, f32[9,128]{1,0:T(8,128)} %constant.58.clone.twc_ref, f32[9,128]{1,0:T(8,128)} %constant.59.clone.tws_ref, bf16[2,256,256]{2,1,0:T(8,128)(2,1)} %constant.74.fwd_ref, ...), custom_call_target="tpu_custom_call" | custom-call | tf_op jit(solution)/shard_map/pallas_call | solution.py:119
  48.4 1.0 %fusion.6 = f32[4,8,1152]{2,1,0:T(8,128)S(1)} fusion(f32[3,8,1152]{2,1,0:T(8,128)S(1)} %bitcast.65, f32[3,8,1152]{2,1,0:T(8,128)S(1)} %get-tuple-element.21, f32[3,8,1152]{2,1,0:T(8,128)S(1)} %get-tuple-element.19, f32[104,1152]{1,0:T(8,128)} %get-tuple-element.10), kind=kLoop, calls=%fused_computation.27 | loop fusion | flops 552960 | bytes 626688 | tf_op jit(solution)/shard_map/mul | solution.py:196
  49.5 0.8 %fusion.52 = (f32[8,3,1152]{2,0,1:T(8,128)}, f32[8,3,1152]{2,0,1:T(8,128)}, f32[8,3,1152]{2,0,1:T(8,128)}) fusion(f32[4,8,1152]{2,1,0:T(8,128)S(1)} %fusion.28, f32[104,1152]{1,0:T(8,128)S(1)} %copy-done.5, f32[3]{0:T(128)S(1)} %compare_convert_fusion, f32[3,8,1151]{2,1,0:T(8,128)S(1)} %slice.235, f32[3,8,1]{2,1,0:T(8,128)S(1)} %slice.234), kind=kLoop, calls=%fused_computation.95 | loop fusion | flops 221184 | bytes 884748 | tf_op jit(solution)/shard_map/transpose | solution.py:205
  50.5 0.8 %fusion.32 = (f32[8,3,1152]{2,0,1:T(8,128)}, f32[8,3,1152]{2,0,1:T(8,128)}) fusion(f32[4,8,1152]{2,1,0:T(8,128)S(1)} %fusion.6, f32[3,8,1]{2,1,0:T(8,128)S(1)} %slice-done, f32[3,8,1151]{2,1,0:T(8,128)S(1)} %slice.303, f32[3,8,1152]{2,1,0:T(8,128)S(1)} %copy-done.4, f32[24,1152]{1,0:T(8,128)S(1)} %copy-done.8, f32[104,1152]{1,0:T(8,128)S(1)} %copy-done.5, ...), kind=kLoop, calls=%fused_computation.63 | loop fusion | flops 387072 | bytes 1327104 | tf_op jit(solution)/shard_map/transpose | solution.py:205
  (46 shorter events, 1.3 us)
Async XLA Ops:
  0.6 35.3 %copy-start = (s32[192]{0:T(256)S(1)}, s32[192]{0:T(256)}, u32[]{:S(2)}) copy-start(s32[192]{0:T(256)} %param.18) | copy-start | bytes 2308
  0.6 0.9 %copy-start.1 = (f32[8,3,1152]{2,0,1:T(8,128)S(1)}, f32[8,3,1152]{2,0,1:T(8,128)}, u32[]{:S(2)}) copy-start(f32[8,3,1152]{2,0,1:T(8,128)} %param.16) | copy-start | bytes 331780
  1.6 9.9 %copy-start.2 = (f32[8,3,1152]{2,0,1:T(8,128)S(1)}, f32[8,3,1152]{2,0,1:T(8,128)}, u32[]{:S(2)}) copy-start(f32[8,3,1152]{2,0,1:T(8,128)} %param.15) | copy-start | bytes 331780
  2.6 11.8 %collective-permute-start.1 = (f32[9,8,1152]{2,1,0:T(8,128)S(1)}, f32[9,8,1152]{2,1,0:T(8,128)S(1)}, u32[]{:S(2)}, u32[]{:S(2)}) collective-permute-start(f32[9,8,1152]{2,1,0:T(8,128)S(1)} %get-tuple-element.26), channel_id=1, source_target_pairs={{0,8},{8,16},{16,24},{24,32},{32,40},{40,48},{48,56},{56,64},{64,7... | collective-permute-start | bytes 995336 | tf_op jit(solution)/shard_map/ppermute | solution.py:151
  4.5 17.8 %collective-permute-start = (f32[9,8,1152]{2,1,0:T(8,128)S(1)}, f32[9,8,1152]{2,1,0:T(8,128)S(1)}, u32[]{:S(2)}, u32[]{:S(2)}) collective-permute-start(f32[9,8,1152]{2,1,0:T(8,128)S(1)} %get-tuple-element.27), channel_id=1, source_target_pairs={{8,0},{16,8},{24,16},{32,24},{40,32},{48,40},{56,48},{64,56},{72,6... | collective-permute-start | bytes 995336 | tf_op jit(solution)/shard_map/ppermute | solution.py:152
  12.5 0.9 %copy-start.7 = (f32[8,3,1152]{2,0,1:T(8,128)S(1)}, f32[8,3,1152]{2,0,1:T(8,128)}, u32[]{:S(2)}) copy-start(f32[8,3,1152]{2,0,1:T(8,128)} %param.13) | copy-start | bytes 331780
  12.7 23.2 %copy-start.3 = (f32[3,8,1152]{2,1,0:T(8,128)}, f32[3,8,1152]{2,1,0:T(8,128)S(1)}, u32[]{:S(2)}) copy-start(f32[3,8,1152]{2,1,0:T(8,128)S(1)} %fusion.45) | copy-start | bytes 331780
  15.1 16.4 %all-to-all-start = ((f32[8,4,1152]{2,1,0:T(4,128)}), f32[8,4,1152]{2,1,0:T(4,128)S(1)}, u32[]{:S(2)}, u32[]{:S(2)}) async-start(f32[8,4,1152]{2,1,0:T(4,128)} %broadcast_in_dim.46), calls=%async_computation | async-start | bytes 294912 | tf_op jit(solution)/shard_map/all_to_all | solution.py:132
  22.4 9.2 %copy-start.6 = (f32[8,3,1152]{2,0,1:T(8,128)S(1)}, f32[8,3,1152]{2,0,1:T(8,128)}, u32[]{:S(2)}) copy-start(f32[8,3,1152]{2,0,1:T(8,128)} %param.14) | copy-start | bytes 331780
  32.4 12.6 %all-to-all-start.1 = ((f32[8,4,1152]{2,1,0:T(4,128)}), f32[8,4,1152]{2,1,0:T(4,128)S(1)}, u32[]{:S(2)}, u32[]{:S(2)}) async-start(f32[8,4,1152]{2,1,0:T(4,128)} %broadcast_in_dim.48), calls=%async_computation.1 | async-start | bytes 294912 | tf_op jit(solution)/shard_map/all_to_all | solution.py:132
  48.4 1.1 %copy-start.5 = (f32[104,1152]{1,0:T(8,128)S(1)}, f32[104,1152]{1,0:T(8,128)}, u32[]{:S(2)}) copy-start(f32[104,1152]{1,0:T(8,128)} %get-tuple-element.10) | copy-start | bytes 1437700
  49.5 0.9 %copy-start.4 = (f32[3,8,1152]{2,1,0:T(8,128)S(1)}, f32[3,8,1152]{2,1,0:T(8,128)}, u32[]{:S(2)}) copy-start(f32[3,8,1152]{2,1,0:T(8,128)} %copy-done.3) | copy-start | bytes 331780
  49.5 0.9 %slice-start = ((f32[3,8,1152]{2,1,0:T(8,128)}), f32[3,8,1]{2,1,0:T(8,128)S(1)}, s32[]{:S(2)}) async-start(f32[3,8,1152]{2,1,0:T(8,128)} %copy-done.3), calls=%async_computation.2 | async-start | bytes 24576 | tf_op jit(solution)/shard_map/jit(_roll_static)/slice | solution.py:195
  49.5 1.0 %copy-start.8 = (f32[24,1152]{1,0:T(8,128)S(1)}, f32[24,1152]{1,0:T(8,128)}, u32[]{:S(2)}) copy-start(f32[24,1152]{1,0:T(8,128)} %get-tuple-element.12) | copy-start | bytes 331780

commit v21 on v16

--- a/solution.py
+++ b/solution.py
@@ -79,10 +79,7 @@
             jnp.concatenate([real_a * twc + imag_a * tws, imag_a * twc - real_a * tws], axis=1)
         )
     spectrum = split_dot(jnp.concatenate(pieces, axis=0), fwd_ref[0], fwd_ref[1])
-    cuts = cut_ref[...]
-    keep = jnp.concatenate(
-        [(fold_ref[k : k + 1, :] <= cuts).astype(jnp.float32) for k in range(half)], axis=0
-    )
+    keep = cut_ref[...]
     back = split_dot(spectrum * keep, inv_ref[0], inv_ref[1])
     real_d, imag_d = [], []
     for k in range(half):
@@ -115,7 +112,8 @@
             jax.ShapeDtypeStruct(values.shape, values.dtype),
             jax.ShapeDtypeStruct((block, length), values.dtype),
         ),
-    )(values, cuts.reshape(count, 1), jnp.asarray(twc), jnp.asarray(tws), split_table(forward),
+    )(values, (jnp.asarray(folded)[: FACTOR_ROWS // 2 + 1, None, :] <= cuts[None, :, None])
+      .astype(jnp.float32).reshape(-1, folded.shape[1]), jnp.asarray(twc), jnp.asarray(tws), split_table(forward),
       split_table(inverse), jnp.asarray(folded))
 
 def prefix_over(value, axis, before):

time: 51.7 us -> 52.7 us (1.019)
  waiting for transfers between devices: 16.1 us -> 14.4 us
  local copies, waits for them, and re-layouts: 5.97 us -> 7.47 us
  other arithmetic: 5.7 us -> 6.64 us
    all_to_all x2, waiting for transfers between devices: 15.3 us -> 13.6 us  [prefix_over(): lax.all_to_all(copies, axis, split_axis=0, concat_axis=0, tiled=True)]
    unnamed x18 -> x22, local copies, waits for them, and re-layouts: 1.07 us -> 2.38 us
    convert_element_type x0 -> x1, other arithmetic: none -> 0.93 us  [filter_rows(): return pl.pallas_call(filter_kernel, out_shape=(jax.ShapeDtypeStruct(valu...]
    slice x1 -> x2, local copies, waits for them, and re-layouts: 0.01 us -> 0.74 us  [local(): from_north[2 * rows:2 * rows + 1]]
    another operation x1 -> x0, local copies, waits for them, and re-layouts: 0.71 us -> none  [filter_rows(): cuts.reshape(count, 1)]
where the time goes in v21:
time: 52.7 us; the launch traced here: 52.1 us
  starting transfers between devices  19.4 us (37%)
  waiting for transfers between devices  14.4 us (27%)
  local copies, waits for them, and re-layouts  7.47 us (14%)
  other arithmetic  6.64 us (13%)
  Pallas kernels  3.33 us (6%)
  between operations  0.96 us (2%)
    all_to_all x2, waiting for transfers between devices, prefix_over(): lax.all_to_all(copies, axis, split_axis=0, concat_axis=0, tiled=True)  13.6 us
    all_to_all x2, starting transfers between devices, prefix_over(): lax.all_to_all(copies, axis, split_axis=0, concat_axis=0, tiled=True)  10.5 us
    ppermute x1, starting transfers between devices, local(): lax.ppermute(to_south, 'lat', [(i + 1, i) for i in range(count - 1)])  6.96 us
    pallas_call x1, Pallas kernels, filter_rows(): pl.pallas_call(filter_kernel, out_shape=(jax.ShapeDtypeStruct(values.shap...  3.33 us
    unnamed x22, local copies, waits for them, and re-layouts  2.38 us
    ppermute x1, starting transfers between devices, local(): lax.ppermute(to_north, 'lat', [(i, i + 1) for i in range(count - 1)])  1.92 us
    transpose x2, other arithmetic, local(): return tuple((jnp.transpose(v, (1, 0, 2)) for v in outputs))  1.58 us
    broadcast_in_dim x2, local copies, waits for them, and re-layouts, prefix_over(): copies = jnp.broadcast_to(value, (count, *value.shape))  1.36 us
  transfers between devices with their start and end apart: 4, of which 3 were waited for; matrix products, arithmetic and copies ran while one was open for 10% of the time, Pallas kernels for 0%

profile of v21, /device:TPU:256, one launch (start us, length us, event | category | flops | bytes accessed | tf_op | source)
XLA Modules:
  0.0 52.1 jit_solution(1085308555960508190)
XLA Ops:
  0.7 0.8 %broadcast_in_dim.44 = f32[3,8,1152]{2,1,0:T(8,128)S(1)} broadcast(f32[3,1152]{1,0:T(4,128)} %param.17), dimensions={0,2} | broadcast | bytes 124416 | tf_op jit(solution)/shard_map/broadcast_in_dim | solution.py:138
  1.4 0.1 copy-done.1
  1.6 1.0 %pad_maximum_fusion.3 = (f32[9,8,1152]{2,1,0:T(8,128)S(1)}, f32[9,8,1152]{2,1,0:T(8,128)S(1)}) fusion(f32[3,8,1152]{2,1,0:T(8,128)S(1)} %broadcast_in_dim.44, f32[3,8,1152]{2,1,0:T(8,128)S(1)} %bitcast.61, f32[3,8,1152]{2,1,0:T(8,128)} %bitcast.70, f32[3,8,1152]{2,1,0:T(8,128)} %bitcast.80), kind=kLoop, calls=%fused_computation.6 | loop fusion | flops 248832 | bytes 1105920 | tf_op jit(solution)/shard_map/concatenate | solution.py:139
  2.6 1.9 %collective-permute-start.1 = (f32[9,8,1152]{2,1,0:T(8,128)S(1)}, f32[9,8,1152]{2,1,0:T(8,128)S(1)}, u32[]{:S(2)}, u32[]{:S(2)}) collective-permute-start(f32[9,8,1152]{2,1,0:T(8,128)S(1)} %get-tuple-element.26), channel_id=1, source_target_pairs={{0,8},{8,16},{16,24},{24,32},{32,40},{40,48},{48,56},{56,64},{64,7... | collective-permute-start | bytes 995336 | tf_op jit(solution)/shard_map/ppermute | solution.py:142
  4.5 7.0 %collective-permute-start = (f32[9,8,1152]{2,1,0:T(8,128)S(1)}, f32[9,8,1152]{2,1,0:T(8,128)S(1)}, u32[]{:S(2)}, u32[]{:S(2)}) collective-permute-start(f32[9,8,1152]{2,1,0:T(8,128)S(1)} %get-tuple-element.27), channel_id=1, source_target_pairs={{8,0},{16,8},{24,16},{32,24},{40,32},{48,40},{56,48},{64,56},{72,6... | collective-permute-start | bytes 995336 | tf_op jit(solution)/shard_map/ppermute | solution.py:143
  12.5 0.2 fusion.46
  12.7 0.7 %copy-done.7 = f32[8,3,1152]{2,0,1:T(8,128)S(1)} copy-done((f32[8,3,1152]{2,0,1:T(8,128)S(1)}, f32[8,3,1152]{2,0,1:T(8,128)}, u32[]{:S(2)}) %copy-start.7) | copy-done | bytes 110616
  13.4 0.2 fusion.38
  13.6 0.7 %collective-permute-done.1 = f32[9,8,1152]{2,1,0:T(8,128)S(1)} collective-permute-done((f32[9,8,1152]{2,1,0:T(8,128)S(1)}, f32[9,8,1152]{2,1,0:T(8,128)S(1)}, u32[]{:S(2)}, u32[]{:S(2)}) %collective-permute-start.1) | collective-permute-done | bytes 331808 | tf_op jit(solution)/shard_map/ppermute | solution.py:142
  14.4 0.7 %broadcast_in_dim.47 = f32[8,4,1152]{2,1,0:T(4,128)} broadcast(f32[4,1152]{1,0:T(4,128)S(1)} %get-tuple-element.29), dimensions={1,2} | broadcast | bytes 165888 | tf_op jit(solution)/shard_map/broadcast_in_dim | solution.py:122
  15.1 7.1 %all-to-all-start = ((f32[8,4,1152]{2,1,0:T(4,128)}), f32[8,4,1152]{2,1,0:T(4,128)S(1)}, u32[]{:S(2)}, u32[]{:S(2)}) async-start(f32[8,4,1152]{2,1,0:T(4,128)} %broadcast_in_dim.47), calls=%async_computation | async-start | bytes 294912 | tf_op jit(solution)/shard_map/all_to_all | solution.py:123
  22.2 0.1 reduce_window_sum.17
  22.4 0.7 %copy-done.8 = f32[9,8,1152]{2,1,0:T(8,128)} copy-done((f32[9,8,1152]{2,1,0:T(8,128)}, f32[9,8,1152]{2,1,0:T(8,128)S(1)}, u32[]{:S(2)}) %copy-start.8) | copy-done | bytes 331800
  23.1 8.3 %all-to-all-done = f32[8,4,1152]{2,1,0:T(4,128)S(1)} async-done(((f32[8,4,1152]{2,1,0:T(4,128)}), f32[8,4,1152]{2,1,0:T(4,128)S(1)}, u32[]{:S(2)}, u32[]{:S(2)}) %all-to-all-start) | async-done | bytes 147488 | tf_op jit(solution)/shard_map/all_to_all | solution.py:123
  31.5 0.1 select_reduce_fusion.1
  31.6 0.7 %slice-done.1 = f32[1,8,1152]{2,1,0:T(8,128)S(1)} async-done(((f32[9,8,1152]{2,1,0:T(8,128)}), f32[1,8,1152]{2,1,0:T(8,128)S(1)}, s32[]{:S(2)}) %slice-start.1) | async-done | bytes 36888 | tf_op jit(solution)/shard_map/slice | solution.py:153
  32.3 0.1 fusion.57
  32.5 0.7 %broadcast_in_dim.49 = f32[8,4,1152]{2,1,0:T(4,128)} broadcast(f32[4,1152]{1,0:T(4,128)S(1)} %get-tuple-element.13), dimensions={1,2} | broadcast | bytes 165888 | tf_op jit(solution)/shard_map/broadcast_in_dim | solution.py:122
  33.2 3.4 %all-to-all-start.1 = ((f32[8,4,1152]{2,1,0:T(4,128)}), f32[8,4,1152]{2,1,0:T(4,128)S(1)}, u32[]{:S(2)}, u32[]{:S(2)}) async-start(f32[8,4,1152]{2,1,0:T(4,128)} %broadcast_in_dim.49), calls=%async_computation.1 | async-start | bytes 294912 | tf_op jit(solution)/shard_map/all_to_all | solution.py:123
  36.7 0.7 %gather_fusion = s32[13]{0:T(128)S(1)} fusion(s32[192]{0:T(256)S(1)} %copy-done, s32[1024]{0:T(1024)S(1)} %pad_clamp_fusion), kind=kCustom, calls=%fused_computation | custom fusion | bytes 156 | tf_op jit(solution)/shard_map/gather | solution.py:172
  37.6 0.6 %copy-done.10 = s32[5,256]{1,0:T(8,128)S(1)} copy-done((s32[5,256]{1,0:T(8,128)S(1)}, s32[5,256]{1,0:T(8,128)}, u32[]{:S(2)}) %copy-start.10) | copy-done | bytes 5144
  38.2 0.9 %fusion.cut_ref = f32[520,256]{1,0:T(8,128)} fusion(s32[520]{0:T(1024)S(1)} %le.26, s32[5,256]{1,0:T(8,128)S(1)} %copy-done.10), kind=kLoop, calls=%fused_computation.2 | loop fusion | flops 266240 | bytes 539680 | tf_op jit(solution)/shard_map/convert_element_type | solution.py:116
  39.1 0.1 rev.7
  39.3 0.1 reduce_window_sum.18
  39.4 0.2 rev.8
  39.6 0.8 %pad_maximum_fusion = f32[13,8,1152]{2,1,0:T(8,128)} fusion(f32[4,8,1152]{2,1,0:T(8,128)S(1)} %get-tuple-element.39, f32[3,8,1152]{2,1,0:T(8,128)S(1)} %fusion.38, f32[3,8,1152]{2,1,0:T(8,128)S(1)} %bitcast.82, f32[3,8,1152]{2,1,0:T(8,128)S(1)} %bitcast.83), kind=kLoop, calls=%fused_computation.3 | loop fusion | flops 359424 | bytes 958464 | tf_op jit(solution)/shard_map/concatenate | solution.py:168
  40.4 5.3 %all-to-all-done.1 = f32[8,4,1152]{2,1,0:T(4,128)S(1)} async-done(((f32[8,4,1152]{2,1,0:T(4,128)}), f32[8,4,1152]{2,1,0:T(4,128)S(1)}, u32[]{:S(2)}, u32[]{:S(2)}) %all-to-all-start.1) | async-done | bytes 147488 | tf_op jit(solution)/shard_map/all_to_all | solution.py:123
  45.7 0.1 select_reduce_fusion
  46.0 3.3 %shard_map.164 = (f32[104,1152]{1,0:T(8,128)}, f32[24,1152]{1,0:T(8,128)}) custom-call(f32[104,1152]{1,0:T(8,128)} %bitcast.79, f32[520,256]{1,0:T(8,128)} %fusion.cut_ref, f32[9,128]{1,0:T(8,128)} %constant.59.clone.twc_ref, f32[9,128]{1,0:T(8,128)} %constant.60.clone.tws_ref, bf16[2,256,256]{2,1,0:T(8,128)(2,1)} %constant.75.fwd_ref, ...), custom_call_target="tpu_custom_call" | custom-call | tf_op jit(solution)/shard_map/pallas_call | solution.py:109
  49.3 1.0 %fusion.7 = f32[4,8,1152]{2,1,0:T(8,128)S(1)} fusion(f32[3,8,1152]{2,1,0:T(8,128)S(1)} %bitcast.69, f32[3,8,1152]{2,1,0:T(8,128)S(1)} %get-tuple-element.21, f32[3,8,1152]{2,1,0:T(8,128)S(1)} %get-tuple-element.19, f32[104,1152]{1,0:T(8,128)} %get-tuple-element.10), kind=kLoop, calls=%fused_computation.29 | loop fusion | flops 552960 | bytes 626688 | tf_op jit(solution)/shard_map/mul | solution.py:187
  50.4 0.8 %fusion.53 = (f32[8,3,1152]{2,0,1:T(8,128)}, f32[8,3,1152]{2,0,1:T(8,128)}, f32[8,3,1152]{2,0,1:T(8,128)}) fusion(f32[4,8,1152]{2,1,0:T(8,128)S(1)} %fusion.29, f32[104,1152]{1,0:T(8,128)S(1)} %copy-done.5, f32[3]{0:T(128)S(1)} %compare_convert_fusion, f32[3,8,1151]{2,1,0:T(8,128)S(1)} %slice.239, f32[3,8,1]{2,1,0:T(8,128)S(1)} %slice.238), kind=kLoop, calls=%fused_computation.97 | loop fusion | flops 221184 | bytes 884748 | tf_op jit(solution)/shard_map/transpose | solution.py:196
  51.4 0.8 %fusion.33 = (f32[8,3,1152]{2,0,1:T(8,128)}, f32[8,3,1152]{2,0,1:T(8,128)}) fusion(f32[4,8,1152]{2,1,0:T(8,128)S(1)} %fusion.7, f32[3,8,1]{2,1,0:T(8,128)S(1)} %slice-done, f32[3,8,1151]{2,1,0:T(8,128)S(1)} %slice.307, f32[3,8,1152]{2,1,0:T(8,128)S(1)} %copy-done.4, f32[24,1152]{1,0:T(8,128)S(1)} %copy-done.9, f32[104,1152]{1,0:T(8,128)S(1)} %copy-done.5, ...), kind=kLoop, calls=%fused_computation.65 | loop fusion | flops 387072 | bytes 1327104 | tf_op jit(solution)/shard_map/transpose | solution.py:196
  (54 shorter events, 1.7 us)
Async XLA Ops:
  0.6 36.0 %copy-start = (s32[192]{0:T(256)S(1)}, s32[192]{0:T(256)}, u32[]{:S(2)}) copy-start(s32[192]{0:T(256)} %param.18) | copy-start | bytes 2308
  0.6 0.9 %copy-start.1 = (f32[8,3,1152]{2,0,1:T(8,128)S(1)}, f32[8,3,1152]{2,0,1:T(8,128)}, u32[]{:S(2)}) copy-start(f32[8,3,1152]{2,0,1:T(8,128)} %param.16) | copy-start | bytes 331780
  1.6 9.9 %copy-start.2 = (f32[8,3,1152]{2,0,1:T(8,128)S(1)}, f32[8,3,1152]{2,0,1:T(8,128)}, u32[]{:S(2)}) copy-start(f32[8,3,1152]{2,0,1:T(8,128)} %param.15) | copy-start | bytes 331780
  2.6 11.8 %collective-permute-start.1 = (f32[9,8,1152]{2,1,0:T(8,128)S(1)}, f32[9,8,1152]{2,1,0:T(8,128)S(1)}, u32[]{:S(2)}, u32[]{:S(2)}) collective-permute-start(f32[9,8,1152]{2,1,0:T(8,128)S(1)} %get-tuple-element.26), channel_id=1, source_target_pairs={{0,8},{8,16},{16,24},{24,32},{32,40},{40,48},{48,56},{56,64},{64,7... | collective-permute-start | bytes 995336 | tf_op jit(solution)/shard_map/ppermute | solution.py:142
  4.5 17.8 %collective-permute-start = (f32[9,8,1152]{2,1,0:T(8,128)S(1)}, f32[9,8,1152]{2,1,0:T(8,128)S(1)}, u32[]{:S(2)}, u32[]{:S(2)}) collective-permute-start(f32[9,8,1152]{2,1,0:T(8,128)S(1)} %get-tuple-element.27), channel_id=1, source_target_pairs={{8,0},{16,8},{24,16},{32,24},{40,32},{48,40},{56,48},{64,56},{72,6... | collective-permute-start | bytes 995336 | tf_op jit(solution)/shard_map/ppermute | solution.py:143
  12.5 0.9 %copy-start.7 = (f32[8,3,1152]{2,0,1:T(8,128)S(1)}, f32[8,3,1152]{2,0,1:T(8,128)}, u32[]{:S(2)}) copy-start(f32[8,3,1152]{2,0,1:T(8,128)} %param.13) | copy-start | bytes 331780
  12.7 23.9 %copy-start.3 = (f32[3,8,1152]{2,1,0:T(8,128)}, f32[3,8,1152]{2,1,0:T(8,128)S(1)}, u32[]{:S(2)}) copy-start(f32[3,8,1152]{2,1,0:T(8,128)S(1)} %fusion.46) | copy-start | bytes 331780
  15.1 16.4 %all-to-all-start = ((f32[8,4,1152]{2,1,0:T(4,128)}), f32[8,4,1152]{2,1,0:T(4,128)S(1)}, u32[]{:S(2)}, u32[]{:S(2)}) async-start(f32[8,4,1152]{2,1,0:T(4,128)} %broadcast_in_dim.47), calls=%async_computation | async-start | bytes 294912 | tf_op jit(solution)/shard_map/all_to_all | solution.py:123
  22.3 0.7 %copy-start.8 = (f32[9,8,1152]{2,1,0:T(8,128)}, f32[9,8,1152]{2,1,0:T(8,128)S(1)}, u32[]{:S(2)}) copy-start(f32[9,8,1152]{2,1,0:T(8,128)S(1)} %collective-permute-done) | copy-start | bytes 995332
  23.1 8.5 %copy-start.6 = (f32[8,3,1152]{2,0,1:T(8,128)S(1)}, f32[8,3,1152]{2,0,1:T(8,128)}, u32[]{:S(2)}) copy-start(f32[8,3,1152]{2,0,1:T(8,128)} %param.14) | copy-start | bytes 331780
  31.6 0.8 %slice-start.1 = ((f32[9,8,1152]{2,1,0:T(8,128)}), f32[1,8,1152]{2,1,0:T(8,128)S(1)}, s32[]{:S(2)}) async-start(f32[9,8,1152]{2,1,0:T(8,128)} %copy-done.8), calls=%async_computation.3 | async-start | bytes 73728 | tf_op jit(solution)/shard_map/slice | solution.py:153
  33.2 12.6 %all-to-all-start.1 = ((f32[8,4,1152]{2,1,0:T(4,128)}), f32[8,4,1152]{2,1,0:T(4,128)S(1)}, u32[]{:S(2)}, u32[]{:S(2)}) async-start(f32[8,4,1152]{2,1,0:T(4,128)} %broadcast_in_dim.49), calls=%async_computation.1 | async-start | bytes 294912 | tf_op jit(solution)/shard_map/all_to_all | solution.py:123
  37.5 0.7 %copy-start.10 = (s32[5,256]{1,0:T(8,128)S(1)}, s32[5,256]{1,0:T(8,128)}, u32[]{:S(2)}) copy-start(s32[5,256]{1,0:T(8,128)} %constant.68) | copy-start | bytes 15364
  49.3 1.1 %copy-start.5 = (f32[104,1152]{1,0:T(8,128)S(1)}, f32[104,1152]{1,0:T(8,128)}, u32[]{:S(2)}) copy-start(f32[104,1152]{1,0:T(8,128)} %get-tuple-element.10) | copy-start | bytes 1437700
  50.4 0.9 %copy-start.4 = (f32[3,8,1152]{2,1,0:T(8,128)S(1)}, f32[3,8,1152]{2,1,0:T(8,128)}, u32[]{:S(2)}) copy-start(f32[3,8,1152]{2,1,0:T(8,128)} %copy-done.3) | copy-start | bytes 331780
  50.4 0.9 %slice-start = ((f32[3,8,1152]{2,1,0:T(8,128)}), f32[3,8,1]{2,1,0:T(8,128)S(1)}, s32[]{:S(2)}) async-start(f32[3,8,1152]{2,1,0:T(8,128)} %copy-done.3), calls=%async_computation.2 | async-start | bytes 24576 | tf_op jit(solution)/shard_map/jit(_roll_static)/slice | solution.py:186
  50.4 1.0 %copy-start.9 = (f32[24,1152]{1,0:T(8,128)S(1)}, f32[24,1152]{1,0:T(8,128)}, u32[]{:S(2)}) copy-start(f32[24,1152]{1,0:T(8,128)} %get-tuple-element.12) | copy-start | bytes 331780
